TPU v7x, 32 devices: a whole 2x2x4 slice. The times are simulated.
32 devices in a mesh: gz: 8 (over z, y), xy: 4 (over x, core).
Axes of the slice: x: 2, y: 2, z: 4, core: 2. Of those that a mesh axis runs over, the one named last changes fastest.
Arguments:
- volume: float32 [128, 128, 128], P('gz', 'xy'), may hold values from -6 to 6
- owners: int32 [4, 32, 1], P('xy', 'gz'), may hold values from 0 to 7; in each aligned block of 4 rows (0 to 3, 4 to 7, ..., all dimensions but the last counted through in order) at most 2 rows name the same one
Outputs:
- denoised: float32 [128, 128, 128], P('gz', 'xy')
- routed: float32 [4, 128, 128, 128], P('xy', 'gz')
Inputs may be any that keep to these rules, and one draw needn't show every extreme that they name: `owners`: among the 4 blocks of one device no destination is named more than 2 times, a bound that some block reaches.
All inputs are finite; a program needn't handle non-finite values.
Results may differ from a plain program's by a relative error of at most 0.0003.
Values sent between devices are 32-bit elements; how exact they have to be, the bound alone decides.
No kernel may reach another device: no remote copies, remote signals or barrier semaphores. Data moves between devices by JAX's collectives and lax.ppermute only.
A program may use at most 64 MiB of HBM per device.

v0:
```python
import jax
import jax.numpy as jnp
from jax import lax
from jax.sharding import PartitionSpec as P

STEPS = 2
MOST = 2
BLOCK_ROWS = 128


TIME_STEP = 30.0
CONTRAST = 4.0


def with_halo(block, sides, width):
    for axis, dim in sides:
        count = lax.axis_size(axis)
        forward = [(i, i + 1) for i in range(count - 1)]
        backward = [(target, source) for source, target in forward]
        low = lax.ppermute(
            lax.slice_in_dim(block, block.shape[dim] - width, None, axis=dim), axis, forward
        )
        high = lax.ppermute(lax.slice_in_dim(block, 0, width, axis=dim), axis, backward)
        block = jnp.concatenate([low, block, high], axis=dim)
    return block


def shifted(field, stride, line_axis, fill, before):
    length = field.shape[line_axis]
    shape = list(field.shape)
    shape[line_axis] = stride
    padding = jnp.full(tuple(shape), fill, field.dtype)
    if before:
        return jnp.concatenate(
            [padding, lax.slice_in_dim(field, 0, length - stride, axis=line_axis)], axis=line_axis
        )
    return jnp.concatenate(
        [lax.slice_in_dim(field, stride, length, axis=line_axis), padding], axis=line_axis
    )


def cyclic_solve(low_diag, main_diag, high_diag, right_side, line_axis, side_axis):
    length = main_diag.shape[line_axis]
    stride = 1
    while stride < length:
        low_prev = shifted(low_diag, stride, line_axis, 0.0, True)
        main_prev = shifted(main_diag, stride, line_axis, 1.0, True)
        high_prev = shifted(high_diag, stride, line_axis, 0.0, True)
        side_prev = shifted(right_side, stride, side_axis, 0.0, True)
        low_next = shifted(low_diag, stride, line_axis, 0.0, False)
        main_next = shifted(main_diag, stride, line_axis, 1.0, False)
        high_next = shifted(high_diag, stride, line_axis, 0.0, False)
        side_next = shifted(right_side, stride, side_axis, 0.0, False)
        factor_low = -low_diag / main_prev
        factor_high = -high_diag / main_next
        main_diag = main_diag + factor_low * high_prev + factor_high * low_next
        right_side = right_side + factor_low * side_prev + factor_high * side_next
        low_diag = factor_low * low_prev
        high_diag = factor_high * high_next
        stride = stride * 2
    return right_side / main_diag


def coefficients(g_line, line_axis, has_before, has_after):
    length = g_line.shape[line_axis] - 2
    weight = 0.5 * (
        lax.slice_in_dim(g_line, 0, length + 1, axis=line_axis)
        + lax.slice_in_dim(g_line, 1, length + 2, axis=line_axis)
    )
    shape = [1] * weight.ndim
    shape[line_axis] = length + 1
    edge_index = lax.broadcasted_iota(jnp.int32, tuple(shape), line_axis)
    keep_mask = jnp.where(edge_index == 0, has_before, 1.0) * jnp.where(
        edge_index == length, has_after, 1.0
    )
    weight = weight * keep_mask
    low_diag = -3.0 * TIME_STEP * lax.slice_in_dim(weight, 0, length, axis=line_axis)
    high_diag = -3.0 * TIME_STEP * lax.slice_in_dim(weight, 1, length + 1, axis=line_axis)
    main_diag = 1.0 - low_diag - high_diag
    return (low_diag, main_diag, high_diag)


def pad_zero(field, line_axis):
    widths = [(0, 0)] * field.ndim
    widths[line_axis] = (1, 1)
    return jnp.pad(field, widths)


def diffusivity(extended, z_start, z_total, y_start, y_total):
    center = extended[1:-1, 1:-1]
    z_index = z_start - 1 + lax.broadcasted_iota(jnp.int32, (center.shape[0], 1, 1), 0)
    z_next = jnp.where(z_index + 1 < z_total, extended[2:, 1:-1], center)
    z_prev = jnp.where(z_index >= 1, extended[:-2, 1:-1], center)
    y_index = y_start - 1 + lax.broadcasted_iota(jnp.int32, (1, center.shape[1], 1), 1)
    y_next = jnp.where(y_index + 1 < y_total, extended[1:-1, 2:], center)
    y_prev = jnp.where(y_index >= 1, extended[1:-1, :-2], center)
    x_next = jnp.concatenate([center[:, :, 1:], center[:, :, -1:]], axis=2)
    x_prev = jnp.concatenate([center[:, :, :1], center[:, :, :-1]], axis=2)
    slope_z = (z_next - z_prev) * 0.5
    slope_y = (y_next - y_prev) * 0.5
    slope_x = (x_next - x_prev) * 0.5
    squares = slope_z * slope_z + slope_y * slope_y + slope_x * slope_x
    return 1.0 / (1.0 + squares / CONTRAST)


def line_solve(g_field, right_side, line_axis):
    low_diag, main_diag, high_diag = coefficients(pad_zero(g_field, line_axis), line_axis, 0.0, 0.0)
    return cyclic_solve(low_diag, main_diag, high_diag, right_side, line_axis, line_axis)


def interface_solve(gathered, position, chain_size):
    parts = tuple((gathered[:, k] for k in range(6)))
    zeros = jnp.zeros_like(parts[0][0])

    def forward(carry, item):
        prev_p, prev_q = carry
        head_y, head_v, head_w, tail_y, tail_v, tail_w = item
        denom = 1.0 - head_v * prev_q
        first_r = (head_y + head_v * prev_p) / denom
        first_s = head_w / denom
        new_p = tail_y + tail_v * (prev_p + prev_q * first_r)
        new_q = tail_v * prev_q * first_s + tail_w
        return ((new_p, new_q), (first_r, first_s, new_p, new_q))

    carry_out, sweep = lax.scan(forward, (zeros, zeros), parts)

    def backward(later_f, item):
        first_r, first_s, new_p, new_q = item
        head_value = first_r + first_s * later_f
        return (head_value, (head_value, new_p + new_q * later_f))

    final_f, (head_values, tail_values) = lax.scan(backward, zeros, sweep, reverse=True)
    left_pick = lax.dynamic_index_in_dim(
        tail_values, jnp.maximum(position - 1, 0), 0, keepdims=False
    )
    right_pick = lax.dynamic_index_in_dim(
        head_values, jnp.minimum(position + 1, chain_size - 1), 0, keepdims=False
    )
    left_value = jnp.where(position > 0, left_pick, 0.0)
    right_value = jnp.where(position < chain_size - 1, right_pick, 0.0)
    return (left_value, right_value)


def split_solve(g_line, right_side, line_axis, position, chain_size, gather_links):
    has_before = (position > 0).astype(jnp.float32)
    has_after = (position < chain_size - 1).astype(jnp.float32)
    low_diag, main_diag, high_diag = coefficients(g_line, line_axis, has_before, has_after)
    length = main_diag.shape[line_axis]
    shape = [1] * 3
    shape[line_axis] = length
    cell_index = lax.broadcasted_iota(jnp.int32, tuple(shape), line_axis)
    first_link = lax.slice_in_dim(low_diag, 0, 1, axis=line_axis)
    last_link = lax.slice_in_dim(high_diag, length - 1, length, axis=line_axis)
    low_local = jnp.where(cell_index == 0, 0.0, low_diag)
    high_local = jnp.where(cell_index == length - 1, 0.0, high_diag)
    left_side = jnp.where(cell_index == 0, -first_link, 0.0)
    right_part = jnp.where(cell_index == length - 1, -last_link, 0.0)
    stacked = jnp.stack([right_side, left_side, right_part])
    solved = cyclic_solve(low_local, main_diag, high_local, stacked, line_axis, line_axis + 1)
    head = lax.index_in_dim(solved, 0, line_axis + 1, keepdims=False)
    tail = lax.index_in_dim(solved, length - 1, line_axis + 1, keepdims=False)
    packed = jnp.concatenate([head, tail], axis=0)
    gathered = gather_links(packed[None])
    left_value, right_value = interface_solve(gathered, position, chain_size)
    return (
        solved[0]
        + solved[1] * jnp.expand_dims(left_value, line_axis)
        + solved[2] * jnp.expand_dims(right_value, line_axis)
    )


def gather_y(packed):
    return lax.all_gather(packed, "xy", axis=0, tiled=True)


def on_device(volume, owners):
    field = volume
    depth, height, width = field.shape
    z_rank = lax.axis_index("gz")
    z_count = lax.axis_size("gz")
    y_rank = lax.axis_index("xy")
    y_count = lax.axis_size("xy")
    for section_index in range(STEPS):
        extended = with_halo(field, (("gz", 0), ("xy", 1)), 2)
        g_ext = diffusivity(
            extended, z_rank * depth, depth * z_count, y_rank * height, height * y_count
        )
        g_own = g_ext[1:-1, 1:-1]
        along_x = line_solve(g_own, field, 2)
        along_y = split_solve(g_ext[1:-1], field, 1, y_rank, y_count, gather_y)
        moved_g, moved_field = (
            lax.all_to_all(g_own, "gz", split_axis=1, concat_axis=0, tiled=True),
            lax.all_to_all(field, "gz", split_axis=1, concat_axis=0, tiled=True),
        )
        along_z = lax.all_to_all(
            line_solve(moved_g, moved_field, 0), "gz", split_axis=0, concat_axis=1, tiled=True
        )
        field = (along_x + along_y + along_z) / 3.0
    blocks = field.reshape(-1, BLOCK_ROWS, width)
    targets = owners.reshape(-1)
    block_count = targets.shape[0]
    same = targets[:, None] == targets[None, :]
    block_iota = jnp.arange(block_count, dtype=jnp.int32)
    earlier = block_iota[:, None] < block_iota[None, :]
    order_rank = jnp.sum((same & earlier).astype(jnp.int32), axis=0)
    slot_index = targets * MOST + order_rank
    outgoing = (
        jnp.zeros((z_count * MOST, BLOCK_ROWS, width), field.dtype).at[slot_index].set(blocks)
    )
    incoming = lax.all_to_all(outgoing, "gz", split_axis=0, concat_axis=0, tiled=True)
    return (field, incoming.reshape(1, z_count * MOST, BLOCK_ROWS, width))


def solution(mesh):
    in_specs = (P("gz", "xy", None), P("xy", "gz", None))
    out_specs = (P("gz", "xy", None), P("xy", "gz", None, None))
    return jax.shard_map(
        on_device, mesh=mesh, in_specs=in_specs, out_specs=out_specs, check_vma=False
    )
```

profile of v0, /device:TPU:0, one launch (start us, length us, event | category | flops | bytes accessed | tf_op | source)
XLA Modules:
  0.0 191.8 jit_solution(1808513915157954361)
XLA Ops:
  0.6 1.8 copy.129
  2.4 7.3 %all-to-all-start = ((f32[16,32,128]{2,0,1:T(8,128)}), f32[16,32,128]{2,0,1:T(8,128)S(1)}, u32[]{:S(2)}, u32[]{:S(2)}) async-start(f32[16,32,128]{2,0,1:T(8,128)} %copy.129), calls=%async_computation | async-start | bytes 524288 | tf_op jit(solution)/shard_map/all_to_all | solution.py:193
  9.7 1.0 fusion.225
  10.8 1.3 collective-permute-start.1
  12.1 4.6 %collective-permute-start = (f32[2,32,128]{2,0,1:T(2,128)S(1)}, f32[2,32,128]{2,0,1:T(2,128)S(1)}, u32[]{:S(2)}, u32[]{:S(2)}) collective-permute-start(f32[2,32,128]{2,0,1:T(2,128)S(1)} %get-tuple-element.1167), channel_id=1, source_target_pairs={{0,4},{4,8},{8,12},{12,16},{16,20},{20,24},{24,28},{1,5},{5,9},{9,... | collective-permute-start | bytes 98312 | tf_op jit(solution)/shard_map/ppermute | solution.py:20
  16.6 1.2 fusion.185
  18.6 0.8 pad_maximum_fusion.21
  19.4 1.3 collective-permute-start.2
  20.7 1.3 collective-permute-start.3
  22.0 3.5 %collective-permute-done.3 = f32[20,2,128]{2,0,1:T(8,128)S(1)} collective-permute-done((f32[20,2,128]{2,0,1:T(8,128)S(1)}, f32[20,2,128]{2,0,1:T(8,128)S(1)}, u32[]{:S(2)}, u32[]{:S(2)}) %collective-permute-start.3) | collective-permute-done | bytes 20512 | tf_op jit(solution)/shard_map/ppermute | solution.py:23
  25.5 1.0 pad_maximum_fusion.2
  26.9 1.6 fusion.39
  29.7 1.2 fusion.15
  31.5 0.8 copy-done.1
  41.8 6.8 %all-gather = f32[24,16,128]{2,1,0:T(8,128)S(1)} all-gather(f32[6,16,128]{2,1,0:T(8,128)S(1)} %pad_maximum_fusion.16), channel_id=2, replica_groups=mesh['gz'=8,'xy'=4] {'xy'}, dimensions={0}, use_global_device_ids=true | all-gather | bytes 245760 | tf_op jit(solution)/shard_map/all_gather | solution.py:173
  49.1 7.3 %all-to-all-start.1 = ((f32[16,32,128]{2,0,1:T(8,128)}), f32[16,32,128]{2,0,1:T(8,128)S(1)}, u32[]{:S(2)}, u32[]{:S(2)}) async-start(f32[16,32,128]{2,0,1:T(8,128)} %slice.1507), calls=%async_computation.1 | async-start | bytes 524288 | tf_op jit(solution)/shard_map/all_to_all | solution.py:192
  56.5 9.1 %all-to-all-done.1 = f32[16,32,128]{2,0,1:T(8,128)S(1)} async-done(((f32[16,32,128]{2,0,1:T(8,128)}), f32[16,32,128]{2,0,1:T(8,128)S(1)}, u32[]{:S(2)}, u32[]{:S(2)}) %all-to-all-start.1) | async-done | bytes 262176 | tf_op jit(solution)/shard_map/all_to_all | solution.py:192
  69.1 0.9 copy.142
  69.9 3.6 %all-to-all-start.2 = ((f32[128,4,128]{2,1,0:T(4,128)}), f32[128,4,128]{2,1,0:T(4,128)S(1)}, u32[]{:S(2)}, u32[]{:S(2)}) async-start(f32[128,4,128]{2,1,0:T(4,128)} %copy.142), calls=%async_computation.2 | async-start | bytes 524288 | tf_op jit(solution)/shard_map/all_to_all | solution.py:195
  73.7 0.9 fusion.160
  74.5 7.6 %all-to-all-done.2 = f32[128,4,128]{2,1,0:T(4,128)S(1)} async-done(((f32[128,4,128]{2,1,0:T(4,128)}), f32[128,4,128]{2,1,0:T(4,128)S(1)}, u32[]{:S(2)}, u32[]{:S(2)}) %all-to-all-start.2) | async-done | bytes 262176 | tf_op jit(solution)/shard_map/all_to_all | solution.py:195
  82.2 0.9 copy-done.2
  83.1 1.0 fusion.61
  84.1 1.0 fusion.159
  85.1 1.3 collective-permute-start.5
  86.4 4.5 %collective-permute-start.4 = (f32[2,32,128]{2,0,1:T(2,128)S(1)}, f32[2,32,128]{2,0,1:T(2,128)S(1)}, u32[]{:S(2)}, u32[]{:S(2)}) collective-permute-start(f32[2,32,128]{2,0,1:T(2,128)S(1)} %get-tuple-element.1035), channel_id=1, source_target_pairs={{0,4},{4,8},{8,12},{12,16},{16,20},{20,24},{24,28},{1,5},{5,9},{9,... | collective-permute-start | bytes 98312 | tf_op jit(solution)/shard_map/ppermute | solution.py:20
  91.0 3.7 %all-to-all-start.3 = ((f32[16,32,128]{2,0,1:T(8,128)}), f32[16,32,128]{2,0,1:T(8,128)S(1)}, u32[]{:S(2)}, u32[]{:S(2)}) async-start(f32[16,32,128]{2,0,1:T(8,128)} %fusion.61), calls=%async_computation.3 | async-start | bytes 524288 | tf_op jit(solution)/shard_map/all_to_all | solution.py:193
  94.7 0.8 pad_maximum_fusion.18
  95.4 1.3 collective-permute-start.6
  96.7 1.3 collective-permute-start.7
  98.0 1.2 fusion.119
  99.2 2.7 %collective-permute-done.7 = f32[20,2,128]{2,0,1:T(8,128)S(1)} collective-permute-done((f32[20,2,128]{2,0,1:T(8,128)S(1)}, f32[20,2,128]{2,0,1:T(8,128)S(1)}, u32[]{:S(2)}, u32[]{:S(2)}) %collective-permute-start.7) | collective-permute-done | bytes 20512 | tf_op jit(solution)/shard_map/ppermute | solution.py:23
  101.9 1.0 pad_maximum_fusion.3
  103.3 1.6 fusion.26
  106.2 1.0 pad_maximum_fusion.1
  107.5 1.2 multiply_add_fusion.3
  110.9 1.2 fusion.17
  112.7 1.3 multiply_add_fusion.35
  120.2 6.8 %all-gather.1 = f32[24,16,128]{2,1,0:T(8,128)S(1)} all-gather(f32[6,16,128]{2,1,0:T(8,128)S(1)} %pad_maximum_fusion.17), channel_id=3, replica_groups=mesh['gz'=8,'xy'=4] {'xy'}, dimensions={0}, use_global_device_ids=true | all-gather | bytes 245760 | tf_op jit(solution)/shard_map/all_gather | solution.py:173
  127.5 6.0 %all-to-all-start.4 = ((f32[16,32,128]{2,0,1:T(8,128)}), f32[16,32,128]{2,0,1:T(8,128)S(1)}, u32[]{:S(2)}, u32[]{:S(2)}) async-start(f32[16,32,128]{2,0,1:T(8,128)} %slice.1684), calls=%async_computation.4 | async-start | bytes 524288 | tf_op jit(solution)/shard_map/all_to_all | solution.py:192
  133.6 9.1 %all-to-all-done.4 = f32[16,32,128]{2,0,1:T(8,128)S(1)} async-done(((f32[16,32,128]{2,0,1:T(8,128)}), f32[16,32,128]{2,0,1:T(8,128)S(1)}, u32[]{:S(2)}, u32[]{:S(2)}) %all-to-all-start.4) | async-done | bytes 262176 | tf_op jit(solution)/shard_map/all_to_all | solution.py:192
  146.1 0.9 copy.154
  147.0 3.6 %all-to-all-start.5 = ((f32[128,4,128]{2,1,0:T(4,128)}), f32[128,4,128]{2,1,0:T(4,128)S(1)}, u32[]{:S(2)}, u32[]{:S(2)}) async-start(f32[128,4,128]{2,1,0:T(4,128)} %copy.154), calls=%async_computation.5 | async-start | bytes 524288 | tf_op jit(solution)/shard_map/all_to_all | solution.py:195
  150.7 0.9 fusion.94
  151.6 7.5 %all-to-all-done.5 = f32[128,4,128]{2,1,0:T(4,128)S(1)} async-done(((f32[128,4,128]{2,1,0:T(4,128)}), f32[128,4,128]{2,1,0:T(4,128)S(1)}, u32[]{:S(2)}, u32[]{:S(2)}) %all-to-all-start.5) | async-done | bytes 262176 | tf_op jit(solution)/shard_map/all_to_all | solution.py:195
  159.2 0.9 copy-done.3
  162.0 28.8 %all_to_all.113 = f32[16,128,128]{2,1,0:T(8,128)S(1)} all-to-all(f32[16,128,128]{2,1,0:T(8,128)S(1)} %scatter_fusion), channel_id=1, replica_groups=mesh['gz'=8,'xy'=4] {'gz'}, dimensions={0} | all-to-all | bytes 2097152 | tf_op jit(solution)/shard_map/all_to_all | solution.py:210
  190.8 1.0 copy.255
  (335 shorter events, 31.8 us)
Async XLA Ops:
  2.4 46.6 %all-to-all-start = ((f32[16,32,128]{2,0,1:T(8,128)}), f32[16,32,128]{2,0,1:T(8,128)S(1)}, u32[]{:S(2)}, u32[]{:S(2)}) async-start(f32[16,32,128]{2,0,1:T(8,128)} %copy.129), calls=%async_computation | async-start | bytes 524288 | tf_op jit(solution)/shard_map/all_to_all | solution.py:193
  10.8 7.8 %collective-permute-start.1 = (f32[2,32,128]{2,0,1:T(2,128)S(1)}, f32[2,32,128]{2,0,1:T(2,128)S(1)}, u32[]{:S(2)}, u32[]{:S(2)}) collective-permute-start(f32[2,32,128]{2,0,1:T(2,128)S(1)} %get-tuple-element.1168), channel_id=1, source_target_pairs={{4,0},{8,4},{12,8},{16,12},{20,16},{24,20},{28,24},{5,1},{9,5},{13... | collective-permute-start | bytes 98312 | tf_op jit(solution)/shard_map/ppermute | solution.py:23
  12.1 6.6 %collective-permute-start = (f32[2,32,128]{2,0,1:T(2,128)S(1)}, f32[2,32,128]{2,0,1:T(2,128)S(1)}, u32[]{:S(2)}, u32[]{:S(2)}) collective-permute-start(f32[2,32,128]{2,0,1:T(2,128)S(1)} %get-tuple-element.1167), channel_id=1, source_target_pairs={{0,4},{4,8},{8,12},{12,16},{16,20},{20,24},{24,28},{1,5},{5,9},{9,... | collective-permute-start | bytes 98312 | tf_op jit(solution)/shard_map/ppermute | solution.py:20
  17.8 0.7 copy-start.5
  19.4 2.7 %collective-permute-start.2 = (f32[20,2,128]{2,0,1:T(8,128)S(1)}, f32[20,2,128]{2,0,1:T(8,128)S(1)}, u32[]{:S(2)}, u32[]{:S(2)}) collective-permute-start(f32[20,2,128]{2,0,1:T(8,128)S(1)} %get-tuple-element.887), channel_id=1, source_target_pairs={{0,1},{1,2},{2,3},{4,5},{5,6},{6,7},{8,9},{9,10},{10,11},{12,13},{... | collective-permute-start | bytes 61448 | tf_op jit(solution)/shard_map/ppermute | solution.py:20
  20.7 4.8 %collective-permute-start.3 = (f32[20,2,128]{2,0,1:T(8,128)S(1)}, f32[20,2,128]{2,0,1:T(8,128)S(1)}, u32[]{:S(2)}, u32[]{:S(2)}) collective-permute-start(f32[20,2,128]{2,0,1:T(8,128)S(1)} %get-tuple-element.886), channel_id=1, source_target_pairs={{1,0},{2,1},{3,2},{5,4},{6,5},{7,6},{9,8},{10,9},{11,10},{13,12},{... | collective-permute-start | bytes 61448 | tf_op jit(solution)/shard_map/ppermute | solution.py:23
  31.4 1.0 copy-start.1
  49.1 16.6 %all-to-all-start.1 = ((f32[16,32,128]{2,0,1:T(8,128)}), f32[16,32,128]{2,0,1:T(8,128)S(1)}, u32[]{:S(2)}, u32[]{:S(2)}) async-start(f32[16,32,128]{2,0,1:T(8,128)} %slice.1507), calls=%async_computation.1 | async-start | bytes 524288 | tf_op jit(solution)/shard_map/all_to_all | solution.py:192
  69.9 12.2 %all-to-all-start.2 = ((f32[128,4,128]{2,1,0:T(4,128)}), f32[128,4,128]{2,1,0:T(4,128)S(1)}, u32[]{:S(2)}, u32[]{:S(2)}) async-start(f32[128,4,128]{2,1,0:T(4,128)} %copy.142), calls=%async_computation.2 | async-start | bytes 524288 | tf_op jit(solution)/shard_map/all_to_all | solution.py:195
  82.1 1.0 copy-start.2
  85.1 9.6 %collective-permute-start.5 = (f32[2,32,128]{2,0,1:T(2,128)S(1)}, f32[2,32,128]{2,0,1:T(2,128)S(1)}, u32[]{:S(2)}, u32[]{:S(2)}) collective-permute-start(f32[2,32,128]{2,0,1:T(2,128)S(1)} %get-tuple-element.1036), channel_id=1, source_target_pairs={{4,0},{8,4},{12,8},{16,12},{20,16},{24,20},{28,24},{5,1},{9,5},{13... | collective-permute-start | bytes 98312 | tf_op jit(solution)/shard_map/ppermute | solution.py:23
  86.4 8.3 %collective-permute-start.4 = (f32[2,32,128]{2,0,1:T(2,128)S(1)}, f32[2,32,128]{2,0,1:T(2,128)S(1)}, u32[]{:S(2)}, u32[]{:S(2)}) collective-permute-start(f32[2,32,128]{2,0,1:T(2,128)S(1)} %get-tuple-element.1035), channel_id=1, source_target_pairs={{0,4},{4,8},{8,12},{12,16},{16,20},{20,24},{24,28},{1,5},{5,9},{9,... | collective-permute-start | bytes 98312 | tf_op jit(solution)/shard_map/ppermute | solution.py:20
  91.0 36.5 %all-to-all-start.3 = ((f32[16,32,128]{2,0,1:T(8,128)}), f32[16,32,128]{2,0,1:T(8,128)S(1)}, u32[]{:S(2)}, u32[]{:S(2)}) async-start(f32[16,32,128]{2,0,1:T(8,128)} %fusion.61), calls=%async_computation.3 | async-start | bytes 524288 | tf_op jit(solution)/shard_map/all_to_all | solution.py:193
  95.4 3.8 %collective-permute-start.6 = (f32[20,2,128]{2,0,1:T(8,128)S(1)}, f32[20,2,128]{2,0,1:T(8,128)S(1)}, u32[]{:S(2)}, u32[]{:S(2)}) collective-permute-start(f32[20,2,128]{2,0,1:T(8,128)S(1)} %get-tuple-element.885), channel_id=1, source_target_pairs={{0,1},{1,2},{2,3},{4,5},{5,6},{6,7},{8,9},{9,10},{10,11},{12,13},{... | collective-permute-start | bytes 61448 | tf_op jit(solution)/shard_map/ppermute | solution.py:20
  96.7 5.2 %collective-permute-start.7 = (f32[20,2,128]{2,0,1:T(8,128)S(1)}, f32[20,2,128]{2,0,1:T(8,128)S(1)}, u32[]{:S(2)}, u32[]{:S(2)}) collective-permute-start(f32[20,2,128]{2,0,1:T(8,128)S(1)} %get-tuple-element.884), channel_id=1, source_target_pairs={{1,0},{2,1},{3,2},{5,4},{6,5},{7,6},{9,8},{10,9},{11,10},{13,12},{... | collective-permute-start | bytes 61448 | tf_op jit(solution)/shard_map/ppermute | solution.py:23
  127.5 15.2 %all-to-all-start.4 = ((f32[16,32,128]{2,0,1:T(8,128)}), f32[16,32,128]{2,0,1:T(8,128)S(1)}, u32[]{:S(2)}, u32[]{:S(2)}) async-start(f32[16,32,128]{2,0,1:T(8,128)} %slice.1684), calls=%async_computation.4 | async-start | bytes 524288 | tf_op jit(solution)/shard_map/all_to_all | solution.py:192
  147.0 12.2 %all-to-all-start.5 = ((f32[128,4,128]{2,1,0:T(4,128)}), f32[128,4,128]{2,1,0:T(4,128)S(1)}, u32[]{:S(2)}, u32[]{:S(2)}) async-start(f32[128,4,128]{2,1,0:T(4,128)} %copy.154), calls=%async_computation.5 | async-start | bytes 524288 | tf_op jit(solution)/shard_map/all_to_all | solution.py:195
  159.2 1.0 copy-start.3
  159.2 1.0 copy-start.4
  160.6 0.7 copy-start
where the time goes:
time: 193 us; the launch traced here: 192 us
  starting transfers between devices  48.3 us (25%)
  blocking collectives  42.4 us (22%)
  waiting for transfers between devices  39.6 us (21%)
  other arithmetic  30.1 us (16%)
  local copies, waits for them, and re-layouts  28 us (15%)
  between operations  2.95 us (2%)
    all_to_all x1, blocking collectives, on_device(): lax.all_to_all(outgoing, 'gz', split_axis=0, concat_axis=0, tiled=True)  28.8 us
    all_to_all x2, waiting for transfers between devices, on_device(): lax.all_to_all(g_own, 'gz', split_axis=1, concat_axis=0, tiled=True)  18.3 us
    all_to_all x2, waiting for transfers between devices, on_device(): lax.all_to_all(line_solve(moved_g, moved_field, 0), 'gz', split_axis=0, c...  15.1 us
    all_gather x2, blocking collectives, gather_y(): return lax.all_gather(packed, 'xy', axis=0, tiled=True)  13.7 us
    all_to_all x2, starting transfers between devices, on_device(): lax.all_to_all(g_own, 'gz', split_axis=1, concat_axis=0, tiled=True)  13.3 us
    ppermute x4, starting transfers between devices, with_halo(): lax.ppermute(lax.slice_in_dim(block, block.shape[dim] - width, None, axis...  11.7 us
    all_to_all x2, starting transfers between devices, on_device(): lax.all_to_all(field, 'gz', split_axis=1, concat_axis=0, tiled=True)  11 us
    slice x82, local copies, waits for them, and re-layouts, shifted(): lax.slice_in_dim(field, 0, length - stride, axis=line_axis)  9.39 us
  transfers between devices with their start and end apart: 14, of which 6 were waited for; matrix products, arithmetic and copies ran while one was open for 21% of the time, Pallas kernels for 0%

commit v1 on v0

v1 whole, which is shorter than its diff:
```python
import functools

import jax
import jax.numpy as jnp
from jax import lax
from jax.experimental import pallas as pl
from jax.experimental.pallas import tpu as pltpu
from jax.sharding import PartitionSpec as P

STEPS = 2
MOST = 2
BLOCK_ROWS = 128
TIME_STEP = 30.0
CONTRAST = 4.0
HALF_LINK = 1.5 * TIME_STEP
THIRD = 1.0 / 3.0
VMEM = pltpu.VMEM


def call(body, outs, ins, name, smem=()):
    specs = [
        pl.BlockSpec(memory_space=pltpu.SMEM if k in smem else VMEM) for k in range(len(ins))
    ]
    return pl.pallas_call(
        body,
        out_shape=[jax.ShapeDtypeStruct(shape, jnp.float32) for shape in outs],
        in_specs=specs,
        out_specs=[pl.BlockSpec(memory_space=VMEM)] * len(outs),
        name=name,
    )(*ins)


def facing(index, low, high):
    odd = lax.rem(index, 2) == 1
    return jnp.where(odd, low, high), jnp.where(odd, high, low)


def edge_kernel(depth, height, field, z_first, z_second, y_first, y_second):
    z_odd = lax.rem(lax.axis_index("gz"), 2) == 1
    y_odd = lax.rem(lax.axis_index("xy"), 2) == 1
    bottom, top = field[pl.ds(0, height), :], field[pl.ds((depth - 1) * height, height), :]
    z_first[...] = jnp.where(z_odd, bottom, top)
    z_second[...] = jnp.where(z_odd, top, bottom)
    near = field[pl.ds(0, depth, stride=height), :]
    far = field[pl.ds(height - 1, depth, stride=height), :]
    y_first[...] = jnp.where(y_odd, near, far)
    y_second[...] = jnp.where(y_odd, far, near)


def chain(g_rows, v_rows, count, solved, head, tail, element):
    g_head = g_prev = g_rows(0)
    pivot = jnp.ones_like(g_prev)
    right = v_rows(0)
    unit = pivot
    for k in range(count - 1):
        g_next = g_rows(k + 1)
        link = HALF_LINK * (g_prev + g_next)
        inverse = 1.0 / (pivot + link)
        ratio = link * inverse
        solved[k] = right * inverse
        head[k] = unit * inverse
        tail[k] = ratio
        pivot = 1.0 + ratio * pivot
        right = v_rows(k + 1) + ratio * right
        unit = ratio * unit
        g_prev = g_next
    inverse = 1.0 / pivot
    value, from_head, from_tail = right * inverse, unit * inverse, inverse
    solved[count - 1] = value
    head[count - 1] = from_head
    tail[count - 1] = from_tail
    element[2] = from_tail
    element[4] = value
    element[5] = g_head
    element[6] = g_prev
    for k in range(count - 2, -1, -1):
        ratio = tail[k]
        value = solved[k] + ratio * value
        from_head = head[k] + ratio * from_head
        from_tail = ratio * from_tail
        solved[k] = value
        head[k] = from_head
        tail[k] = from_tail
    element[0] = from_head
    element[1] = from_tail
    element[3] = value


def z_kernel(depth, height, late, *refs):
    if late:
        field, z_first, z_second, y_first, y_second, z_low, z_high = refs[:7]
    else:
        field, z_first, z_second, y_first, y_second = refs[:5]
    g_out, solved, head, tail, element = refs[-5:]
    z_index, y_index = lax.axis_index("gz"), lax.axis_index("xy")
    z_odd, y_odd = lax.rem(z_index, 2) == 1, lax.rem(y_index, 2) == 1
    plane = lambda k: field[pl.ds(k * height, height), :]
    first, second = z_first[...], z_second[...]
    low, high = jnp.where(z_odd, first, second), jnp.where(z_odd, second, first)
    if late:
        low, high = (low + z_low[...]) * THIRD, (high + z_high[...]) * THIRD
    low = jnp.where(z_index == 0, plane(0), low)
    high = jnp.where(z_index == lax.axis_size("gz") - 1, plane(depth - 1), high)
    width = field.shape[1]
    rows = lax.broadcasted_iota(jnp.int32, (height, width), 0)
    lanes = lax.broadcasted_iota(jnp.int32, (height, width), 1)
    y_begin, y_end = y_index == 0, y_index == lax.axis_size("xy") - 1

    def g_rows(k):
        here = plane(k)
        slope = (plane(k + 1) if k < depth - 1 else high) - (plane(k - 1) if k else low)
        squares = (slope * 0.5) * (slope * 0.5)
        one, two = y_first[pl.ds(k, 1), :], y_second[pl.ds(k, 1), :]
        near, far = jnp.where(y_odd, one, two), jnp.where(y_odd, two, one)
        near = jnp.where(y_begin, here[:1], near)
        far = jnp.where(y_end, here[height - 1 :], far)
        after = jnp.where(rows == height - 1, far, pltpu.roll(here, height - 1, 0))
        before = jnp.where(rows == 0, near, pltpu.roll(here, 1, 0))
        slope = (after - before) * 0.5
        squares = squares + slope * slope
        after = jnp.where(lanes == width - 1, here, pltpu.roll(here, width - 1, 1))
        before = jnp.where(lanes == 0, here, pltpu.roll(here, 1, 1))
        slope = (after - before) * 0.5
        squares = squares + slope * slope
        g = 1.0 / (1.0 + squares * (1.0 / CONTRAST))
        g_out[pl.ds(k * height, height), :] = g
        return g

    chain(g_rows, plane, depth, solved, head, tail, element)


def y_kernel(depth, height, g_field, field, solved, head, tail, element):
    g_rows = lambda k: g_field[pl.ds(k, depth, stride=height), :]
    v_rows = lambda k: field[pl.ds(k, depth, stride=height), :]
    chain(g_rows, v_rows, height, solved, head, tail, element)


def x_kernel(rows, g_field, field, solved):
    width = field.shape[1]
    lanes = lax.broadcasted_iota(jnp.int32, (rows, width), 1)

    def piece(step, carry):
        at = pl.ds(pl.multiple_of(step * rows, rows), rows)
        g = g_field[at, :]
        right = field[at, :]
        link = jnp.where(
            lanes == width - 1, 0.0, HALF_LINK * (g + pltpu.roll(g, width - 1, 1))
        )
        main = 1.0 + link + pltpu.roll(link, 1, 1)
        stride = 1
        while stride < width:
            inverse = 1.0 / main
            factor = link * inverse
            back = width - stride
            ahead = link * pltpu.roll(inverse, back, 1)
            main = main - pltpu.roll(link * factor, stride, 1) - link * ahead
            right = right + pltpu.roll(factor * right, stride, 1) + ahead * pltpu.roll(right, back, 1)
            link = ahead * pltpu.roll(link, back, 1)
            stride *= 2
        solved[at, :] = right / main
        return carry

    lax.fori_loop(0, field.shape[0] // rows, piece, 0)


def sum_kernel(depth, height, along_x, solved, head, tail, from_low, from_high, total, z_first, z_second):
    low, high = from_low[...], from_high[...]
    for k in range(height):
        at = pl.ds(k, depth, stride=height)
        total[at, :] = along_x[at, :] + (solved[k] + low * head[k] + high * tail[k])
    z_odd = lax.rem(lax.axis_index("gz"), 2) == 1
    bottom, top = total[pl.ds(0, height), :], total[pl.ds((depth - 1) * height, height), :]
    z_first[...] = jnp.where(z_odd, bottom, top)
    z_second[...] = jnp.where(z_odd, top, bottom)


def step_kernel(depth, height, total, solved, head, tail, from_low, from_high, jump_low, jump_high,
                field, y_first, y_second, z_low, z_high):
    low, high = from_low[...], from_high[...]
    for k in range(depth):
        at = pl.ds(k * height, height)
        along_z = solved[k] + low * head[k] + high * tail[k]
        if k == 0:
            z_low[...] = along_z + jump_low[...]
        if k == depth - 1:
            z_high[...] = along_z - jump_high[...]
        field[at, :] = (total[at, :] + along_z) * THIRD
    y_odd = lax.rem(lax.axis_index("xy"), 2) == 1
    near = field[pl.ds(0, depth, stride=height), :]
    far = field[pl.ds(height - 1, depth, stride=height), :]
    y_first[...] = jnp.where(y_odd, near, far)
    y_second[...] = jnp.where(y_odd, far, near)


def last_kernel(depth, height, total, solved, head, tail, from_low, from_high, owners, field, outgoing):
    low, high = from_low[...], from_high[...]
    outgoing[...] = jnp.zeros_like(outgoing)
    planes = BLOCK_ROWS // height
    for block in range(depth // planes):
        owner = owners[0, block]
        rank = jnp.int32(0)
        for other in range(block):
            rank = rank + (owners[0, other] == owner).astype(jnp.int32)
        slot = owner * MOST + rank
        for j in range(planes):
            k = block * planes + j
            at = pl.ds(k * height, height)
            value = (total[at, :] + (solved[k] + low * head[k] + high * tail[k])) * THIRD
            field[at, :] = value
            outgoing[slot, pl.ds(j * height, height), :] = value


def swap(values, axis, stride):
    count = lax.axis_size(axis)
    return lax.ppermute(values, axis, [(i, i ^ stride) for i in range(count)])


def neighbours(first, second, axis):
    count = lax.axis_size(axis)
    other = [(i, i + 1) for i in range(1, count - 1, 2)]
    return swap(first, axis, 1), lax.ppermute(second, axis, other + [(j, i) for i, j in other])


def flows(element, axis):
    index, count = lax.axis_index(axis), lax.axis_size(axis)
    own = [element[k] for k in range(7)]
    zero = jnp.zeros_like(own[0])
    levels = []
    stride = 1
    while stride < count:
        upper = (index // stride) % 2 == 1
        pick = lambda a, b: jnp.where(upper, a, b)
        if stride * 2 < count:
            got = swap(element, axis, stride)
            left = [pick(got[k], own[k]) for k in range(7)]
            right = [pick(own[k], got[k]) for k in range(7)]
        else:
            sent = jnp.stack([pick(own[0], own[2]), pick(own[3], own[4]), pick(own[5], own[6])])
            got = swap(sent, axis, stride)
            left = [None, zero, pick(got[0], own[2]), None, pick(got[1], own[4]), None, pick(got[2], own[6])]
            right = [pick(own[0], got[0]), zero, None, pick(own[3], got[1]), None, pick(own[5], got[2]), None]
        link = HALF_LINK * (left[6] + right[5])
        inverse = 1.0 / (1.0 + link * (left[2] + right[0]))
        gap = left[4] - right[3]
        levels.append((upper, link, inverse, gap, left[1], right[1]))
        stride *= 2
        if stride < count:
            share = link * inverse
            first, second = share * left[1], share * right[1]
            own = [
                left[0] - first * left[1],
                first * right[1],
                right[2] - second * right[1],
                left[3] - first * gap,
                right[4] + second * gap,
                left[5],
                right[6],
            ]
            element = jnp.stack(own)
    from_low = from_high = jump_low = jump_high = zero
    for upper, link, inverse, gap, before, after in reversed(levels):
        jump = (gap + before * from_low - after * from_high) * inverse
        flow = link * jump
        from_low, jump_low = jnp.where(upper, flow, from_low), jnp.where(upper, jump, jump_low)
        from_high, jump_high = jnp.where(upper, from_high, -flow), jnp.where(upper, jump_high, jump)
    return from_low, from_high, jump_low, jump_high


def on_device(volume, owners):
    depth, height, width = volume.shape
    z_count = lax.axis_size("gz")
    flat, plane, side = (depth * height, width), (height, width), (depth, width)
    z_parts, y_parts = (depth, height, width), (height, depth, width)
    part = functools.partial
    field = volume.reshape(flat)
    edges = call(part(edge_kernel, depth, height), [plane, plane, side, side], [field], "edges")
    z_sides, y_sides = neighbours(*edges[:2], "gz"), neighbours(*edges[2:], "xy")
    ghosts = ()
    for step in range(STEPS):
        g_field, z_solved, z_head, z_tail, z_element = call(
            part(z_kernel, depth, height, step > 0),
            [flat, z_parts, z_parts, z_parts, (7,) + plane],
            [field, *z_sides, *y_sides, *ghosts],
            "z_pieces",
        )
        z_low, z_high, jump_low, jump_high = flows(z_element, "gz")
        y_solved, y_head, y_tail, y_element = call(
            part(y_kernel, depth, height),
            [y_parts, y_parts, y_parts, (7,) + side],
            [g_field, field],
            "y_pieces",
        )
        y_low, y_high, _, _ = flows(y_element, "xy")
        (along_x,) = call(part(x_kernel, 64), [flat], [g_field, field], "x_lines")
        total, *z_edges = call(
            part(sum_kernel, depth, height),
            [flat, plane, plane],
            [along_x, y_solved, y_head, y_tail, y_low, y_high],
            "sum_xy",
        )
        if step < STEPS - 1:
            z_sides = neighbours(*z_edges, "gz")
            field, *rest = call(
                part(step_kernel, depth, height),
                [flat, side, side, plane, plane],
                [total, z_solved, z_head, z_tail, z_low, z_high, jump_low, jump_high],
                "new_field",
            )
            y_sides, ghosts = neighbours(*rest[:2], "xy"), rest[2:]
    blocks = owners.shape[1]
    field, outgoing = call(
        part(last_kernel, depth, height),
        [flat, (z_count * MOST, BLOCK_ROWS, width)],
        [total, z_solved, z_head, z_tail, z_low, z_high, owners.reshape(1, blocks)],
        "denoised",
        smem=(6,),
    )
    incoming = lax.all_to_all(outgoing, "gz", split_axis=0, concat_axis=0, tiled=True)
    return field.reshape(volume.shape), incoming.reshape(1, z_count * MOST, BLOCK_ROWS, width)


def solution(mesh):
    in_specs = (P("gz", "xy", None), P("xy", "gz", None))
    out_specs = (P("gz", "xy", None), P("xy", "gz", None, None))
    return jax.shard_map(
        on_device, mesh=mesh, in_specs=in_specs, out_specs=out_specs, check_vma=False
    )
```

time: 193 us -> 118 us (0.61)
  Pallas kernels: 0 us -> 36 us
  waiting for transfers between devices: 39.6 us -> 13.8 us
  local copies, waits for them, and re-layouts: 28 us -> 2.76 us
  other arithmetic: 30.1 us -> 5.43 us
  starting transfers between devices: 48.3 us -> 31.3 us
  blocking collectives: 42.4 us -> 27.7 us
  between operations: 2.95 us -> 0.94 us
    pallas_call x0 -> x11, Pallas kernels: none -> 36 us  [call(): pl.pallas_call(body, out_shape=[jax.ShapeDtypeStruct(shape, jnp.float32)...]
    all_to_all x6 -> x0, waiting for transfers between devices: 33.4 us -> none  [the longest x2 18.3 us: on_device(): lax.all_to_all(g_own, 'gz', split_axis=1, concat_axis=0, tiled=True)]
    all_to_all x6 -> x0, starting transfers between devices: 31.4 us -> none  [the longest x2 13.3 us: on_device(): lax.all_to_all(g_own, 'gz', split_axis=1, concat_axis=0, tiled=True)]
    slice x158 -> x0, local copies, waits for them, and re-layouts: 18.4 us -> none  [the longest x82 9.39 us: shifted(): lax.slice_in_dim(field, 0, length - stride, axis=line_axis)]
    ppermute x8 -> x18, starting transfers between devices: 16.9 us -> 31.3 us  [the longest x14 28.7 us: swap(): return lax.ppermute(values, axis, [(i, i ^ stride) for i in range(count)])]
    add x58 -> x1, other arithmetic: 14 us -> 0.01 us  [flows(): right[4] + second * gap]
    all_gather x2 -> x0, blocking collectives: 13.7 us -> none  [gather_y(): return lax.all_gather(packed, 'xy', axis=0, tiled=True)]
    ppermute x8 -> x18, waiting for transfers between devices: 6.18 us -> 13.8 us  [the longest x14 13.8 us: swap(): return lax.ppermute(values, axis, [(i, i ^ stride) for i in range(count)])]
  transfers between devices with their start and end apart: 14 -> 18, of which waited for: 6 -> 7; matrix products, arithmetic and copies ran while one was open for 21% -> 3% of each run, Pallas kernels for 0% -> 19%
where the time goes in v1:
time: 118 us
  Pallas kernels  36 us (31%)
  starting transfers between devices  31.3 us (27%)
  blocking collectives  27.7 us (23%)
  waiting for transfers between devices  13.8 us (12%)
  other arithmetic  5.43 us (5%)
  local copies, waits for them, and re-layouts  2.76 us (2%)
    pallas_call x11, Pallas kernels, call(): pl.pallas_call(body, out_shape=[jax.ShapeDtypeStruct(shape, jnp.float32)...  36 us
    ppermute x14, starting transfers between devices, swap(): return lax.ppermute(values, axis, [(i, i ^ stride) for i in range(count)])  28.7 us
    all_to_all x1, blocking collectives, on_device(): lax.all_to_all(outgoing, 'gz', split_axis=0, concat_axis=0, tiled=True)  27.7 us
    ppermute x14, waiting for transfers between devices, swap(): return lax.ppermute(values, axis, [(i, i ^ stride) for i in range(count)])  13.8 us
    unnamed x25, local copies, waits for them, and re-layouts  2.76 us
    ppermute x4, starting transfers between devices, neighbours(): lax.ppermute(second, axis, other + [(j, i) for i, j in other])  2.62 us
    select_n x4, other arithmetic, flows(): jnp.where(upper, from_high, -flow)  2.54 us
  transfers between devices with their start and end apart: 18, of which 7 were waited for; matrix products, arithmetic and copies ran while one was open for 3% of the time, Pallas kernels for 19%

profile of v1, /device:TPU:0, one launch (start us, length us, event | category | flops | bytes accessed | tf_op | source)
XLA Modules:
  0.0 117.8 jit_solution(11381717692513910076)
XLA Ops:
  0.6 1.6 %edges.1 = (f32[32,128]{1,0:T(8,128)}, f32[32,128]{1,0:T(8,128)}, f32[16,128]{1,0:T(8,128)}, f32[16,128]{1,0:T(8,128)}) custom-call(f32[512,128]{1,0:T(8,128)} %bitcast.807), custom_call_target="tpu_custom_call" | custom-call | tf_op jit(solution)/shard_map/edges/pallas_call | solution.py:24
  2.2 3.0 %collective-permute-start = (f32[32,128]{1,0:T(8,128)}, f32[32,128]{1,0:T(8,128)S(1)}, u32[]{:S(2)}, u32[]{:S(2)}) collective-permute-start(f32[32,128]{1,0:T(8,128)} %get-tuple-element.35), channel_id=1, source_target_pairs={{0,4},{4,0},{8,12},{12,8},{16,20},{20,16},{24,28},{28,24},{1,5},{5... | collective-permute-start | bytes 49160 | tf_op jit(solution)/shard_map/ppermute | solution.py:215
  5.2 0.7 collective-permute-start.1
  5.9 0.1 collective-permute-start.2
  5.9 0.7 collective-permute-start.3
  6.6 0.7 collective-permute-done.2.refs_3_
  7.3 0.6 copy-done.9
  7.9 0.6 copy-done.5
  8.5 2.3 %z_pieces.2 = (f32[512,128]{1,0:T(8,128)}, f32[16,32,128]{2,1,0:T(8,128)}, f32[16,32,128]{2,1,0:T(8,128)}, f32[16,32,128]{2,1,0:T(8,128)}, f32[7,32,128]{2,1,0:T(8,128)}) custom-call(f32[512,128]{1,0:T(8,128)} %bitcast.808, f32[32,128]{1,0:T(8,128)} %copy-done.4, f32[32,128]{1,0:T(8,128)} %copy-done.5, f32[16,128]{1,0:T(8,128)} %copy-done.9, ...), custom_call_target="tpu_custom_call" | custom-call | tf_op jit(solution)/shard_map/z_pieces/pallas_call | solution.py:24
  10.8 2.4 %y_pieces.2 = (f32[32,16,128]{2,1,0:T(8,128)}, f32[32,16,128]{2,1,0:T(8,128)}, f32[32,16,128]{2,1,0:T(8,128)}, f32[7,16,128]{2,1,0:T(8,128)}) custom-call(f32[512,128]{1,0:T(8,128)} %get-tuple-element.39.g_field, f32[512,128]{1,0:T(8,128)} %bitcast.809), custom_call_target="tpu_custom_call" | custom-call | tf_op jit(solution)/shard_map/y_pieces/pallas_call | solution.py:24
  13.2 4.3 %collective-permute-start.4 = (f32[7,16,128]{2,1,0:T(8,128)}, f32[7,16,128]{2,1,0:T(8,128)S(1)}, u32[]{:S(2)}, u32[]{:S(2)}) collective-permute-start(f32[7,16,128]{2,1,0:T(8,128)} %get-tuple-element.43), channel_id=1, source_target_pairs={{0,1},{1,0},{2,3},{3,2},{4,5},{5,4},{6,7},{7,6},{8,9},{9,8},{10,11... | collective-permute-start | bytes 172040 | tf_op jit(solution)/shard_map/ppermute | solution.py:215
  17.5 8.1 %x_lines.2.along_x = f32[512,128]{1,0:T(8,128)} custom-call(f32[512,128]{1,0:T(8,128)} %get-tuple-element.39.g_field, f32[512,128]{1,0:T(8,128)} %bitcast.810), custom_call_target="tpu_custom_call" | custom-call | tf_op jit(solution)/shard_map/x_lines/pallas_call | solution.py:24
  25.6 4.3 %collective-permute-start.6 = (f32[7,32,128]{2,1,0:T(8,128)S(1)}, f32[7,32,128]{2,1,0:T(8,128)S(1)}, u32[]{:S(2)}, u32[]{:S(2)}) collective-permute-start(f32[7,32,128]{2,1,0:T(8,128)S(1)} %copy-done.1), channel_id=1, source_target_pairs={{0,4},{4,0},{8,12},{12,8},{16,20},{20,16},{24,28},{28,24},{1,5},{5... | collective-permute-start | bytes 344072 | tf_op jit(solution)/shard_map/ppermute | solution.py:215
  30.0 1.1 collective-permute-start.5
  31.0 2.2 %collective-permute-done.6 = f32[7,32,128]{2,1,0:T(8,128)S(1)} collective-permute-done((f32[7,32,128]{2,1,0:T(8,128)S(1)}, f32[7,32,128]{2,1,0:T(8,128)S(1)}, u32[]{:S(2)}, u32[]{:S(2)}) %collective-permute-start.6) | collective-permute-done | bytes 114720 | tf_op jit(solution)/shard_map/ppermute | solution.py:215
  33.4 1.6 %collective-permute-start.7 = (f32[7,32,128]{2,1,0:T(8,128)S(1)}, f32[7,32,128]{2,1,0:T(8,128)S(1)}, u32[]{:S(2)}, u32[]{:S(2)}) collective-permute-start(f32[7,32,128]{2,1,0:T(8,128)S(1)} %get-tuple-element.114), channel_id=1, source_target_pairs={{0,8},{4,12},{8,0},{12,4},{16,24},{20,28},{24,16},{28,20},{1,9},{5... | collective-permute-start | bytes 344072 | tf_op jit(solution)/shard_map/ppermute | solution.py:215
  35.0 0.6 negate_select_fusion.8
  35.6 2.6 %collective-permute-done.7 = f32[7,32,128]{2,1,0:T(8,128)S(1)} collective-permute-done((f32[7,32,128]{2,1,0:T(8,128)S(1)}, f32[7,32,128]{2,1,0:T(8,128)S(1)}, u32[]{:S(2)}, u32[]{:S(2)}) %collective-permute-start.7) | collective-permute-done | bytes 114720 | tf_op jit(solution)/shard_map/ppermute | solution.py:215
  38.3 2.7 %collective-permute-start.8 = (f32[3,32,128]{2,1,0:T(8,128)S(1)}, f32[3,32,128]{2,1,0:T(8,128)S(1)}, u32[]{:S(2)}, u32[]{:S(2)}) collective-permute-start(f32[3,32,128]{2,1,0:T(8,128)S(1)} %pad_maximum_fusion), channel_id=1, source_target_pairs={{0,16},{4,20},{8,24},{12,28},{16,0},{20,4},{24,8},{28,12},{1,17},{... | collective-permute-start | bytes 147464 | tf_op jit(solution)/shard_map/ppermute | solution.py:215
  40.9 0.6 select_select_fusion.5.from_low
  41.5 2.2 %sum_xy.2 = (f32[512,128]{1,0:T(8,128)}, f32[32,128]{1,0:T(8,128)}, f32[32,128]{1,0:T(8,128)}) custom-call(f32[512,128]{1,0:T(8,128)} %x_lines.2.along_x, f32[32,16,128]{2,1,0:T(8,128)} %get-tuple-element.40.solved, f32[32,16,128]{2,1,0:T(8,128)} %get-tuple-element.41.head, f32[32,16,128]{2,1,0:T(8,128)} %get-tuple-element.42.tail, ...), custom_call_target="tpu_custom_call" | custom-call | tf_op jit(solution)/shard_map/sum_xy/pallas_call | solution.py:24
  43.8 0.7 collective-permute-start.10
  44.4 3.4 %collective-permute-start.9 = (f32[32,128]{1,0:T(8,128)}, f32[32,128]{1,0:T(8,128)S(1)}, u32[]{:S(2)}, u32[]{:S(2)}) collective-permute-start(f32[32,128]{1,0:T(8,128)} %get-tuple-element.50), channel_id=1, source_target_pairs={{0,4},{4,0},{8,12},{12,8},{16,20},{20,16},{24,28},{28,24},{1,5},{5... | collective-permute-start | bytes 49160 | tf_op jit(solution)/shard_map/ppermute | solution.py:215
  47.9 0.7 select_select_fusion
  48.5 0.6 negate_select_fusion.3
  49.2 2.0 %new_field.1 = (f32[512,128]{1,0:T(8,128)}, f32[16,128]{1,0:T(8,128)}, f32[16,128]{1,0:T(8,128)}, f32[32,128]{1,0:T(8,128)}, f32[32,128]{1,0:T(8,128)}) custom-call(f32[512,128]{1,0:T(8,128)} %get-tuple-element.44.total, f32[16,32,128]{2,1,0:T(8,128)} %get-tuple-element.45.solved, f32[16,32,128]{2,1,0:T(8,128)} %get-tuple-element.46.head, ...), custom_call_target="tpu_custom_call" | custom-call | tf_op jit(solution)/shard_map/new_field/pallas_call | solution.py:24
  51.2 0.7 collective-permute-start.12
  51.9 0.7 collective-permute-done.11.refs_3_
  52.6 0.6 copy-done.8
  53.1 2.3 %z_pieces.3 = (f32[512,128]{1,0:T(8,128)}, f32[16,32,128]{2,1,0:T(8,128)}, f32[16,32,128]{2,1,0:T(8,128)}, f32[16,32,128]{2,1,0:T(8,128)}, f32[7,32,128]{2,1,0:T(8,128)}) custom-call(f32[512,128]{1,0:T(8,128)} %get-tuple-element.49.refs_0_.field, f32[32,128]{1,0:T(8,128)} %copy-done.7, f32[32,128]{1,0:T(8,128)} %copy-done.6, f32[16,128]{1,0:T(8,128)} %copy-done.8, ...), custom_call_target="tpu_custom_call" | custom-call | tf_op jit(solution)/shard_map/z_pieces/pallas_call | solution.py:24
  55.5 2.4 %y_pieces.3 = (f32[32,16,128]{2,1,0:T(8,128)}, f32[32,16,128]{2,1,0:T(8,128)}, f32[32,16,128]{2,1,0:T(8,128)}, f32[7,16,128]{2,1,0:T(8,128)}) custom-call(f32[512,128]{1,0:T(8,128)} %get-tuple-element.56.g_field, f32[512,128]{1,0:T(8,128)} %get-tuple-element.49.refs_0_.field), custom_call_target="tpu_custom_call" | custom-call | tf_op jit(solution)/shard_map/y_pieces/pallas_call | solution.py:24
  57.9 4.3 %collective-permute-start.13 = (f32[7,16,128]{2,1,0:T(8,128)}, f32[7,16,128]{2,1,0:T(8,128)S(1)}, u32[]{:S(2)}, u32[]{:S(2)}) collective-permute-start(f32[7,16,128]{2,1,0:T(8,128)} %get-tuple-element.60), channel_id=1, source_target_pairs={{0,1},{1,0},{2,3},{3,2},{4,5},{5,4},{6,7},{7,6},{8,9},{9,8},{10,11... | collective-permute-start | bytes 172040 | tf_op jit(solution)/shard_map/ppermute | solution.py:215
  62.2 8.1 %x_lines.3.along_x = f32[512,128]{1,0:T(8,128)} custom-call(f32[512,128]{1,0:T(8,128)} %get-tuple-element.56.g_field, f32[512,128]{1,0:T(8,128)} %get-tuple-element.49.refs_0_.field), custom_call_target="tpu_custom_call" | custom-call | tf_op jit(solution)/shard_map/x_lines/pallas_call | solution.py:24
  70.3 0.0 collective-permute-start.15
  70.4 1.1 collective-permute-start.14
  71.5 3.9 %collective-permute-done.15 = f32[7,32,128]{2,1,0:T(8,128)S(1)} collective-permute-done((f32[7,32,128]{2,1,0:T(8,128)S(1)}, f32[7,32,128]{2,1,0:T(8,128)S(1)}, u32[]{:S(2)}, u32[]{:S(2)}) %collective-permute-start.15) | collective-permute-done | bytes 114720 | tf_op jit(solution)/shard_map/ppermute | solution.py:215
  75.5 1.4 %collective-permute-start.16 = (f32[7,32,128]{2,1,0:T(8,128)S(1)}, f32[7,32,128]{2,1,0:T(8,128)S(1)}, u32[]{:S(2)}, u32[]{:S(2)}) collective-permute-start(f32[7,32,128]{2,1,0:T(8,128)S(1)} %get-tuple-element.80), channel_id=1, source_target_pairs={{0,8},{4,12},{8,0},{12,4},{16,24},{20,28},{24,16},{28,20},{1,9},{5... | collective-permute-start | bytes 344072 | tf_op jit(solution)/shard_map/ppermute | solution.py:215
  77.0 0.6 negate_select_fusion.6
  77.6 2.8 %collective-permute-done.16 = f32[7,32,128]{2,1,0:T(8,128)S(1)} collective-permute-done((f32[7,32,128]{2,1,0:T(8,128)S(1)}, f32[7,32,128]{2,1,0:T(8,128)S(1)}, u32[]{:S(2)}, u32[]{:S(2)}) %collective-permute-start.16) | collective-permute-done | bytes 114720 | tf_op jit(solution)/shard_map/ppermute | solution.py:215
  80.5 1.3 %collective-permute-start.17 = (f32[3,32,128]{2,1,0:T(8,128)S(1)}, f32[3,32,128]{2,1,0:T(8,128)S(1)}, u32[]{:S(2)}, u32[]{:S(2)}) collective-permute-start(f32[3,32,128]{2,1,0:T(8,128)S(1)} %pad_maximum_fusion.1), channel_id=1, source_target_pairs={{0,16},{4,20},{8,24},{12,28},{16,0},{20,4},{24,8},{28,12},{1,17},{... | collective-permute-start | bytes 147464 | tf_op jit(solution)/shard_map/ppermute | solution.py:215
  81.8 0.6 select_select_fusion.4.from_low
  82.4 2.2 %sum_xy.3 = (f32[512,128]{1,0:T(8,128)}, f32[32,128]{1,0:T(8,128)}, f32[32,128]{1,0:T(8,128)}) custom-call(f32[512,128]{1,0:T(8,128)} %x_lines.3.along_x, f32[32,16,128]{2,1,0:T(8,128)} %get-tuple-element.57.solved, f32[32,16,128]{2,1,0:T(8,128)} %get-tuple-element.58.head, f32[32,16,128]{2,1,0:T(8,128)} %get-tuple-element.59.tail, ...), custom_call_target="tpu_custom_call" | custom-call | tf_op jit(solution)/shard_map/sum_xy/pallas_call | solution.py:24
  84.6 0.9 collective-permute-done.17
  85.5 0.7 negate_select_fusion
  86.2 0.6 broadcast_select_fusion.2.from_low
  86.8 2.4 %denoised.1 = (f32[512,128]{1,0:T(8,128)}, f32[16,128,128]{2,1,0:T(8,128)}) custom-call(f32[512,128]{1,0:T(8,128)} %get-tuple-element.61.total, f32[16,32,128]{2,1,0:T(8,128)} %get-tuple-element.62.solved, f32[16,32,128]{2,1,0:T(8,128)} %get-tuple-element.63.head, f32[16,32,128]{2,1,0:T(8,128)} %get-tuple-element.64.tail, ...), custom_call_target="tpu_custom_call" | custom-call | tf_op jit(solution)/shard_map/denoised/pallas_call | solution.py:24
  89.2 27.7 %all_to_all.5 = f32[16,128,128]{2,1,0:T(8,128)S(1)} all-to-all(f32[16,128,128]{2,1,0:T(8,128)} %get-tuple-element.67), channel_id=1, replica_groups=mesh['gz'=8,'xy'=4] {'gz'}, dimensions={0} | all-to-all | bytes 2097152 | tf_op jit(solution)/shard_map/all_to_all | solution.py:318
  116.9 1.0 copy.17
  (61 shorter events, 0.5 us)
Async XLA Ops:
  2.2 5.1 %collective-permute-start = (f32[32,128]{1,0:T(8,128)}, f32[32,128]{1,0:T(8,128)S(1)}, u32[]{:S(2)}, u32[]{:S(2)}) collective-permute-start(f32[32,128]{1,0:T(8,128)} %get-tuple-element.35), channel_id=1, source_target_pairs={{0,4},{4,0},{8,12},{12,8},{16,20},{20,16},{24,28},{28,24},{1,5},{5... | collective-permute-start | bytes 49160 | tf_op jit(solution)/shard_map/ppermute | solution.py:215
  5.2 2.1 %collective-permute-start.1 = (f32[32,128]{1,0:T(8,128)}, f32[32,128]{1,0:T(8,128)S(1)}, u32[]{:S(2)}, u32[]{:S(2)}) collective-permute-start(f32[32,128]{1,0:T(8,128)} %get-tuple-element.36), channel_id=1, source_target_pairs={{4,8},{12,16},{20,24},{8,4},{16,12},{24,20},{5,9},{13,17},{21,25},... | collective-permute-start | bytes 49160 | tf_op jit(solution)/shard_map/ppermute | solution.py:221
  5.9 1.4 %collective-permute-start.2 = (f32[16,128]{1,0:T(8,128)}, f32[16,128]{1,0:T(8,128)S(1)}, u32[]{:S(2)}, u32[]{:S(2)}) collective-permute-start(f32[16,128]{1,0:T(8,128)} %get-tuple-element.37), channel_id=1, source_target_pairs={{0,1},{1,0},{2,3},{3,2},{4,5},{5,4},{6,7},{7,6},{8,9},{9,8},{10,11... | collective-permute-start | bytes 24584 | tf_op jit(solution)/shard_map/ppermute | solution.py:215
  5.9 1.4 %collective-permute-start.3 = (f32[16,128]{1,0:T(8,128)}, f32[16,128]{1,0:T(8,128)S(1)}, u32[]{:S(2)}, u32[]{:S(2)}) collective-permute-start(f32[16,128]{1,0:T(8,128)} %get-tuple-element.38), channel_id=1, source_target_pairs={{1,2},{2,1},{5,6},{6,5},{9,10},{10,9},{13,14},{14,13},{17,18},{18,... | collective-permute-start | bytes 24584 | tf_op jit(solution)/shard_map/ppermute | solution.py:221
  7.3 0.6 copy-start.9
  7.3 0.6 copy-start.11
  7.3 0.6 copy-start.4
  7.9 0.6 copy-start.5
  13.2 16.7 %collective-permute-start.4 = (f32[7,16,128]{2,1,0:T(8,128)}, f32[7,16,128]{2,1,0:T(8,128)S(1)}, u32[]{:S(2)}, u32[]{:S(2)}) collective-permute-start(f32[7,16,128]{2,1,0:T(8,128)} %get-tuple-element.43), channel_id=1, source_target_pairs={{0,1},{1,0},{2,3},{3,2},{4,5},{5,4},{6,7},{7,6},{8,9},{9,8},{10,11... | collective-permute-start | bytes 172040 | tf_op jit(solution)/shard_map/ppermute | solution.py:215
  17.5 8.1 %copy-start.1 = (f32[7,32,128]{2,1,0:T(8,128)S(1)}, f32[7,32,128]{2,1,0:T(8,128)}, u32[]{:S(2)}) copy-start(f32[7,32,128]{2,1,0:T(8,128)} %get-tuple-element.48) | copy-start | bytes 344068
  17.5 12.4 %copy-start.2 = (f32[7,16,128]{2,1,0:T(8,128)S(1)}, f32[7,16,128]{2,1,0:T(8,128)}, u32[]{:S(2)}) copy-start(f32[7,16,128]{2,1,0:T(8,128)} %get-tuple-element.43) | copy-start | bytes 172036
  25.6 7.6 %collective-permute-start.6 = (f32[7,32,128]{2,1,0:T(8,128)S(1)}, f32[7,32,128]{2,1,0:T(8,128)S(1)}, u32[]{:S(2)}, u32[]{:S(2)}) collective-permute-start(f32[7,32,128]{2,1,0:T(8,128)S(1)} %copy-done.1), channel_id=1, source_target_pairs={{0,4},{4,0},{8,12},{12,8},{16,20},{20,16},{24,28},{28,24},{1,5},{5... | collective-permute-start | bytes 344072 | tf_op jit(solution)/shard_map/ppermute | solution.py:215
  30.0 5.0 %collective-permute-start.5 = (f32[3,16,128]{2,1,0:T(8,128)S(1)}, f32[3,16,128]{2,1,0:T(8,128)S(1)}, u32[]{:S(2)}, u32[]{:S(2)}) collective-permute-start(f32[3,16,128]{2,1,0:T(8,128)S(1)} %pad_maximum_fusion.2), channel_id=1, source_target_pairs={{0,2},{1,3},{2,0},{3,1},{4,6},{5,7},{6,4},{7,5},{8,10},{9,11},{10,... | collective-permute-start | bytes 73736 | tf_op jit(solution)/shard_map/ppermute | solution.py:215
  33.4 4.9 %collective-permute-start.7 = (f32[7,32,128]{2,1,0:T(8,128)S(1)}, f32[7,32,128]{2,1,0:T(8,128)S(1)}, u32[]{:S(2)}, u32[]{:S(2)}) collective-permute-start(f32[7,32,128]{2,1,0:T(8,128)S(1)} %get-tuple-element.114), channel_id=1, source_target_pairs={{0,8},{4,12},{8,0},{12,4},{16,24},{20,28},{24,16},{28,20},{1,9},{5... | collective-permute-start | bytes 344072 | tf_op jit(solution)/shard_map/ppermute | solution.py:215
  38.3 9.6 %collective-permute-start.8 = (f32[3,32,128]{2,1,0:T(8,128)S(1)}, f32[3,32,128]{2,1,0:T(8,128)S(1)}, u32[]{:S(2)}, u32[]{:S(2)}) collective-permute-start(f32[3,32,128]{2,1,0:T(8,128)S(1)} %pad_maximum_fusion), channel_id=1, source_target_pairs={{0,16},{4,20},{8,24},{12,28},{16,0},{20,4},{24,8},{28,12},{1,17},{... | collective-permute-start | bytes 147464 | tf_op jit(solution)/shard_map/ppermute | solution.py:215
  43.8 8.1 %collective-permute-start.10 = (f32[32,128]{1,0:T(8,128)}, f32[32,128]{1,0:T(8,128)S(1)}, u32[]{:S(2)}, u32[]{:S(2)}) collective-permute-start(f32[32,128]{1,0:T(8,128)} %get-tuple-element.51), channel_id=1, source_target_pairs={{4,8},{12,16},{20,24},{8,4},{16,12},{24,20},{5,9},{13,17},{21,25},... | collective-permute-start | bytes 49160 | tf_op jit(solution)/shard_map/ppermute | solution.py:221
  44.4 7.4 %collective-permute-start.9 = (f32[32,128]{1,0:T(8,128)}, f32[32,128]{1,0:T(8,128)S(1)}, u32[]{:S(2)}, u32[]{:S(2)}) collective-permute-start(f32[32,128]{1,0:T(8,128)} %get-tuple-element.50), channel_id=1, source_target_pairs={{0,4},{4,0},{8,12},{12,8},{16,20},{20,16},{24,28},{28,24},{1,5},{5... | collective-permute-start | bytes 49160 | tf_op jit(solution)/shard_map/ppermute | solution.py:215
  51.2 1.4 %collective-permute-start.11 = (f32[16,128]{1,0:T(8,128)}, f32[16,128]{1,0:T(8,128)S(1)}, u32[]{:S(2)}, u32[]{:S(2)}) collective-permute-start(f32[16,128]{1,0:T(8,128)} %get-tuple-element.52), channel_id=1, source_target_pairs={{0,1},{1,0},{2,3},{3,2},{4,5},{5,4},{6,7},{7,6},{8,9},{9,8},{10,11... | collective-permute-start | bytes 24584 | tf_op jit(solution)/shard_map/ppermute | solution.py:215
  51.2 1.4 %collective-permute-start.12 = (f32[16,128]{1,0:T(8,128)}, f32[16,128]{1,0:T(8,128)S(1)}, u32[]{:S(2)}, u32[]{:S(2)}) collective-permute-start(f32[16,128]{1,0:T(8,128)} %get-tuple-element.53), channel_id=1, source_target_pairs={{1,2},{2,1},{5,6},{6,5},{9,10},{10,9},{13,14},{14,13},{17,18},{18,... | collective-permute-start | bytes 24584 | tf_op jit(solution)/shard_map/ppermute | solution.py:221
  51.8 0.7 copy-start.6
  51.9 0.7 copy-start.7
  52.5 0.6 copy-start.8
  52.5 0.6 copy-start.10
  57.9 12.4 %copy-start = (f32[7,32,128]{2,1,0:T(8,128)S(1)}, f32[7,32,128]{2,1,0:T(8,128)}, u32[]{:S(2)}) copy-start(f32[7,32,128]{2,1,0:T(8,128)} %get-tuple-element.65) | copy-start | bytes 344068
  57.9 12.5 %copy-start.3 = (f32[7,16,128]{2,1,0:T(8,128)S(1)}, f32[7,16,128]{2,1,0:T(8,128)}, u32[]{:S(2)}) copy-start(f32[7,16,128]{2,1,0:T(8,128)} %get-tuple-element.60) | copy-start | bytes 172036
  57.9 12.5 %collective-permute-start.13 = (f32[7,16,128]{2,1,0:T(8,128)}, f32[7,16,128]{2,1,0:T(8,128)S(1)}, u32[]{:S(2)}, u32[]{:S(2)}) collective-permute-start(f32[7,16,128]{2,1,0:T(8,128)} %get-tuple-element.60), channel_id=1, source_target_pairs={{0,1},{1,0},{2,3},{3,2},{4,5},{5,4},{6,7},{7,6},{8,9},{9,8},{10,11... | collective-permute-start | bytes 172040 | tf_op jit(solution)/shard_map/ppermute | solution.py:215
  70.3 5.1 %collective-permute-start.15 = (f32[7,32,128]{2,1,0:T(8,128)S(1)}, f32[7,32,128]{2,1,0:T(8,128)S(1)}, u32[]{:S(2)}, u32[]{:S(2)}) collective-permute-start(f32[7,32,128]{2,1,0:T(8,128)S(1)} %copy-done), channel_id=1, source_target_pairs={{0,4},{4,0},{8,12},{12,8},{16,20},{20,16},{24,28},{28,24},{1,5},{5... | collective-permute-start | bytes 344072 | tf_op jit(solution)/shard_map/ppermute | solution.py:215
  70.4 6.6 %collective-permute-start.14 = (f32[3,16,128]{2,1,0:T(8,128)S(1)}, f32[3,16,128]{2,1,0:T(8,128)S(1)}, u32[]{:S(2)}, u32[]{:S(2)}) collective-permute-start(f32[3,16,128]{2,1,0:T(8,128)S(1)} %pad_maximum_fusion.3), channel_id=1, source_target_pairs={{0,2},{1,3},{2,0},{3,1},{4,6},{5,7},{6,4},{7,5},{8,10},{9,11},{10,... | collective-permute-start | bytes 73736 | tf_op jit(solution)/shard_map/ppermute | solution.py:215
  75.5 4.9 %collective-permute-start.16 = (f32[7,32,128]{2,1,0:T(8,128)S(1)}, f32[7,32,128]{2,1,0:T(8,128)S(1)}, u32[]{:S(2)}, u32[]{:S(2)}) collective-permute-start(f32[7,32,128]{2,1,0:T(8,128)S(1)} %get-tuple-element.80), channel_id=1, source_target_pairs={{0,8},{4,12},{8,0},{12,4},{16,24},{20,28},{24,16},{28,20},{1,9},{5... | collective-permute-start | bytes 344072 | tf_op jit(solution)/shard_map/ppermute | solution.py:215
  80.5 5.1 %collective-permute-start.17 = (f32[3,32,128]{2,1,0:T(8,128)S(1)}, f32[3,32,128]{2,1,0:T(8,128)S(1)}, u32[]{:S(2)}, u32[]{:S(2)}) collective-permute-start(f32[3,32,128]{2,1,0:T(8,128)S(1)} %pad_maximum_fusion.1), channel_id=1, source_target_pairs={{0,16},{4,20},{8,24},{12,28},{16,0},{20,4},{24,8},{28,12},{1,17},{... | collective-permute-start | bytes 147464 | tf_op jit(solution)/shard_map/ppermute | solution.py:215

commit v2 on v1

--- a/solution.py
+++ b/solution.py
@@ -14,28 +14,26 @@
 CONTRAST = 4.0
 HALF_LINK = 1.5 * TIME_STEP
 THIRD = 1.0 / 3.0
+VMEM_LIMIT = 16 * 1024 * 1024
 VMEM = pltpu.VMEM
 
 
-def call(body, outs, ins, name, smem=()):
+def call(body, outs, ins, name, smem=(), after=()):
+    count = len(ins)
     specs = [
-        pl.BlockSpec(memory_space=pltpu.SMEM if k in smem else VMEM) for k in range(len(ins))
-    ]
+        pl.BlockSpec(memory_space=pltpu.SMEM if k in smem else VMEM) for k in range(count)
+    ] + [pl.BlockSpec(memory_space=pl.ANY)] * len(after)
     return pl.pallas_call(
-        body,
+        lambda *refs: body(*refs[:count], *refs[count + len(after) :]),
         out_shape=[jax.ShapeDtypeStruct(shape, jnp.float32) for shape in outs],
         in_specs=specs,
         out_specs=[pl.BlockSpec(memory_space=VMEM)] * len(outs),
+        compiler_params=pltpu.CompilerParams(vmem_limit_bytes=VMEM_LIMIT),
         name=name,
-    )(*ins)
-
-
-def facing(index, low, high):
-    odd = lax.rem(index, 2) == 1
-    return jnp.where(odd, low, high), jnp.where(odd, high, low)
-
-
-def edge_kernel(depth, height, field, z_first, z_second, y_first, y_second):
+    )(*ins, *after)
+
+
+def edge_kernel(depth, height, owners, field, z_first, z_second, y_first, y_second, slots):
     z_odd = lax.rem(lax.axis_index("gz"), 2) == 1
     y_odd = lax.rem(lax.axis_index("xy"), 2) == 1
     bottom, top = field[pl.ds(0, height), :], field[pl.ds((depth - 1) * height, height), :]
@@ -45,6 +43,12 @@
     far = field[pl.ds(height - 1, depth, stride=height), :]
     y_first[...] = jnp.where(y_odd, near, far)
     y_second[...] = jnp.where(y_odd, far, near)
+    for block in range(slots.shape[0]):
+        rank = jnp.int32(0)
+        for other in range(block):
+            rank = rank + (owners[0, other] == owners[0, block]).astype(jnp.int32)
+        slot = owners[0, block] * MOST + rank
+        slots[pl.ds(block, 1), :] = jnp.full((1, slots.shape[1]), slot.astype(jnp.float32))
 
 
 def chain(g_rows, v_rows, count, solved, head, tail, element):
@@ -163,27 +167,87 @@
     lax.fori_loop(0, field.shape[0] // rows, piece, 0)
 
 
-def sum_kernel(depth, height, along_x, solved, head, tail, from_low, from_high, total, z_first, z_second):
-    low, high = from_low[...], from_high[...]
+def join(lower, upper_piece):
+    link = HALF_LINK * (lower[6] + upper_piece[5])
+    inverse = 1.0 / (1.0 + link * (lower[2] + upper_piece[0]))
+    return link, inverse, lower[4] - upper_piece[3]
+
+
+def sides(upper, own, got, last):
+    pick = lambda a, b: jnp.where(upper, a, b)
+    if not last:
+        return [pick(got[k], own[k]) for k in range(7)], [pick(own[k], got[k]) for k in range(7)]
+    zero = jnp.zeros_like(own[0])
+    lower = [None, zero, pick(got[0], own[2]), None, pick(got[1], own[4]), None, pick(got[2], own[6])]
+    return lower, [pick(own[0], got[0]), zero, None, pick(own[3], got[1]), None, pick(own[5], got[2]), None]
+
+
+def is_upper(axis, level):
+    return lax.rem(lax.div(lax.axis_index(axis), 1 << level), 2) == 1
+
+
+def merge_kernel(axis, level, own, got, *outs):
+    upper = is_upper(axis, level)
+    lower, higher = sides(upper, own, got, False)
+    link, inverse, gap = join(lower, higher)
+    share = link * inverse
+    first, second = share * lower[1], share * higher[1]
+    merged = [
+        lower[0] - first * lower[1],
+        first * higher[1],
+        higher[2] - second * higher[1],
+        lower[3] - first * gap,
+        higher[4] + second * gap,
+        lower[5],
+        higher[6],
+    ]
+    for k in range(7):
+        outs[0][k] = merged[k]
+    if len(outs) > 1:
+        above = is_upper(axis, level + 1)
+        for k, (high, low) in enumerate(((0, 2), (3, 4), (5, 6))):
+            outs[1][k] = jnp.where(above, merged[high], merged[low])
+
+
+def unwind(axis, pairs):
+    zero = jnp.zeros_like(pairs[0][0])
+    from_low = from_high = jump_low = jump_high = zero
+    for level in range(len(pairs) // 2 - 1, -1, -1):
+        upper = is_upper(axis, level)
+        own, got = pairs[2 * level], pairs[2 * level + 1]
+        lower, higher = sides(upper, own, got, level == len(pairs) // 2 - 1)
+        link, inverse, gap = join(lower, higher)
+        jump = (gap + lower[1] * from_low - higher[1] * from_high) * inverse
+        flow = link * jump
+        from_low, jump_low = jnp.where(upper, flow, from_low), jnp.where(upper, jump, jump_low)
+        from_high, jump_high = jnp.where(upper, from_high, -flow), jnp.where(upper, jump_high, jump)
+    return from_low, from_high, jump_low, jump_high
+
+
+def sum_kernel(depth, height, edges, along_x, solved, head, tail, *refs):
+    pairs, outs = refs[: len(refs) - 1 - 2 * edges], refs[len(refs) - 1 - 2 * edges :]
+    total = outs[0]
+    low, high, _, _ = unwind("xy", [[ref[k] for k in range(ref.shape[0])] for ref in pairs])
     for k in range(height):
         at = pl.ds(k, depth, stride=height)
         total[at, :] = along_x[at, :] + (solved[k] + low * head[k] + high * tail[k])
-    z_odd = lax.rem(lax.axis_index("gz"), 2) == 1
-    bottom, top = total[pl.ds(0, height), :], total[pl.ds((depth - 1) * height, height), :]
-    z_first[...] = jnp.where(z_odd, bottom, top)
-    z_second[...] = jnp.where(z_odd, top, bottom)
-
-
-def step_kernel(depth, height, total, solved, head, tail, from_low, from_high, jump_low, jump_high,
-                field, y_first, y_second, z_low, z_high):
-    low, high = from_low[...], from_high[...]
+    if edges:
+        z_odd = lax.rem(lax.axis_index("gz"), 2) == 1
+        bottom, top = total[pl.ds(0, height), :], total[pl.ds((depth - 1) * height, height), :]
+        outs[1][...] = jnp.where(z_odd, bottom, top)
+        outs[2][...] = jnp.where(z_odd, top, bottom)
+
+
+def step_kernel(depth, height, total, solved, head, tail, *refs):
+    field, y_first, y_second, z_low, z_high = refs[-5:]
+    low, high, jump_low, jump_high = unwind("gz", [[ref[k] for k in range(ref.shape[0])] for ref in refs[:-5]])
     for k in range(depth):
         at = pl.ds(k * height, height)
         along_z = solved[k] + low * head[k] + high * tail[k]
         if k == 0:
-            z_low[...] = along_z + jump_low[...]
+            z_low[...] = along_z + jump_low
         if k == depth - 1:
-            z_high[...] = along_z - jump_high[...]
+            z_high[...] = along_z - jump_high
         field[at, :] = (total[at, :] + along_z) * THIRD
     y_odd = lax.rem(lax.axis_index("xy"), 2) == 1
     near = field[pl.ds(0, depth, stride=height), :]
@@ -192,16 +256,13 @@
     y_second[...] = jnp.where(y_odd, far, near)
 
 
-def last_kernel(depth, height, total, solved, head, tail, from_low, from_high, owners, field, outgoing):
-    low, high = from_low[...], from_high[...]
+def last_kernel(depth, height, slots, total, solved, head, tail, *refs):
+    field, outgoing = refs[-2:]
+    low, high, _, _ = unwind("gz", [[ref[k] for k in range(ref.shape[0])] for ref in refs[:-2]])
     outgoing[...] = jnp.zeros_like(outgoing)
     planes = BLOCK_ROWS // height
     for block in range(depth // planes):
-        owner = owners[0, block]
-        rank = jnp.int32(0)
-        for other in range(block):
-            rank = rank + (owners[0, other] == owner).astype(jnp.int32)
-        slot = owner * MOST + rank
+        slot = jnp.max(slots[pl.ds(block, 1), :]).astype(jnp.int32)
         for j in range(planes):
             k = block * planes + j
             at = pl.ds(k * height, height)
@@ -217,103 +278,88 @@
 
 def neighbours(first, second, axis):
     count = lax.axis_size(axis)
-    other = [(i, i + 1) for i in range(1, count - 1, 2)]
+    other = [(i, (i + 1) % count) for i in range(1, count, 2)]
     return swap(first, axis, 1), lax.ppermute(second, axis, other + [(j, i) for i, j in other])
 
 
-def flows(element, axis):
-    index, count = lax.axis_index(axis), lax.axis_size(axis)
-    own = [element[k] for k in range(7)]
-    zero = jnp.zeros_like(own[0])
-    levels = []
-    stride = 1
-    while stride < count:
-        upper = (index // stride) % 2 == 1
-        pick = lambda a, b: jnp.where(upper, a, b)
-        if stride * 2 < count:
-            got = swap(element, axis, stride)
-            left = [pick(got[k], own[k]) for k in range(7)]
-            right = [pick(own[k], got[k]) for k in range(7)]
-        else:
-            sent = jnp.stack([pick(own[0], own[2]), pick(own[3], own[4]), pick(own[5], own[6])])
-            got = swap(sent, axis, stride)
-            left = [None, zero, pick(got[0], own[2]), None, pick(got[1], own[4]), None, pick(got[2], own[6])]
-            right = [pick(own[0], got[0]), zero, None, pick(own[3], got[1]), None, pick(own[5], got[2]), None]
-        link = HALF_LINK * (left[6] + right[5])
-        inverse = 1.0 / (1.0 + link * (left[2] + right[0]))
-        gap = left[4] - right[3]
-        levels.append((upper, link, inverse, gap, left[1], right[1]))
-        stride *= 2
-        if stride < count:
-            share = link * inverse
-            first, second = share * left[1], share * right[1]
-            own = [
-                left[0] - first * left[1],
-                first * right[1],
-                right[2] - second * right[1],
-                left[3] - first * gap,
-                right[4] + second * gap,
-                left[5],
-                right[6],
-            ]
-            element = jnp.stack(own)
-    from_low = from_high = jump_low = jump_high = zero
-    for upper, link, inverse, gap, before, after in reversed(levels):
-        jump = (gap + before * from_low - after * from_high) * inverse
-        flow = link * jump
-        from_low, jump_low = jnp.where(upper, flow, from_low), jnp.where(upper, jump, jump_low)
-        from_high, jump_high = jnp.where(upper, from_high, -flow), jnp.where(upper, jump_high, jump)
-    return from_low, from_high, jump_low, jump_high
+def merge(element, got, axis, level, after=()):
+    shape = element.shape[1:]
+    outs = [(7,) + shape] + [(3,) + shape] * (4 << level >= lax.axis_size(axis))
+    merged = call(
+        functools.partial(merge_kernel, axis, level), outs, [element, got], f"merge_{axis}_{level}", after=after
+    )
+    return merged[0], merged[-1]
 
 
 def on_device(volume, owners):
     depth, height, width = volume.shape
-    z_count = lax.axis_size("gz")
+    z_count, y_count = lax.axis_size("gz"), lax.axis_size("xy")
+    z_rounds, y_rounds = z_count.bit_length() - 1, y_count.bit_length() - 1
+    blocks = owners.shape[1]
     flat, plane, side = (depth * height, width), (height, width), (depth, width)
     z_parts, y_parts = (depth, height, width), (height, depth, width)
     part = functools.partial
     field = volume.reshape(flat)
-    edges = call(part(edge_kernel, depth, height), [plane, plane, side, side], [field], "edges")
+    *edges, slots = call(
+        part(edge_kernel, depth, height),
+        [plane, plane, side, side, (blocks, width)],
+        [owners.reshape(1, blocks), field],
+        "edges",
+        smem=(0,),
+    )
     z_sides, y_sides = neighbours(*edges[:2], "gz"), neighbours(*edges[2:], "xy")
     ghosts = ()
     for step in range(STEPS):
-        g_field, z_solved, z_head, z_tail, z_element = call(
+        last = step == STEPS - 1
+        g_field, *z_pieces, z_element = call(
             part(z_kernel, depth, height, step > 0),
             [flat, z_parts, z_parts, z_parts, (7,) + plane],
             [field, *z_sides, *y_sides, *ghosts],
             "z_pieces",
         )
-        z_low, z_high, jump_low, jump_high = flows(z_element, "gz")
-        y_solved, y_head, y_tail, y_element = call(
+        *y_pieces, y_element = call(
             part(y_kernel, depth, height),
             [y_parts, y_parts, y_parts, (7,) + side],
             [g_field, field],
             "y_pieces",
+            after=[z_element],
         )
-        y_low, y_high, _, _ = flows(y_element, "xy")
-        (along_x,) = call(part(x_kernel, 64), [flat], [g_field, field], "x_lines")
-        total, *z_edges = call(
-            part(sum_kernel, depth, height),
-            [flat, plane, plane],
-            [along_x, y_solved, y_head, y_tail, y_low, y_high],
-            "sum_xy",
-        )
-        if step < STEPS - 1:
+        y_sent, y_pairs = y_element, []
+        z_sent, z_pairs = z_element, []
+        for level in range(y_rounds):
+            y_pairs += [y_element, swap(y_sent, "xy", 1 << level)]
+            if level + 1 < y_rounds:
+                y_element, y_sent = merge(*y_pairs[-2:], "xy", level)
+        for level in range(z_rounds):
+            z_pairs += [z_element, swap(z_sent, "gz", 1 << level)]
+            behind = [y_element] if level == 0 else []
+            if level == 1:
+                (along_x,) = call(
+                    part(x_kernel, depth * height), [flat], [g_field, field], "x_lines", after=[z_element]
+                )
+                total, *z_edges = call(
+                    part(sum_kernel, depth, height, not last),
+                    [flat] + [plane, plane] * (not last),
+                    [along_x, *y_pieces, *y_pairs],
+                    "sum_xy",
+                )
+                behind = [total]
+            if level + 1 < z_rounds:
+                z_element, z_sent = merge(*z_pairs[-2:], "gz", level, behind)
+        if not last:
             z_sides = neighbours(*z_edges, "gz")
             field, *rest = call(
                 part(step_kernel, depth, height),
                 [flat, side, side, plane, plane],
-                [total, z_solved, z_head, z_tail, z_low, z_high, jump_low, jump_high],
+                [total, *z_pieces, *z_pairs],
                 "new_field",
             )
             y_sides, ghosts = neighbours(*rest[:2], "xy"), rest[2:]
-    blocks = owners.shape[1]
     field, outgoing = call(
         part(last_kernel, depth, height),
         [flat, (z_count * MOST, BLOCK_ROWS, width)],
-        [total, z_solved, z_head, z_tail, z_low, z_high, owners.reshape(1, blocks)],
+        [slots, total, *z_pieces, *z_pairs],
         "denoised",
-        smem=(6,),
     )
     incoming = lax.all_to_all(outgoing, "gz", split_axis=0, concat_axis=0, tiled=True)
     return field.reshape(volume.shape), incoming.reshape(1, z_count * MOST, BLOCK_ROWS, width)

time: 118 us -> 78.9 us (0.67)
  Pallas kernels: 36 us -> 9.12 us
  starting transfers between devices: 31.3 us -> 20.9 us
  other arithmetic: 5.43 us -> 0 us
  waiting for transfers between devices: 13.8 us -> 17.3 us
    pallas_call x11 -> x17, Pallas kernels: 36 us -> 9.12 us  [call(): pl.pallas_call(lambda *refs: body(*refs[:count], *refs[count + len(after)...]
    ppermute x14, starting transfers between devices: 28.7 us -> 12.2 us  [swap(): return lax.ppermute(values, axis, [(i, i ^ stride) for i in range(count)])]
    ppermute x4, starting transfers between devices: 2.62 us -> 8.68 us  [neighbours(): lax.ppermute(second, axis, other + [(j, i) for i, j in other])]
    select_n x16 -> x0, other arithmetic: 5.21 us -> none  [the longest x4 2.54 us: flows(): jnp.where(upper, from_high, -flow)]
    ppermute x4, waiting for transfers between devices: 0.01 us -> 4.16 us  [neighbours(): lax.ppermute(second, axis, other + [(j, i) for i, j in other])]
    unnamed x25 -> x7, local copies, waits for them, and re-layouts: 2.76 us -> 2.57 us
  transfers between devices with their start and end apart: 18 -> 18, of which waited for: 7 -> 8; matrix products, arithmetic and copies ran while one was open for 3% -> 0% of each run, Pallas kernels for 19% -> 9%
where the time goes in v2:
time: 78.9 us; the launch traced here: 78.7 us
  blocking collectives  28 us (35%)
  starting transfers between devices  20.9 us (26%)
  waiting for transfers between devices  17.3 us (22%)
  Pallas kernels  9.12 us (12%)
  local copies, waits for them, and re-layouts  2.57 us (3%)
  between operations  0.82 us (1%)
    all_to_all x1, blocking collectives, on_device(): lax.all_to_all(outgoing, 'gz', split_axis=0, concat_axis=0, tiled=True)  28 us
    ppermute x14, waiting for transfers between devices, swap(): return lax.ppermute(values, axis, [(i, i ^ stride) for i in range(count)])  13.2 us
    ppermute x14, starting transfers between devices, swap(): return lax.ppermute(values, axis, [(i, i ^ stride) for i in range(count)])  12.2 us
    pallas_call x17, Pallas kernels, call(): pl.pallas_call(lambda *refs: body(*refs[:count], *refs[count + len(after)...  9.12 us
    ppermute x4, starting transfers between devices, neighbours(): lax.ppermute(second, axis, other + [(j, i) for i, j in other])  8.68 us
    ppermute x4, waiting for transfers between devices, neighbours(): lax.ppermute(second, axis, other + [(j, i) for i, j in other])  4.16 us
    unnamed x7, local copies, waits for them, and re-layouts  2.57 us
  transfers between devices with their start and end apart: 18, of which 8 were waited for; matrix products, arithmetic and copies ran while one was open for 0% of the time, Pallas kernels for 9%

profile of v2, /device:TPU:0, one launch (start us, length us, event | category | flops | bytes accessed | tf_op | source)
XLA Modules:
  0.0 78.7 jit_solution(10266639252328594519)
XLA Ops:
  0.6 0.6 copy-done.2
  1.3 0.9 %copy-done = f32[16,32,128]{2,1,0:T(8,128)S(1)} copy-done((f32[16,32,128]{2,1,0:T(8,128)S(1)}, f32[16,32,128]{2,1,0:T(8,128)}, u32[]{:S(2)}) %copy-start) | copy-done | bytes 262168
  2.2 0.6 edges.1
  2.8 3.1 %collective-permute-start = (f32[32,128]{1,0:T(8,128)S(1)}, f32[32,128]{1,0:T(8,128)S(1)}, u32[]{:S(2)}, u32[]{:S(2)}) collective-permute-start(f32[32,128]{1,0:T(8,128)S(1)} %get-tuple-element.44), channel_id=1, source_target_pairs={{0,4},{4,0},{8,12},{12,8},{16,20},{20,16},{24,28},{28,24},{1,5},{5... | collective-permute-start | bytes 49160 | tf_op jit(solution)/shard_map/ppermute | solution.py:276
  5.9 3.5 %collective-permute-start.1 = (f32[32,128]{1,0:T(8,128)S(1)}, f32[32,128]{1,0:T(8,128)S(1)}, u32[]{:S(2)}, u32[]{:S(2)}) collective-permute-start(f32[32,128]{1,0:T(8,128)S(1)} %get-tuple-element.45), channel_id=1, source_target_pairs={{4,8},{12,16},{20,24},{28,0},{8,4},{16,12},{24,20},{0,28},{5,9},{1... | collective-permute-start | bytes 49160 | tf_op jit(solution)/shard_map/ppermute | solution.py:282
  9.4 0.0 collective-permute-start.2
  9.4 1.6 %collective-permute-start.3 = (f32[16,128]{1,0:T(8,128)S(1)}, f32[16,128]{1,0:T(8,128)S(1)}, u32[]{:S(2)}, u32[]{:S(2)}) collective-permute-start(f32[16,128]{1,0:T(8,128)S(1)} %get-tuple-element.47), channel_id=1, source_target_pairs={{1,2},{3,0},{2,1},{0,3},{5,6},{7,4},{6,5},{4,7},{9,10},{11,8},{10,... | collective-permute-start | bytes 24584 | tf_op jit(solution)/shard_map/ppermute | solution.py:282
  11.0 0.0 collective-permute-done.2.refs_3_
  11.0 1.5 %collective-permute-done.3.refs_4_ = f32[16,128]{1,0:T(8,128)S(1)} collective-permute-done((f32[16,128]{1,0:T(8,128)S(1)}, f32[16,128]{1,0:T(8,128)S(1)}, u32[]{:S(2)}, u32[]{:S(2)}) %collective-permute-start.3) | collective-permute-done | bytes 8224 | tf_op jit(solution)/shard_map/ppermute | solution.py:282
  12.5 0.0 collective-permute-done.refs_1_
  12.5 0.0 collective-permute-done.1.refs_2_
  12.5 0.4 z_pieces.2
  12.9 0.1 collective-permute-start.4
  13.0 0.4 y_pieces.2
  13.4 0.6 collective-permute-start.5
  14.0 0.9 %collective-permute-done.5.refs_1_.refs_5_ = f32[7,16,128]{2,1,0:T(8,128)S(1)} collective-permute-done((f32[7,16,128]{2,1,0:T(8,128)S(1)}, f32[7,16,128]{2,1,0:T(8,128)S(1)}, u32[]{:S(2)}, u32[]{:S(2)}) %collective-permute-start.5) | collective-permute-done | bytes 57376 | tf_op jit(solution)/shard_map/ppermute | solution.py:276
  14.9 3.6 %collective-permute-done.4.refs_1_.refs_5_ = f32[7,32,128]{2,1,0:T(8,128)S(1)} collective-permute-done((f32[7,32,128]{2,1,0:T(8,128)S(1)}, f32[7,32,128]{2,1,0:T(8,128)S(1)}, u32[]{:S(2)}, u32[]{:S(2)}) %collective-permute-start.4) | collective-permute-done | bytes 114720 | tf_op jit(solution)/shard_map/ppermute | solution.py:276
  18.6 0.1 collective-permute-start.7
  18.7 1.6 %collective-permute-start.6 = (f32[3,16,128]{2,1,0:T(8,128)S(1)}, f32[3,16,128]{2,1,0:T(8,128)S(1)}, u32[]{:S(2)}, u32[]{:S(2)}) collective-permute-start(f32[3,16,128]{2,1,0:T(8,128)S(1)} %get-tuple-element.55), channel_id=1, source_target_pairs={{0,2},{1,3},{2,0},{3,1},{4,6},{5,7},{6,4},{7,5},{8,10},{9,11},{10,... | collective-permute-start | bytes 73736 | tf_op jit(solution)/shard_map/ppermute | solution.py:276
  20.2 2.5 %x_lines.2.refs_0_ = f32[512,128]{1,0:T(8,128)S(1)} custom-call(f32[512,128]{1,0:T(8,128)S(1)} %get-tuple-element.48.refs_0_, f32[512,128]{1,0:T(8,128)S(1)} %bitcast.7, f32[7,32,128]{2,1,0:T(8,128)S(1)} %merge_gz_0.2.refs_2_.refs_0_.refs_6_), custom_call_target="tpu_custom_call" | custom-call | tf_op jit(solution)/shard_map/x_lines/pallas_call | solution.py:26
  22.7 0.0 collective-permute-done.6.refs_7_
  22.8 0.4 sum_xy.2
  23.1 0.3 collective-permute-done.7.refs_1_.refs_7_
  23.5 1.4 %collective-permute-start.8 = (f32[3,32,128]{2,1,0:T(8,128)S(1)}, f32[3,32,128]{2,1,0:T(8,128)S(1)}, u32[]{:S(2)}, u32[]{:S(2)}) collective-permute-start(f32[3,32,128]{2,1,0:T(8,128)S(1)} %get-tuple-element.61), channel_id=1, source_target_pairs={{0,16},{4,20},{8,24},{12,28},{16,0},{20,4},{24,8},{28,12},{1,17},{... | collective-permute-start | bytes 147464 | tf_op jit(solution)/shard_map/ppermute | solution.py:276
  24.9 2.0 %collective-permute-start.9 = (f32[32,128]{1,0:T(8,128)S(1)}, f32[32,128]{1,0:T(8,128)S(1)}, u32[]{:S(2)}, u32[]{:S(2)}) collective-permute-start(f32[32,128]{1,0:T(8,128)S(1)} %get-tuple-element.63), channel_id=1, source_target_pairs={{0,4},{4,0},{8,12},{12,8},{16,20},{20,16},{24,28},{28,24},{1,5},{5... | collective-permute-start | bytes 49160 | tf_op jit(solution)/shard_map/ppermute | solution.py:276
  26.9 2.1 %collective-permute-start.10 = (f32[32,128]{1,0:T(8,128)S(1)}, f32[32,128]{1,0:T(8,128)S(1)}, u32[]{:S(2)}, u32[]{:S(2)}) collective-permute-start(f32[32,128]{1,0:T(8,128)S(1)} %get-tuple-element.64), channel_id=1, source_target_pairs={{4,8},{12,16},{20,24},{28,0},{8,4},{16,12},{24,20},{0,28},{5,9},{1... | collective-permute-start | bytes 49160 | tf_op jit(solution)/shard_map/ppermute | solution.py:282
  29.0 0.0 collective-permute-done.8.refs_9_
  29.0 0.1 new_field.1
  29.2 0.1 collective-permute-start.11
  29.2 1.4 %collective-permute-start.12 = (f32[16,128]{1,0:T(8,128)S(1)}, f32[16,128]{1,0:T(8,128)S(1)}, u32[]{:S(2)}, u32[]{:S(2)}) collective-permute-start(f32[16,128]{1,0:T(8,128)S(1)} %get-tuple-element.66), channel_id=1, source_target_pairs={{1,2},{3,0},{2,1},{0,3},{5,6},{7,4},{6,5},{4,7},{9,10},{11,8},{10,... | collective-permute-start | bytes 24584 | tf_op jit(solution)/shard_map/ppermute | solution.py:282
  30.6 2.7 %collective-permute-done.10.refs_2_ = f32[32,128]{1,0:T(8,128)S(1)} collective-permute-done((f32[32,128]{1,0:T(8,128)S(1)}, f32[32,128]{1,0:T(8,128)S(1)}, u32[]{:S(2)}, u32[]{:S(2)}) %collective-permute-start.10) | collective-permute-done | bytes 16416 | tf_op jit(solution)/shard_map/ppermute | solution.py:282
  33.3 0.0 collective-permute-done.12.refs_4_
  33.3 0.4 z_pieces.3
  33.7 0.1 collective-permute-start.13
  33.8 0.4 y_pieces.3
  34.2 0.1 collective-permute-start.14
  34.3 1.2 %collective-permute-done.14.refs_1_.refs_5_ = f32[7,16,128]{2,1,0:T(8,128)S(1)} collective-permute-done((f32[7,16,128]{2,1,0:T(8,128)S(1)}, f32[7,16,128]{2,1,0:T(8,128)S(1)}, u32[]{:S(2)}, u32[]{:S(2)}) %collective-permute-start.14) | collective-permute-done | bytes 57376 | tf_op jit(solution)/shard_map/ppermute | solution.py:276
  35.6 3.1 %collective-permute-done.13.refs_1_.refs_6_ = f32[7,32,128]{2,1,0:T(8,128)S(1)} collective-permute-done((f32[7,32,128]{2,1,0:T(8,128)S(1)}, f32[7,32,128]{2,1,0:T(8,128)S(1)}, u32[]{:S(2)}, u32[]{:S(2)}) %collective-permute-start.13) | collective-permute-done | bytes 114720 | tf_op jit(solution)/shard_map/ppermute | solution.py:276
  38.7 0.9 %collective-permute-start.16 = (f32[7,32,128]{2,1,0:T(8,128)S(1)}, f32[7,32,128]{2,1,0:T(8,128)S(1)}, u32[]{:S(2)}, u32[]{:S(2)}) collective-permute-start(f32[7,32,128]{2,1,0:T(8,128)S(1)} %merge_gz_0.3.refs_2_.refs_0_.refs_7_), channel_id=1, source_target_pairs={{0,8},{4,12},{8,0},{12,4},{16,24},{20,28},{24,16},{28,20},{1,9},{5... | collective-permute-start | bytes 344072 | tf_op jit(solution)/shard_map/ppermute | solution.py:276
  39.6 1.3 %collective-permute-start.15 = (f32[3,16,128]{2,1,0:T(8,128)S(1)}, f32[3,16,128]{2,1,0:T(8,128)S(1)}, u32[]{:S(2)}, u32[]{:S(2)}) collective-permute-start(f32[3,16,128]{2,1,0:T(8,128)S(1)} %get-tuple-element.76), channel_id=1, source_target_pairs={{0,2},{1,3},{2,0},{3,1},{4,6},{5,7},{6,4},{7,5},{8,10},{9,11},{10,... | collective-permute-start | bytes 73736 | tf_op jit(solution)/shard_map/ppermute | solution.py:276
  40.9 2.5 %x_lines.3.refs_0_ = f32[512,128]{1,0:T(8,128)S(1)} custom-call(f32[512,128]{1,0:T(8,128)S(1)} %get-tuple-element.69.refs_0_, f32[512,128]{1,0:T(8,128)S(1)} %get-tuple-element.62.refs_0_.refs_1_, f32[7,32,128]{2,1,0:T(8,128)S(1)} %merge_gz_0.3.refs_2_.refs_0_.refs_7_), custom_call_target="tpu_custom_call" | custom-call | tf_op jit(solution)/shard_map/x_lines/pallas_call | solution.py:26
  43.4 0.0 collective-permute-done.15.refs_7_
  43.4 0.3 sum_xy.3.refs_2_.refs_1_
  43.9 1.1 %collective-permute-start.17 = (f32[3,32,128]{2,1,0:T(8,128)S(1)}, f32[3,32,128]{2,1,0:T(8,128)S(1)}, u32[]{:S(2)}, u32[]{:S(2)}) collective-permute-start(f32[3,32,128]{2,1,0:T(8,128)S(1)} %get-tuple-element.81), channel_id=1, source_target_pairs={{0,16},{4,20},{8,24},{12,28},{16,0},{20,4},{24,8},{28,12},{1,17},{... | collective-permute-start | bytes 147464 | tf_op jit(solution)/shard_map/ppermute | solution.py:276
  44.9 4.0 %collective-permute-done.17.refs_10_ = f32[3,32,128]{2,1,0:T(8,128)S(1)} collective-permute-done((f32[3,32,128]{2,1,0:T(8,128)S(1)}, f32[3,32,128]{2,1,0:T(8,128)S(1)}, u32[]{:S(2)}, u32[]{:S(2)}) %collective-permute-start.17) | collective-permute-done | bytes 49184 | tf_op jit(solution)/shard_map/ppermute | solution.py:276
  48.9 0.9 %denoised.1 = (f32[512,128]{1,0:T(8,128)}, f32[16,128,128]{2,1,0:T(8,128)S(1)}) custom-call(f32[4,128]{1,0:T(4,128)S(1)} %get-tuple-element.43.refs_0_, f32[512,128]{1,0:T(8,128)S(1)} %sum_xy.3.refs_2_.refs_1_, f32[16,32,128]{2,1,0:T(8,128)S(1)} %get-tuple-element.77.refs_2_, f32[16,32,128]{2,1,0:T(8,128)S(1)} %get-tuple-element.78.refs_3_, ...), custom_call_target="tpu_custom_call" | custom-call | tf_op jit(solution)/shard_map/denoised/pallas_call | solution.py:26
  49.8 28.0 %all_to_all.5 = f32[16,128,128]{2,1,0:T(8,128)S(1)} all-to-all(f32[16,128,128]{2,1,0:T(8,128)S(1)} %get-tuple-element.83), channel_id=1, replica_groups=mesh['gz'=8,'xy'=4] {'gz'}, dimensions={0} | all-to-all | bytes 2097152 | tf_op jit(solution)/shard_map/all_to_all | solution.py:364
  77.7 1.0 %copy.5 = f32[1,16,128,128]{3,2,1,0:T(8,128)} copy(f32[1,16,128,128]{3,2,1,0:T(8,128)S(1)} %bitcast.9) | data formatting | bytes 2097152
  (13 shorter events, 0.2 us)
Async XLA Ops:
  0.6 0.7 copy-start.2
  1.3 0.9 %copy-start = (f32[16,32,128]{2,1,0:T(8,128)S(1)}, f32[16,32,128]{2,1,0:T(8,128)}, u32[]{:S(2)}) copy-start(f32[16,32,128]{2,1,0:T(8,128)} %param.2) | copy-start | bytes 786436
  2.2 10.3 %copy-start.1 = (f32[16,32,128]{2,1,0:T(8,128)S(1)}, f32[16,32,128]{2,1,0:T(8,128)}, u32[]{:S(2)}) copy-start(f32[16,32,128]{2,1,0:T(8,128)} %param.2) | copy-start | bytes 786436
  2.8 9.7 %collective-permute-start = (f32[32,128]{1,0:T(8,128)S(1)}, f32[32,128]{1,0:T(8,128)S(1)}, u32[]{:S(2)}, u32[]{:S(2)}) collective-permute-start(f32[32,128]{1,0:T(8,128)S(1)} %get-tuple-element.44), channel_id=1, source_target_pairs={{0,4},{4,0},{8,12},{12,8},{16,20},{20,16},{24,28},{28,24},{1,5},{5... | collective-permute-start | bytes 49160 | tf_op jit(solution)/shard_map/ppermute | solution.py:276
  5.9 6.6 %collective-permute-start.1 = (f32[32,128]{1,0:T(8,128)S(1)}, f32[32,128]{1,0:T(8,128)S(1)}, u32[]{:S(2)}, u32[]{:S(2)}) collective-permute-start(f32[32,128]{1,0:T(8,128)S(1)} %get-tuple-element.45), channel_id=1, source_target_pairs={{4,8},{12,16},{20,24},{28,0},{8,4},{16,12},{24,20},{0,28},{5,9},{1... | collective-permute-start | bytes 49160 | tf_op jit(solution)/shard_map/ppermute | solution.py:282
  9.4 1.6 %collective-permute-start.2 = (f32[16,128]{1,0:T(8,128)S(1)}, f32[16,128]{1,0:T(8,128)S(1)}, u32[]{:S(2)}, u32[]{:S(2)}) collective-permute-start(f32[16,128]{1,0:T(8,128)S(1)} %get-tuple-element.46), channel_id=1, source_target_pairs={{0,1},{1,0},{2,3},{3,2},{4,5},{5,4},{6,7},{7,6},{8,9},{9,8},{10,11... | collective-permute-start | bytes 24584 | tf_op jit(solution)/shard_map/ppermute | solution.py:276
  9.4 3.1 %collective-permute-start.3 = (f32[16,128]{1,0:T(8,128)S(1)}, f32[16,128]{1,0:T(8,128)S(1)}, u32[]{:S(2)}, u32[]{:S(2)}) collective-permute-start(f32[16,128]{1,0:T(8,128)S(1)} %get-tuple-element.47), channel_id=1, source_target_pairs={{1,2},{3,0},{2,1},{0,3},{5,6},{7,4},{6,5},{4,7},{9,10},{11,8},{10,... | collective-permute-start | bytes 24584 | tf_op jit(solution)/shard_map/ppermute | solution.py:282
  12.9 5.6 %collective-permute-start.4 = (f32[7,32,128]{2,1,0:T(8,128)S(1)}, f32[7,32,128]{2,1,0:T(8,128)S(1)}, u32[]{:S(2)}, u32[]{:S(2)}) collective-permute-start(f32[7,32,128]{2,1,0:T(8,128)S(1)} %get-tuple-element.49.refs_2_.refs_0_.refs_4_), channel_id=1, source_target_pairs={{0,4},{4,0},{8,12},{12,8},{16,20},{20,16},{24,28},{28,24},{1,5},{5... | collective-permute-start | bytes 344072 | tf_op jit(solution)/shard_map/ppermute | solution.py:276
  13.4 1.5 %collective-permute-start.5 = (f32[7,16,128]{2,1,0:T(8,128)S(1)}, f32[7,16,128]{2,1,0:T(8,128)S(1)}, u32[]{:S(2)}, u32[]{:S(2)}) collective-permute-start(f32[7,16,128]{2,1,0:T(8,128)S(1)} %get-tuple-element.50.refs_0_.refs_4_), channel_id=1, source_target_pairs={{0,1},{1,0},{2,3},{3,2},{4,5},{5,4},{6,7},{7,6},{8,9},{9,8},{10,11... | collective-permute-start | bytes 172040 | tf_op jit(solution)/shard_map/ppermute | solution.py:276
  18.6 4.9 %collective-permute-start.7 = (f32[7,32,128]{2,1,0:T(8,128)S(1)}, f32[7,32,128]{2,1,0:T(8,128)S(1)}, u32[]{:S(2)}, u32[]{:S(2)}) collective-permute-start(f32[7,32,128]{2,1,0:T(8,128)S(1)} %merge_gz_0.2.refs_2_.refs_0_.refs_6_), channel_id=1, source_target_pairs={{0,8},{4,12},{8,0},{12,4},{16,24},{20,28},{24,16},{28,20},{1,9},{5... | collective-permute-start | bytes 344072 | tf_op jit(solution)/shard_map/ppermute | solution.py:276
  18.7 4.1 %collective-permute-start.6 = (f32[3,16,128]{2,1,0:T(8,128)S(1)}, f32[3,16,128]{2,1,0:T(8,128)S(1)}, u32[]{:S(2)}, u32[]{:S(2)}) collective-permute-start(f32[3,16,128]{2,1,0:T(8,128)S(1)} %get-tuple-element.55), channel_id=1, source_target_pairs={{0,2},{1,3},{2,0},{3,1},{4,6},{5,7},{6,4},{7,5},{8,10},{9,11},{10,... | collective-permute-start | bytes 73736 | tf_op jit(solution)/shard_map/ppermute | solution.py:276
  23.5 5.5 %collective-permute-start.8 = (f32[3,32,128]{2,1,0:T(8,128)S(1)}, f32[3,32,128]{2,1,0:T(8,128)S(1)}, u32[]{:S(2)}, u32[]{:S(2)}) collective-permute-start(f32[3,32,128]{2,1,0:T(8,128)S(1)} %get-tuple-element.61), channel_id=1, source_target_pairs={{0,16},{4,20},{8,24},{12,28},{16,0},{20,4},{24,8},{28,12},{1,17},{... | collective-permute-start | bytes 147464 | tf_op jit(solution)/shard_map/ppermute | solution.py:276
  24.9 5.8 %collective-permute-start.9 = (f32[32,128]{1,0:T(8,128)S(1)}, f32[32,128]{1,0:T(8,128)S(1)}, u32[]{:S(2)}, u32[]{:S(2)}) collective-permute-start(f32[32,128]{1,0:T(8,128)S(1)} %get-tuple-element.63), channel_id=1, source_target_pairs={{0,4},{4,0},{8,12},{12,8},{16,20},{20,16},{24,28},{28,24},{1,5},{5... | collective-permute-start | bytes 49160 | tf_op jit(solution)/shard_map/ppermute | solution.py:276
  26.9 6.4 %collective-permute-start.10 = (f32[32,128]{1,0:T(8,128)S(1)}, f32[32,128]{1,0:T(8,128)S(1)}, u32[]{:S(2)}, u32[]{:S(2)}) collective-permute-start(f32[32,128]{1,0:T(8,128)S(1)} %get-tuple-element.64), channel_id=1, source_target_pairs={{4,8},{12,16},{20,24},{28,0},{8,4},{16,12},{24,20},{0,28},{5,9},{1... | collective-permute-start | bytes 49160 | tf_op jit(solution)/shard_map/ppermute | solution.py:282
  29.2 4.2 %collective-permute-start.11 = (f32[16,128]{1,0:T(8,128)S(1)}, f32[16,128]{1,0:T(8,128)S(1)}, u32[]{:S(2)}, u32[]{:S(2)}) collective-permute-start(f32[16,128]{1,0:T(8,128)S(1)} %get-tuple-element.65), channel_id=1, source_target_pairs={{0,1},{1,0},{2,3},{3,2},{4,5},{5,4},{6,7},{7,6},{8,9},{9,8},{10,11... | collective-permute-start | bytes 24584 | tf_op jit(solution)/shard_map/ppermute | solution.py:276
  29.2 4.1 %collective-permute-start.12 = (f32[16,128]{1,0:T(8,128)S(1)}, f32[16,128]{1,0:T(8,128)S(1)}, u32[]{:S(2)}, u32[]{:S(2)}) collective-permute-start(f32[16,128]{1,0:T(8,128)S(1)} %get-tuple-element.66), channel_id=1, source_target_pairs={{1,2},{3,0},{2,1},{0,3},{5,6},{7,4},{6,5},{4,7},{9,10},{11,8},{10,... | collective-permute-start | bytes 24584 | tf_op jit(solution)/shard_map/ppermute | solution.py:282
  33.7 4.9 %collective-permute-start.13 = (f32[7,32,128]{2,1,0:T(8,128)S(1)}, f32[7,32,128]{2,1,0:T(8,128)S(1)}, u32[]{:S(2)}, u32[]{:S(2)}) collective-permute-start(f32[7,32,128]{2,1,0:T(8,128)S(1)} %get-tuple-element.70.refs_2_.refs_0_.refs_5_), channel_id=1, source_target_pairs={{0,4},{4,0},{8,12},{12,8},{16,20},{20,16},{24,28},{28,24},{1,5},{5... | collective-permute-start | bytes 344072 | tf_op jit(solution)/shard_map/ppermute | solution.py:276
  34.2 1.3 %collective-permute-start.14 = (f32[7,16,128]{2,1,0:T(8,128)S(1)}, f32[7,16,128]{2,1,0:T(8,128)S(1)}, u32[]{:S(2)}, u32[]{:S(2)}) collective-permute-start(f32[7,16,128]{2,1,0:T(8,128)S(1)} %get-tuple-element.71.refs_0_.refs_4_), channel_id=1, source_target_pairs={{0,1},{1,0},{2,3},{3,2},{4,5},{5,4},{6,7},{7,6},{8,9},{9,8},{10,11... | collective-permute-start | bytes 172040 | tf_op jit(solution)/shard_map/ppermute | solution.py:276
  38.7 5.1 %collective-permute-start.16 = (f32[7,32,128]{2,1,0:T(8,128)S(1)}, f32[7,32,128]{2,1,0:T(8,128)S(1)}, u32[]{:S(2)}, u32[]{:S(2)}) collective-permute-start(f32[7,32,128]{2,1,0:T(8,128)S(1)} %merge_gz_0.3.refs_2_.refs_0_.refs_7_), channel_id=1, source_target_pairs={{0,8},{4,12},{8,0},{12,4},{16,24},{20,28},{24,16},{28,20},{1,9},{5... | collective-permute-start | bytes 344072 | tf_op jit(solution)/shard_map/ppermute | solution.py:276
  39.6 3.8 %collective-permute-start.15 = (f32[3,16,128]{2,1,0:T(8,128)S(1)}, f32[3,16,128]{2,1,0:T(8,128)S(1)}, u32[]{:S(2)}, u32[]{:S(2)}) collective-permute-start(f32[3,16,128]{2,1,0:T(8,128)S(1)} %get-tuple-element.76), channel_id=1, source_target_pairs={{0,2},{1,3},{2,0},{3,1},{4,6},{5,7},{6,4},{7,5},{8,10},{9,11},{10,... | collective-permute-start | bytes 73736 | tf_op jit(solution)/shard_map/ppermute | solution.py:276
  43.9 5.1 %collective-permute-start.17 = (f32[3,32,128]{2,1,0:T(8,128)S(1)}, f32[3,32,128]{2,1,0:T(8,128)S(1)}, u32[]{:S(2)}, u32[]{:S(2)}) collective-permute-start(f32[3,32,128]{2,1,0:T(8,128)S(1)} %get-tuple-element.81), channel_id=1, source_target_pairs={{0,16},{4,20},{8,24},{12,28},{16,0},{20,4},{24,8},{28,12},{1,17},{... | collective-permute-start | bytes 147464 | tf_op jit(solution)/shard_map/ppermute | solution.py:276

commit v3 on v2

--- a/solution.py
+++ b/solution.py
@@ -9,6 +9,7 @@
 
 STEPS = 2
 MOST = 2
+CHUNKS = 2
 BLOCK_ROWS = 128
 TIME_STEP = 30.0
 CONTRAST = 4.0
@@ -33,7 +34,7 @@
     )(*ins, *after)
 
 
-def edge_kernel(depth, height, owners, field, z_first, z_second, y_first, y_second, slots):
+def edge_kernel(depth, height, field, z_first, z_second, y_first, y_second):
     z_odd = lax.rem(lax.axis_index("gz"), 2) == 1
     y_odd = lax.rem(lax.axis_index("xy"), 2) == 1
     bottom, top = field[pl.ds(0, height), :], field[pl.ds((depth - 1) * height, height), :]
@@ -43,7 +44,11 @@
     far = field[pl.ds(height - 1, depth, stride=height), :]
     y_first[...] = jnp.where(y_odd, near, far)
     y_second[...] = jnp.where(y_odd, far, near)
-    for block in range(slots.shape[0]):
+
+
+def slot_kernel(owners, slots):
+    slots[...] = jnp.zeros_like(slots)
+    for block in range(owners.shape[1]):
         rank = jnp.int32(0)
         for other in range(block):
             rank = rank + (owners[0, other] == owners[0, block]).astype(jnp.int32)
@@ -139,32 +144,24 @@
     chain(g_rows, v_rows, height, solved, head, tail, element)
 
 
-def x_kernel(rows, g_field, field, solved):
+def x_kernel(first, rows, g_field, field, solved):
     width = field.shape[1]
+    at = pl.ds(first, rows)
+    g, right = g_field[at, :], field[at, :]
     lanes = lax.broadcasted_iota(jnp.int32, (rows, width), 1)
-
-    def piece(step, carry):
-        at = pl.ds(pl.multiple_of(step * rows, rows), rows)
-        g = g_field[at, :]
-        right = field[at, :]
-        link = jnp.where(
-            lanes == width - 1, 0.0, HALF_LINK * (g + pltpu.roll(g, width - 1, 1))
-        )
-        main = 1.0 + link + pltpu.roll(link, 1, 1)
-        stride = 1
-        while stride < width:
-            inverse = 1.0 / main
-            factor = link * inverse
-            back = width - stride
-            ahead = link * pltpu.roll(inverse, back, 1)
-            main = main - pltpu.roll(link * factor, stride, 1) - link * ahead
-            right = right + pltpu.roll(factor * right, stride, 1) + ahead * pltpu.roll(right, back, 1)
-            link = ahead * pltpu.roll(link, back, 1)
-            stride *= 2
-        solved[at, :] = right / main
-        return carry
-
-    lax.fori_loop(0, field.shape[0] // rows, piece, 0)
+    link = jnp.where(lanes == width - 1, 0.0, HALF_LINK * (g + pltpu.roll(g, width - 1, 1)))
+    main = 1.0 + link + pltpu.roll(link, 1, 1)
+    stride = 1
+    while stride < width:
+        inverse = 1.0 / main
+        factor = link * inverse
+        back = width - stride
+        ahead = link * pltpu.roll(inverse, back, 1)
+        main = main - pltpu.roll(link * factor, stride, 1) - link * ahead
+        right = right + pltpu.roll(factor * right, stride, 1) + ahead * pltpu.roll(right, back, 1)
+        link = ahead * pltpu.roll(link, back, 1)
+        stride *= 2
+    solved[...] = right / main
 
 
 def join(lower, upper_piece):
@@ -186,7 +183,14 @@
     return lax.rem(lax.div(lax.axis_index(axis), 1 << level), 2) == 1
 
 
-def merge_kernel(axis, level, own, got, *outs):
+def parts(ref, rows):
+    if len(ref.shape) == 3:
+        return [ref[k] for k in range(ref.shape[0])]
+    return [ref[pl.ds(k * rows, rows), :] for k in range(3)]
+
+
+def merge_kernel(axis, level, notes, own, got, *refs):
+    outs = refs[notes:]
     upper = is_upper(axis, level)
     lower, higher = sides(upper, own, got, False)
     link, inverse, gap = join(lower, higher)
@@ -205,8 +209,11 @@
         outs[0][k] = merged[k]
     if len(outs) > 1:
         above = is_upper(axis, level + 1)
+        rows = own.shape[1]
         for k, (high, low) in enumerate(((0, 2), (3, 4), (5, 6))):
-            outs[1][k] = jnp.where(above, merged[high], merged[low])
+            outs[1][pl.ds(k * rows, rows), :] = jnp.where(above, merged[high], merged[low])
+        if notes:
+            outs[1][pl.ds(3 * rows, refs[0].shape[0]), :] = refs[0][...]
 
 
 def unwind(axis, pairs):
@@ -224,13 +231,16 @@
     return from_low, from_high, jump_low, jump_high
 
 
-def sum_kernel(depth, height, edges, along_x, solved, head, tail, *refs):
+def sum_kernel(depth, height, edges, near_x, far_x, solved, head, tail, *refs):
     pairs, outs = refs[: len(refs) - 1 - 2 * edges], refs[len(refs) - 1 - 2 * edges :]
     total = outs[0]
-    low, high, _, _ = unwind("xy", [[ref[k] for k in range(ref.shape[0])] for ref in pairs])
+    low, high, _, _ = unwind("xy", [parts(ref, depth) for ref in pairs])
+    half = depth // 2
     for k in range(height):
-        at = pl.ds(k, depth, stride=height)
-        total[at, :] = along_x[at, :] + (solved[k] + low * head[k] + high * tail[k])
+        along_y = solved[k] + low * head[k] + high * tail[k]
+        at = pl.ds(k, half, stride=height)
+        total[at, :] = near_x[at, :] + along_y[:half]
+        total[pl.ds(half * height + k, half, stride=height), :] = far_x[at, :] + along_y[half:]
     if edges:
         z_odd = lax.rem(lax.axis_index("gz"), 2) == 1
         bottom, top = total[pl.ds(0, height), :], total[pl.ds((depth - 1) * height, height), :]
@@ -240,7 +250,7 @@
 
 def step_kernel(depth, height, total, solved, head, tail, *refs):
     field, y_first, y_second, z_low, z_high = refs[-5:]
-    low, high, jump_low, jump_high = unwind("gz", [[ref[k] for k in range(ref.shape[0])] for ref in refs[:-5]])
+    low, high, jump_low, jump_high = unwind("gz", [parts(ref, height) for ref in refs[:-5]])
     for k in range(depth):
         at = pl.ds(k * height, height)
         along_z = solved[k] + low * head[k] + high * tail[k]
@@ -256,19 +266,66 @@
     y_second[...] = jnp.where(y_odd, far, near)
 
 
-def last_kernel(depth, height, slots, total, solved, head, tail, *refs):
-    field, outgoing = refs[-2:]
-    low, high, _, _ = unwind("gz", [[ref[k] for k in range(ref.shape[0])] for ref in refs[:-2]])
-    outgoing[...] = jnp.zeros_like(outgoing)
-    planes = BLOCK_ROWS // height
-    for block in range(depth // planes):
+def last_kernel(depth, height, total, solved, head, tail, *refs):
+    field, halves = refs[-1 - CHUNKS], refs[-CHUNKS:]
+    low, high, _, _ = unwind("gz", [parts(ref, height) for ref in refs[: -1 - CHUNKS]])
+    planes, piece = BLOCK_ROWS // height, BLOCK_ROWS // CHUNKS
+    for k in range(depth):
+        at = pl.ds(k * height, height)
+        value = (total[at, :] + (solved[k] + low * head[k] + high * tail[k])) * THIRD
+        field[at, :] = value
+        block, row = k // planes, (k % planes) * height
+        halves[row // piece][block, pl.ds(row % piece, height), :] = value
+
+
+def pack_kernel(ways, blocks, slots, *outs):
+    place = lax.rem(lax.axis_index("gz"), ways)
+    base = lax.axis_index("gz") - place
+    for out in outs:
+        out[...] = jnp.zeros_like(out)
+    for block in range(blocks.shape[0]):
         slot = jnp.max(slots[pl.ds(block, 1), :]).astype(jnp.int32)
-        for j in range(planes):
-            k = block * planes + j
-            at = pl.ds(k * height, height)
-            value = (total[at, :] + (solved[k] + low * head[k] + high * tail[k])) * THIRD
-            field[at, :] = value
-            outgoing[slot, pl.ds(j * height, height), :] = value
+        rank, target = lax.rem(slot, MOST), lax.div(slot, MOST) - base
+        for way, out in enumerate(outs):
+
+            @pl.when(target == lax.bitwise_xor(place, way))
+            def _():
+                out[rank] = blocks[block]
+
+
+def pack(ways, blocks, slots, name, after=()):
+    shape = (MOST,) + blocks.shape[1:]
+    return call(functools.partial(pack_kernel, ways), [shape] * ways, [blocks, slots], name, after=after)
+
+
+def place_kernel(plan, count, *refs):
+    incoming, sems = refs[-2:]
+    me = lax.axis_index("gz")
+    copies = []
+    for k, (way, row) in enumerate(plan):
+        rows = refs[k].shape[1]
+        source = lax.bitwise_xor(me, way)
+        target = incoming.at[pl.ds(source * MOST, MOST), pl.ds(row, rows), :]
+        copies.append(pltpu.make_async_copy(refs[k], target, sems.at[k]))
+    for copy in copies:
+        copy.start()
+    for copy in copies:
+        copy.wait()
+
+
+def place(arrays, plan, incoming, shape, name):
+    count = len(arrays)
+    extra = [] if incoming is None else [incoming]
+    return pl.pallas_call(
+        functools.partial(place_kernel, plan, count),
+        out_shape=jax.ShapeDtypeStruct(shape, jnp.float32),
+        in_specs=[pl.BlockSpec(memory_space=VMEM)] * count + [pl.BlockSpec(memory_space=pl.ANY)] * len(extra),
+        out_specs=pl.BlockSpec(memory_space=pl.ANY),
+        scratch_shapes=[pltpu.SemaphoreType.DMA((count,))],
+        input_output_aliases={count: 0} if extra else {},
+        compiler_params=pltpu.CompilerParams(vmem_limit_bytes=VMEM_LIMIT),
+        name=name,
+    )(*arrays, *extra)
 
 
 def swap(values, axis, stride):
@@ -278,17 +335,49 @@
 
 def neighbours(first, second, axis):
     count = lax.axis_size(axis)
-    other = [(i, (i + 1) % count) for i in range(1, count, 2)]
-    return swap(first, axis, 1), lax.ppermute(second, axis, other + [(j, i) for i, j in other])
-
-
-def merge(element, got, axis, level, after=()):
-    shape = element.shape[1:]
-    outs = [(7,) + shape] + [(3,) + shape] * (4 << level >= lax.axis_size(axis))
+    if axis == "xy":
+        other = [(i, (i + 1) % count) for i in range(1, count, 2)]
+        got = lax.ppermute(second, axis, other + [(j, i) for i, j in other])
+    else:
+        near = lax.axis_size("xy")
+        pairs = []
+        for i in range(count):
+            end = i in (0, count - 1)
+            j = i if end else i + 1 if i % 2 else i - 1
+            pairs += [(i * near + c, j * near + (c ^ 1 if end else c)) for c in range(near)]
+        got = lax.ppermute(second, (axis, "xy"), pairs)
+    return swap(first, axis, 1), got
+
+
+def merge(element, got, axis, level, after=(), notes=()):
+    rows, width = element.shape[1:]
+    last = 4 << level >= lax.axis_size(axis)
+    notes = notes if last else ()
+    outs = [element.shape] + [(3 * rows + sum(note.shape[0] for note in notes), width)] * last
     merged = call(
-        functools.partial(merge_kernel, axis, level), outs, [element, got], f"merge_{axis}_{level}", after=after
+        functools.partial(merge_kernel, axis, level, len(notes)),
+        outs,
+        [element, got, *notes],
+        f"merge_{axis}_{level}",
+        after=after,
     )
     return merged[0], merged[-1]
+
+
+def route(halves, blocks, slots, across):
+    count, width = lax.axis_size("gz"), blocks.shape[2]
+    ways, piece = count // 2, BLOCK_ROWS // CHUNKS
+    crossed = [swap(half, "gz", ways) for half in halves]
+    straight = pack(ways, blocks, slots, "straight")
+    arrays = [straight[0]] + [swap(straight[way], "gz", way) for way in range(1, ways)]
+    shape = (count * MOST, BLOCK_ROWS, width)
+    incoming = place(arrays, [(way, 0) for way in range(ways)], None, shape, "place_straight")
+    for chunk in range(CHUNKS):
+        passed = pack(ways, crossed[chunk], across, f"relay_{chunk}")
+        arrays = [passed[0]] + [swap(passed[way], "gz", way) for way in range(1, ways)]
+        plan = [(way ^ ways, chunk * piece) for way in range(ways)]
+        incoming = place(arrays, plan, incoming, shape, f"place_{chunk}")
+    return incoming
 
 
 def on_device(volume, owners):
@@ -300,14 +389,11 @@
     z_parts, y_parts = (depth, height, width), (height, depth, width)
     part = functools.partial
     field = volume.reshape(flat)
-    *edges, slots = call(
-        part(edge_kernel, depth, height),
-        [plane, plane, side, side, (blocks, width)],
-        [owners.reshape(1, blocks), field],
-        "edges",
-        smem=(0,),
+    edges = call(part(edge_kernel, depth, height), [plane, plane, side, side], [field], "edges")
+    z_sides, y_sides = neighbours(*edges[:2], "gz"), neighbours(*edges[2:], "xy")
+    (slots,) = call(
+        slot_kernel, [(-(-blocks // 8) * 8, width)], [owners.reshape(1, blocks)], "slots", smem=(0,), after=edges[:1]
     )
-    z_sides, y_sides = neighbours(*edges[:2], "gz"), neighbours(*edges[2:], "xy")
     ghosts = ()
     for step in range(STEPS):
         last = step == STEPS - 1
@@ -330,22 +416,30 @@
             y_pairs += [y_element, swap(y_sent, "xy", 1 << level)]
             if level + 1 < y_rounds:
                 y_element, y_sent = merge(*y_pairs[-2:], "xy", level)
+        half = (depth // 2 * height, width)
         for level in range(z_rounds):
             z_pairs += [z_element, swap(z_sent, "gz", 1 << level)]
-            behind = [y_element] if level == 0 else []
+            behind = []
+            if level == 0:
+                (near_x,) = call(
+                    part(x_kernel, 0, half[0]), [half], [g_field, field], "x_near", after=[y_element]
+                )
+                behind = [near_x]
             if level == 1:
-                (along_x,) = call(
-                    part(x_kernel, depth * height), [flat], [g_field, field], "x_lines", after=[z_element]
+                (far_x,) = call(
+                    part(x_kernel, half[0], half[0]), [half], [g_field, field], "x_far", after=[z_element]
                 )
                 total, *z_edges = call(
                     part(sum_kernel, depth, height, not last),
                     [flat] + [plane, plane] * (not last),
-                    [along_x, *y_pieces, *y_pairs],
+                    [near_x, far_x, *y_pieces, *y_pairs],
                     "sum_xy",
                 )
                 behind = [total]
             if level + 1 < z_rounds:
-                z_element, z_sent = merge(*z_pairs[-2:], "gz", level, behind)
+                z_element, z_sent = merge(*z_pairs[-2:], "gz", level, behind, () if step else (slots,))
+        if step == 0:
+            across = z_pairs[-1][3 * height :]
         if not last:
             z_sides = neighbours(*z_edges, "gz")
             field, *rest = call(
@@ -355,14 +449,14 @@
                 "new_field",
             )
             y_sides, ghosts = neighbours(*rest[:2], "xy"), rest[2:]
-    field, outgoing = call(
+    field, *halves = call(
         part(last_kernel, depth, height),
-        [flat, (z_count * MOST, BLOCK_ROWS, width)],
-        [slots, total, *z_pieces, *z_pairs],
+        [flat] + [(blocks, BLOCK_ROWS // CHUNKS, width)] * CHUNKS,
+        [total, *z_pieces, *z_pairs],
         "denoised",
     )
-    incoming = lax.all_to_all(outgoing, "gz", split_axis=0, concat_axis=0, tiled=True)
-    return field.reshape(volume.shape), incoming.reshape(1, z_count * MOST, BLOCK_ROWS, width)
+    incoming = route(halves, field.reshape(blocks, BLOCK_ROWS, width), slots, across)
+    return field.reshape(volume.shape), incoming[None]
 
 
 def solution(mesh):

time: 78.9 us -> 69.5 us (0.88)
  blocking collectives: 28 us -> 0 us
  starting transfers between devices: 20.9 us -> 32.6 us
  Pallas kernels: 9.12 us -> 13.6 us
  waiting for transfers between devices: 17.3 us -> 20.4 us
    all_to_all x1 -> x0, blocking collectives: 28 us -> none  [on_device(): lax.all_to_all(outgoing, 'gz', split_axis=0, concat_axis=0, tiled=True)]
    ppermute x14 -> x25, starting transfers between devices: 12.2 us -> 28.8 us  [swap(): return lax.ppermute(values, axis, [(i, i ^ stride) for i in range(count)])]
    ppermute x4, starting transfers between devices: 8.68 us -> 3.76 us  [the longest x2 3.2 us: neighbours(): got = lax.ppermute(second, axis, other + [(j, i) for i, j in other])]
    ppermute x14 -> x25, waiting for transfers between devices: 13.2 us -> 17.4 us  [swap(): return lax.ppermute(values, axis, [(i, i ^ stride) for i in range(count)])]
    pallas_call x0 -> x3, Pallas kernels: none -> 2.27 us  [place(): pl.pallas_call(functools.partial(place_kernel, plan, count), out_shape=ja...]
    pallas_call x17 -> x23, Pallas kernels: 9.12 us -> 11.3 us  [call(): pl.pallas_call(lambda *refs: body(*refs[:count], *refs[count + len(after)...]
    ppermute x4, waiting for transfers between devices: 4.16 us -> 3.01 us  [the longest x2 3.01 us: neighbours(): got = lax.ppermute(second, axis, other + [(j, i) for i, j in other])]
    unnamed x7 -> x8, local copies, waits for them, and re-layouts: 2.57 us -> 1.9 us
  transfers between devices with their start and end apart: 18 -> 29, of which waited for: 8 -> 15; matrix products, arithmetic and copies ran while one was open for 0% -> 0% of each run, Pallas kernels for 9% -> 16%
where the time goes in v3:
time: 69.5 us; the launch traced here: 69.4 us
  starting transfers between devices  32.6 us (47%)
  waiting for transfers between devices  20.4 us (29%)
  Pallas kernels  13.6 us (20%)
  local copies, waits for them, and re-layouts  1.9 us (3%)
  between operations  0.88 us (1%)
    ppermute x25, starting transfers between devices, swap(): return lax.ppermute(values, axis, [(i, i ^ stride) for i in range(count)])  28.8 us
    ppermute x25, waiting for transfers between devices, swap(): return lax.ppermute(values, axis, [(i, i ^ stride) for i in range(count)])  17.4 us
    pallas_call x23, Pallas kernels, call(): pl.pallas_call(lambda *refs: body(*refs[:count], *refs[count + len(after)...  11.3 us
    ppermute x2, starting transfers between devices, neighbours(): got = lax.ppermute(second, axis, other + [(j, i) for i, j in other])  3.2 us
    ppermute x2, waiting for transfers between devices, neighbours(): got = lax.ppermute(second, axis, other + [(j, i) for i, j in other])  3.01 us
    pallas_call x3, Pallas kernels, place(): pl.pallas_call(functools.partial(place_kernel, plan, count), out_shape=ja...  2.27 us
    unnamed x8, local copies, waits for them, and re-layouts  1.9 us
  transfers between devices with their start and end apart: 29, of which 15 were waited for; matrix products, arithmetic and copies ran while one was open for 0% of the time, Pallas kernels for 16%

profile of v3, /device:TPU:0, one launch (start us, length us, event | category | flops | bytes accessed | tf_op | source)
XLA Modules:
  0.0 69.4 jit_solution(16163483693723927082)
XLA Ops:
  0.6 0.9 %copy-done = f32[16,32,128]{2,1,0:T(8,128)S(1)} copy-done((f32[16,32,128]{2,1,0:T(8,128)S(1)}, f32[16,32,128]{2,1,0:T(8,128)}, u32[]{:S(2)}) %copy-start) | copy-done | bytes 262168
  1.6 0.6 collective-permute-start.1
  2.2 4.0 %collective-permute-start = (f32[32,128]{1,0:T(8,128)S(1)}, f32[32,128]{1,0:T(8,128)S(1)}, u32[]{:S(2)}, u32[]{:S(2)}) collective-permute-start(f32[32,128]{1,0:T(8,128)S(1)} %get-tuple-element.55.refs_1_), channel_id=1, source_target_pairs={{0,4},{4,0},{8,12},{12,8},{16,20},{20,16},{24,28},{28,24},{1,5},{5... | collective-permute-start | bytes 49160 | tf_op jit(solution)/shard_map/ppermute | solution.py:333
  6.2 1.6 %collective-permute-start.3 = (f32[16,128]{1,0:T(8,128)S(1)}, f32[16,128]{1,0:T(8,128)S(1)}, u32[]{:S(2)}, u32[]{:S(2)}) collective-permute-start(f32[16,128]{1,0:T(8,128)S(1)} %get-tuple-element.58), channel_id=1, source_target_pairs={{1,2},{3,0},{2,1},{0,3},{5,6},{7,4},{6,5},{4,7},{9,10},{11,8},{10,... | collective-permute-start | bytes 24584 | tf_op jit(solution)/shard_map/ppermute | solution.py:340
  7.8 1.5 %collective-permute-done.3.refs_4_ = f32[16,128]{1,0:T(8,128)S(1)} collective-permute-done((f32[16,128]{1,0:T(8,128)S(1)}, f32[16,128]{1,0:T(8,128)S(1)}, u32[]{:S(2)}, u32[]{:S(2)}) %collective-permute-start.3) | collective-permute-done | bytes 8224 | tf_op jit(solution)/shard_map/ppermute | solution.py:340
  9.7 0.7 %collective-permute-start.5 = (f32[7,32,128]{2,1,0:T(8,128)S(1)}, f32[7,32,128]{2,1,0:T(8,128)S(1)}, u32[]{:S(2)}, u32[]{:S(2)}) collective-permute-start(f32[7,32,128]{2,1,0:T(8,128)S(1)} %get-tuple-element.60.refs_2_.refs_0_.refs_4_), channel_id=1, source_target_pairs={{0,4},{4,0},{8,12},{12,8},{16,20},{20,16},{24,28},{28,24},{1,5},{5... | collective-permute-start | bytes 344072 | tf_op jit(solution)/shard_map/ppermute | solution.py:333
  10.4 0.4 y_pieces.2
  10.9 1.2 %collective-permute-done.4.refs_1_.refs_6_ = f32[7,16,128]{2,1,0:T(8,128)S(1)} collective-permute-done((f32[7,16,128]{2,1,0:T(8,128)S(1)}, f32[7,16,128]{2,1,0:T(8,128)S(1)}, u32[]{:S(2)}, u32[]{:S(2)}) %collective-permute-start.4) | collective-permute-done | bytes 57376 | tf_op jit(solution)/shard_map/ppermute | solution.py:333
  12.2 1.4 %x_near.2.refs_2_.refs_0_ = f32[256,128]{1,0:T(8,128)S(1)} custom-call(f32[512,128]{1,0:T(8,128)S(1)} %get-tuple-element.59.refs_0_, f32[512,128]{1,0:T(8,128)S(1)} %bitcast.8, f32[7,16,128]{2,1,0:T(8,128)S(1)} %get-tuple-element.62.refs_2_.refs_7_), custom_call_target="tpu_custom_call" | custom-call | tf_op jit(solution)/shard_map/x_near/pallas_call | solution.py:27
  13.5 1.8 %collective-permute-done.5.refs_1_.refs_5_ = f32[7,32,128]{2,1,0:T(8,128)S(1)} collective-permute-done((f32[7,32,128]{2,1,0:T(8,128)S(1)}, f32[7,32,128]{2,1,0:T(8,128)S(1)}, u32[]{:S(2)}, u32[]{:S(2)}) %collective-permute-start.5) | collective-permute-done | bytes 114720 | tf_op jit(solution)/shard_map/ppermute | solution.py:333
  15.3 1.6 %collective-permute-start.7 = (f32[7,32,128]{2,1,0:T(8,128)S(1)}, f32[7,32,128]{2,1,0:T(8,128)S(1)}, u32[]{:S(2)}, u32[]{:S(2)}) collective-permute-start(f32[7,32,128]{2,1,0:T(8,128)S(1)} %merge_gz_0.2.refs_2_.refs_0_.refs_6_), channel_id=1, source_target_pairs={{0,8},{4,12},{8,0},{12,4},{16,24},{20,28},{24,16},{28,20},{1,9},{5... | collective-permute-start | bytes 344072 | tf_op jit(solution)/shard_map/ppermute | solution.py:333
  17.0 1.5 %collective-permute-start.6 = (f32[48,128]{1,0:T(8,128)S(1)}, f32[48,128]{1,0:T(8,128)S(1)}, u32[]{:S(2)}, u32[]{:S(2)}) collective-permute-start(f32[48,128]{1,0:T(8,128)S(1)} %get-tuple-element.66), channel_id=1, source_target_pairs={{0,2},{1,3},{2,0},{3,1},{4,6},{5,7},{6,4},{7,5},{8,10},{9,11},{10,... | collective-permute-start | bytes 73736 | tf_op jit(solution)/shard_map/ppermute | solution.py:333
  18.5 0.6 slots.1.refs_2_.refs_1_
  19.1 1.4 %x_far.2.refs_1_ = f32[256,128]{1,0:T(8,128)S(1)} custom-call(f32[512,128]{1,0:T(8,128)S(1)} %get-tuple-element.59.refs_0_, f32[512,128]{1,0:T(8,128)S(1)} %bitcast.9, f32[7,32,128]{2,1,0:T(8,128)S(1)} %merge_gz_0.2.refs_2_.refs_0_.refs_6_), custom_call_target="tpu_custom_call" | custom-call | tf_op jit(solution)/shard_map/x_far/pallas_call | solution.py:27
  21.2 1.7 %collective-permute-start.8 = (f32[104,128]{1,0:T(8,128)S(1)}, f32[104,128]{1,0:T(8,128)S(1)}, u32[]{:S(2)}, u32[]{:S(2)}) collective-permute-start(f32[104,128]{1,0:T(8,128)S(1)} %get-tuple-element.72), channel_id=1, source_target_pairs={{0,16},{4,20},{8,24},{12,28},{16,0},{20,4},{24,8},{28,12},{1,17},{... | collective-permute-start | bytes 159752 | tf_op jit(solution)/shard_map/ppermute | solution.py:333
  22.9 1.4 %collective-permute-start.9 = (f32[32,128]{1,0:T(8,128)S(1)}, f32[32,128]{1,0:T(8,128)S(1)}, u32[]{:S(2)}, u32[]{:S(2)}) collective-permute-start(f32[32,128]{1,0:T(8,128)S(1)} %get-tuple-element.74), channel_id=1, source_target_pairs={{0,4},{4,0},{8,12},{12,8},{16,20},{20,16},{24,28},{28,24},{1,5},{5... | collective-permute-start | bytes 49160 | tf_op jit(solution)/shard_map/ppermute | solution.py:333
  24.3 2.8 %collective-permute-done.8.refs_9_ = f32[104,128]{1,0:T(8,128)S(1)} collective-permute-done((f32[104,128]{1,0:T(8,128)S(1)}, f32[104,128]{1,0:T(8,128)S(1)}, u32[]{:S(2)}, u32[]{:S(2)}) %collective-permute-start.8) | collective-permute-done | bytes 53280 | tf_op jit(solution)/shard_map/ppermute | solution.py:333
  27.3 1.6 %collective-permute-start.12 = (f32[16,128]{1,0:T(8,128)S(1)}, f32[16,128]{1,0:T(8,128)S(1)}, u32[]{:S(2)}, u32[]{:S(2)}) collective-permute-start(f32[16,128]{1,0:T(8,128)S(1)} %get-tuple-element.77), channel_id=1, source_target_pairs={{1,2},{3,0},{2,1},{0,3},{5,6},{7,4},{6,5},{4,7},{9,10},{11,8},{10,... | collective-permute-start | bytes 24584 | tf_op jit(solution)/shard_map/ppermute | solution.py:340
  28.9 1.5 %collective-permute-done.12.refs_4_ = f32[16,128]{1,0:T(8,128)S(1)} collective-permute-done((f32[16,128]{1,0:T(8,128)S(1)}, f32[16,128]{1,0:T(8,128)S(1)}, u32[]{:S(2)}, u32[]{:S(2)}) %collective-permute-start.12) | collective-permute-done | bytes 8224 | tf_op jit(solution)/shard_map/ppermute | solution.py:340
  30.4 0.4 z_pieces.3
  31.8 1.0 %collective-permute-done.13.refs_1_.refs_6_ = f32[7,16,128]{2,1,0:T(8,128)S(1)} collective-permute-done((f32[7,16,128]{2,1,0:T(8,128)S(1)}, f32[7,16,128]{2,1,0:T(8,128)S(1)}, u32[]{:S(2)}, u32[]{:S(2)}) %collective-permute-start.13) | collective-permute-done | bytes 57376 | tf_op jit(solution)/shard_map/ppermute | solution.py:333
  32.9 1.4 %x_near.3.refs_2_.refs_0_ = f32[256,128]{1,0:T(8,128)S(1)} custom-call(f32[512,128]{1,0:T(8,128)S(1)} %get-tuple-element.80.refs_0_, f32[512,128]{1,0:T(8,128)S(1)} %get-tuple-element.73.refs_0_.refs_1_, f32[7,16,128]{2,1,0:T(8,128)S(1)} %get-tuple-element.83.refs_2_.refs_7_), custom_call_target="tpu_custom_call" | custom-call | tf_op jit(solution)/shard_map/x_near/pallas_call | solution.py:27
  34.3 2.1 %collective-permute-done.14.refs_1_.refs_5_ = f32[7,32,128]{2,1,0:T(8,128)S(1)} collective-permute-done((f32[7,32,128]{2,1,0:T(8,128)S(1)}, f32[7,32,128]{2,1,0:T(8,128)S(1)}, u32[]{:S(2)}, u32[]{:S(2)}) %collective-permute-start.14) | collective-permute-done | bytes 114720 | tf_op jit(solution)/shard_map/ppermute | solution.py:333
  36.5 1.5 %collective-permute-start.15 = (f32[48,128]{1,0:T(8,128)S(1)}, f32[48,128]{1,0:T(8,128)S(1)}, u32[]{:S(2)}, u32[]{:S(2)}) collective-permute-start(f32[48,128]{1,0:T(8,128)S(1)} %get-tuple-element.87), channel_id=1, source_target_pairs={{0,2},{1,3},{2,0},{3,1},{4,6},{5,7},{6,4},{7,5},{8,10},{9,11},{10,... | collective-permute-start | bytes 73736 | tf_op jit(solution)/shard_map/ppermute | solution.py:333
  38.1 1.4 %x_far.3.refs_1_ = f32[256,128]{1,0:T(8,128)S(1)} custom-call(f32[512,128]{1,0:T(8,128)S(1)} %get-tuple-element.80.refs_0_, f32[512,128]{1,0:T(8,128)S(1)} %get-tuple-element.73.refs_0_.refs_1_, f32[7,32,128]{2,1,0:T(8,128)S(1)} %merge_gz_0.3.refs_2_.refs_0_.refs_6_), custom_call_target="tpu_custom_call" | custom-call | tf_op jit(solution)/shard_map/x_far/pallas_call | solution.py:27
  39.5 0.9 %collective-permute-done.15.refs_8_ = f32[48,128]{1,0:T(8,128)S(1)} collective-permute-done((f32[48,128]{1,0:T(8,128)S(1)}, f32[48,128]{1,0:T(8,128)S(1)}, u32[]{:S(2)}, u32[]{:S(2)}) %collective-permute-start.15) | collective-permute-done | bytes 24608 | tf_op jit(solution)/shard_map/ppermute | solution.py:333
  40.8 0.5 collective-permute-done.16.refs_1_.refs_7_
  41.3 2.3 %collective-permute-start.17 = (f32[96,128]{1,0:T(8,128)S(1)}, f32[96,128]{1,0:T(8,128)S(1)}, u32[]{:S(2)}, u32[]{:S(2)}) collective-permute-start(f32[96,128]{1,0:T(8,128)S(1)} %get-tuple-element.92), channel_id=1, source_target_pairs={{0,16},{4,20},{8,24},{12,28},{16,0},{20,4},{24,8},{28,12},{1,17},{... | collective-permute-start | bytes 147464 | tf_op jit(solution)/shard_map/ppermute | solution.py:333
  43.7 2.7 %collective-permute-done.17.refs_9_ = f32[96,128]{1,0:T(8,128)S(1)} collective-permute-done((f32[96,128]{1,0:T(8,128)S(1)}, f32[96,128]{1,0:T(8,128)S(1)}, u32[]{:S(2)}, u32[]{:S(2)}) %collective-permute-start.17) | collective-permute-done | bytes 49184 | tf_op jit(solution)/shard_map/ppermute | solution.py:333
  46.4 0.9 %denoised.1 = (f32[512,128]{1,0:T(8,128)}, f32[4,64,128]{2,1,0:T(8,128)S(1)}, f32[4,64,128]{2,1,0:T(8,128)S(1)}) custom-call(f32[512,128]{1,0:T(8,128)S(1)} %sum_xy.3.refs_2_.refs_0_, f32[16,32,128]{2,1,0:T(8,128)S(1)} %get-tuple-element.88.refs_1_, f32[16,32,128]{2,1,0:T(8,128)S(1)} %get-tuple-element.89.refs_2_, ...), custom_call_target="tpu_custom_call" | custom-call | tf_op jit(solution)/shard_map/denoised/pallas_call | solution.py:27
  47.3 2.3 %collective-permute-start.22 = (f32[4,64,128]{2,1,0:T(8,128)S(1)}, f32[4,64,128]{2,1,0:T(8,128)S(1)}, u32[]{:S(2)}, u32[]{:S(2)}) collective-permute-start(f32[4,64,128]{2,1,0:T(8,128)S(1)} %get-tuple-element.99), channel_id=1, source_target_pairs={{0,16},{4,20},{8,24},{12,28},{16,0},{20,4},{24,8},{28,12},{1,17},{... | collective-permute-start | bytes 393224 | tf_op jit(solution)/shard_map/ppermute | solution.py:333
  49.5 0.6 collective-permute-start.18
  50.2 0.9 %copy-done.2 = f32[512,128]{1,0:T(8,128)S(1)} copy-done((f32[512,128]{1,0:T(8,128)S(1)}, f32[512,128]{1,0:T(8,128)}, u32[]{:S(2)}) %copy-start.2) | copy-done | bytes 262168
  51.1 0.6 straight.1
  52.1 1.4 %collective-permute-start.27 = (f32[2,128,128]{2,1,0:T(8,128)S(1)}, f32[2,128,128]{2,1,0:T(8,128)S(1)}, u32[]{:S(2)}, u32[]{:S(2)}) collective-permute-start(f32[2,128,128]{2,1,0:T(8,128)S(1)} %get-tuple-element.106), channel_id=1, source_target_pairs={{0,8},{4,12},{8,0},{12,4},{16,24},{20,28},{24,16},{28,20},{1,9},{5... | collective-permute-start | bytes 393224 | tf_op jit(solution)/shard_map/ppermute | solution.py:333
  53.5 1.8 %collective-permute-start.28 = (f32[2,128,128]{2,1,0:T(8,128)S(1)}, f32[2,128,128]{2,1,0:T(8,128)S(1)}, u32[]{:S(2)}, u32[]{:S(2)}) collective-permute-start(f32[2,128,128]{2,1,0:T(8,128)S(1)} %get-tuple-element.107), channel_id=1, source_target_pairs={{0,12},{4,8},{8,4},{12,0},{16,28},{20,24},{24,20},{28,16},{1,13},{... | collective-permute-start | bytes 393224 | tf_op jit(solution)/shard_map/ppermute | solution.py:333
  55.3 1.7 %collective-permute-done.22.refs_0_ = f32[4,64,128]{2,1,0:T(8,128)S(1)} collective-permute-done((f32[4,64,128]{2,1,0:T(8,128)S(1)}, f32[4,64,128]{2,1,0:T(8,128)S(1)}, u32[]{:S(2)}, u32[]{:S(2)}) %collective-permute-start.22) | collective-permute-done | bytes 131104 | tf_op jit(solution)/shard_map/ppermute | solution.py:333
  57.0 0.6 relay_0.1
  57.5 1.3 %collective-permute-start.23 = (f32[2,64,128]{2,1,0:T(8,128)S(1)}, f32[2,64,128]{2,1,0:T(8,128)S(1)}, u32[]{:S(2)}, u32[]{:S(2)}) collective-permute-start(f32[2,64,128]{2,1,0:T(8,128)S(1)} %get-tuple-element.101), channel_id=1, source_target_pairs={{0,4},{4,0},{8,12},{12,8},{16,20},{20,16},{24,28},{28,24},{1,5},{5... | collective-permute-start | bytes 196616 | tf_op jit(solution)/shard_map/ppermute | solution.py:333
  59.3 0.6 relay_1.1
  59.8 0.5 collective-permute-start.19
  60.7 2.7 %collective-permute-start.25 = (f32[2,64,128]{2,1,0:T(8,128)S(1)}, f32[2,64,128]{2,1,0:T(8,128)S(1)}, u32[]{:S(2)}, u32[]{:S(2)}) collective-permute-start(f32[2,64,128]{2,1,0:T(8,128)S(1)} %get-tuple-element.103), channel_id=1, source_target_pairs={{0,12},{4,8},{8,4},{12,0},{16,28},{20,24},{24,20},{28,16},{1,13},{... | collective-permute-start | bytes 196616 | tf_op jit(solution)/shard_map/ppermute | solution.py:333
  63.5 1.8 %collective-permute-start.21 = (f32[2,64,128]{2,1,0:T(8,128)S(1)}, f32[2,64,128]{2,1,0:T(8,128)S(1)}, u32[]{:S(2)}, u32[]{:S(2)}) collective-permute-start(f32[2,64,128]{2,1,0:T(8,128)S(1)} %get-tuple-element.98), channel_id=1, source_target_pairs={{0,12},{4,8},{8,4},{12,0},{16,28},{20,24},{24,20},{28,16},{1,13},{... | collective-permute-start | bytes 196616 | tf_op jit(solution)/shard_map/ppermute | solution.py:333
  65.2 0.8 %place_straight.1.refs_4_ = f32[16,128,128]{2,1,0:T(8,128)} custom-call(f32[2,128,128]{2,1,0:T(8,128)S(1)} %get-tuple-element.104.refs_0_, f32[2,128,128]{2,1,0:T(8,128)S(1)} %collective-permute-done.26.refs_1_, f32[2,128,128]{2,1,0:T(8,128)S(1)} %collective-permute-done.27.refs_2_, f32[2,128,128]{2,1,0:T(8,128)S(1)} %collective-permute-done.28.refs_3_), custom_call_target="tpu_custom_call" | custom-call | tf_op jit(solution)/shard_map/place_straight/pallas_call | solution.py:319
  66.1 0.9 %collective-permute-done.25.refs_3_ = f32[2,64,128]{2,1,0:T(8,128)S(1)} collective-permute-done((f32[2,64,128]{2,1,0:T(8,128)S(1)}, f32[2,64,128]{2,1,0:T(8,128)S(1)}, u32[]{:S(2)}, u32[]{:S(2)}) %collective-permute-start.25) | collective-permute-done | bytes 65568 | tf_op jit(solution)/shard_map/ppermute | solution.py:333
  67.0 0.7 %place_0.1.refs_4_ = f32[16,128,128]{2,1,0:T(8,128)} custom-call(f32[2,64,128]{2,1,0:T(8,128)S(1)} %get-tuple-element.100.refs_0_, f32[2,64,128]{2,1,0:T(8,128)S(1)} %collective-permute-done.23.refs_1_, f32[2,64,128]{2,1,0:T(8,128)S(1)} %collective-permute-done.24.refs_2_, ...), custom_call_target="tpu_custom_call", output_to_operand_aliasing={{}: (4, {})} | custom-call | tf_op jit(solution)/shard_map/place_0/pallas_call | solution.py:319
  67.8 0.8 %collective-permute-done.21.refs_3_ = f32[2,64,128]{2,1,0:T(8,128)S(1)} collective-permute-done((f32[2,64,128]{2,1,0:T(8,128)S(1)}, f32[2,64,128]{2,1,0:T(8,128)S(1)}, u32[]{:S(2)}, u32[]{:S(2)}) %collective-permute-start.21) | collective-permute-done | bytes 65568 | tf_op jit(solution)/shard_map/ppermute | solution.py:333
  68.6 0.7 %place_1.1 = f32[16,128,128]{2,1,0:T(8,128)} custom-call(f32[2,64,128]{2,1,0:T(8,128)S(1)} %get-tuple-element.95.refs_0_, f32[2,64,128]{2,1,0:T(8,128)S(1)} %collective-permute-done.19.refs_1_, f32[2,64,128]{2,1,0:T(8,128)S(1)} %collective-permute-done.20.refs_2_, f32[2,64,128]{2,1,0:T(8,128)S(1)} %collective-permute-done.21.refs_3_, ...), custom_call_target="tpu_custom_call", output_to_operand_aliasing={{}: (4, {})} | custom-call | tf_op jit(solution)/shard_map/place_1/pallas_call | solution.py:319
  (45 shorter events, 4.3 us)
Async XLA Ops:
  0.6 1.0 %copy-start = (f32[16,32,128]{2,1,0:T(8,128)S(1)}, f32[16,32,128]{2,1,0:T(8,128)}, u32[]{:S(2)}) copy-start(f32[16,32,128]{2,1,0:T(8,128)} %param.2) | copy-start | bytes 786436
  1.6 7.7 %collective-permute-start.1 = (f32[32,128]{1,0:T(8,128)S(1)}, f32[32,128]{1,0:T(8,128)S(1)}, u32[]{:S(2)}, u32[]{:S(2)}) collective-permute-start(f32[32,128]{1,0:T(8,128)S(1)} %get-tuple-element.56), channel_id=1, source_target_pairs={{0,1},{1,0},{2,3},{3,2},{4,8},{5,9},{6,10},{7,11},{8,4},{9,5},{10,... | collective-permute-start | bytes 49160 | tf_op jit(solution)/shard_map/ppermute | solution.py:348
  2.2 7.1 %collective-permute-start = (f32[32,128]{1,0:T(8,128)S(1)}, f32[32,128]{1,0:T(8,128)S(1)}, u32[]{:S(2)}, u32[]{:S(2)}) collective-permute-start(f32[32,128]{1,0:T(8,128)S(1)} %get-tuple-element.55.refs_1_), channel_id=1, source_target_pairs={{0,4},{4,0},{8,12},{12,8},{16,20},{20,16},{24,28},{28,24},{1,5},{5... | collective-permute-start | bytes 49160 | tf_op jit(solution)/shard_map/ppermute | solution.py:333
  6.2 1.6 %collective-permute-start.2 = (f32[16,128]{1,0:T(8,128)S(1)}, f32[16,128]{1,0:T(8,128)S(1)}, u32[]{:S(2)}, u32[]{:S(2)}) collective-permute-start(f32[16,128]{1,0:T(8,128)S(1)} %get-tuple-element.57), channel_id=1, source_target_pairs={{0,1},{1,0},{2,3},{3,2},{4,5},{5,4},{6,7},{7,6},{8,9},{9,8},{10,11... | collective-permute-start | bytes 24584 | tf_op jit(solution)/shard_map/ppermute | solution.py:333
  6.2 3.1 %collective-permute-start.3 = (f32[16,128]{1,0:T(8,128)S(1)}, f32[16,128]{1,0:T(8,128)S(1)}, u32[]{:S(2)}, u32[]{:S(2)}) collective-permute-start(f32[16,128]{1,0:T(8,128)S(1)} %get-tuple-element.58), channel_id=1, source_target_pairs={{1,2},{3,0},{2,1},{0,3},{5,6},{7,4},{6,5},{4,7},{9,10},{11,8},{10,... | collective-permute-start | bytes 24584 | tf_op jit(solution)/shard_map/ppermute | solution.py:340
  9.7 5.6 %collective-permute-start.5 = (f32[7,32,128]{2,1,0:T(8,128)S(1)}, f32[7,32,128]{2,1,0:T(8,128)S(1)}, u32[]{:S(2)}, u32[]{:S(2)}) collective-permute-start(f32[7,32,128]{2,1,0:T(8,128)S(1)} %get-tuple-element.60.refs_2_.refs_0_.refs_4_), channel_id=1, source_target_pairs={{0,4},{4,0},{8,12},{12,8},{16,20},{20,16},{24,28},{28,24},{1,5},{5... | collective-permute-start | bytes 344072 | tf_op jit(solution)/shard_map/ppermute | solution.py:333
  10.4 1.8 %copy-start.1 = (f32[16,32,128]{2,1,0:T(8,128)S(1)}, f32[16,32,128]{2,1,0:T(8,128)}, u32[]{:S(2)}) copy-start(f32[16,32,128]{2,1,0:T(8,128)} %param.2) | copy-start | bytes 786436
  10.8 1.3 %collective-permute-start.4 = (f32[7,16,128]{2,1,0:T(8,128)S(1)}, f32[7,16,128]{2,1,0:T(8,128)S(1)}, u32[]{:S(2)}, u32[]{:S(2)}) collective-permute-start(f32[7,16,128]{2,1,0:T(8,128)S(1)} %get-tuple-element.61.refs_0_.refs_5_), channel_id=1, source_target_pairs={{0,1},{1,0},{2,3},{3,2},{4,5},{5,4},{6,7},{7,6},{8,9},{9,8},{10,11... | collective-permute-start | bytes 172040 | tf_op jit(solution)/shard_map/ppermute | solution.py:333
  15.3 5.8 %collective-permute-start.7 = (f32[7,32,128]{2,1,0:T(8,128)S(1)}, f32[7,32,128]{2,1,0:T(8,128)S(1)}, u32[]{:S(2)}, u32[]{:S(2)}) collective-permute-start(f32[7,32,128]{2,1,0:T(8,128)S(1)} %merge_gz_0.2.refs_2_.refs_0_.refs_6_), channel_id=1, source_target_pairs={{0,8},{4,12},{8,0},{12,4},{16,24},{20,28},{24,16},{28,20},{1,9},{5... | collective-permute-start | bytes 344072 | tf_op jit(solution)/shard_map/ppermute | solution.py:333
  17.0 1.5 %copy-start.3 = (s32[1,4,1]{1,2,0:T(1,128)S(1)}, s32[1,4,1]{1,2,0:T(1,128)}, u32[]{:S(2)}) copy-start(s32[1,4,1]{1,2,0:T(1,128)} %param.3) | copy-start | bytes 52
  17.0 3.8 %collective-permute-start.6 = (f32[48,128]{1,0:T(8,128)S(1)}, f32[48,128]{1,0:T(8,128)S(1)}, u32[]{:S(2)}, u32[]{:S(2)}) collective-permute-start(f32[48,128]{1,0:T(8,128)S(1)} %get-tuple-element.66), channel_id=1, source_target_pairs={{0,2},{1,3},{2,0},{3,1},{4,6},{5,7},{6,4},{7,5},{8,10},{9,11},{10,... | collective-permute-start | bytes 73736 | tf_op jit(solution)/shard_map/ppermute | solution.py:333
  21.2 5.8 %collective-permute-start.8 = (f32[104,128]{1,0:T(8,128)S(1)}, f32[104,128]{1,0:T(8,128)S(1)}, u32[]{:S(2)}, u32[]{:S(2)}) collective-permute-start(f32[104,128]{1,0:T(8,128)S(1)} %get-tuple-element.72), channel_id=1, source_target_pairs={{0,16},{4,20},{8,24},{12,28},{16,0},{20,4},{24,8},{28,12},{1,17},{... | collective-permute-start | bytes 159752 | tf_op jit(solution)/shard_map/ppermute | solution.py:333
  22.9 6.0 %collective-permute-start.9 = (f32[32,128]{1,0:T(8,128)S(1)}, f32[32,128]{1,0:T(8,128)S(1)}, u32[]{:S(2)}, u32[]{:S(2)}) collective-permute-start(f32[32,128]{1,0:T(8,128)S(1)} %get-tuple-element.74), channel_id=1, source_target_pairs={{0,4},{4,0},{8,12},{12,8},{16,20},{20,16},{24,28},{28,24},{1,5},{5... | collective-permute-start | bytes 49160 | tf_op jit(solution)/shard_map/ppermute | solution.py:333
  24.3 4.6 %collective-permute-start.10 = (f32[32,128]{1,0:T(8,128)S(1)}, f32[32,128]{1,0:T(8,128)S(1)}, u32[]{:S(2)}, u32[]{:S(2)}) collective-permute-start(f32[32,128]{1,0:T(8,128)S(1)} %get-tuple-element.75), channel_id=1, source_target_pairs={{0,1},{1,0},{2,3},{3,2},{4,8},{5,9},{6,10},{7,11},{8,4},{9,5},{10,... | collective-permute-start | bytes 49160 | tf_op jit(solution)/shard_map/ppermute | solution.py:348
  27.2 1.7 %collective-permute-start.11 = (f32[16,128]{1,0:T(8,128)S(1)}, f32[16,128]{1,0:T(8,128)S(1)}, u32[]{:S(2)}, u32[]{:S(2)}) collective-permute-start(f32[16,128]{1,0:T(8,128)S(1)} %get-tuple-element.76), channel_id=1, source_target_pairs={{0,1},{1,0},{2,3},{3,2},{4,5},{5,4},{6,7},{7,6},{8,9},{9,8},{10,11... | collective-permute-start | bytes 24584 | tf_op jit(solution)/shard_map/ppermute | solution.py:333
  27.3 3.1 %collective-permute-start.12 = (f32[16,128]{1,0:T(8,128)S(1)}, f32[16,128]{1,0:T(8,128)S(1)}, u32[]{:S(2)}, u32[]{:S(2)}) collective-permute-start(f32[16,128]{1,0:T(8,128)S(1)} %get-tuple-element.77), channel_id=1, source_target_pairs={{1,2},{3,0},{2,1},{0,3},{5,6},{7,4},{6,5},{4,7},{9,10},{11,8},{10,... | collective-permute-start | bytes 24584 | tf_op jit(solution)/shard_map/ppermute | solution.py:340
  30.9 5.5 %collective-permute-start.14 = (f32[7,32,128]{2,1,0:T(8,128)S(1)}, f32[7,32,128]{2,1,0:T(8,128)S(1)}, u32[]{:S(2)}, u32[]{:S(2)}) collective-permute-start(f32[7,32,128]{2,1,0:T(8,128)S(1)} %get-tuple-element.81.refs_2_.refs_0_.refs_4_), channel_id=1, source_target_pairs={{0,4},{4,0},{8,12},{12,8},{16,20},{20,16},{24,28},{28,24},{1,5},{5... | collective-permute-start | bytes 344072 | tf_op jit(solution)/shard_map/ppermute | solution.py:333
  31.5 1.3 %collective-permute-start.13 = (f32[7,16,128]{2,1,0:T(8,128)S(1)}, f32[7,16,128]{2,1,0:T(8,128)S(1)}, u32[]{:S(2)}, u32[]{:S(2)}) collective-permute-start(f32[7,16,128]{2,1,0:T(8,128)S(1)} %get-tuple-element.82.refs_0_.refs_5_), channel_id=1, source_target_pairs={{0,1},{1,0},{2,3},{3,2},{4,5},{5,4},{6,7},{7,6},{8,9},{9,8},{10,11... | collective-permute-start | bytes 172040 | tf_op jit(solution)/shard_map/ppermute | solution.py:333
  36.4 4.9 %collective-permute-start.16 = (f32[7,32,128]{2,1,0:T(8,128)S(1)}, f32[7,32,128]{2,1,0:T(8,128)S(1)}, u32[]{:S(2)}, u32[]{:S(2)}) collective-permute-start(f32[7,32,128]{2,1,0:T(8,128)S(1)} %merge_gz_0.3.refs_2_.refs_0_.refs_6_), channel_id=1, source_target_pairs={{0,8},{4,12},{8,0},{12,4},{16,24},{20,28},{24,16},{28,20},{1,9},{5... | collective-permute-start | bytes 344072 | tf_op jit(solution)/shard_map/ppermute | solution.py:333
  36.5 3.9 %collective-permute-start.15 = (f32[48,128]{1,0:T(8,128)S(1)}, f32[48,128]{1,0:T(8,128)S(1)}, u32[]{:S(2)}, u32[]{:S(2)}) collective-permute-start(f32[48,128]{1,0:T(8,128)S(1)} %get-tuple-element.87), channel_id=1, source_target_pairs={{0,2},{1,3},{2,0},{3,1},{4,6},{5,7},{6,4},{7,5},{8,10},{9,11},{10,... | collective-permute-start | bytes 73736 | tf_op jit(solution)/shard_map/ppermute | solution.py:333
  41.3 5.1 %collective-permute-start.17 = (f32[96,128]{1,0:T(8,128)S(1)}, f32[96,128]{1,0:T(8,128)S(1)}, u32[]{:S(2)}, u32[]{:S(2)}) collective-permute-start(f32[96,128]{1,0:T(8,128)S(1)} %get-tuple-element.92), channel_id=1, source_target_pairs={{0,16},{4,20},{8,24},{12,28},{16,0},{20,4},{24,8},{28,12},{1,17},{... | collective-permute-start | bytes 147464 | tf_op jit(solution)/shard_map/ppermute | solution.py:333
  47.3 9.7 %collective-permute-start.22 = (f32[4,64,128]{2,1,0:T(8,128)S(1)}, f32[4,64,128]{2,1,0:T(8,128)S(1)}, u32[]{:S(2)}, u32[]{:S(2)}) collective-permute-start(f32[4,64,128]{2,1,0:T(8,128)S(1)} %get-tuple-element.99), channel_id=1, source_target_pairs={{0,16},{4,20},{8,24},{12,28},{16,0},{20,4},{24,8},{28,12},{1,17},{... | collective-permute-start | bytes 393224 | tf_op jit(solution)/shard_map/ppermute | solution.py:333
  49.5 9.7 %collective-permute-start.18 = (f32[4,64,128]{2,1,0:T(8,128)S(1)}, f32[4,64,128]{2,1,0:T(8,128)S(1)}, u32[]{:S(2)}, u32[]{:S(2)}) collective-permute-start(f32[4,64,128]{2,1,0:T(8,128)S(1)} %get-tuple-element.94), channel_id=1, source_target_pairs={{0,16},{4,20},{8,24},{12,28},{16,0},{20,4},{24,8},{28,12},{1,17},{... | collective-permute-start | bytes 393224 | tf_op jit(solution)/shard_map/ppermute | solution.py:333
  50.2 0.9 %copy-start.2 = (f32[512,128]{1,0:T(8,128)S(1)}, f32[512,128]{1,0:T(8,128)}, u32[]{:S(2)}) copy-start(f32[512,128]{1,0:T(8,128)} %get-tuple-element.93) | copy-start | bytes 786436
  51.7 8.6 %collective-permute-start.26 = (f32[2,128,128]{2,1,0:T(8,128)S(1)}, f32[2,128,128]{2,1,0:T(8,128)S(1)}, u32[]{:S(2)}, u32[]{:S(2)}) collective-permute-start(f32[2,128,128]{2,1,0:T(8,128)S(1)} %get-tuple-element.105), channel_id=1, source_target_pairs={{0,4},{4,0},{8,12},{12,8},{16,20},{20,16},{24,28},{28,24},{1,5},{5... | collective-permute-start | bytes 393224 | tf_op jit(solution)/shard_map/ppermute | solution.py:333
  52.1 8.6 %collective-permute-start.27 = (f32[2,128,128]{2,1,0:T(8,128)S(1)}, f32[2,128,128]{2,1,0:T(8,128)S(1)}, u32[]{:S(2)}, u32[]{:S(2)}) collective-permute-start(f32[2,128,128]{2,1,0:T(8,128)S(1)} %get-tuple-element.106), channel_id=1, source_target_pairs={{0,8},{4,12},{8,0},{12,4},{16,24},{20,28},{24,16},{28,20},{1,9},{5... | collective-permute-start | bytes 393224 | tf_op jit(solution)/shard_map/ppermute | solution.py:333
  53.5 9.9 %collective-permute-start.28 = (f32[2,128,128]{2,1,0:T(8,128)S(1)}, f32[2,128,128]{2,1,0:T(8,128)S(1)}, u32[]{:S(2)}, u32[]{:S(2)}) collective-permute-start(f32[2,128,128]{2,1,0:T(8,128)S(1)} %get-tuple-element.107), channel_id=1, source_target_pairs={{0,12},{4,8},{8,4},{12,0},{16,28},{20,24},{24,20},{28,16},{1,13},{... | collective-permute-start | bytes 393224 | tf_op jit(solution)/shard_map/ppermute | solution.py:333
  57.5 5.9 %collective-permute-start.23 = (f32[2,64,128]{2,1,0:T(8,128)S(1)}, f32[2,64,128]{2,1,0:T(8,128)S(1)}, u32[]{:S(2)}, u32[]{:S(2)}) collective-permute-start(f32[2,64,128]{2,1,0:T(8,128)S(1)} %get-tuple-element.101), channel_id=1, source_target_pairs={{0,4},{4,0},{8,12},{12,8},{16,20},{20,16},{24,28},{28,24},{1,5},{5... | collective-permute-start | bytes 196616 | tf_op jit(solution)/shard_map/ppermute | solution.py:333
  59.8 7.9 %collective-permute-start.19 = (f32[2,64,128]{2,1,0:T(8,128)S(1)}, f32[2,64,128]{2,1,0:T(8,128)S(1)}, u32[]{:S(2)}, u32[]{:S(2)}) collective-permute-start(f32[2,64,128]{2,1,0:T(8,128)S(1)} %get-tuple-element.96), channel_id=1, source_target_pairs={{0,4},{4,0},{8,12},{12,8},{16,20},{20,16},{24,28},{28,24},{1,5},{5... | collective-permute-start | bytes 196616 | tf_op jit(solution)/shard_map/ppermute | solution.py:333
  60.3 5.8 %collective-permute-start.24 = (f32[2,64,128]{2,1,0:T(8,128)S(1)}, f32[2,64,128]{2,1,0:T(8,128)S(1)}, u32[]{:S(2)}, u32[]{:S(2)}) collective-permute-start(f32[2,64,128]{2,1,0:T(8,128)S(1)} %get-tuple-element.102), channel_id=1, source_target_pairs={{0,8},{4,12},{8,0},{12,4},{16,24},{20,28},{24,16},{28,20},{1,9},{5... | collective-permute-start | bytes 196616 | tf_op jit(solution)/shard_map/ppermute | solution.py:333
  60.7 6.3 %collective-permute-start.25 = (f32[2,64,128]{2,1,0:T(8,128)S(1)}, f32[2,64,128]{2,1,0:T(8,128)S(1)}, u32[]{:S(2)}, u32[]{:S(2)}) collective-permute-start(f32[2,64,128]{2,1,0:T(8,128)S(1)} %get-tuple-element.103), channel_id=1, source_target_pairs={{0,12},{4,8},{8,4},{12,0},{16,28},{20,24},{24,20},{28,16},{1,13},{... | collective-permute-start | bytes 196616 | tf_op jit(solution)/shard_map/ppermute | solution.py:333
  63.4 4.4 %collective-permute-start.20 = (f32[2,64,128]{2,1,0:T(8,128)S(1)}, f32[2,64,128]{2,1,0:T(8,128)S(1)}, u32[]{:S(2)}, u32[]{:S(2)}) collective-permute-start(f32[2,64,128]{2,1,0:T(8,128)S(1)} %get-tuple-element.97), channel_id=1, source_target_pairs={{0,8},{4,12},{8,0},{12,4},{16,24},{20,28},{24,16},{28,20},{1,9},{5... | collective-permute-start | bytes 196616 | tf_op jit(solution)/shard_map/ppermute | solution.py:333
  63.5 5.2 %collective-permute-start.21 = (f32[2,64,128]{2,1,0:T(8,128)S(1)}, f32[2,64,128]{2,1,0:T(8,128)S(1)}, u32[]{:S(2)}, u32[]{:S(2)}) collective-permute-start(f32[2,64,128]{2,1,0:T(8,128)S(1)} %get-tuple-element.98), channel_id=1, source_target_pairs={{0,12},{4,8},{8,4},{12,0},{16,28},{20,24},{24,20},{28,16},{1,13},{... | collective-permute-start | bytes 196616 | tf_op jit(solution)/shard_map/ppermute | solution.py:333

commit v4 on v3

--- a/solution.py
+++ b/solution.py
@@ -6,6 +6,7 @@
 from jax.experimental import pallas as pl
 from jax.experimental.pallas import tpu as pltpu
 from jax.sharding import PartitionSpec as P
+
 
 STEPS = 2
 MOST = 2
@@ -19,7 +20,7 @@
 VMEM = pltpu.VMEM
 
 
-def call(body, outs, ins, name, smem=(), after=()):
+def call(body, outs, ins, smem=(), after=()):
     count = len(ins)
     specs = [
         pl.BlockSpec(memory_space=pltpu.SMEM if k in smem else VMEM) for k in range(count)
@@ -30,7 +31,6 @@
         in_specs=specs,
         out_specs=[pl.BlockSpec(memory_space=VMEM)] * len(outs),
         compiler_params=pltpu.CompilerParams(vmem_limit_bytes=VMEM_LIMIT),
-        name=name,
     )(*ins, *after)
 
 
@@ -267,45 +267,52 @@
 
 
 def last_kernel(depth, height, total, solved, head, tail, *refs):
-    field, halves = refs[-1 - CHUNKS], refs[-CHUNKS:]
-    low, high, _, _ = unwind("gz", [parts(ref, height) for ref in refs[: -1 - CHUNKS]])
+    chunks = refs[-CHUNKS:]
+    low, high, _, _ = unwind("gz", [parts(ref, height) for ref in refs[:-CHUNKS]])
     planes, piece = BLOCK_ROWS // height, BLOCK_ROWS // CHUNKS
     for k in range(depth):
-        at = pl.ds(k * height, height)
-        value = (total[at, :] + (solved[k] + low * head[k] + high * tail[k])) * THIRD
-        field[at, :] = value
+        value = (total[pl.ds(k * height, height), :] + (solved[k] + low * head[k] + high * tail[k])) * THIRD
         block, row = k // planes, (k % planes) * height
-        halves[row // piece][block, pl.ds(row % piece, height), :] = value
-
-
-def pack_kernel(ways, blocks, slots, *outs):
-    place = lax.rem(lax.axis_index("gz"), ways)
-    base = lax.axis_index("gz") - place
+        chunks[row // piece][block, pl.ds(row % piece, height), :] = value
+
+
+def pack_kernel(ways, count, *refs):
+    pieces, slots, outs = refs[:count], refs[count], refs[count + 1 :]
+    me = lax.axis_index("gz")
+    place = lax.rem(me, ways)
+    number, rows = pieces[0].shape[:2]
+    placed = [jnp.max(slots[pl.ds(block, 1), :]).astype(jnp.int32) for block in range(number)]
     for out in outs:
         out[...] = jnp.zeros_like(out)
-    for block in range(blocks.shape[0]):
-        slot = jnp.max(slots[pl.ds(block, 1), :]).astype(jnp.int32)
-        rank, target = lax.rem(slot, MOST), lax.div(slot, MOST) - base
+    for block, slot in enumerate(placed):
+        rank, target = lax.rem(slot, MOST), lax.div(slot, MOST) - (me - place)
         for way, out in enumerate(outs):
 
             @pl.when(target == lax.bitwise_xor(place, way))
             def _():
-                out[rank] = blocks[block]
-
-
-def pack(ways, blocks, slots, name, after=()):
-    shape = (MOST,) + blocks.shape[1:]
-    return call(functools.partial(pack_kernel, ways), [shape] * ways, [blocks, slots], name, after=after)
-
-
-def place_kernel(plan, count, *refs):
-    incoming, sems = refs[-2:]
+                for k, piece in enumerate(pieces):
+                    out[rank, pl.ds(k * rows, rows), :] = piece[block]
+
+
+def pack(ways, pieces, slots):
+    rows, width = pieces[0].shape[1:]
+    shape = (MOST, rows * len(pieces), width)
+    return call(functools.partial(pack_kernel, ways, len(pieces)), [shape] * ways, [*pieces, slots])
+
+
+def place_kernel(plan, kept, fresh, *refs):
+    count = len(plan) + kept
+    outs, sems = refs[count + (not fresh) : -1], refs[-1]
     me = lax.axis_index("gz")
     copies = []
-    for k, (way, row) in enumerate(plan):
+    for k in range(count):
         rows = refs[k].shape[1]
-        source = lax.bitwise_xor(me, way)
-        target = incoming.at[pl.ds(source * MOST, MOST), pl.ds(row, rows), :]
+        if k < len(plan):
+            way, row = plan[k]
+            source = lax.bitwise_xor(me, way)
+            target = outs[0].at[pl.ds(source * MOST, MOST), pl.ds(row, rows), :]
+        else:
+            target = outs[1].at[:, pl.ds((k - len(plan)) * rows, rows), :]
         copies.append(pltpu.make_async_copy(refs[k], target, sems.at[k]))
     for copy in copies:
         copy.start()
@@ -313,19 +320,18 @@
         copy.wait()
 
 
-def place(arrays, plan, incoming, shape, name):
-    count = len(arrays)
+def place(arrays, plan, incoming, shapes, kept=()):
+    count = len(arrays) + len(kept)
     extra = [] if incoming is None else [incoming]
     return pl.pallas_call(
-        functools.partial(place_kernel, plan, count),
-        out_shape=jax.ShapeDtypeStruct(shape, jnp.float32),
+        functools.partial(place_kernel, plan, len(kept), not extra),
+        out_shape=[jax.ShapeDtypeStruct(shape, jnp.float32) for shape in shapes],
         in_specs=[pl.BlockSpec(memory_space=VMEM)] * count + [pl.BlockSpec(memory_space=pl.ANY)] * len(extra),
-        out_specs=pl.BlockSpec(memory_space=pl.ANY),
+        out_specs=[pl.BlockSpec(memory_space=pl.ANY)] * len(shapes),
         scratch_shapes=[pltpu.SemaphoreType.DMA((count,))],
         input_output_aliases={count: 0} if extra else {},
         compiler_params=pltpu.CompilerParams(vmem_limit_bytes=VMEM_LIMIT),
-        name=name,
-    )(*arrays, *extra)
+    )(*arrays, *kept, *extra)
 
 
 def swap(values, axis, stride):
@@ -333,20 +339,27 @@
     return lax.ppermute(values, axis, [(i, i ^ stride) for i in range(count)])
 
 
-def neighbours(first, second, axis):
+def near(first, axis):
+    return swap(first, axis, 1)
+
+
+def far(second, axis):
     count = lax.axis_size(axis)
     if axis == "xy":
         other = [(i, (i + 1) % count) for i in range(1, count, 2)]
-        got = lax.ppermute(second, axis, other + [(j, i) for i, j in other])
-    else:
-        near = lax.axis_size("xy")
-        pairs = []
-        for i in range(count):
-            end = i in (0, count - 1)
-            j = i if end else i + 1 if i % 2 else i - 1
-            pairs += [(i * near + c, j * near + (c ^ 1 if end else c)) for c in range(near)]
-        got = lax.ppermute(second, (axis, "xy"), pairs)
-    return swap(first, axis, 1), got
+        return lax.ppermute(second, axis, other + [(j, i) for i, j in other])
+    beside = lax.axis_size("xy")
+    pairs = []
+    for i in range(count):
+        end = i in (0, count - 1)
+        j = i if end else i + 1 if i % 2 else i - 1
+        pairs += [(i * beside + c, j * beside + (c ^ 1 if end else c)) for c in range(beside)]
+    return lax.ppermute(second, (axis, "xy"), pairs)
+
+
+def neighbours(first, second, axis):
+    got = far(second, axis)
+    return near(first, axis), got
 
 
 def merge(element, got, axis, level, after=(), notes=()):
@@ -354,30 +367,26 @@
     last = 4 << level >= lax.axis_size(axis)
     notes = notes if last else ()
     outs = [element.shape] + [(3 * rows + sum(note.shape[0] for note in notes), width)] * last
-    merged = call(
-        functools.partial(merge_kernel, axis, level, len(notes)),
-        outs,
-        [element, got, *notes],
-        f"merge_{axis}_{level}",
-        after=after,
-    )
+    merged = call(functools.partial(merge_kernel, axis, level, len(notes)), outs, [element, got, *notes], after=after)
     return merged[0], merged[-1]
 
 
-def route(halves, blocks, slots, across):
-    count, width = lax.axis_size("gz"), blocks.shape[2]
-    ways, piece = count // 2, BLOCK_ROWS // CHUNKS
-    crossed = [swap(half, "gz", ways) for half in halves]
-    straight = pack(ways, blocks, slots, "straight")
+def route(chunks, slots, across):
+    count = lax.axis_size("gz")
+    number, piece, width = chunks[0].shape
+    ways = count // 2
+    crossed = [swap(chunk, "gz", ways) for chunk in chunks]
+    straight = pack(ways, chunks, slots)
     arrays = [straight[0]] + [swap(straight[way], "gz", way) for way in range(1, ways)]
-    shape = (count * MOST, BLOCK_ROWS, width)
-    incoming = place(arrays, [(way, 0) for way in range(ways)], None, shape, "place_straight")
-    for chunk in range(CHUNKS):
-        passed = pack(ways, crossed[chunk], across, f"relay_{chunk}")
+    shapes = [(count * MOST, BLOCK_ROWS, width), (number, BLOCK_ROWS, width)]
+    plan = [(way, 0) for way in range(ways)]
+    incoming, field = place(arrays, plan, None, shapes, chunks)
+    for k in range(CHUNKS):
+        passed = pack(ways, crossed[k : k + 1], across)
         arrays = [passed[0]] + [swap(passed[way], "gz", way) for way in range(1, ways)]
-        plan = [(way ^ ways, chunk * piece) for way in range(ways)]
-        incoming = place(arrays, plan, incoming, shape, f"place_{chunk}")
-    return incoming
+        plan = [(way ^ ways, k * piece) for way in range(ways)]
+        (incoming,) = place(arrays, plan, incoming, shapes[:1])
+    return field, incoming
 
 
 def on_device(volume, owners):
@@ -389,10 +398,10 @@
     z_parts, y_parts = (depth, height, width), (height, depth, width)
     part = functools.partial
     field = volume.reshape(flat)
-    edges = call(part(edge_kernel, depth, height), [plane, plane, side, side], [field], "edges")
+    edges = call(part(edge_kernel, depth, height), [plane, plane, side, side], [field])
     z_sides, y_sides = neighbours(*edges[:2], "gz"), neighbours(*edges[2:], "xy")
     (slots,) = call(
-        slot_kernel, [(-(-blocks // 8) * 8, width)], [owners.reshape(1, blocks)], "slots", smem=(0,), after=edges[:1]
+        slot_kernel, [(-(-blocks // 8) * 8, width)], [owners.reshape(1, blocks)], smem=(0,), after=edges[:1]
     )
     ghosts = ()
     for step in range(STEPS):
@@ -401,14 +410,10 @@
             part(z_kernel, depth, height, step > 0),
             [flat, z_parts, z_parts, z_parts, (7,) + plane],
             [field, *z_sides, *y_sides, *ghosts],
-            "z_pieces",
+            after=[slots],
         )
         *y_pieces, y_element = call(
-            part(y_kernel, depth, height),
-            [y_parts, y_parts, y_parts, (7,) + side],
-            [g_field, field],
-            "y_pieces",
-            after=[z_element],
+            part(y_kernel, depth, height), [y_parts, y_parts, y_parts, (7,) + side], [g_field, field], after=[z_element]
         )
         y_sent, y_pairs = y_element, []
         z_sent, z_pairs = z_element, []
@@ -421,21 +426,16 @@
             z_pairs += [z_element, swap(z_sent, "gz", 1 << level)]
             behind = []
             if level == 0:
-                (near_x,) = call(
-                    part(x_kernel, 0, half[0]), [half], [g_field, field], "x_near", after=[y_element]
-                )
+                (near_x,) = call(part(x_kernel, 0, half[0]), [half], [g_field, field], after=[y_element])
                 behind = [near_x]
             if level == 1:
-                (far_x,) = call(
-                    part(x_kernel, half[0], half[0]), [half], [g_field, field], "x_far", after=[z_element]
-                )
+                (far_x,) = call(part(x_kernel, half[0], half[0]), [half], [g_field, field], after=[z_element])
                 total, *z_edges = call(
                     part(sum_kernel, depth, height, not last),
                     [flat] + [plane, plane] * (not last),
                     [near_x, far_x, *y_pieces, *y_pairs],
-                    "sum_xy",
                 )
-                behind = [total]
+                behind = [far_x]
             if level + 1 < z_rounds:
                 z_element, z_sent = merge(*z_pairs[-2:], "gz", level, behind, () if step else (slots,))
         if step == 0:
@@ -443,25 +443,18 @@
         if not last:
             z_sides = neighbours(*z_edges, "gz")
             field, *rest = call(
-                part(step_kernel, depth, height),
-                [flat, side, side, plane, plane],
-                [total, *z_pieces, *z_pairs],
-                "new_field",
+                part(step_kernel, depth, height), [flat, side, side, plane, plane], [total, *z_pieces, *z_pairs]
             )
             y_sides, ghosts = neighbours(*rest[:2], "xy"), rest[2:]
-    field, *halves = call(
-        part(last_kernel, depth, height),
-        [flat] + [(blocks, BLOCK_ROWS // CHUNKS, width)] * CHUNKS,
-        [total, *z_pieces, *z_pairs],
-        "denoised",
+    chunks = call(
+        part(last_kernel, depth, height), [(blocks, BLOCK_ROWS // CHUNKS, width)] * CHUNKS, [total, *z_pieces, *z_pairs]
     )
-    incoming = route(halves, field.reshape(blocks, BLOCK_ROWS, width), slots, across)
+    field, incoming = route(chunks, slots, across)
     return field.reshape(volume.shape), incoming[None]
 
 
 def solution(mesh):
     in_specs = (P("gz", "xy", None), P("xy", "gz", None))
     out_specs = (P("gz", "xy", None), P("xy", "gz", None, None))
-    return jax.shard_map(
-        on_device, mesh=mesh, in_specs=in_specs, out_specs=out_specs, check_vma=False
-    )
+
+    return jax.shard_map(on_device, mesh=mesh, in_specs=in_specs, out_specs=out_specs, check_vma=False)

time: 69.5 us -> 71.7 us (1.032)
  starting transfers between devices: 32.6 us -> 37.4 us
  Pallas kernels: 13.6 us -> 11.9 us
  local copies, waits for them, and re-layouts: 1.9 us -> 0.95 us
    ppermute x25, starting transfers between devices: 28.8 us -> 34.1 us  [swap(): return lax.ppermute(values, axis, [(i, i ^ stride) for i in range(count)])]
    pallas_call x23, Pallas kernels: 11.3 us -> 9.55 us  [call(): pl.pallas_call(lambda *refs: body(*refs[:count], *refs[count + len(after)...]
    ppermute x4, waiting for transfers between devices: 3.01 us -> 1.34 us  [the longest x2 1.33 us: far(): return lax.ppermute(second, axis, other + [(j, i) for i, j in other])]
    ppermute x25, waiting for transfers between devices: 17.4 us -> 19 us  [swap(): return lax.ppermute(values, axis, [(i, i ^ stride) for i in range(count)])]
    unnamed x8 -> x6, local copies, waits for them, and re-layouts: 1.9 us -> 0.95 us
  transfers between devices with their start and end apart: 29 -> 29, of which waited for: 15 -> 14; matrix products, arithmetic and copies ran while one was open for 0% -> 0% of each run, Pallas kernels for 16% -> 14%
where the time goes in v4:
time: 71.7 us; the launch traced here: 71.5 us
  starting transfers between devices  37.4 us (52%)
  waiting for transfers between devices  20.3 us (28%)
  Pallas kernels  11.9 us (17%)
  local copies, waits for them, and re-layouts  0.95 us (1%)
  between operations  0.89 us (1%)
    ppermute x25, starting transfers between devices, swap(): return lax.ppermute(values, axis, [(i, i ^ stride) for i in range(count)])  34.1 us
    ppermute x25, waiting for transfers between devices, swap(): return lax.ppermute(values, axis, [(i, i ^ stride) for i in range(count)])  19 us
    pallas_call x23, Pallas kernels, call(): pl.pallas_call(lambda *refs: body(*refs[:count], *refs[count + len(after)...  9.55 us
    ppermute x2, starting transfers between devices, far(): return lax.ppermute(second, axis, other + [(j, i) for i, j in other])  2.78 us
    pallas_call x3, Pallas kernels, place(): pl.pallas_call(functools.partial(place_kernel, plan, len(kept), not extra...  2.39 us
  transfers between devices with their start and end apart: 29, of which 14 were waited for; matrix products, arithmetic and copies ran while one was open for 0% of the time, Pallas kernels for 14%

profile of v4, /device:TPU:0, one launch (start us, length us, event | category | flops | bytes accessed | tf_op | source)
XLA Modules:
  0.0 71.5 jit_solution(5775152848674041414)
XLA Ops:
  0.6 0.9 %copy-done = f32[16,32,128]{2,1,0:T(8,128)S(1)} copy-done((f32[16,32,128]{2,1,0:T(8,128)S(1)}, f32[16,32,128]{2,1,0:T(8,128)}, u32[]{:S(2)}) %copy-start) | copy-done | bytes 262168
  1.6 0.6 collective-permute-start.1
  2.2 4.0 %collective-permute-start = (f32[32,128]{1,0:T(8,128)S(1)}, f32[32,128]{1,0:T(8,128)S(1)}, u32[]{:S(2)}, u32[]{:S(2)}) collective-permute-start(f32[32,128]{1,0:T(8,128)S(1)} %get-tuple-element.56.refs_1_), channel_id=1, source_target_pairs={{0,4},{4,0},{8,12},{12,8},{16,20},{20,16},{24,28},{28,24},{1,5},{5... | collective-permute-start | bytes 49160 | tf_op jit(solution)/shard_map/ppermute | solution.py:339
  6.2 1.6 %collective-permute-start.3 = (f32[16,128]{1,0:T(8,128)S(1)}, f32[16,128]{1,0:T(8,128)S(1)}, u32[]{:S(2)}, u32[]{:S(2)}) collective-permute-start(f32[16,128]{1,0:T(8,128)S(1)} %get-tuple-element.59), channel_id=1, source_target_pairs={{1,2},{3,0},{2,1},{0,3},{5,6},{7,4},{6,5},{4,7},{9,10},{11,8},{10,... | collective-permute-start | bytes 24584 | tf_op jit(solution)/shard_map/ppermute | solution.py:350
  7.8 0.6 shard_map.42.refs_5_.refs_2_.refs_7_
  8.4 0.9 %collective-permute-done.3.refs_4_ = f32[16,128]{1,0:T(8,128)S(1)} collective-permute-done((f32[16,128]{1,0:T(8,128)S(1)}, f32[16,128]{1,0:T(8,128)S(1)}, u32[]{:S(2)}, u32[]{:S(2)}) %collective-permute-start.3) | collective-permute-done | bytes 8224 | tf_op jit(solution)/shard_map/ppermute | solution.py:350
  9.3 0.4 shard_map.43
  9.7 0.7 collective-permute-start.5
  10.9 1.2 %collective-permute-done.4.refs_1_.refs_6_ = f32[7,16,128]{2,1,0:T(8,128)S(1)} collective-permute-done((f32[7,16,128]{2,1,0:T(8,128)S(1)}, f32[7,16,128]{2,1,0:T(8,128)S(1)}, u32[]{:S(2)}, u32[]{:S(2)}) %collective-permute-start.4) | collective-permute-done | bytes 57376 | tf_op jit(solution)/shard_map/ppermute | solution.py:339
  12.2 1.4 %shard_map.46.refs_2_.refs_0_ = f32[256,128]{1,0:T(8,128)S(1)} custom-call(f32[512,128]{1,0:T(8,128)S(1)} %get-tuple-element.60.refs_0_, f32[512,128]{1,0:T(8,128)S(1)} %bitcast.7, f32[7,16,128]{2,1,0:T(8,128)S(1)} %get-tuple-element.63.refs_2_.refs_7_), custom_call_target="tpu_custom_call" | custom-call | tf_op jit(solution)/shard_map/pallas_call | solution.py:28
  13.5 1.8 %collective-permute-done.5.refs_1_.refs_5_ = f32[7,32,128]{2,1,0:T(8,128)S(1)} collective-permute-done((f32[7,32,128]{2,1,0:T(8,128)S(1)}, f32[7,32,128]{2,1,0:T(8,128)S(1)}, u32[]{:S(2)}, u32[]{:S(2)}) %collective-permute-start.5) | collective-permute-done | bytes 114720 | tf_op jit(solution)/shard_map/ppermute | solution.py:339
  15.4 1.6 %collective-permute-start.7 = (f32[7,32,128]{2,1,0:T(8,128)S(1)}, f32[7,32,128]{2,1,0:T(8,128)S(1)}, u32[]{:S(2)}, u32[]{:S(2)}) collective-permute-start(f32[7,32,128]{2,1,0:T(8,128)S(1)} %shard_map.47.refs_2_.refs_0_.refs_6_), channel_id=1, source_target_pairs={{0,8},{4,12},{8,0},{12,4},{16,24},{20,28},{24,16},{28,20},{1,9},{5... | collective-permute-start | bytes 344072 | tf_op jit(solution)/shard_map/ppermute | solution.py:339
  17.0 1.4 %shard_map.48.refs_1_.refs_3_ = f32[256,128]{1,0:T(8,128)S(1)} custom-call(f32[512,128]{1,0:T(8,128)S(1)} %get-tuple-element.60.refs_0_, f32[512,128]{1,0:T(8,128)S(1)} %bitcast.8, f32[7,32,128]{2,1,0:T(8,128)S(1)} %shard_map.47.refs_2_.refs_0_.refs_6_), custom_call_target="tpu_custom_call" | custom-call | tf_op jit(solution)/shard_map/pallas_call | solution.py:28
  18.4 1.8 %collective-permute-done.7.refs_1_.refs_7_ = f32[7,32,128]{2,1,0:T(8,128)S(1)} collective-permute-done((f32[7,32,128]{2,1,0:T(8,128)S(1)}, f32[7,32,128]{2,1,0:T(8,128)S(1)}, u32[]{:S(2)}, u32[]{:S(2)}) %collective-permute-start.7) | collective-permute-done | bytes 114720 | tf_op jit(solution)/shard_map/ppermute | solution.py:339
  20.3 2.7 %collective-permute-start.8 = (f32[104,128]{1,0:T(8,128)S(1)}, f32[104,128]{1,0:T(8,128)S(1)}, u32[]{:S(2)}, u32[]{:S(2)}) collective-permute-start(f32[104,128]{1,0:T(8,128)S(1)} %get-tuple-element.73), channel_id=1, source_target_pairs={{0,16},{4,20},{8,24},{12,28},{16,0},{20,4},{24,8},{28,12},{1,17},{... | collective-permute-start | bytes 159752 | tf_op jit(solution)/shard_map/ppermute | solution.py:339
  22.9 1.5 %collective-permute-start.6 = (f32[48,128]{1,0:T(8,128)S(1)}, f32[48,128]{1,0:T(8,128)S(1)}, u32[]{:S(2)}, u32[]{:S(2)}) collective-permute-start(f32[48,128]{1,0:T(8,128)S(1)} %get-tuple-element.67), channel_id=1, source_target_pairs={{0,2},{1,3},{2,0},{3,1},{4,6},{5,7},{6,4},{7,5},{8,10},{9,11},{10,... | collective-permute-start | bytes 73736 | tf_op jit(solution)/shard_map/ppermute | solution.py:339
  24.4 2.3 %collective-permute-done.6.refs_8_ = f32[48,128]{1,0:T(8,128)S(1)} collective-permute-done((f32[48,128]{1,0:T(8,128)S(1)}, f32[48,128]{1,0:T(8,128)S(1)}, u32[]{:S(2)}, u32[]{:S(2)}) %collective-permute-start.6) | collective-permute-done | bytes 24608 | tf_op jit(solution)/shard_map/ppermute | solution.py:339
  27.1 0.5 collective-permute-start.9
  27.7 0.6 collective-permute-start.11
  28.3 1.2 %collective-permute-start.12 = (f32[16,128]{1,0:T(8,128)S(1)}, f32[16,128]{1,0:T(8,128)S(1)}, u32[]{:S(2)}, u32[]{:S(2)}) collective-permute-start(f32[16,128]{1,0:T(8,128)S(1)} %get-tuple-element.78), channel_id=1, source_target_pairs={{1,2},{3,0},{2,1},{0,3},{5,6},{7,4},{6,5},{4,7},{9,10},{11,8},{10,... | collective-permute-start | bytes 24584 | tf_op jit(solution)/shard_map/ppermute | solution.py:350
  29.4 1.5 %collective-permute-done.9.refs_1_ = f32[32,128]{1,0:T(8,128)S(1)} collective-permute-done((f32[32,128]{1,0:T(8,128)S(1)}, f32[32,128]{1,0:T(8,128)S(1)}, u32[]{:S(2)}, u32[]{:S(2)}) %collective-permute-start.9) | collective-permute-done | bytes 16416 | tf_op jit(solution)/shard_map/ppermute | solution.py:339
  30.9 0.4 collective-permute-done.12.refs_4_
  31.4 0.4 shard_map.52
  31.8 2.7 %collective-permute-start.14 = (f32[7,32,128]{2,1,0:T(8,128)S(1)}, f32[7,32,128]{2,1,0:T(8,128)S(1)}, u32[]{:S(2)}, u32[]{:S(2)}) collective-permute-start(f32[7,32,128]{2,1,0:T(8,128)S(1)} %get-tuple-element.82.refs_2_.refs_0_.refs_4_), channel_id=1, source_target_pairs={{0,4},{4,0},{8,12},{12,8},{16,20},{20,16},{24,28},{28,24},{1,5},{5... | collective-permute-start | bytes 344072 | tf_op jit(solution)/shard_map/ppermute | solution.py:339
  34.4 0.4 shard_map.53
  35.1 1.1 %collective-permute-done.13.refs_1_.refs_6_ = f32[7,16,128]{2,1,0:T(8,128)S(1)} collective-permute-done((f32[7,16,128]{2,1,0:T(8,128)S(1)}, f32[7,16,128]{2,1,0:T(8,128)S(1)}, u32[]{:S(2)}, u32[]{:S(2)}) %collective-permute-start.13) | collective-permute-done | bytes 57376 | tf_op jit(solution)/shard_map/ppermute | solution.py:339
  36.2 1.4 %shard_map.55.refs_2_.refs_0_ = f32[256,128]{1,0:T(8,128)S(1)} custom-call(f32[512,128]{1,0:T(8,128)S(1)} %get-tuple-element.81.refs_0_, f32[512,128]{1,0:T(8,128)S(1)} %get-tuple-element.74.refs_0_.refs_1_, f32[7,16,128]{2,1,0:T(8,128)S(1)} %get-tuple-element.84.refs_2_.refs_7_), custom_call_target="tpu_custom_call" | custom-call | tf_op jit(solution)/shard_map/pallas_call | solution.py:28
  37.6 0.6 collective-permute-done.14.refs_1_.refs_5_
  38.2 1.9 %collective-permute-start.16 = (f32[7,32,128]{2,1,0:T(8,128)S(1)}, f32[7,32,128]{2,1,0:T(8,128)S(1)}, u32[]{:S(2)}, u32[]{:S(2)}) collective-permute-start(f32[7,32,128]{2,1,0:T(8,128)S(1)} %shard_map.56.refs_2_.refs_0_.refs_6_), channel_id=1, source_target_pairs={{0,8},{4,12},{8,0},{12,4},{16,24},{20,28},{24,16},{28,20},{1,9},{5... | collective-permute-start | bytes 344072 | tf_op jit(solution)/shard_map/ppermute | solution.py:339
  40.1 1.4 %shard_map.57.refs_1_.refs_2_ = f32[256,128]{1,0:T(8,128)S(1)} custom-call(f32[512,128]{1,0:T(8,128)S(1)} %get-tuple-element.81.refs_0_, f32[512,128]{1,0:T(8,128)S(1)} %get-tuple-element.74.refs_0_.refs_1_, f32[7,32,128]{2,1,0:T(8,128)S(1)} %shard_map.56.refs_2_.refs_0_.refs_6_), custom_call_target="tpu_custom_call" | custom-call | tf_op jit(solution)/shard_map/pallas_call | solution.py:28
  41.5 1.7 %collective-permute-done.16.refs_1_.refs_7_ = f32[7,32,128]{2,1,0:T(8,128)S(1)} collective-permute-done((f32[7,32,128]{2,1,0:T(8,128)S(1)}, f32[7,32,128]{2,1,0:T(8,128)S(1)}, u32[]{:S(2)}, u32[]{:S(2)}) %collective-permute-start.16) | collective-permute-done | bytes 114720 | tf_op jit(solution)/shard_map/ppermute | solution.py:339
  43.2 1.4 %collective-permute-start.17 = (f32[96,128]{1,0:T(8,128)S(1)}, f32[96,128]{1,0:T(8,128)S(1)}, u32[]{:S(2)}, u32[]{:S(2)}) collective-permute-start(f32[96,128]{1,0:T(8,128)S(1)} %get-tuple-element.93), channel_id=1, source_target_pairs={{0,16},{4,20},{8,24},{12,28},{16,0},{20,4},{24,8},{28,12},{1,17},{... | collective-permute-start | bytes 147464 | tf_op jit(solution)/shard_map/ppermute | solution.py:339
  44.7 1.5 %collective-permute-start.15 = (f32[48,128]{1,0:T(8,128)S(1)}, f32[48,128]{1,0:T(8,128)S(1)}, u32[]{:S(2)}, u32[]{:S(2)}) collective-permute-start(f32[48,128]{1,0:T(8,128)S(1)} %get-tuple-element.88), channel_id=1, source_target_pairs={{0,2},{1,3},{2,0},{3,1},{4,6},{5,7},{6,4},{7,5},{8,10},{9,11},{10,... | collective-permute-start | bytes 73736 | tf_op jit(solution)/shard_map/ppermute | solution.py:339
  46.1 2.3 %collective-permute-done.15.refs_8_ = f32[48,128]{1,0:T(8,128)S(1)} collective-permute-done((f32[48,128]{1,0:T(8,128)S(1)}, f32[48,128]{1,0:T(8,128)S(1)}, u32[]{:S(2)}, u32[]{:S(2)}) %collective-permute-start.15) | collective-permute-done | bytes 24608 | tf_op jit(solution)/shard_map/ppermute | solution.py:339
  49.0 1.6 %collective-permute-start.25 = (f32[4,64,128]{2,1,0:T(8,128)S(1)}, f32[4,64,128]{2,1,0:T(8,128)S(1)}, u32[]{:S(2)}, u32[]{:S(2)}) collective-permute-start(f32[4,64,128]{2,1,0:T(8,128)S(1)} %get-tuple-element.94.refs_0_.refs_4_), channel_id=1, source_target_pairs={{0,16},{4,20},{8,24},{12,28},{16,0},{20,4},{24,8},{28,12},{1,17},{... | collective-permute-start | bytes 393224 | tf_op jit(solution)/shard_map/ppermute | solution.py:339
  50.6 1.4 %collective-permute-start.21 = (f32[4,64,128]{2,1,0:T(8,128)S(1)}, f32[4,64,128]{2,1,0:T(8,128)S(1)}, u32[]{:S(2)}, u32[]{:S(2)}) collective-permute-start(f32[4,64,128]{2,1,0:T(8,128)S(1)} %get-tuple-element.95.refs_1_.refs_5_), channel_id=1, source_target_pairs={{0,16},{4,20},{8,24},{12,28},{16,0},{20,4},{24,8},{28,12},{1,17},{... | collective-permute-start | bytes 393224 | tf_op jit(solution)/shard_map/ppermute | solution.py:339
  52.2 1.5 %collective-permute-start.18 = (f32[2,128,128]{2,1,0:T(8,128)S(1)}, f32[2,128,128]{2,1,0:T(8,128)S(1)}, u32[]{:S(2)}, u32[]{:S(2)}) collective-permute-start(f32[2,128,128]{2,1,0:T(8,128)S(1)} %get-tuple-element.97), channel_id=1, source_target_pairs={{0,4},{4,0},{8,12},{12,8},{16,20},{20,16},{24,28},{28,24},{1,5},{5... | collective-permute-start | bytes 393224 | tf_op jit(solution)/shard_map/ppermute | solution.py:339
  53.8 2.0 %collective-permute-start.20 = (f32[2,128,128]{2,1,0:T(8,128)S(1)}, f32[2,128,128]{2,1,0:T(8,128)S(1)}, u32[]{:S(2)}, u32[]{:S(2)}) collective-permute-start(f32[2,128,128]{2,1,0:T(8,128)S(1)} %get-tuple-element.99), channel_id=1, source_target_pairs={{0,12},{4,8},{8,4},{12,0},{16,28},{20,24},{24,20},{28,16},{1,13},{... | collective-permute-start | bytes 393224 | tf_op jit(solution)/shard_map/ppermute | solution.py:339
  55.8 2.8 %collective-permute-done.25.refs_0_ = f32[4,64,128]{2,1,0:T(8,128)S(1)} collective-permute-done((f32[4,64,128]{2,1,0:T(8,128)S(1)}, f32[4,64,128]{2,1,0:T(8,128)S(1)}, u32[]{:S(2)}, u32[]{:S(2)}) %collective-permute-start.25) | collective-permute-done | bytes 131104 | tf_op jit(solution)/shard_map/ppermute | solution.py:339
  58.8 1.8 %collective-permute-start.26 = (f32[2,64,128]{2,1,0:T(8,128)S(1)}, f32[2,64,128]{2,1,0:T(8,128)S(1)}, u32[]{:S(2)}, u32[]{:S(2)}) collective-permute-start(f32[2,64,128]{2,1,0:T(8,128)S(1)} %get-tuple-element.106), channel_id=1, source_target_pairs={{0,4},{4,0},{8,12},{12,8},{16,20},{20,16},{24,28},{28,24},{1,5},{5... | collective-permute-start | bytes 196616 | tf_op jit(solution)/shard_map/ppermute | solution.py:339
  60.5 0.5 collective-permute-done.21.refs_0_
  61.3 3.0 %collective-permute-start.28 = (f32[2,64,128]{2,1,0:T(8,128)S(1)}, f32[2,64,128]{2,1,0:T(8,128)S(1)}, u32[]{:S(2)}, u32[]{:S(2)}) collective-permute-start(f32[2,64,128]{2,1,0:T(8,128)S(1)} %get-tuple-element.108), channel_id=1, source_target_pairs={{0,12},{4,8},{8,4},{12,0},{16,28},{20,24},{24,20},{28,16},{1,13},{... | collective-permute-start | bytes 196616 | tf_op jit(solution)/shard_map/ppermute | solution.py:339
  64.4 0.5 collective-permute-start.22
  65.0 2.8 %collective-permute-start.24 = (f32[2,64,128]{2,1,0:T(8,128)S(1)}, f32[2,64,128]{2,1,0:T(8,128)S(1)}, u32[]{:S(2)}, u32[]{:S(2)}) collective-permute-start(f32[2,64,128]{2,1,0:T(8,128)S(1)} %get-tuple-element.104), channel_id=1, source_target_pairs={{0,12},{4,8},{8,4},{12,0},{16,28},{20,24},{24,20},{28,16},{1,13},{... | collective-permute-start | bytes 196616 | tf_op jit(solution)/shard_map/ppermute | solution.py:339
  67.9 0.9 %shard_map.62 = (f32[16,128,128]{2,1,0:T(8,128)}, f32[4,128,128]{2,1,0:T(8,128)}) custom-call(f32[2,128,128]{2,1,0:T(8,128)S(1)} %get-tuple-element.96.refs_0_, f32[2,128,128]{2,1,0:T(8,128)S(1)} %collective-permute-done.18.refs_1_, f32[2,128,128]{2,1,0:T(8,128)S(1)} %collective-permute-done.19.refs_2_, f32[2,128,128]{2,1,0:T(8,128)S(1)} %collective-permute-done.20.refs_3_, ...), custom_call_target="tpu_custom_call" | custom-call | tf_op jit(solution)/shard_map/pallas_call | solution.py:326
  68.8 0.7 %shard_map.65.refs_4_ = f32[16,128,128]{2,1,0:T(8,128)} custom-call(f32[2,64,128]{2,1,0:T(8,128)S(1)} %get-tuple-element.105.refs_0_, f32[2,64,128]{2,1,0:T(8,128)S(1)} %collective-permute-done.26.refs_1_, f32[2,64,128]{2,1,0:T(8,128)S(1)} %collective-permute-done.27.refs_2_, ...), custom_call_target="tpu_custom_call", output_to_operand_aliasing={{}: (4, {})} | custom-call | tf_op jit(solution)/shard_map/pallas_call | solution.py:326
  69.6 1.2 %collective-permute-done.24.refs_3_ = f32[2,64,128]{2,1,0:T(8,128)S(1)} collective-permute-done((f32[2,64,128]{2,1,0:T(8,128)S(1)}, f32[2,64,128]{2,1,0:T(8,128)S(1)}, u32[]{:S(2)}, u32[]{:S(2)}) %collective-permute-start.24) | collective-permute-done | bytes 65568 | tf_op jit(solution)/shard_map/ppermute | solution.py:339
  70.8 0.7 %shard_map.66 = f32[16,128,128]{2,1,0:T(8,128)} custom-call(f32[2,64,128]{2,1,0:T(8,128)S(1)} %get-tuple-element.101.refs_0_, f32[2,64,128]{2,1,0:T(8,128)S(1)} %collective-permute-done.22.refs_1_, f32[2,64,128]{2,1,0:T(8,128)S(1)} %collective-permute-done.23.refs_2_, ...), custom_call_target="tpu_custom_call", output_to_operand_aliasing={{}: (4, {})} | custom-call | tf_op jit(solution)/shard_map/pallas_call | solution.py:326
  (43 shorter events, 2.8 us)
Async XLA Ops:
  0.6 1.0 %copy-start = (f32[16,32,128]{2,1,0:T(8,128)S(1)}, f32[16,32,128]{2,1,0:T(8,128)}, u32[]{:S(2)}) copy-start(f32[16,32,128]{2,1,0:T(8,128)} %param.2) | copy-start | bytes 786436
  1.6 7.7 %copy-start.1 = (f32[16,32,128]{2,1,0:T(8,128)S(1)}, f32[16,32,128]{2,1,0:T(8,128)}, u32[]{:S(2)}) copy-start(f32[16,32,128]{2,1,0:T(8,128)} %param.2) | copy-start | bytes 786436
  1.6 7.7 %collective-permute-start.1 = (f32[32,128]{1,0:T(8,128)S(1)}, f32[32,128]{1,0:T(8,128)S(1)}, u32[]{:S(2)}, u32[]{:S(2)}) collective-permute-start(f32[32,128]{1,0:T(8,128)S(1)} %get-tuple-element.57), channel_id=1, source_target_pairs={{0,1},{1,0},{2,3},{3,2},{4,8},{5,9},{6,10},{7,11},{8,4},{9,5},{10,... | collective-permute-start | bytes 49160 | tf_op jit(solution)/shard_map/ppermute | solution.py:357
  2.2 7.1 %collective-permute-start = (f32[32,128]{1,0:T(8,128)S(1)}, f32[32,128]{1,0:T(8,128)S(1)}, u32[]{:S(2)}, u32[]{:S(2)}) collective-permute-start(f32[32,128]{1,0:T(8,128)S(1)} %get-tuple-element.56.refs_1_), channel_id=1, source_target_pairs={{0,4},{4,0},{8,12},{12,8},{16,20},{20,16},{24,28},{28,24},{1,5},{5... | collective-permute-start | bytes 49160 | tf_op jit(solution)/shard_map/ppermute | solution.py:339
  6.2 2.2 %collective-permute-start.2 = (f32[16,128]{1,0:T(8,128)S(1)}, f32[16,128]{1,0:T(8,128)S(1)}, u32[]{:S(2)}, u32[]{:S(2)}) collective-permute-start(f32[16,128]{1,0:T(8,128)S(1)} %get-tuple-element.58), channel_id=1, source_target_pairs={{0,1},{1,0},{2,3},{3,2},{4,5},{5,4},{6,7},{7,6},{8,9},{9,8},{10,11... | collective-permute-start | bytes 24584 | tf_op jit(solution)/shard_map/ppermute | solution.py:339
  6.2 1.6 %copy-start.2 = (s32[1,4,1]{1,2,0:T(1,128)S(1)}, s32[1,4,1]{1,2,0:T(1,128)}, u32[]{:S(2)}) copy-start(s32[1,4,1]{1,2,0:T(1,128)} %param.3) | copy-start | bytes 52
  6.2 3.1 %collective-permute-start.3 = (f32[16,128]{1,0:T(8,128)S(1)}, f32[16,128]{1,0:T(8,128)S(1)}, u32[]{:S(2)}, u32[]{:S(2)}) collective-permute-start(f32[16,128]{1,0:T(8,128)S(1)} %get-tuple-element.59), channel_id=1, source_target_pairs={{1,2},{3,0},{2,1},{0,3},{5,6},{7,4},{6,5},{4,7},{9,10},{11,8},{10,... | collective-permute-start | bytes 24584 | tf_op jit(solution)/shard_map/ppermute | solution.py:350
  9.7 5.6 %collective-permute-start.5 = (f32[7,32,128]{2,1,0:T(8,128)S(1)}, f32[7,32,128]{2,1,0:T(8,128)S(1)}, u32[]{:S(2)}, u32[]{:S(2)}) collective-permute-start(f32[7,32,128]{2,1,0:T(8,128)S(1)} %get-tuple-element.61.refs_2_.refs_0_.refs_4_), channel_id=1, source_target_pairs={{0,4},{4,0},{8,12},{12,8},{16,20},{20,16},{24,28},{28,24},{1,5},{5... | collective-permute-start | bytes 344072 | tf_op jit(solution)/shard_map/ppermute | solution.py:339
  10.8 1.3 %collective-permute-start.4 = (f32[7,16,128]{2,1,0:T(8,128)S(1)}, f32[7,16,128]{2,1,0:T(8,128)S(1)}, u32[]{:S(2)}, u32[]{:S(2)}) collective-permute-start(f32[7,16,128]{2,1,0:T(8,128)S(1)} %get-tuple-element.62.refs_0_.refs_5_), channel_id=1, source_target_pairs={{0,1},{1,0},{2,3},{3,2},{4,5},{5,4},{6,7},{7,6},{8,9},{9,8},{10,11... | collective-permute-start | bytes 172040 | tf_op jit(solution)/shard_map/ppermute | solution.py:339
  15.4 4.9 %collective-permute-start.7 = (f32[7,32,128]{2,1,0:T(8,128)S(1)}, f32[7,32,128]{2,1,0:T(8,128)S(1)}, u32[]{:S(2)}, u32[]{:S(2)}) collective-permute-start(f32[7,32,128]{2,1,0:T(8,128)S(1)} %shard_map.47.refs_2_.refs_0_.refs_6_), channel_id=1, source_target_pairs={{0,8},{4,12},{8,0},{12,4},{16,24},{20,28},{24,16},{28,20},{1,9},{5... | collective-permute-start | bytes 344072 | tf_op jit(solution)/shard_map/ppermute | solution.py:339
  20.3 7.3 %collective-permute-start.8 = (f32[104,128]{1,0:T(8,128)S(1)}, f32[104,128]{1,0:T(8,128)S(1)}, u32[]{:S(2)}, u32[]{:S(2)}) collective-permute-start(f32[104,128]{1,0:T(8,128)S(1)} %get-tuple-element.73), channel_id=1, source_target_pairs={{0,16},{4,20},{8,24},{12,28},{16,0},{20,4},{24,8},{28,12},{1,17},{... | collective-permute-start | bytes 159752 | tf_op jit(solution)/shard_map/ppermute | solution.py:339
  22.9 3.8 %collective-permute-start.6 = (f32[48,128]{1,0:T(8,128)S(1)}, f32[48,128]{1,0:T(8,128)S(1)}, u32[]{:S(2)}, u32[]{:S(2)}) collective-permute-start(f32[48,128]{1,0:T(8,128)S(1)} %get-tuple-element.67), channel_id=1, source_target_pairs={{0,2},{1,3},{2,0},{3,1},{4,6},{5,7},{6,4},{7,5},{8,10},{9,11},{10,... | collective-permute-start | bytes 73736 | tf_op jit(solution)/shard_map/ppermute | solution.py:339
  27.1 3.8 %collective-permute-start.9 = (f32[32,128]{1,0:T(8,128)S(1)}, f32[32,128]{1,0:T(8,128)S(1)}, u32[]{:S(2)}, u32[]{:S(2)}) collective-permute-start(f32[32,128]{1,0:T(8,128)S(1)} %get-tuple-element.75), channel_id=1, source_target_pairs={{0,4},{4,0},{8,12},{12,8},{16,20},{20,16},{24,28},{28,24},{1,5},{5... | collective-permute-start | bytes 49160 | tf_op jit(solution)/shard_map/ppermute | solution.py:339
  27.6 3.3 %collective-permute-start.10 = (f32[32,128]{1,0:T(8,128)S(1)}, f32[32,128]{1,0:T(8,128)S(1)}, u32[]{:S(2)}, u32[]{:S(2)}) collective-permute-start(f32[32,128]{1,0:T(8,128)S(1)} %get-tuple-element.76), channel_id=1, source_target_pairs={{0,1},{1,0},{2,3},{3,2},{4,8},{5,9},{6,10},{7,11},{8,4},{9,5},{10,... | collective-permute-start | bytes 49160 | tf_op jit(solution)/shard_map/ppermute | solution.py:357
  27.7 3.2 %collective-permute-start.11 = (f32[16,128]{1,0:T(8,128)S(1)}, f32[16,128]{1,0:T(8,128)S(1)}, u32[]{:S(2)}, u32[]{:S(2)}) collective-permute-start(f32[16,128]{1,0:T(8,128)S(1)} %get-tuple-element.77), channel_id=1, source_target_pairs={{0,1},{1,0},{2,3},{3,2},{4,5},{5,4},{6,7},{7,6},{8,9},{9,8},{10,11... | collective-permute-start | bytes 24584 | tf_op jit(solution)/shard_map/ppermute | solution.py:339
  28.3 3.1 %collective-permute-start.12 = (f32[16,128]{1,0:T(8,128)S(1)}, f32[16,128]{1,0:T(8,128)S(1)}, u32[]{:S(2)}, u32[]{:S(2)}) collective-permute-start(f32[16,128]{1,0:T(8,128)S(1)} %get-tuple-element.78), channel_id=1, source_target_pairs={{1,2},{3,0},{2,1},{0,3},{5,6},{7,4},{6,5},{4,7},{9,10},{11,8},{10,... | collective-permute-start | bytes 24584 | tf_op jit(solution)/shard_map/ppermute | solution.py:350
  31.8 6.4 %collective-permute-start.14 = (f32[7,32,128]{2,1,0:T(8,128)S(1)}, f32[7,32,128]{2,1,0:T(8,128)S(1)}, u32[]{:S(2)}, u32[]{:S(2)}) collective-permute-start(f32[7,32,128]{2,1,0:T(8,128)S(1)} %get-tuple-element.82.refs_2_.refs_0_.refs_4_), channel_id=1, source_target_pairs={{0,4},{4,0},{8,12},{12,8},{16,20},{20,16},{24,28},{28,24},{1,5},{5... | collective-permute-start | bytes 344072 | tf_op jit(solution)/shard_map/ppermute | solution.py:339
  34.8 1.3 %collective-permute-start.13 = (f32[7,16,128]{2,1,0:T(8,128)S(1)}, f32[7,16,128]{2,1,0:T(8,128)S(1)}, u32[]{:S(2)}, u32[]{:S(2)}) collective-permute-start(f32[7,16,128]{2,1,0:T(8,128)S(1)} %get-tuple-element.83.refs_0_.refs_5_), channel_id=1, source_target_pairs={{0,1},{1,0},{2,3},{3,2},{4,5},{5,4},{6,7},{7,6},{8,9},{9,8},{10,11... | collective-permute-start | bytes 172040 | tf_op jit(solution)/shard_map/ppermute | solution.py:339
  38.2 5.0 %collective-permute-start.16 = (f32[7,32,128]{2,1,0:T(8,128)S(1)}, f32[7,32,128]{2,1,0:T(8,128)S(1)}, u32[]{:S(2)}, u32[]{:S(2)}) collective-permute-start(f32[7,32,128]{2,1,0:T(8,128)S(1)} %shard_map.56.refs_2_.refs_0_.refs_6_), channel_id=1, source_target_pairs={{0,8},{4,12},{8,0},{12,4},{16,24},{20,28},{24,16},{28,20},{1,9},{5... | collective-permute-start | bytes 344072 | tf_op jit(solution)/shard_map/ppermute | solution.py:339
  43.2 5.6 %collective-permute-start.17 = (f32[96,128]{1,0:T(8,128)S(1)}, f32[96,128]{1,0:T(8,128)S(1)}, u32[]{:S(2)}, u32[]{:S(2)}) collective-permute-start(f32[96,128]{1,0:T(8,128)S(1)} %get-tuple-element.93), channel_id=1, source_target_pairs={{0,16},{4,20},{8,24},{12,28},{16,0},{20,4},{24,8},{28,12},{1,17},{... | collective-permute-start | bytes 147464 | tf_op jit(solution)/shard_map/ppermute | solution.py:339
  44.7 3.8 %collective-permute-start.15 = (f32[48,128]{1,0:T(8,128)S(1)}, f32[48,128]{1,0:T(8,128)S(1)}, u32[]{:S(2)}, u32[]{:S(2)}) collective-permute-start(f32[48,128]{1,0:T(8,128)S(1)} %get-tuple-element.88), channel_id=1, source_target_pairs={{0,2},{1,3},{2,0},{3,1},{4,6},{5,7},{6,4},{7,5},{8,10},{9,11},{10,... | collective-permute-start | bytes 73736 | tf_op jit(solution)/shard_map/ppermute | solution.py:339
  49.0 9.6 %collective-permute-start.25 = (f32[4,64,128]{2,1,0:T(8,128)S(1)}, f32[4,64,128]{2,1,0:T(8,128)S(1)}, u32[]{:S(2)}, u32[]{:S(2)}) collective-permute-start(f32[4,64,128]{2,1,0:T(8,128)S(1)} %get-tuple-element.94.refs_0_.refs_4_), channel_id=1, source_target_pairs={{0,16},{4,20},{8,24},{12,28},{16,0},{20,4},{24,8},{28,12},{1,17},{... | collective-permute-start | bytes 393224 | tf_op jit(solution)/shard_map/ppermute | solution.py:339
  50.6 10.4 %collective-permute-start.21 = (f32[4,64,128]{2,1,0:T(8,128)S(1)}, f32[4,64,128]{2,1,0:T(8,128)S(1)}, u32[]{:S(2)}, u32[]{:S(2)}) collective-permute-start(f32[4,64,128]{2,1,0:T(8,128)S(1)} %get-tuple-element.95.refs_1_.refs_5_), channel_id=1, source_target_pairs={{0,16},{4,20},{8,24},{12,28},{16,0},{20,4},{24,8},{28,12},{1,17},{... | collective-permute-start | bytes 393224 | tf_op jit(solution)/shard_map/ppermute | solution.py:339
  52.2 9.1 %collective-permute-start.18 = (f32[2,128,128]{2,1,0:T(8,128)S(1)}, f32[2,128,128]{2,1,0:T(8,128)S(1)}, u32[]{:S(2)}, u32[]{:S(2)}) collective-permute-start(f32[2,128,128]{2,1,0:T(8,128)S(1)} %get-tuple-element.97), channel_id=1, source_target_pairs={{0,4},{4,0},{8,12},{12,8},{16,20},{20,16},{24,28},{28,24},{1,5},{5... | collective-permute-start | bytes 393224 | tf_op jit(solution)/shard_map/ppermute | solution.py:339
  53.7 10.6 %collective-permute-start.19 = (f32[2,128,128]{2,1,0:T(8,128)S(1)}, f32[2,128,128]{2,1,0:T(8,128)S(1)}, u32[]{:S(2)}, u32[]{:S(2)}) collective-permute-start(f32[2,128,128]{2,1,0:T(8,128)S(1)} %get-tuple-element.98), channel_id=1, source_target_pairs={{0,8},{4,12},{8,0},{12,4},{16,24},{20,28},{24,16},{28,20},{1,9},{5... | collective-permute-start | bytes 393224 | tf_op jit(solution)/shard_map/ppermute | solution.py:339
  53.8 11.1 %collective-permute-start.20 = (f32[2,128,128]{2,1,0:T(8,128)S(1)}, f32[2,128,128]{2,1,0:T(8,128)S(1)}, u32[]{:S(2)}, u32[]{:S(2)}) collective-permute-start(f32[2,128,128]{2,1,0:T(8,128)S(1)} %get-tuple-element.99), channel_id=1, source_target_pairs={{0,12},{4,8},{8,4},{12,0},{16,28},{20,24},{24,20},{28,16},{1,13},{... | collective-permute-start | bytes 393224 | tf_op jit(solution)/shard_map/ppermute | solution.py:339
  58.8 6.2 %collective-permute-start.26 = (f32[2,64,128]{2,1,0:T(8,128)S(1)}, f32[2,64,128]{2,1,0:T(8,128)S(1)}, u32[]{:S(2)}, u32[]{:S(2)}) collective-permute-start(f32[2,64,128]{2,1,0:T(8,128)S(1)} %get-tuple-element.106), channel_id=1, source_target_pairs={{0,4},{4,0},{8,12},{12,8},{16,20},{20,16},{24,28},{28,24},{1,5},{5... | collective-permute-start | bytes 196616 | tf_op jit(solution)/shard_map/ppermute | solution.py:339
  61.1 7.7 %collective-permute-start.27 = (f32[2,64,128]{2,1,0:T(8,128)S(1)}, f32[2,64,128]{2,1,0:T(8,128)S(1)}, u32[]{:S(2)}, u32[]{:S(2)}) collective-permute-start(f32[2,64,128]{2,1,0:T(8,128)S(1)} %get-tuple-element.107), channel_id=1, source_target_pairs={{0,8},{4,12},{8,0},{12,4},{16,24},{20,28},{24,16},{28,20},{1,9},{5... | collective-permute-start | bytes 196616 | tf_op jit(solution)/shard_map/ppermute | solution.py:339
  61.3 7.5 %collective-permute-start.28 = (f32[2,64,128]{2,1,0:T(8,128)S(1)}, f32[2,64,128]{2,1,0:T(8,128)S(1)}, u32[]{:S(2)}, u32[]{:S(2)}) collective-permute-start(f32[2,64,128]{2,1,0:T(8,128)S(1)} %get-tuple-element.108), channel_id=1, source_target_pairs={{0,12},{4,8},{8,4},{12,0},{16,28},{20,24},{24,20},{28,16},{1,13},{... | collective-permute-start | bytes 196616 | tf_op jit(solution)/shard_map/ppermute | solution.py:339
  64.4 5.2 %collective-permute-start.22 = (f32[2,64,128]{2,1,0:T(8,128)S(1)}, f32[2,64,128]{2,1,0:T(8,128)S(1)}, u32[]{:S(2)}, u32[]{:S(2)}) collective-permute-start(f32[2,64,128]{2,1,0:T(8,128)S(1)} %get-tuple-element.102), channel_id=1, source_target_pairs={{0,4},{4,0},{8,12},{12,8},{16,20},{20,16},{24,28},{28,24},{1,5},{5... | collective-permute-start | bytes 196616 | tf_op jit(solution)/shard_map/ppermute | solution.py:339
  64.9 4.7 %collective-permute-start.23 = (f32[2,64,128]{2,1,0:T(8,128)S(1)}, f32[2,64,128]{2,1,0:T(8,128)S(1)}, u32[]{:S(2)}, u32[]{:S(2)}) collective-permute-start(f32[2,64,128]{2,1,0:T(8,128)S(1)} %get-tuple-element.103), channel_id=1, source_target_pairs={{0,8},{4,12},{8,0},{12,4},{16,24},{20,28},{24,16},{28,20},{1,9},{5... | collective-permute-start | bytes 196616 | tf_op jit(solution)/shard_map/ppermute | solution.py:339
  65.0 5.8 %collective-permute-start.24 = (f32[2,64,128]{2,1,0:T(8,128)S(1)}, f32[2,64,128]{2,1,0:T(8,128)S(1)}, u32[]{:S(2)}, u32[]{:S(2)}) collective-permute-start(f32[2,64,128]{2,1,0:T(8,128)S(1)} %get-tuple-element.104), channel_id=1, source_target_pairs={{0,12},{4,8},{8,4},{12,0},{16,28},{20,24},{24,20},{28,16},{1,13},{... | collective-permute-start | bytes 196616 | tf_op jit(solution)/shard_map/ppermute | solution.py:339

commit v5 on v4

v5 whole, which is shorter than its diff:
```python
import functools

import jax
import jax.numpy as jnp
from jax import lax
from jax.experimental import pallas as pl
from jax.experimental.pallas import tpu as pltpu
from jax.sharding import PartitionSpec as P


MOST = 2
CHUNKS = (128,)
BLOCK_ROWS = 128
TIME_STEP = 30.0
CONTRAST = 4.0
HALF_LINK = 1.5 * TIME_STEP
THIRD = 1.0 / 3.0
GHOSTS = 8
LAST_SENT = ((0, 2), (3, 4), (5, 6))
VMEM_LIMIT = 16 * 1024 * 1024
VMEM = pltpu.VMEM


def call(body, outs, ins, after=()):
    count = len(ins)
    specs = [pl.BlockSpec(memory_space=VMEM)] * count + [pl.BlockSpec(memory_space=pl.ANY)] * len(after)
    return pl.pallas_call(
        lambda *refs: body(*refs[:count], *refs[count + len(after) :]),
        out_shape=[jax.ShapeDtypeStruct(shape, jnp.float32) for shape in outs],
        in_specs=specs,
        out_specs=[pl.BlockSpec(memory_space=VMEM)] * len(outs),
        compiler_params=pltpu.CompilerParams(vmem_limit_bytes=VMEM_LIMIT),
    )(*ins, *after)


def edge_kernel(depth, height, field, y_first, y_second):
    y_odd = lax.rem(lax.axis_index("xy"), 2) == 1
    for k in range(2):
        near = field[pl.ds(k, depth, stride=height), :]
        far = field[pl.ds(height - 1 - k, depth, stride=height), :]
        y_first[pl.ds(k * depth, depth), :] = jnp.where(y_odd, near, far)
        y_second[pl.ds(k * depth, depth), :] = jnp.where(y_odd, far, near)


def slab_kernel(depth, height, field, y_first, y_second, slabs, z_first, z_second):
    slab = height + GHOSTS
    y_odd = lax.rem(lax.axis_index("xy"), 2) == 1
    for k in range(depth):
        slabs[pl.ds(k * slab, height), :] = field[pl.ds(k * height, height), :]
    for k in range(2):
        one, two = y_first[pl.ds(k * depth, depth), :], y_second[pl.ds(k * depth, depth), :]
        slabs[pl.ds(height + 2 * k, depth, stride=slab), :] = jnp.where(y_odd, one, two)
        slabs[pl.ds(height + 2 * k + 1, depth, stride=slab), :] = jnp.where(y_odd, two, one)
    for k in range(4, GHOSTS):
        slabs[pl.ds(height + k, depth, stride=slab), :] = jnp.zeros((depth, field.shape[1]), field.dtype)
    z_odd = lax.rem(lax.axis_index("gz"), 2) == 1
    for k in range(2):
        low, high = slabs[pl.ds(k * slab, slab), :], slabs[pl.ds((depth - 1 - k) * slab, slab), :]
        z_first[pl.ds(k * slab, slab), :] = jnp.where(z_odd, low, high)
        z_second[pl.ds(k * slab, slab), :] = jnp.where(z_odd, high, low)


def slot_kernel(given, first, slots, owners, sem):
    copy = pltpu.make_async_copy(given, owners, sem)
    copy.start()
    slots[...] = jnp.zeros_like(slots)
    copy.wait()
    for block in range(owners.shape[1]):
        rank = jnp.int32(0)
        for other in range(block):
            rank = rank + (owners[0, other] == owners[0, block]).astype(jnp.int32)
        slot = owners[0, block] * MOST + rank
        slots[pl.ds(block, 1), :] = jnp.full((1, slots.shape[1]), slot.astype(jnp.float32))


def slots_of(owners, width, after):
    blocks = owners.shape[1]
    return pl.pallas_call(
        slot_kernel,
        out_shape=jax.ShapeDtypeStruct((-(-blocks // 8) * 8, width), jnp.float32),
        in_specs=[pl.BlockSpec(memory_space=pl.ANY)] * 2,
        out_specs=pl.BlockSpec(memory_space=VMEM),
        scratch_shapes=[pltpu.SMEM((1, blocks), jnp.int32), pltpu.SemaphoreType.DMA],
        compiler_params=pltpu.CompilerParams(vmem_limit_bytes=VMEM_LIMIT),
        name="slots",
    )(owners.reshape(1, blocks), after)


def chain(g_rows, v_rows, count, solved, head, tail, element):
    g_head = g_prev = g_rows(0)
    pivot = jnp.ones_like(g_prev)
    right = v_rows(0)
    unit = pivot
    for k in range(count - 1):
        g_next = g_rows(k + 1)
        link = HALF_LINK * (g_prev + g_next)
        inverse = 1.0 / (pivot + link)
        ratio = link * inverse
        solved[k] = right * inverse
        head[k] = unit * inverse
        tail[k] = ratio
        pivot = 1.0 + ratio * pivot
        right = v_rows(k + 1) + ratio * right
        unit = ratio * unit
        g_prev = g_next
    inverse = 1.0 / pivot
    value, from_head, from_tail = right * inverse, unit * inverse, inverse
    solved[count - 1] = value
    head[count - 1] = from_head
    tail[count - 1] = from_tail
    element[2] = from_tail
    element[4] = value
    if element.shape[0] > 5:
        element[5] = g_head
        element[6] = g_prev
    for k in range(count - 2, -1, -1):
        ratio = tail[k]
        value = solved[k] + ratio * value
        from_head = head[k] + ratio * from_head
        from_tail = ratio * from_tail
        solved[k] = value
        head[k] = from_head
        tail[k] = from_tail
    element[0] = from_head
    element[1] = from_tail
    element[3] = value


def diffusivity(up, down, after, before, right, left):
    squares = ((up - down) * 0.5) * ((up - down) * 0.5)
    slope = (after - before) * 0.5
    squares = squares + slope * slope
    slope = (right - left) * 0.5
    squares = squares + slope * slope
    return 1.0 / (1.0 + squares * (1.0 / CONTRAST))


def x_sides(here):
    width = here.shape[1]
    lanes = lax.broadcasted_iota(jnp.int32, here.shape, 1)
    right = jnp.where(lanes == width - 1, here, pltpu.roll(here, width - 1, 1))
    return right, jnp.where(lanes == 0, here, pltpu.roll(here, 1, 1))


def ends(axis):
    index = lax.axis_index(axis)
    return index == 0, index == lax.axis_size(axis) - 1


def wide_kernel(depth, height, slabs, z_first, z_second, field, g_out, solved, head, tail, element, w_low, w_high):
    slab = height + GHOSTS
    width = slabs.shape[1]
    z_odd = lax.rem(lax.axis_index("gz"), 2) == 1
    z_begin, z_end = ends("gz")
    y_begin, y_end = ends("xy")
    rows = lax.broadcasted_iota(jnp.int32, (slab, width), 0)
    own = depth * slab
    field[pl.ds(0, own), :] = slabs[...]
    for k in range(2):
        one, two = z_first[pl.ds(k * slab, slab), :], z_second[pl.ds(k * slab, slab), :]
        field[pl.ds(own + 2 * k * slab, slab), :] = jnp.where(z_odd, one, two)
        field[pl.ds(own + (2 * k + 1) * slab, slab), :] = jnp.where(z_odd, two, one)
    spare = field.shape[0] - own - 4 * slab
    field[pl.ds(own + 4 * slab, spare), :] = jnp.zeros((spare, width), field.dtype)
    g_out[pl.ds(own + 2 * slab, spare + 2 * slab), :] = jnp.ones((spare + 2 * slab, width), field.dtype)

    def begin(k):
        if k < 0:
            return own + (2 if k < -1 else 0) * slab
        return own + (1 + 2 * (k - depth)) * slab if k >= depth else k * slab

    plane = lambda k: field[pl.ds(begin(k), slab), :]

    def g_rows(k):
        here, up, down = plane(k), plane(k + 1), plane(k - 1)
        if k == 0:
            down = jnp.where(z_begin, here, down)
        if k == depth - 1:
            up = jnp.where(z_end, here, up)
        row = lambda r: field[pl.ds(begin(k) + r, 1), :]
        first, final = row(0), row(height - 1)
        after = jnp.where(rows == height - 1, jnp.where(y_end, final, row(height + 1)), pltpu.roll(here, slab - 1, 0))
        after = jnp.where(rows == height, first, jnp.where(rows == height + 1, row(height + 3), after))
        before = jnp.where(rows == 0, jnp.where(y_begin, first, row(height)), pltpu.roll(here, 1, 0))
        before = jnp.where(rows == height, row(height + 2), jnp.where(rows == height + 1, final, before))
        g = diffusivity(up, down, after, before, *x_sides(here))
        g_out[pl.ds(begin(k), slab), :] = g
        return g

    chain(g_rows, plane, depth, solved, head, tail, element)
    g_own = lambda k: g_out[pl.ds(k * slab, slab), :]
    w_low[...] = HALF_LINK * (g_own(0) + g_rows(-1))
    link = HALF_LINK * (g_own(depth - 1) + g_rows(depth))
    w_high[...] = link
    element[2] = element[2] + 1.0 / link


def z_kernel(depth, height, field, near, far, low, high, g_out, solved, head, tail, element):
    plane = lambda k: field[pl.ds(k * height, height), :]
    z_begin, z_end = ends("gz")
    y_begin, y_end = ends("xy")
    below = jnp.where(z_begin, plane(0), low[...])
    above = jnp.where(z_end, plane(depth - 1), high[...])
    rows = lax.broadcasted_iota(jnp.int32, (height, field.shape[1]), 0)

    def g_rows(k):
        here = plane(k)
        up, down = plane(k + 1) if k < depth - 1 else above, plane(k - 1) if k else below
        first = jnp.where(y_begin, here[:1], near[pl.ds(k, 1), :])
        final = jnp.where(y_end, here[height - 1 :], far[pl.ds(k, 1), :])
        after = jnp.where(rows == height - 1, final, pltpu.roll(here, height - 1, 0))
        before = jnp.where(rows == 0, first, pltpu.roll(here, 1, 0))
        g = diffusivity(up, down, after, before, *x_sides(here))
        g_out[pl.ds(k * height, height), :] = g
        return g

    chain(g_rows, plane, depth, solved, head, tail, element)


def y_kernel(planes, height, slab, g_field, field, solved, head, tail, element):
    g_rows = lambda k: g_field[pl.ds(k, planes, stride=slab), :]
    v_rows = lambda k: field[pl.ds(k, planes, stride=slab), :]
    chain(g_rows, v_rows, height, solved, head, tail, element)


def x_kernel(first, rows, g_field, field, solved):
    width = field.shape[1]
    at = pl.ds(first, rows)
    g, right = g_field[at, :], field[at, :]
    lanes = lax.broadcasted_iota(jnp.int32, (rows, width), 1)
    link = jnp.where(lanes == width - 1, 0.0, HALF_LINK * (g + pltpu.roll(g, width - 1, 1)))
    main = 1.0 + link + pltpu.roll(link, 1, 1)
    stride = 1
    while stride < width:
        inverse = 1.0 / main
        factor = link * inverse
        back = width - stride
        ahead = link * pltpu.roll(inverse, back, 1)
        main = main - pltpu.roll(link * factor, stride, 1) - link * ahead
        right = right + pltpu.roll(factor * right, stride, 1) + ahead * pltpu.roll(right, back, 1)
        link = ahead * pltpu.roll(link, back, 1)
        stride *= 2
    solved[pl.ds(0, rows), :] = right / main


def sides(upper, own, got, last):
    pick = lambda a, b: jnp.where(upper, a, b)
    if not last:
        return [pick(g, o) for o, g in zip(own, got)], [pick(o, g) for o, g in zip(own, got)]
    zero = jnp.zeros_like(own[0])
    lower = [None, zero, pick(got[0], own[2]), None, pick(got[1], own[4])]
    higher = [pick(own[0], got[0]), zero, None, pick(own[3], got[1]), None]
    if len(own) > 5:
        lower += [None, pick(got[2], own[6])]
        higher += [pick(own[5], got[2]), None]
    return lower, higher


def join(lower, higher):
    if len(lower) == 5:
        return 1.0 / (lower[2] + higher[0]), None
    link = HALF_LINK * (lower[6] + higher[5])
    inverse = 1.0 / (1.0 + link * (lower[2] + higher[0]))
    return link * inverse, inverse


def is_upper(axis, level):
    return lax.rem(lax.div(lax.axis_index(axis), 1 << level), 2) == 1


def parts(ref, rows):
    if len(ref.shape) == 3:
        return [ref[k] for k in range(ref.shape[0])]
    return [ref[pl.ds(k * rows, rows), :] for k in range(ref.shape[0] // rows)]


def merge_kernel(axis, level, own, got, *outs):
    upper = is_upper(axis, level)
    size, rows = own.shape[:2]
    lower, higher = sides(upper, parts(own, rows), parts(got, rows), False)
    share, _ = join(lower, higher)
    gap = lower[4] - higher[3]
    first, second = share * lower[1], share * higher[1]
    merged = [
        lower[0] - first * lower[1],
        first * higher[1],
        higher[2] - second * higher[1],
        lower[3] - first * gap,
        higher[4] + second * gap,
        *([lower[5], higher[6]] if size > 5 else []),
    ]
    for k in range(size):
        outs[0][k] = merged[k]
    if len(outs) > 1:
        above = is_upper(axis, level + 1)
        for k, (high, low) in enumerate(LAST_SENT[: (size - 1) // 2]):
            outs[1][pl.ds(k * rows, rows), :] = jnp.where(above, merged[high], merged[low])


def unwind(axis, refs):
    rows = refs[0].shape[1]
    pairs = [parts(ref, rows) for ref in refs]
    zero = jnp.zeros_like(pairs[0][0])
    from_low = from_high = jump_low = jump_high = zero
    for level in range(len(pairs) // 2 - 1, -1, -1):
        upper = is_upper(axis, level)
        lower, higher = sides(upper, *pairs[2 * level : 2 * level + 2], level == len(pairs) // 2 - 1)
        share, inverse = join(lower, higher)
        gap = lower[4] - higher[3] + lower[1] * from_low - higher[1] * from_high
        flow = share * gap
        if inverse is not None:
            jump = inverse * gap
            jump_low, jump_high = jnp.where(upper, jump, jump_low), jnp.where(upper, jump_high, jump)
        from_low, from_high = jnp.where(upper, flow, from_low), jnp.where(upper, from_high, -flow)
    return from_low, from_high, jump_low, jump_high


def wide_sum_kernel(cut, height, slab, *refs):
    count = refs[-1].shape[0] // (cut * slab)
    along_x, (solved, head, tail), total = refs[:count], refs[count : count + 3], refs[-1]
    low, high, jump_low, jump_high = unwind("xy", refs[count + 3 : -1])

    def put(row, along_y):
        for k, piece in enumerate(along_x):
            at = pl.ds(k * cut * slab + row, cut, stride=slab)
            total[at, :] = piece[pl.ds(row, cut, stride=slab), :] + along_y[k * cut : (k + 1) * cut]

    for k in range(height):
        along_y = solved[k] + low * head[k] + high * tail[k]
        put(k, along_y)
        if k == 0:
            put(height, along_y + jump_low)
        if k == height - 1:
            put(height + 1, along_y - jump_high)


def sum_kernel(cut, height, *refs):
    count = refs[-1].shape[0] // (cut * height)
    along_x, (solved, head, tail), total = refs[:count], refs[count : count + 3], refs[-1]
    low, high, _, _ = unwind("xy", refs[count + 3 : -1])
    for row in range(height):
        along_y = solved[row] + low * head[row] + high * tail[row]
        for k, piece in enumerate(along_x):
            at = pl.ds(k * cut * height + row, cut, stride=height)
            total[at, :] = piece[pl.ds(row, cut, stride=height), :] + along_y[k * cut : (k + 1) * cut]


def step_kernel(depth, height, total, solved, head, tail, w_low, w_high, *refs):
    field, near, far, below, above = refs[-5:]
    slab = height + GHOSTS
    low, high, _, _ = unwind("gz", refs[:-5])
    for k in range(depth):
        along_z = solved[k] + low * head[k] + high * tail[k]
        value = (total[pl.ds(k * slab, slab), :] + along_z) * THIRD
        field[pl.ds(k * height, height), :] = value[:height]
        near[pl.ds(k, 1), :] = value[height : height + 1]
        far[pl.ds(k, 1), :] = value[height + 1 : height + 2]
        if k == 0:
            along_z = along_z + low / w_low[...]
            below[...] = (total[pl.ds(depth * slab, height), :] + along_z[:height]) * THIRD
        if k == depth - 1:
            along_z = solved[k] + low * head[k] + high * tail[k] + high / w_high[...]
            above[...] = (total[pl.ds((depth + 1) * slab, height), :] + along_z[:height]) * THIRD


def last_kernel(depth, height, total, solved, head, tail, slots, *refs):
    chunks = refs[-len(CHUNKS) :]
    low, high, _, _ = unwind("gz", refs[: -len(CHUNKS)])
    planes = BLOCK_ROWS // height
    for k in range(depth):
        value = (total[pl.ds(k * height, height), :] + (solved[k] + low * head[k] + high * tail[k])) * THIRD
        block, row, chunk = k // planes, (k % planes) * height, 0
        while row >= CHUNKS[chunk]:
            row, chunk = row - CHUNKS[chunk], chunk + 1
        chunks[chunk][pl.ds(block * CHUNKS[chunk] + row, height), :] = value
    chunks[0][pl.ds(depth // planes * CHUNKS[0], slots.shape[0]), :] = slots[...]


def pack_kernel(ways, number, sizes, *refs):
    pieces, outs = refs[: len(sizes)], refs[-ways:]
    slots, begin = (refs[0], number * sizes[0]) if len(refs) == len(sizes) + ways else (refs[len(sizes)], 0)
    me = lax.axis_index("gz")
    place = lax.rem(me, ways)
    placed = [jnp.max(slots[pl.ds(begin + block, 1), :]).astype(jnp.int32) for block in range(number)]
    for out in outs:
        out[...] = jnp.zeros_like(out)
    for block, slot in enumerate(placed):
        rank, target = lax.rem(slot, MOST), lax.div(slot, MOST) - (me - place)
        for way, out in enumerate(outs):

            @pl.when(target == lax.bitwise_xor(place, way))
            def _():
                row = 0
                for size, piece in zip(sizes, pieces):
                    out[rank, pl.ds(row, size), :] = piece[pl.ds(block * size, size), :]
                    row += size


def pack(ways, number, pieces, sizes, slots):
    shape = (MOST, sum(sizes), pieces[0].shape[1])
    return call(functools.partial(pack_kernel, ways, number, sizes), [shape] * ways, [*pieces, *slots])


def place_kernel(plan, kept, fresh, *refs):
    count = len(plan) + len(kept)
    outs, sems = refs[count + (not fresh) : -1], refs[-1]
    me = lax.axis_index("gz")
    moves, row = [], 0
    for k, (way, begin) in enumerate(plan):
        source = lax.bitwise_xor(me, way)
        rows = refs[k].shape[1]
        moves.append((refs[k], outs[0].at[pl.ds(source * MOST, MOST), pl.ds(begin, rows), :]))
    for size, ref in zip(kept, refs[len(plan) : count]):
        for block in range(outs[1].shape[0]):
            moves.append((ref.at[pl.ds(block * size, size), :], outs[1].at[block, pl.ds(row, size), :]))
        row += size
    copies = [pltpu.make_async_copy(*move, sems.at[k]) for k, move in enumerate(moves)]
    for copy in copies:
        copy.start()
    for copy in copies:
        copy.wait()


def place(arrays, plan, incoming, shapes, kept=()):
    count = len(arrays) + len(kept)
    copies = len(arrays) + len(kept) * (shapes[1][0] if kept else 0)
    extra = [] if incoming is None else [incoming]
    return pl.pallas_call(
        functools.partial(place_kernel, plan, CHUNKS if kept else (), not extra),
        out_shape=[jax.ShapeDtypeStruct(shape, jnp.float32) for shape in shapes],
        in_specs=[pl.BlockSpec(memory_space=VMEM)] * count + [pl.BlockSpec(memory_space=pl.ANY)] * len(extra),
        out_specs=[pl.BlockSpec(memory_space=pl.ANY)] * len(shapes),
        scratch_shapes=[pltpu.SemaphoreType.DMA((copies,))],
        input_output_aliases={count: 0} if extra else {},
        compiler_params=pltpu.CompilerParams(vmem_limit_bytes=VMEM_LIMIT),
    )(*arrays, *kept, *extra)


def swap(values, axis, stride):
    count = lax.axis_size(axis)
    return lax.ppermute(values, axis, [(i, i ^ stride) for i in range(count)])


def near(first, axis):
    return swap(first, axis, 1)


def far(second, axis):
    count = lax.axis_size(axis)
    if axis == "xy":
        other = [(i, (i + 1) % count) for i in range(1, count, 2)]
        return lax.ppermute(second, axis, other + [(j, i) for i, j in other])
    beside = lax.axis_size("xy")
    pairs = []
    for i in range(count):
        end = i in (0, count - 1)
        j = i if end else i + 1 if i % 2 else i - 1
        pairs += [(i * beside + c, j * beside + (c ^ 1 if end else c)) for c in range(beside)]
    return lax.ppermute(second, (axis, "xy"), pairs)


def neighbours(first, second, axis):
    got = far(second, axis)
    return near(first, axis), got


def merge(element, got, axis, level, after=()):
    size, rows, width = element.shape
    outs = [element.shape] + [((size - 1) // 2 * rows, width)] * (4 << level >= lax.axis_size(axis))
    merged = call(functools.partial(merge_kernel, axis, level), outs, [element, got], after=after)
    return merged[0], merged[-1]


def route(chunks, slots, number):
    count, width = lax.axis_size("gz"), chunks[0].shape[1]
    ways = count // 2
    order = range(ways - 1, 0, -1)
    crossed = []
    for chunk in chunks:
        crossed.append(swap(chunk, "gz", ways))
    straight = pack(ways, number, chunks, CHUNKS, [slots])
    arrays = [straight[0]]
    for way in order:
        arrays.append(swap(straight[way], "gz", way))
    shapes = [(count * MOST, BLOCK_ROWS, width), (number, BLOCK_ROWS, width)]
    plan = [(way, 0) for way in (0, *order)]
    incoming, field = place(arrays, plan, None, shapes, chunks)
    row = 0
    for k, size in enumerate(CHUNKS):
        others = [] if k == 0 else [lax.slice_in_dim(crossed[0], number * CHUNKS[0], None, axis=0)]
        passed = pack(ways, number, crossed[k : k + 1], (size,), others)
        arrays = [passed[0]]
        for way in order:
            arrays.append(swap(passed[way], "gz", way))
        plan = [(way ^ ways, row) for way in (0, *order)]
        (incoming,) = place(arrays, plan, incoming, shapes[:1])
        row += size
    return field, incoming


def lines(field, g_field, z_element, planes, height, slab, used, sum_body):
    width = field.shape[1]
    part = functools.partial
    z_rounds, y_rounds = (lax.axis_size(axis).bit_length() - 1 for axis in ("gz", "xy"))
    y_shape = (height, planes, width)
    *y_pieces, y_element = call(
        part(y_kernel, planes, height, slab),
        [y_shape, y_shape, y_shape, (7, planes, width)],
        [g_field, field],
        after=[z_element],
    )
    y_start, y_sent, y_pairs = y_element, y_element, []
    for level in range(y_rounds):
        y_pairs += [y_element, swap(y_sent, "xy", 1 << level)]
        if level + 1 < y_rounds:
            y_element, y_sent = merge(*y_pairs[-2:], "xy", level)
    cut, along_x = 8, []

    def x_part(after):
        k = len(along_x)
        rows = min(cut, used - k * cut) * slab
        along_x.extend(call(part(x_kernel, k * cut * slab, rows), [(cut * slab, width)], [g_field, field], after=after))

    z_sent, z_pairs = z_element, []
    for level in range(z_rounds):
        z_pairs += [z_element, swap(z_sent, "gz", 1 << level)]
        behind = []
        if level == 0:
            x_part([y_start])
            behind = [along_x[0], y_element]
        if level == 1:
            x_part([z_element])
            behind = [along_x[1]]
        if level == 2:
            while len(along_x) * cut < planes:
                x_part([z_element])
            (total,) = call(part(sum_body, cut), [(planes * slab, width)], [*along_x, *y_pieces, *y_pairs])
        if level + 1 < z_rounds:
            z_element, z_sent = merge(*z_pairs[-2:], "gz", level, behind)
    return total, z_pairs


def on_device(volume, owners):
    depth, height, width = volume.shape
    slab = height + GHOSTS
    planes = -(-(depth + 4) // 8) * 8
    blocks = owners.shape[1]
    part = functools.partial
    flat, plane, side = (depth * height, width), (height, width), (depth, width)

    field = volume.reshape(flat)
    edges = call(part(edge_kernel, depth, height), [(2 * depth, width)] * 2, [field])
    y_sides = neighbours(*edges, "xy")
    slabs, *edges = call(
        part(slab_kernel, depth, height), [(depth * slab, width)] + [(2 * slab, width)] * 2, [field, *y_sides]
    )
    z_sides = neighbours(*edges, "gz")
    slots = slots_of(owners, width, edges[0])
    field, g_field, *z_pieces, z_element, w_low, w_high = call(
        part(wide_kernel, depth, height),
        [(planes * slab, width)] * 2 + [(depth, slab, width)] * 3 + [(5, slab, width)] + [(slab, width)] * 2,
        [slabs, *z_sides],
        after=[slots],
    )
    total, z_pairs = lines(
        field, g_field, z_element, planes, height, slab, depth + 2, lambda cut, *refs: wide_sum_kernel(cut, height, slab, *refs)
    )
    field, *around = call(
        part(step_kernel, depth, height), [flat, side, side, plane, plane], [total, *z_pieces, w_low, w_high, *z_pairs]
    )
    g_field, *z_pieces, z_element = call(
        part(z_kernel, depth, height), [flat] + [(depth, height, width)] * 3 + [(7, height, width)], [field, *around]
    )
    total, z_pairs = lines(
        field, g_field, z_element, depth, height, height, depth, lambda cut, *refs: sum_kernel(cut, height, *refs)
    )
    rows = slots.shape[0]
    chunks = call(
        part(last_kernel, depth, height),
        [(blocks * size + rows * (k == 0), width) for k, size in enumerate(CHUNKS)],
        [total, *z_pieces, slots, *z_pairs],
    )
    field, incoming = route(chunks, slots, blocks)
    return field.reshape(volume.shape), incoming[None]


def solution(mesh):
    in_specs = (P("gz", "xy", None), P("xy", "gz", None))
    out_specs = (P("gz", "xy", None), P("xy", "gz", None, None))

    return jax.shard_map(on_device, mesh=mesh, in_specs=in_specs, out_specs=out_specs, check_vma=False)
```

time: 71.7 us -> 67.2 us (0.937)
  starting transfers between devices: 37.4 us -> 31.2 us
  waiting for transfers between devices: 20.3 us -> 21.5 us
    ppermute x25 -> x19, starting transfers between devices: 34.1 us -> 28.5 us  [swap(): return lax.ppermute(values, axis, [(i, i ^ stride) for i in range(count)])]
    ppermute x25 -> x19, waiting for transfers between devices: 19 us -> 20.1 us  [swap(): return lax.ppermute(values, axis, [(i, i ^ stride) for i in range(count)])]
    ppermute x2 -> x1, starting transfers between devices: 2.78 us -> 2.59 us  [far(): return lax.ppermute(second, axis, other + [(j, i) for i, j in other])]
    ppermute x2 -> x1, waiting for transfers between devices: 1.33 us -> 1.44 us  [far(): return lax.ppermute(second, axis, other + [(j, i) for i, j in other])]
  transfers between devices with their start and end apart: 29 -> 21, of which waited for: 14 -> 11; matrix products, arithmetic and copies ran while one was open for 0% -> 0% of each run, Pallas kernels for 14% -> 15%
where the time goes in v5:
time: 67.2 us; the launch traced here: 67 us
  starting transfers between devices  31.2 us (46%)
  waiting for transfers between devices  21.5 us (32%)
  Pallas kernels  12.5 us (19%)
  local copies, waits for them, and re-layouts  0.95 us (1%)
  between operations  0.86 us (1%)
    ppermute x19, starting transfers between devices, swap(): return lax.ppermute(values, axis, [(i, i ^ stride) for i in range(count)])  28.5 us
    ppermute x19, waiting for transfers between devices, swap(): return lax.ppermute(values, axis, [(i, i ^ stride) for i in range(count)])  20.1 us
    pallas_call x23, Pallas kernels, call(): pl.pallas_call(lambda *refs: body(*refs[:count], *refs[count + len(after)...  10.2 us
    ppermute x1, starting transfers between devices, far(): return lax.ppermute(second, axis, other + [(j, i) for i, j in other])  2.59 us
    pallas_call x2, Pallas kernels, place(): pl.pallas_call(functools.partial(place_kernel, plan, CHUNKS if kept else...  1.75 us
    ppermute x1, waiting for transfers between devices, far(): return lax.ppermute(second, axis, other + [(j, i) for i, j in other])  1.44 us
  transfers between devices with their start and end apart: 21, of which 11 were waited for; matrix products, arithmetic and copies ran while one was open for 0% of the time, Pallas kernels for 15%

profile of v5, /device:TPU:0, one launch (start us, length us, event | category | flops | bytes accessed | tf_op | source)
XLA Modules:
  0.0 67.0 jit_solution(17887636424284092852)
XLA Ops:
  0.6 0.9 %copy-done = f32[16,32,128]{2,1,0:T(8,128)S(1)} copy-done((f32[16,32,128]{2,1,0:T(8,128)S(1)}, f32[16,32,128]{2,1,0:T(8,128)}, u32[]{:S(2)}) %copy-start) | copy-done | bytes 262168
  1.6 0.6 collective-permute-start
  2.2 2.6 %collective-permute-start.1 = (f32[32,128]{1,0:T(8,128)S(1)}, f32[32,128]{1,0:T(8,128)S(1)}, u32[]{:S(2)}, u32[]{:S(2)}) collective-permute-start(f32[32,128]{1,0:T(8,128)S(1)} %get-tuple-element.52), channel_id=1, source_target_pairs={{1,2},{3,0},{2,1},{0,3},{5,6},{7,4},{6,5},{4,7},{9,10},{11,8},{10,... | collective-permute-start | bytes 49160 | tf_op jit(solution)/shard_map/ppermute | solution.py:452
  4.8 1.4 %collective-permute-done.1.refs_2_ = f32[32,128]{1,0:T(8,128)S(1)} collective-permute-done((f32[32,128]{1,0:T(8,128)S(1)}, f32[32,128]{1,0:T(8,128)S(1)}, u32[]{:S(2)}, u32[]{:S(2)}) %collective-permute-start.1) | collective-permute-done | bytes 16416 | tf_op jit(solution)/shard_map/ppermute | solution.py:452
  6.2 0.2 collective-permute-start.3
  6.4 3.1 %collective-permute-start.2 = (f32[80,128]{1,0:T(8,128)S(1)}, f32[80,128]{1,0:T(8,128)S(1)}, u32[]{:S(2)}, u32[]{:S(2)}) collective-permute-start(f32[80,128]{1,0:T(8,128)S(1)} %get-tuple-element.54.first), channel_id=1, source_target_pairs={{0,4},{4,0},{8,12},{12,8},{16,20},{20,16},{24,28},{28,24},{1,5},{5... | collective-permute-start | bytes 122888 | tf_op jit(solution)/shard_map/ppermute | solution.py:441
  9.5 0.6 slots.1.refs_3_.refs_4_.refs_1_
  10.1 1.4 %collective-permute-done.2.refs_1_ = f32[80,128]{1,0:T(8,128)S(1)} collective-permute-done((f32[80,128]{1,0:T(8,128)S(1)}, f32[80,128]{1,0:T(8,128)S(1)}, u32[]{:S(2)}, u32[]{:S(2)}) %collective-permute-start.2) | collective-permute-done | bytes 40992 | tf_op jit(solution)/shard_map/ppermute | solution.py:441
  11.5 0.5 shard_map.43
  12.1 2.2 %collective-permute-start.4 = (f32[5,40,128]{2,1,0:T(8,128)S(1)}, f32[5,40,128]{2,1,0:T(8,128)S(1)}, u32[]{:S(2)}, u32[]{:S(2)}) collective-permute-start(f32[5,40,128]{2,1,0:T(8,128)S(1)} %get-tuple-element.58.refs_2_.refs_0_.refs_6_), channel_id=1, source_target_pairs={{0,4},{4,0},{8,12},{12,8},{16,20},{20,16},{24,28},{28,24},{1,5},{5... | collective-permute-start | bytes 307208 | tf_op jit(solution)/shard_map/ppermute | solution.py:441
  14.3 0.4 shard_map.44
  14.7 0.1 collective-permute-start.5
  14.8 1.6 %shard_map.45.refs_2_.refs_0_ = f32[320,128]{1,0:T(8,128)S(1)} custom-call(f32[960,128]{1,0:T(8,128)S(1)} %get-tuple-element.56.refs_0_, f32[960,128]{1,0:T(8,128)S(1)} %get-tuple-element.57.refs_1_, f32[7,24,128]{2,1,0:T(8,128)S(1)} %get-tuple-element.59.refs_2_.refs_0_.refs_6_), custom_call_target="tpu_custom_call" | custom-call | tf_op jit(solution)/shard_map/pallas_call | solution.py:27
  16.5 0.7 %collective-permute-done.4.refs_1_.refs_7_ = f32[5,40,128]{2,1,0:T(8,128)S(1)} collective-permute-done((f32[5,40,128]{2,1,0:T(8,128)S(1)}, f32[5,40,128]{2,1,0:T(8,128)S(1)}, u32[]{:S(2)}, u32[]{:S(2)}) %collective-permute-start.4) | collective-permute-done | bytes 102432 | tf_op jit(solution)/shard_map/ppermute | solution.py:441
  17.2 2.0 %collective-permute-start.6 = (f32[5,40,128]{2,1,0:T(8,128)S(1)}, f32[5,40,128]{2,1,0:T(8,128)S(1)}, u32[]{:S(2)}, u32[]{:S(2)}) collective-permute-start(f32[5,40,128]{2,1,0:T(8,128)S(1)} %shard_map.47.refs_2_.refs_0_.refs_8_), channel_id=1, source_target_pairs={{0,8},{4,12},{8,0},{12,4},{16,24},{20,28},{24,16},{28,20},{1,9},{5... | collective-permute-start | bytes 307208 | tf_op jit(solution)/shard_map/ppermute | solution.py:441
  19.2 1.6 %shard_map.48.refs_2_.refs_1_ = f32[320,128]{1,0:T(8,128)S(1)} custom-call(f32[960,128]{1,0:T(8,128)S(1)} %get-tuple-element.56.refs_0_, f32[960,128]{1,0:T(8,128)S(1)} %get-tuple-element.57.refs_1_, f32[5,40,128]{2,1,0:T(8,128)S(1)} %shard_map.47.refs_2_.refs_0_.refs_8_), custom_call_target="tpu_custom_call" | custom-call | tf_op jit(solution)/shard_map/pallas_call | solution.py:27
  20.8 1.1 %collective-permute-done.6.refs_1_.refs_9_ = f32[5,40,128]{2,1,0:T(8,128)S(1)} collective-permute-done((f32[5,40,128]{2,1,0:T(8,128)S(1)}, f32[5,40,128]{2,1,0:T(8,128)S(1)}, u32[]{:S(2)}, u32[]{:S(2)}) %collective-permute-start.6) | collective-permute-done | bytes 102432 | tf_op jit(solution)/shard_map/ppermute | solution.py:441
  22.0 3.0 %collective-permute-start.8 = (f32[80,128]{1,0:T(8,128)S(1)}, f32[80,128]{1,0:T(8,128)S(1)}, u32[]{:S(2)}, u32[]{:S(2)}) collective-permute-start(f32[80,128]{1,0:T(8,128)S(1)} %get-tuple-element.71), channel_id=1, source_target_pairs={{0,16},{4,20},{8,24},{12,28},{16,0},{20,4},{24,8},{28,12},{1,17},{... | collective-permute-start | bytes 122888 | tf_op jit(solution)/shard_map/ppermute | solution.py:441
  25.0 1.5 %collective-permute-start.7 = (f32[72,128]{1,0:T(8,128)S(1)}, f32[72,128]{1,0:T(8,128)S(1)}, u32[]{:S(2)}, u32[]{:S(2)}) collective-permute-start(f32[72,128]{1,0:T(8,128)S(1)} %get-tuple-element.65), channel_id=1, source_target_pairs={{0,2},{1,3},{2,0},{3,1},{4,6},{5,7},{6,4},{7,5},{8,10},{9,11},{10,... | collective-permute-start | bytes 110600 | tf_op jit(solution)/shard_map/ppermute | solution.py:441
  26.4 0.9 %shard_map.50.refs_2_ = f32[320,128]{1,0:T(8,128)S(1)} custom-call(f32[960,128]{1,0:T(8,128)S(1)} %get-tuple-element.56.refs_0_, f32[960,128]{1,0:T(8,128)S(1)} %get-tuple-element.57.refs_1_, f32[5,40,128]{2,1,0:T(8,128)S(1)} %get-tuple-element.61.refs_2_.refs_10_), custom_call_target="tpu_custom_call" | custom-call | tf_op jit(solution)/shard_map/pallas_call | solution.py:27
  27.3 1.6 %collective-permute-done.7.refs_9_ = f32[72,128]{1,0:T(8,128)S(1)} collective-permute-done((f32[72,128]{1,0:T(8,128)S(1)}, f32[72,128]{1,0:T(8,128)S(1)}, u32[]{:S(2)}, u32[]{:S(2)}) %collective-permute-start.7) | collective-permute-done | bytes 36896 | tf_op jit(solution)/shard_map/ppermute | solution.py:441
  28.9 0.2 shard_map.51.refs_0_
  29.1 0.1 shard_map.52
  29.3 0.4 shard_map.53
  29.7 1.5 %collective-permute-start.9 = (f32[7,32,128]{2,1,0:T(8,128)S(1)}, f32[7,32,128]{2,1,0:T(8,128)S(1)}, u32[]{:S(2)}, u32[]{:S(2)}) collective-permute-start(f32[7,32,128]{2,1,0:T(8,128)S(1)} %get-tuple-element.78.refs_2_.refs_0_.refs_5_), channel_id=1, source_target_pairs={{0,4},{4,0},{8,12},{12,8},{16,20},{20,16},{24,28},{28,24},{1,5},{5... | collective-permute-start | bytes 344072 | tf_op jit(solution)/shard_map/ppermute | solution.py:441
  31.2 0.4 shard_map.54
  31.7 1.4 %shard_map.55.refs_2_.refs_0_ = f32[256,128]{1,0:T(8,128)S(1)} custom-call(f32[512,128]{1,0:T(8,128)S(1)} %get-tuple-element.77.refs_0_, f32[512,128]{1,0:T(8,128)S(1)} %get-tuple-element.72.refs_0_.refs_1_, f32[7,16,128]{2,1,0:T(8,128)S(1)} %get-tuple-element.79.refs_2_.refs_0_.refs_5_), custom_call_target="tpu_custom_call" | custom-call | tf_op jit(solution)/shard_map/pallas_call | solution.py:27
  33.1 1.4 %collective-permute-done.9.refs_1_.refs_6_ = f32[7,32,128]{2,1,0:T(8,128)S(1)} collective-permute-done((f32[7,32,128]{2,1,0:T(8,128)S(1)}, f32[7,32,128]{2,1,0:T(8,128)S(1)}, u32[]{:S(2)}, u32[]{:S(2)}) %collective-permute-start.9) | collective-permute-done | bytes 114720 | tf_op jit(solution)/shard_map/ppermute | solution.py:441
  34.6 1.6 %collective-permute-start.12 = (f32[7,32,128]{2,1,0:T(8,128)S(1)}, f32[7,32,128]{2,1,0:T(8,128)S(1)}, u32[]{:S(2)}, u32[]{:S(2)}) collective-permute-start(f32[7,32,128]{2,1,0:T(8,128)S(1)} %shard_map.57.refs_2_.refs_0_.refs_7_), channel_id=1, source_target_pairs={{0,8},{4,12},{8,0},{12,4},{16,24},{20,28},{24,16},{28,20},{1,9},{5... | collective-permute-start | bytes 344072 | tf_op jit(solution)/shard_map/ppermute | solution.py:441
  36.2 1.4 %shard_map.58.refs_1_.refs_2_ = f32[256,128]{1,0:T(8,128)S(1)} custom-call(f32[512,128]{1,0:T(8,128)S(1)} %get-tuple-element.77.refs_0_, f32[512,128]{1,0:T(8,128)S(1)} %get-tuple-element.72.refs_0_.refs_1_, f32[7,32,128]{2,1,0:T(8,128)S(1)} %shard_map.57.refs_2_.refs_0_.refs_7_), custom_call_target="tpu_custom_call" | custom-call | tf_op jit(solution)/shard_map/pallas_call | solution.py:27
  37.6 1.8 %collective-permute-done.12.refs_1_.refs_8_ = f32[7,32,128]{2,1,0:T(8,128)S(1)} collective-permute-done((f32[7,32,128]{2,1,0:T(8,128)S(1)}, f32[7,32,128]{2,1,0:T(8,128)S(1)}, u32[]{:S(2)}, u32[]{:S(2)}) %collective-permute-start.12) | collective-permute-done | bytes 114720 | tf_op jit(solution)/shard_map/ppermute | solution.py:441
  39.5 0.8 %collective-permute-start.13 = (f32[96,128]{1,0:T(8,128)S(1)}, f32[96,128]{1,0:T(8,128)S(1)}, u32[]{:S(2)}, u32[]{:S(2)}) collective-permute-start(f32[96,128]{1,0:T(8,128)S(1)} %get-tuple-element.89), channel_id=1, source_target_pairs={{0,16},{4,20},{8,24},{12,28},{16,0},{20,4},{24,8},{28,12},{1,17},{... | collective-permute-start | bytes 147464 | tf_op jit(solution)/shard_map/ppermute | solution.py:441
  40.3 1.5 %collective-permute-start.11 = (f32[48,128]{1,0:T(8,128)S(1)}, f32[48,128]{1,0:T(8,128)S(1)}, u32[]{:S(2)}, u32[]{:S(2)}) collective-permute-start(f32[48,128]{1,0:T(8,128)S(1)} %get-tuple-element.84), channel_id=1, source_target_pairs={{0,2},{1,3},{2,0},{3,1},{4,6},{5,7},{6,4},{7,5},{8,10},{9,11},{10,... | collective-permute-start | bytes 73736 | tf_op jit(solution)/shard_map/ppermute | solution.py:441
  41.8 2.3 %collective-permute-done.11.refs_8_ = f32[48,128]{1,0:T(8,128)S(1)} collective-permute-done((f32[48,128]{1,0:T(8,128)S(1)}, f32[48,128]{1,0:T(8,128)S(1)}, u32[]{:S(2)}, u32[]{:S(2)}) %collective-permute-start.11) | collective-permute-done | bytes 24608 | tf_op jit(solution)/shard_map/ppermute | solution.py:441
  44.1 0.4 shard_map.59.refs_0_
  44.6 0.1 shard_map.61.refs_0_.refs_4_
  44.7 2.2 %collective-permute-start.17 = (f32[520,128]{1,0:T(8,128)S(1)}, f32[520,128]{1,0:T(8,128)S(1)}, u32[]{:S(2)}, u32[]{:S(2)}) collective-permute-start(f32[520,128]{1,0:T(8,128)S(1)} %shard_map.61.refs_0_.refs_4_), channel_id=1, source_target_pairs={{0,16},{4,20},{8,24},{12,28},{16,0},{20,4},{24,8},{28,12},{1,17},{... | collective-permute-start | bytes 798728 | tf_op jit(solution)/shard_map/ppermute | solution.py:441
  46.9 0.2 shard_map.62
  47.1 1.4 %collective-permute-start.14 = (f32[2,128,128]{2,1,0:T(8,128)S(1)}, f32[2,128,128]{2,1,0:T(8,128)S(1)}, u32[]{:S(2)}, u32[]{:S(2)}) collective-permute-start(f32[2,128,128]{2,1,0:T(8,128)S(1)} %get-tuple-element.91), channel_id=1, source_target_pairs={{0,12},{4,8},{8,4},{12,0},{16,28},{20,24},{24,20},{28,16},{1,13},{... | collective-permute-start | bytes 393224 | tf_op jit(solution)/shard_map/ppermute | solution.py:441
  48.5 3.3 %collective-permute-start.15 = (f32[2,128,128]{2,1,0:T(8,128)S(1)}, f32[2,128,128]{2,1,0:T(8,128)S(1)}, u32[]{:S(2)}, u32[]{:S(2)}) collective-permute-start(f32[2,128,128]{2,1,0:T(8,128)S(1)} %get-tuple-element.92), channel_id=1, source_target_pairs={{0,8},{4,12},{8,0},{12,4},{16,24},{20,28},{24,16},{28,20},{1,9},{5... | collective-permute-start | bytes 393224 | tf_op jit(solution)/shard_map/ppermute | solution.py:441
  51.8 5.5 %collective-permute-done.17.refs_0_ = f32[520,128]{1,0:T(8,128)S(1)} collective-permute-done((f32[520,128]{1,0:T(8,128)S(1)}, f32[520,128]{1,0:T(8,128)S(1)}, u32[]{:S(2)}, u32[]{:S(2)}) %collective-permute-start.17) | collective-permute-done | bytes 266272 | tf_op jit(solution)/shard_map/ppermute | solution.py:441
  57.3 0.2 shard_map.64
  57.6 2.3 %collective-permute-start.19 = (f32[2,128,128]{2,1,0:T(8,128)S(1)}, f32[2,128,128]{2,1,0:T(8,128)S(1)}, u32[]{:S(2)}, u32[]{:S(2)}) collective-permute-start(f32[2,128,128]{2,1,0:T(8,128)S(1)} %get-tuple-element.97), channel_id=1, source_target_pairs={{0,8},{4,12},{8,0},{12,4},{16,24},{20,28},{24,16},{28,20},{1,9},{5... | collective-permute-start | bytes 393224 | tf_op jit(solution)/shard_map/ppermute | solution.py:441
  59.9 1.2 %collective-permute-start.20 = (f32[2,128,128]{2,1,0:T(8,128)S(1)}, f32[2,128,128]{2,1,0:T(8,128)S(1)}, u32[]{:S(2)}, u32[]{:S(2)}) collective-permute-start(f32[2,128,128]{2,1,0:T(8,128)S(1)} %get-tuple-element.98), channel_id=1, source_target_pairs={{0,4},{4,0},{8,12},{12,8},{16,20},{20,16},{24,28},{28,24},{1,5},{5... | collective-permute-start | bytes 393224 | tf_op jit(solution)/shard_map/ppermute | solution.py:441
  61.1 0.9 %shard_map.63 = (f32[16,128,128]{2,1,0:T(8,128)}, f32[4,128,128]{2,1,0:T(8,128)}) custom-call(f32[2,128,128]{2,1,0:T(8,128)S(1)} %get-tuple-element.90.refs_0_, f32[2,128,128]{2,1,0:T(8,128)S(1)} %collective-permute-done.14.refs_1_, f32[2,128,128]{2,1,0:T(8,128)S(1)} %collective-permute-done.15.refs_2_, f32[2,128,128]{2,1,0:T(8,128)S(1)} %collective-permute-done.16.refs_3_, ...), custom_call_target="tpu_custom_call" | custom-call | tf_op jit(solution)/shard_map/pallas_call | solution.py:428
  62.1 2.7 %collective-permute-done.18.refs_1_ = f32[2,128,128]{2,1,0:T(8,128)S(1)} collective-permute-done((f32[2,128,128]{2,1,0:T(8,128)S(1)}, f32[2,128,128]{2,1,0:T(8,128)S(1)}, u32[]{:S(2)}, u32[]{:S(2)}) %collective-permute-start.18) | collective-permute-done | bytes 131104 | tf_op jit(solution)/shard_map/ppermute | solution.py:441
  64.8 1.4 %collective-permute-done.20.refs_3_ = f32[2,128,128]{2,1,0:T(8,128)S(1)} collective-permute-done((f32[2,128,128]{2,1,0:T(8,128)S(1)}, f32[2,128,128]{2,1,0:T(8,128)S(1)}, u32[]{:S(2)}, u32[]{:S(2)}) %collective-permute-start.20) | collective-permute-done | bytes 131104 | tf_op jit(solution)/shard_map/ppermute | solution.py:441
  66.2 0.8 %shard_map.65 = f32[16,128,128]{2,1,0:T(8,128)} custom-call(f32[2,128,128]{2,1,0:T(8,128)S(1)} %get-tuple-element.95.refs_0_, f32[2,128,128]{2,1,0:T(8,128)S(1)} %collective-permute-done.18.refs_1_, f32[2,128,128]{2,1,0:T(8,128)S(1)} %collective-permute-done.19.refs_2_, ...), custom_call_target="tpu_custom_call", output_to_operand_aliasing={{}: (4, {})} | custom-call | tf_op jit(solution)/shard_map/pallas_call | solution.py:428
  (24 shorter events, 0.5 us)
Async XLA Ops:
  0.6 1.0 %copy-start = (f32[16,32,128]{2,1,0:T(8,128)S(1)}, f32[16,32,128]{2,1,0:T(8,128)}, u32[]{:S(2)}) copy-start(f32[16,32,128]{2,1,0:T(8,128)} %param.2) | copy-start | bytes 786436
  1.6 3.2 %collective-permute-start = (f32[32,128]{1,0:T(8,128)S(1)}, f32[32,128]{1,0:T(8,128)S(1)}, u32[]{:S(2)}, u32[]{:S(2)}) collective-permute-start(f32[32,128]{1,0:T(8,128)S(1)} %get-tuple-element.51), channel_id=1, source_target_pairs={{0,1},{1,0},{2,3},{3,2},{4,5},{5,4},{6,7},{7,6},{8,9},{9,8},{10,11... | collective-permute-start | bytes 49160 | tf_op jit(solution)/shard_map/ppermute | solution.py:441
  2.2 4.0 %collective-permute-start.1 = (f32[32,128]{1,0:T(8,128)S(1)}, f32[32,128]{1,0:T(8,128)S(1)}, u32[]{:S(2)}, u32[]{:S(2)}) collective-permute-start(f32[32,128]{1,0:T(8,128)S(1)} %get-tuple-element.52), channel_id=1, source_target_pairs={{1,2},{3,0},{2,1},{0,3},{5,6},{7,4},{6,5},{4,7},{9,10},{11,8},{10,... | collective-permute-start | bytes 49160 | tf_op jit(solution)/shard_map/ppermute | solution.py:452
  6.2 3.9 %collective-permute-start.3 = (f32[80,128]{1,0:T(8,128)S(1)}, f32[80,128]{1,0:T(8,128)S(1)}, u32[]{:S(2)}, u32[]{:S(2)}) collective-permute-start(f32[80,128]{1,0:T(8,128)S(1)} %get-tuple-element.55), channel_id=1, source_target_pairs={{0,1},{1,0},{2,3},{3,2},{4,8},{5,9},{6,10},{7,11},{8,4},{9,5},{10,... | collective-permute-start | bytes 122888 | tf_op jit(solution)/shard_map/ppermute | solution.py:459
  6.4 3.1 %copy-start.1 = (s32[1,4,1]{1,2,0:T(1,128)S(1)}, s32[1,4,1]{1,2,0:T(1,128)}, u32[]{:S(2)}) copy-start(s32[1,4,1]{1,2,0:T(1,128)} %param.3) | copy-start | bytes 52
  6.4 5.1 %collective-permute-start.2 = (f32[80,128]{1,0:T(8,128)S(1)}, f32[80,128]{1,0:T(8,128)S(1)}, u32[]{:S(2)}, u32[]{:S(2)}) collective-permute-start(f32[80,128]{1,0:T(8,128)S(1)} %get-tuple-element.54.first), channel_id=1, source_target_pairs={{0,4},{4,0},{8,12},{12,8},{16,20},{20,16},{24,28},{28,24},{1,5},{5... | collective-permute-start | bytes 122888 | tf_op jit(solution)/shard_map/ppermute | solution.py:441
  12.1 5.1 %collective-permute-start.4 = (f32[5,40,128]{2,1,0:T(8,128)S(1)}, f32[5,40,128]{2,1,0:T(8,128)S(1)}, u32[]{:S(2)}, u32[]{:S(2)}) collective-permute-start(f32[5,40,128]{2,1,0:T(8,128)S(1)} %get-tuple-element.58.refs_2_.refs_0_.refs_6_), channel_id=1, source_target_pairs={{0,4},{4,0},{8,12},{12,8},{16,20},{20,16},{24,28},{28,24},{1,5},{5... | collective-permute-start | bytes 307208 | tf_op jit(solution)/shard_map/ppermute | solution.py:441
  14.7 1.7 %collective-permute-start.5 = (f32[7,24,128]{2,1,0:T(8,128)S(1)}, f32[7,24,128]{2,1,0:T(8,128)S(1)}, u32[]{:S(2)}, u32[]{:S(2)}) collective-permute-start(f32[7,24,128]{2,1,0:T(8,128)S(1)} %get-tuple-element.59.refs_2_.refs_0_.refs_6_), channel_id=1, source_target_pairs={{0,1},{1,0},{2,3},{3,2},{4,5},{5,4},{6,7},{7,6},{8,9},{9,8},{10,11... | collective-permute-start | bytes 258056 | tf_op jit(solution)/shard_map/ppermute | solution.py:441
  17.2 4.7 %collective-permute-start.6 = (f32[5,40,128]{2,1,0:T(8,128)S(1)}, f32[5,40,128]{2,1,0:T(8,128)S(1)}, u32[]{:S(2)}, u32[]{:S(2)}) collective-permute-start(f32[5,40,128]{2,1,0:T(8,128)S(1)} %shard_map.47.refs_2_.refs_0_.refs_8_), channel_id=1, source_target_pairs={{0,8},{4,12},{8,0},{12,4},{16,24},{20,28},{24,16},{28,20},{1,9},{5... | collective-permute-start | bytes 307208 | tf_op jit(solution)/shard_map/ppermute | solution.py:441
  22.0 7.2 %collective-permute-start.8 = (f32[80,128]{1,0:T(8,128)S(1)}, f32[80,128]{1,0:T(8,128)S(1)}, u32[]{:S(2)}, u32[]{:S(2)}) collective-permute-start(f32[80,128]{1,0:T(8,128)S(1)} %get-tuple-element.71), channel_id=1, source_target_pairs={{0,16},{4,20},{8,24},{12,28},{16,0},{20,4},{24,8},{28,12},{1,17},{... | collective-permute-start | bytes 122888 | tf_op jit(solution)/shard_map/ppermute | solution.py:441
  25.0 4.0 %collective-permute-start.7 = (f32[72,128]{1,0:T(8,128)S(1)}, f32[72,128]{1,0:T(8,128)S(1)}, u32[]{:S(2)}, u32[]{:S(2)}) collective-permute-start(f32[72,128]{1,0:T(8,128)S(1)} %get-tuple-element.65), channel_id=1, source_target_pairs={{0,2},{1,3},{2,0},{3,1},{4,6},{5,7},{6,4},{7,5},{8,10},{9,11},{10,... | collective-permute-start | bytes 110600 | tf_op jit(solution)/shard_map/ppermute | solution.py:441
  29.7 4.9 %collective-permute-start.9 = (f32[7,32,128]{2,1,0:T(8,128)S(1)}, f32[7,32,128]{2,1,0:T(8,128)S(1)}, u32[]{:S(2)}, u32[]{:S(2)}) collective-permute-start(f32[7,32,128]{2,1,0:T(8,128)S(1)} %get-tuple-element.78.refs_2_.refs_0_.refs_5_), channel_id=1, source_target_pairs={{0,4},{4,0},{8,12},{12,8},{16,20},{20,16},{24,28},{28,24},{1,5},{5... | collective-permute-start | bytes 344072 | tf_op jit(solution)/shard_map/ppermute | solution.py:441
  31.6 1.5 %collective-permute-start.10 = (f32[7,16,128]{2,1,0:T(8,128)S(1)}, f32[7,16,128]{2,1,0:T(8,128)S(1)}, u32[]{:S(2)}, u32[]{:S(2)}) collective-permute-start(f32[7,16,128]{2,1,0:T(8,128)S(1)} %get-tuple-element.79.refs_2_.refs_0_.refs_5_), channel_id=1, source_target_pairs={{0,1},{1,0},{2,3},{3,2},{4,5},{5,4},{6,7},{7,6},{8,9},{9,8},{10,11... | collective-permute-start | bytes 172040 | tf_op jit(solution)/shard_map/ppermute | solution.py:441
  34.6 4.9 %collective-permute-start.12 = (f32[7,32,128]{2,1,0:T(8,128)S(1)}, f32[7,32,128]{2,1,0:T(8,128)S(1)}, u32[]{:S(2)}, u32[]{:S(2)}) collective-permute-start(f32[7,32,128]{2,1,0:T(8,128)S(1)} %shard_map.57.refs_2_.refs_0_.refs_7_), channel_id=1, source_target_pairs={{0,8},{4,12},{8,0},{12,4},{16,24},{20,28},{24,16},{28,20},{1,9},{5... | collective-permute-start | bytes 344072 | tf_op jit(solution)/shard_map/ppermute | solution.py:441
  39.5 5.1 %collective-permute-start.13 = (f32[96,128]{1,0:T(8,128)S(1)}, f32[96,128]{1,0:T(8,128)S(1)}, u32[]{:S(2)}, u32[]{:S(2)}) collective-permute-start(f32[96,128]{1,0:T(8,128)S(1)} %get-tuple-element.89), channel_id=1, source_target_pairs={{0,16},{4,20},{8,24},{12,28},{16,0},{20,4},{24,8},{28,12},{1,17},{... | collective-permute-start | bytes 147464 | tf_op jit(solution)/shard_map/ppermute | solution.py:441
  40.3 3.8 %collective-permute-start.11 = (f32[48,128]{1,0:T(8,128)S(1)}, f32[48,128]{1,0:T(8,128)S(1)}, u32[]{:S(2)}, u32[]{:S(2)}) collective-permute-start(f32[48,128]{1,0:T(8,128)S(1)} %get-tuple-element.84), channel_id=1, source_target_pairs={{0,2},{1,3},{2,0},{3,1},{4,6},{5,7},{6,4},{7,5},{8,10},{9,11},{10,... | collective-permute-start | bytes 73736 | tf_op jit(solution)/shard_map/ppermute | solution.py:441
  44.7 12.7 %collective-permute-start.17 = (f32[520,128]{1,0:T(8,128)S(1)}, f32[520,128]{1,0:T(8,128)S(1)}, u32[]{:S(2)}, u32[]{:S(2)}) collective-permute-start(f32[520,128]{1,0:T(8,128)S(1)} %shard_map.61.refs_0_.refs_4_), channel_id=1, source_target_pairs={{0,16},{4,20},{8,24},{12,28},{16,0},{20,4},{24,8},{28,12},{1,17},{... | collective-permute-start | bytes 798728 | tf_op jit(solution)/shard_map/ppermute | solution.py:441
  47.1 12.8 %collective-permute-start.14 = (f32[2,128,128]{2,1,0:T(8,128)S(1)}, f32[2,128,128]{2,1,0:T(8,128)S(1)}, u32[]{:S(2)}, u32[]{:S(2)}) collective-permute-start(f32[2,128,128]{2,1,0:T(8,128)S(1)} %get-tuple-element.91), channel_id=1, source_target_pairs={{0,12},{4,8},{8,4},{12,0},{16,28},{20,24},{24,20},{28,16},{1,13},{... | collective-permute-start | bytes 393224 | tf_op jit(solution)/shard_map/ppermute | solution.py:441
  48.5 12.6 %collective-permute-start.15 = (f32[2,128,128]{2,1,0:T(8,128)S(1)}, f32[2,128,128]{2,1,0:T(8,128)S(1)}, u32[]{:S(2)}, u32[]{:S(2)}) collective-permute-start(f32[2,128,128]{2,1,0:T(8,128)S(1)} %get-tuple-element.92), channel_id=1, source_target_pairs={{0,8},{4,12},{8,0},{12,4},{16,24},{20,28},{24,16},{28,20},{1,9},{5... | collective-permute-start | bytes 393224 | tf_op jit(solution)/shard_map/ppermute | solution.py:441
  51.8 9.3 %collective-permute-start.16 = (f32[2,128,128]{2,1,0:T(8,128)S(1)}, f32[2,128,128]{2,1,0:T(8,128)S(1)}, u32[]{:S(2)}, u32[]{:S(2)}) collective-permute-start(f32[2,128,128]{2,1,0:T(8,128)S(1)} %get-tuple-element.93), channel_id=1, source_target_pairs={{0,4},{4,0},{8,12},{12,8},{16,20},{20,16},{24,28},{28,24},{1,5},{5... | collective-permute-start | bytes 393224 | tf_op jit(solution)/shard_map/ppermute | solution.py:441
  57.6 7.2 %collective-permute-start.18 = (f32[2,128,128]{2,1,0:T(8,128)S(1)}, f32[2,128,128]{2,1,0:T(8,128)S(1)}, u32[]{:S(2)}, u32[]{:S(2)}) collective-permute-start(f32[2,128,128]{2,1,0:T(8,128)S(1)} %get-tuple-element.96), channel_id=1, source_target_pairs={{0,12},{4,8},{8,4},{12,0},{16,28},{20,24},{24,20},{28,16},{1,13},{... | collective-permute-start | bytes 393224 | tf_op jit(solution)/shard_map/ppermute | solution.py:441
  57.6 7.2 %collective-permute-start.19 = (f32[2,128,128]{2,1,0:T(8,128)S(1)}, f32[2,128,128]{2,1,0:T(8,128)S(1)}, u32[]{:S(2)}, u32[]{:S(2)}) collective-permute-start(f32[2,128,128]{2,1,0:T(8,128)S(1)} %get-tuple-element.97), channel_id=1, source_target_pairs={{0,8},{4,12},{8,0},{12,4},{16,24},{20,28},{24,16},{28,20},{1,9},{5... | collective-permute-start | bytes 393224 | tf_op jit(solution)/shard_map/ppermute | solution.py:441
  59.9 6.3 %collective-permute-start.20 = (f32[2,128,128]{2,1,0:T(8,128)S(1)}, f32[2,128,128]{2,1,0:T(8,128)S(1)}, u32[]{:S(2)}, u32[]{:S(2)}) collective-permute-start(f32[2,128,128]{2,1,0:T(8,128)S(1)} %get-tuple-element.98), channel_id=1, source_target_pairs={{0,4},{4,0},{8,12},{12,8},{16,20},{20,16},{24,28},{28,24},{1,5},{5... | collective-permute-start | bytes 393224 | tf_op jit(solution)/shard_map/ppermute | solution.py:441

commit v6 on v5

--- a/solution.py
+++ b/solution.py
@@ -147,7 +147,7 @@
     return index == 0, index == lax.axis_size(axis) - 1
 
 
-def wide_kernel(depth, height, slabs, z_first, z_second, field, g_out, solved, head, tail, element, w_low, w_high):
+def wide_kernel(depth, height, slabs, z_first, z_second, field, g_out, solved, head, tail, element, w_low, w_high, sent):
     slab = height + GHOSTS
     width = slabs.shape[1]
     z_odd = lax.rem(lax.axis_index("gz"), 2) == 1
@@ -193,6 +193,7 @@
     link = HALF_LINK * (g_own(depth - 1) + g_rows(depth))
     w_high[...] = link
     element[2] = element[2] + 1.0 / link
+    put(sent, [element[k] for k in range(5)], True)
 
 
 def z_kernel(depth, height, field, near, far, low, high, g_out, solved, head, tail, element):
@@ -268,16 +269,40 @@
     return lax.rem(lax.div(lax.axis_index(axis), 1 << level), 2) == 1
 
 
-def parts(ref, rows):
+def packed(count, rows, wide):
+    return count * (rows - GHOSTS) + -(-2 * count // 8) * 8 if wide else count * rows
+
+
+def put(ref, values, wide):
+    rows = values[0].shape[0] - GHOSTS * wide
+    for k, value in enumerate(values):
+        ref[pl.ds(k * rows, rows), :] = value[:rows]
+        if wide:
+            ref[pl.ds(len(values) * rows + 2 * k, 2), :] = value[rows : rows + 2]
+
+
+def parts(ref, rows, wide):
     if len(ref.shape) == 3:
         return [ref[k] for k in range(ref.shape[0])]
-    return [ref[pl.ds(k * rows, rows), :] for k in range(ref.shape[0] // rows)]
-
-
-def merge_kernel(axis, level, own, got, *outs):
+    rows -= GHOSTS * wide
+    count = ref.shape[0] // rows
+    values = [ref[pl.ds(k * rows, rows), :] for k in range(count)]
+    if wide:
+        for k in range(count):
+            begin = count * rows + 2 * k
+            fitting = min(begin, ref.shape[0] - 8)
+            ghosts = ref[pl.ds(fitting, 8), :]
+            if begin > fitting:
+                ghosts = pltpu.roll(ghosts, 8 - begin + fitting, 0)
+            values[k] = jnp.concatenate([values[k], ghosts], axis=0)
+    return values
+
+
+def merge_kernel(axis, level, last, own, got, *outs):
     upper = is_upper(axis, level)
     size, rows = own.shape[:2]
-    lower, higher = sides(upper, parts(own, rows), parts(got, rows), False)
+    wide = size == 5
+    lower, higher = sides(upper, parts(own, rows, wide), parts(got, rows, wide), False)
     share, _ = join(lower, higher)
     gap = lower[4] - higher[3]
     first, second = share * lower[1], share * higher[1]
@@ -287,19 +312,19 @@
         higher[2] - second * higher[1],
         lower[3] - first * gap,
         higher[4] + second * gap,
-        *([lower[5], higher[6]] if size > 5 else []),
+        *([] if wide else [lower[5], higher[6]]),
     ]
     for k in range(size):
         outs[0][k] = merged[k]
     if len(outs) > 1:
         above = is_upper(axis, level + 1)
-        for k, (high, low) in enumerate(LAST_SENT[: (size - 1) // 2]):
-            outs[1][pl.ds(k * rows, rows), :] = jnp.where(above, merged[high], merged[low])
+        sent = [jnp.where(above, merged[high], merged[low]) for high, low in LAST_SENT[: (size - 1) // 2]]
+        put(outs[1], sent if last else merged, wide)
 
 
 def unwind(axis, refs):
     rows = refs[0].shape[1]
-    pairs = [parts(ref, rows) for ref in refs]
+    pairs = [parts(ref, rows, refs[0].shape[0] == 5) for ref in refs]
     zero = jnp.zeros_like(pairs[0][0])
     from_low = from_high = jump_low = jump_high = zero
     for level in range(len(pairs) // 2 - 1, -1, -1):
@@ -466,8 +491,10 @@
 
 def merge(element, got, axis, level, after=()):
     size, rows, width = element.shape
-    outs = [element.shape] + [((size - 1) // 2 * rows, width)] * (4 << level >= lax.axis_size(axis))
-    merged = call(functools.partial(merge_kernel, axis, level), outs, [element, got], after=after)
+    last, wide = 4 << level >= lax.axis_size(axis), size == 5
+    count = (size - 1) // 2 if last else size
+    outs = [element.shape] + [(packed(count, rows, wide), width)] * (last or wide)
+    merged = call(functools.partial(merge_kernel, axis, level, last), outs, [element, got], after=after)
     return merged[0], merged[-1]
 
 
@@ -498,7 +525,7 @@
     return field, incoming
 
 
-def lines(field, g_field, z_element, planes, height, slab, used, sum_body):
+def lines(field, g_field, z_element, z_sent, planes, height, slab, used, sum_body):
     width = field.shape[1]
     part = functools.partial
     z_rounds, y_rounds = (lax.axis_size(axis).bit_length() - 1 for axis in ("gz", "xy"))
@@ -521,7 +548,7 @@
         rows = min(cut, used - k * cut) * slab
         along_x.extend(call(part(x_kernel, k * cut * slab, rows), [(cut * slab, width)], [g_field, field], after=after))
 
-    z_sent, z_pairs = z_element, []
+    z_pairs = []
     for level in range(z_rounds):
         z_pairs += [z_element, swap(z_sent, "gz", 1 << level)]
         behind = []
@@ -556,14 +583,14 @@
     )
     z_sides = neighbours(*edges, "gz")
     slots = slots_of(owners, width, edges[0])
-    field, g_field, *z_pieces, z_element, w_low, w_high = call(
+    field, g_field, *z_pieces, z_element, w_low, w_high, z_sent = call(
         part(wide_kernel, depth, height),
-        [(planes * slab, width)] * 2 + [(depth, slab, width)] * 3 + [(5, slab, width)] + [(slab, width)] * 2,
+        [(planes * slab, width)] * 2 + [(depth, slab, width)] * 3 + [(5, slab, width)] + [(slab, width)] * 2 + [(packed(5, slab, True), width)],
         [slabs, *z_sides],
         after=[slots],
     )
     total, z_pairs = lines(
-        field, g_field, z_element, planes, height, slab, depth + 2, lambda cut, *refs: wide_sum_kernel(cut, height, slab, *refs)
+        field, g_field, z_element, z_sent, planes, height, slab, depth + 2, lambda cut, *refs: wide_sum_kernel(cut, height, slab, *refs)
     )
     field, *around = call(
         part(step_kernel, depth, height), [flat, side, side, plane, plane], [total, *z_pieces, w_low, w_high, *z_pairs]
@@ -572,7 +599,7 @@
         part(z_kernel, depth, height), [flat] + [(depth, height, width)] * 3 + [(7, height, width)], [field, *around]
     )
     total, z_pairs = lines(
-        field, g_field, z_element, depth, height, height, depth, lambda cut, *refs: sum_kernel(cut, height, *refs)
+        field, g_field, z_element, z_element, depth, height, height, depth, lambda cut, *refs: sum_kernel(cut, height, *refs)
     )
     rows = slots.shape[0]
     chunks = call(

time: 67.2 us -> 64.5 us (0.960)
  waiting for transfers between devices: 21.5 us -> 16.6 us
  starting transfers between devices: 31.2 us -> 33.4 us
    ppermute x19, waiting for transfers between devices: 20.1 us -> 15.2 us  [swap(): return lax.ppermute(values, axis, [(i, i ^ stride) for i in range(count)])]
    ppermute x19, starting transfers between devices: 28.5 us -> 30.6 us  [swap(): return lax.ppermute(values, axis, [(i, i ^ stride) for i in range(count)])]
  transfers between devices with their start and end apart: 21 -> 21, of which waited for: 11 -> 11; matrix products, arithmetic and copies ran while one was open for 0% -> 0% of each run, Pallas kernels for 15% -> 16%
where the time goes in v6:
time: 64.5 us; the launch traced here: 64.3 us
  starting transfers between devices  33.4 us (52%)
  waiting for transfers between devices  16.6 us (26%)
  Pallas kernels  12.5 us (19%)
  local copies, waits for them, and re-layouts  0.95 us (1%)
  between operations  0.89 us (1%)
    ppermute x19, starting transfers between devices, swap(): return lax.ppermute(values, axis, [(i, i ^ stride) for i in range(count)])  30.6 us
    ppermute x19, waiting for transfers between devices, swap(): return lax.ppermute(values, axis, [(i, i ^ stride) for i in range(count)])  15.2 us
    pallas_call x23, Pallas kernels, call(): pl.pallas_call(lambda *refs: body(*refs[:count], *refs[count + len(after)...  10.2 us
    ppermute x1, starting transfers between devices, far(): return lax.ppermute(second, axis, other + [(j, i) for i, j in other])  2.59 us
    pallas_call x2, Pallas kernels, place(): pl.pallas_call(functools.partial(place_kernel, plan, CHUNKS if kept else...  1.75 us
    ppermute x1, waiting for transfers between devices, far(): return lax.ppermute(second, axis, other + [(j, i) for i, j in other])  1.44 us
  transfers between devices with their start and end apart: 21, of which 11 were waited for; matrix products, arithmetic and copies ran while one was open for 0% of the time, Pallas kernels for 16%

profile of v6, /device:TPU:0, one launch (start us, length us, event | category | flops | bytes accessed | tf_op | source)
XLA Modules:
  0.0 64.3 jit_solution(11602607692671053866)
XLA Ops:
  0.6 0.9 %copy-done = f32[16,32,128]{2,1,0:T(8,128)S(1)} copy-done((f32[16,32,128]{2,1,0:T(8,128)S(1)}, f32[16,32,128]{2,1,0:T(8,128)}, u32[]{:S(2)}) %copy-start) | copy-done | bytes 262168
  1.6 0.6 collective-permute-start
  2.2 2.6 %collective-permute-start.1 = (f32[32,128]{1,0:T(8,128)S(1)}, f32[32,128]{1,0:T(8,128)S(1)}, u32[]{:S(2)}, u32[]{:S(2)}) collective-permute-start(f32[32,128]{1,0:T(8,128)S(1)} %get-tuple-element.55), channel_id=1, source_target_pairs={{1,2},{3,0},{2,1},{0,3},{5,6},{7,4},{6,5},{4,7},{9,10},{11,8},{10,... | collective-permute-start | bytes 49160 | tf_op jit(solution)/shard_map/ppermute | solution.py:477
  4.8 1.4 %collective-permute-done.1.refs_2_ = f32[32,128]{1,0:T(8,128)S(1)} collective-permute-done((f32[32,128]{1,0:T(8,128)S(1)}, f32[32,128]{1,0:T(8,128)S(1)}, u32[]{:S(2)}, u32[]{:S(2)}) %collective-permute-start.1) | collective-permute-done | bytes 16416 | tf_op jit(solution)/shard_map/ppermute | solution.py:477
  6.2 0.2 collective-permute-start.3
  6.4 3.1 %collective-permute-start.2 = (f32[80,128]{1,0:T(8,128)S(1)}, f32[80,128]{1,0:T(8,128)S(1)}, u32[]{:S(2)}, u32[]{:S(2)}) collective-permute-start(f32[80,128]{1,0:T(8,128)S(1)} %get-tuple-element.57.first), channel_id=1, source_target_pairs={{0,4},{4,0},{8,12},{12,8},{16,20},{20,16},{24,28},{28,24},{1,5},{5... | collective-permute-start | bytes 122888 | tf_op jit(solution)/shard_map/ppermute | solution.py:466
  9.5 0.6 slots.1.refs_3_.refs_4_.refs_1_
  10.1 1.4 %collective-permute-done.2.refs_1_ = f32[80,128]{1,0:T(8,128)S(1)} collective-permute-done((f32[80,128]{1,0:T(8,128)S(1)}, f32[80,128]{1,0:T(8,128)S(1)}, u32[]{:S(2)}, u32[]{:S(2)}) %collective-permute-start.2) | collective-permute-done | bytes 40992 | tf_op jit(solution)/shard_map/ppermute | solution.py:466
  11.5 0.5 shard_map.43
  12.1 2.2 %collective-permute-start.4 = (f32[176,128]{1,0:T(8,128)S(1)}, f32[176,128]{1,0:T(8,128)S(1)}, u32[]{:S(2)}, u32[]{:S(2)}) collective-permute-start(f32[176,128]{1,0:T(8,128)S(1)} %get-tuple-element.63), channel_id=1, source_target_pairs={{0,4},{4,0},{8,12},{12,8},{16,20},{20,16},{24,28},{28,24},{1,5},{5... | collective-permute-start | bytes 270344 | tf_op jit(solution)/shard_map/ppermute | solution.py:466
  14.3 0.4 shard_map.44
  14.8 1.7 %shard_map.45.refs_2_.refs_0_ = f32[320,128]{1,0:T(8,128)S(1)} custom-call(f32[960,128]{1,0:T(8,128)S(1)} %get-tuple-element.59.refs_0_, f32[960,128]{1,0:T(8,128)S(1)} %get-tuple-element.60.refs_1_, f32[7,24,128]{2,1,0:T(8,128)S(1)} %get-tuple-element.62.refs_2_.refs_0_.refs_6_), custom_call_target="tpu_custom_call" | custom-call | tf_op jit(solution)/shard_map/pallas_call | solution.py:27
  16.5 0.4 collective-permute-done.4.refs_1_.refs_7_
  17.0 2.0 %collective-permute-start.6 = (f32[176,128]{1,0:T(8,128)S(1)}, f32[176,128]{1,0:T(8,128)S(1)}, u32[]{:S(2)}, u32[]{:S(2)}) collective-permute-start(f32[176,128]{1,0:T(8,128)S(1)} %get-tuple-element.66), channel_id=1, source_target_pairs={{0,8},{4,12},{8,0},{12,4},{16,24},{20,28},{24,16},{28,20},{1,9},{5... | collective-permute-start | bytes 270344 | tf_op jit(solution)/shard_map/ppermute | solution.py:466
  19.0 1.5 %collective-permute-start.7 = (f32[72,128]{1,0:T(8,128)S(1)}, f32[72,128]{1,0:T(8,128)S(1)}, u32[]{:S(2)}, u32[]{:S(2)}) collective-permute-start(f32[72,128]{1,0:T(8,128)S(1)} %get-tuple-element.71), channel_id=1, source_target_pairs={{0,2},{1,3},{2,0},{3,1},{4,6},{5,7},{6,4},{7,5},{8,10},{9,11},{10,... | collective-permute-start | bytes 110600 | tf_op jit(solution)/shard_map/ppermute | solution.py:466
  20.5 1.6 %shard_map.48.refs_2_.refs_1_ = f32[320,128]{1,0:T(8,128)S(1)} custom-call(f32[960,128]{1,0:T(8,128)S(1)} %get-tuple-element.59.refs_0_, f32[960,128]{1,0:T(8,128)S(1)} %get-tuple-element.60.refs_1_, f32[5,40,128]{2,1,0:T(8,128)S(1)} %get-tuple-element.65.refs_2_.refs_0_.refs_8_), custom_call_target="tpu_custom_call" | custom-call | tf_op jit(solution)/shard_map/pallas_call | solution.py:27
  22.2 2.7 %collective-permute-start.8 = (f32[72,128]{1,0:T(8,128)S(1)}, f32[72,128]{1,0:T(8,128)S(1)}, u32[]{:S(2)}, u32[]{:S(2)}) collective-permute-start(f32[72,128]{1,0:T(8,128)S(1)} %get-tuple-element.77), channel_id=1, source_target_pairs={{0,16},{4,20},{8,24},{12,28},{16,0},{20,4},{24,8},{28,12},{1,17},{... | collective-permute-start | bytes 110600 | tf_op jit(solution)/shard_map/ppermute | solution.py:466
  24.9 0.9 %shard_map.50.refs_2_ = f32[320,128]{1,0:T(8,128)S(1)} custom-call(f32[960,128]{1,0:T(8,128)S(1)} %get-tuple-element.59.refs_0_, f32[960,128]{1,0:T(8,128)S(1)} %get-tuple-element.60.refs_1_, f32[5,40,128]{2,1,0:T(8,128)S(1)} %get-tuple-element.67.refs_2_.refs_10_), custom_call_target="tpu_custom_call" | custom-call | tf_op jit(solution)/shard_map/pallas_call | solution.py:27
  25.7 0.2 shard_map.51.refs_0_
  25.9 1.2 %collective-permute-done.8.refs_11_ = f32[72,128]{1,0:T(8,128)S(1)} collective-permute-done((f32[72,128]{1,0:T(8,128)S(1)}, f32[72,128]{1,0:T(8,128)S(1)}, u32[]{:S(2)}, u32[]{:S(2)}) %collective-permute-start.8) | collective-permute-done | bytes 36896 | tf_op jit(solution)/shard_map/ppermute | solution.py:466
  27.1 0.1 shard_map.52
  27.3 0.4 shard_map.53
  27.7 1.6 %collective-permute-start.9 = (f32[7,32,128]{2,1,0:T(8,128)S(1)}, f32[7,32,128]{2,1,0:T(8,128)S(1)}, u32[]{:S(2)}, u32[]{:S(2)}) collective-permute-start(f32[7,32,128]{2,1,0:T(8,128)S(1)} %get-tuple-element.84.refs_2_.refs_0_.refs_5_), channel_id=1, source_target_pairs={{0,4},{4,0},{8,12},{12,8},{16,20},{20,16},{24,28},{28,24},{1,5},{5... | collective-permute-start | bytes 344072 | tf_op jit(solution)/shard_map/ppermute | solution.py:466
  29.3 0.4 shard_map.54
  29.8 1.4 %shard_map.55.refs_2_.refs_0_ = f32[256,128]{1,0:T(8,128)S(1)} custom-call(f32[512,128]{1,0:T(8,128)S(1)} %get-tuple-element.83.refs_0_, f32[512,128]{1,0:T(8,128)S(1)} %get-tuple-element.78.refs_0_.refs_1_, f32[7,16,128]{2,1,0:T(8,128)S(1)} %get-tuple-element.85.refs_2_.refs_0_.refs_5_), custom_call_target="tpu_custom_call" | custom-call | tf_op jit(solution)/shard_map/pallas_call | solution.py:27
  31.2 1.3 %collective-permute-done.9.refs_1_.refs_6_ = f32[7,32,128]{2,1,0:T(8,128)S(1)} collective-permute-done((f32[7,32,128]{2,1,0:T(8,128)S(1)}, f32[7,32,128]{2,1,0:T(8,128)S(1)}, u32[]{:S(2)}, u32[]{:S(2)}) %collective-permute-start.9) | collective-permute-done | bytes 114720 | tf_op jit(solution)/shard_map/ppermute | solution.py:466
  32.6 1.4 %collective-permute-start.12 = (f32[7,32,128]{2,1,0:T(8,128)S(1)}, f32[7,32,128]{2,1,0:T(8,128)S(1)}, u32[]{:S(2)}, u32[]{:S(2)}) collective-permute-start(f32[7,32,128]{2,1,0:T(8,128)S(1)} %shard_map.57.refs_2_.refs_0_.refs_7_), channel_id=1, source_target_pairs={{0,8},{4,12},{8,0},{12,4},{16,24},{20,28},{24,16},{28,20},{1,9},{5... | collective-permute-start | bytes 344072 | tf_op jit(solution)/shard_map/ppermute | solution.py:466
  34.0 1.4 %shard_map.58.refs_1_.refs_2_ = f32[256,128]{1,0:T(8,128)S(1)} custom-call(f32[512,128]{1,0:T(8,128)S(1)} %get-tuple-element.83.refs_0_, f32[512,128]{1,0:T(8,128)S(1)} %get-tuple-element.78.refs_0_.refs_1_, f32[7,32,128]{2,1,0:T(8,128)S(1)} %shard_map.57.refs_2_.refs_0_.refs_7_), custom_call_target="tpu_custom_call" | custom-call | tf_op jit(solution)/shard_map/pallas_call | solution.py:27
  35.4 2.0 %collective-permute-done.12.refs_1_.refs_8_ = f32[7,32,128]{2,1,0:T(8,128)S(1)} collective-permute-done((f32[7,32,128]{2,1,0:T(8,128)S(1)}, f32[7,32,128]{2,1,0:T(8,128)S(1)}, u32[]{:S(2)}, u32[]{:S(2)}) %collective-permute-start.12) | collective-permute-done | bytes 114720 | tf_op jit(solution)/shard_map/ppermute | solution.py:466
  37.5 2.8 %collective-permute-start.13 = (f32[96,128]{1,0:T(8,128)S(1)}, f32[96,128]{1,0:T(8,128)S(1)}, u32[]{:S(2)}, u32[]{:S(2)}) collective-permute-start(f32[96,128]{1,0:T(8,128)S(1)} %get-tuple-element.95), channel_id=1, source_target_pairs={{0,16},{4,20},{8,24},{12,28},{16,0},{20,4},{24,8},{28,12},{1,17},{... | collective-permute-start | bytes 147464 | tf_op jit(solution)/shard_map/ppermute | solution.py:466
  40.3 1.2 %collective-permute-start.11 = (f32[48,128]{1,0:T(8,128)S(1)}, f32[48,128]{1,0:T(8,128)S(1)}, u32[]{:S(2)}, u32[]{:S(2)}) collective-permute-start(f32[48,128]{1,0:T(8,128)S(1)} %get-tuple-element.90), channel_id=1, source_target_pairs={{0,2},{1,3},{2,0},{3,1},{4,6},{5,7},{6,4},{7,5},{8,10},{9,11},{10,... | collective-permute-start | bytes 73736 | tf_op jit(solution)/shard_map/ppermute | solution.py:466
  41.5 2.6 %collective-permute-done.11.refs_8_ = f32[48,128]{1,0:T(8,128)S(1)} collective-permute-done((f32[48,128]{1,0:T(8,128)S(1)}, f32[48,128]{1,0:T(8,128)S(1)}, u32[]{:S(2)}, u32[]{:S(2)}) %collective-permute-start.11) | collective-permute-done | bytes 24608 | tf_op jit(solution)/shard_map/ppermute | solution.py:466
  44.1 0.4 shard_map.59.refs_0_
  44.5 0.1 shard_map.61.refs_0_.refs_4_
  44.6 0.9 %collective-permute-start.17 = (f32[520,128]{1,0:T(8,128)S(1)}, f32[520,128]{1,0:T(8,128)S(1)}, u32[]{:S(2)}, u32[]{:S(2)}) collective-permute-start(f32[520,128]{1,0:T(8,128)S(1)} %shard_map.61.refs_0_.refs_4_), channel_id=1, source_target_pairs={{0,16},{4,20},{8,24},{12,28},{16,0},{20,4},{24,8},{28,12},{1,17},{... | collective-permute-start | bytes 798728 | tf_op jit(solution)/shard_map/ppermute | solution.py:466
  45.5 0.2 shard_map.62
  45.7 1.8 %collective-permute-start.14 = (f32[2,128,128]{2,1,0:T(8,128)S(1)}, f32[2,128,128]{2,1,0:T(8,128)S(1)}, u32[]{:S(2)}, u32[]{:S(2)}) collective-permute-start(f32[2,128,128]{2,1,0:T(8,128)S(1)} %get-tuple-element.97), channel_id=1, source_target_pairs={{0,12},{4,8},{8,4},{12,0},{16,28},{20,24},{24,20},{28,16},{1,13},{... | collective-permute-start | bytes 393224 | tf_op jit(solution)/shard_map/ppermute | solution.py:466
  47.5 3.8 %collective-permute-start.15 = (f32[2,128,128]{2,1,0:T(8,128)S(1)}, f32[2,128,128]{2,1,0:T(8,128)S(1)}, u32[]{:S(2)}, u32[]{:S(2)}) collective-permute-start(f32[2,128,128]{2,1,0:T(8,128)S(1)} %get-tuple-element.98), channel_id=1, source_target_pairs={{0,8},{4,12},{8,0},{12,4},{16,24},{20,28},{24,16},{28,20},{1,9},{5... | collective-permute-start | bytes 393224 | tf_op jit(solution)/shard_map/ppermute | solution.py:466
  51.3 1.4 %collective-permute-start.16 = (f32[2,128,128]{2,1,0:T(8,128)S(1)}, f32[2,128,128]{2,1,0:T(8,128)S(1)}, u32[]{:S(2)}, u32[]{:S(2)}) collective-permute-start(f32[2,128,128]{2,1,0:T(8,128)S(1)} %get-tuple-element.99), channel_id=1, source_target_pairs={{0,4},{4,0},{8,12},{12,8},{16,20},{20,16},{24,28},{28,24},{1,5},{5... | collective-permute-start | bytes 393224 | tf_op jit(solution)/shard_map/ppermute | solution.py:466
  52.7 3.3 %collective-permute-done.17.refs_0_ = f32[520,128]{1,0:T(8,128)S(1)} collective-permute-done((f32[520,128]{1,0:T(8,128)S(1)}, f32[520,128]{1,0:T(8,128)S(1)}, u32[]{:S(2)}, u32[]{:S(2)}) %collective-permute-start.17) | collective-permute-done | bytes 266272 | tf_op jit(solution)/shard_map/ppermute | solution.py:466
  56.0 0.2 shard_map.64
  56.3 2.2 %collective-permute-start.19 = (f32[2,128,128]{2,1,0:T(8,128)S(1)}, f32[2,128,128]{2,1,0:T(8,128)S(1)}, u32[]{:S(2)}, u32[]{:S(2)}) collective-permute-start(f32[2,128,128]{2,1,0:T(8,128)S(1)} %get-tuple-element.103), channel_id=1, source_target_pairs={{0,8},{4,12},{8,0},{12,4},{16,24},{20,28},{24,16},{28,20},{1,9},{5... | collective-permute-start | bytes 393224 | tf_op jit(solution)/shard_map/ppermute | solution.py:466
  58.5 1.3 %collective-permute-start.20 = (f32[2,128,128]{2,1,0:T(8,128)S(1)}, f32[2,128,128]{2,1,0:T(8,128)S(1)}, u32[]{:S(2)}, u32[]{:S(2)}) collective-permute-start(f32[2,128,128]{2,1,0:T(8,128)S(1)} %get-tuple-element.104), channel_id=1, source_target_pairs={{0,4},{4,0},{8,12},{12,8},{16,20},{20,16},{24,28},{28,24},{1,5},{5... | collective-permute-start | bytes 393224 | tf_op jit(solution)/shard_map/ppermute | solution.py:466
  59.8 0.9 %shard_map.63 = (f32[16,128,128]{2,1,0:T(8,128)}, f32[4,128,128]{2,1,0:T(8,128)}) custom-call(f32[2,128,128]{2,1,0:T(8,128)S(1)} %get-tuple-element.96.refs_0_, f32[2,128,128]{2,1,0:T(8,128)S(1)} %collective-permute-done.14.refs_1_, f32[2,128,128]{2,1,0:T(8,128)S(1)} %collective-permute-done.15.refs_2_, f32[2,128,128]{2,1,0:T(8,128)S(1)} %collective-permute-done.16.refs_3_, ...), custom_call_target="tpu_custom_call" | custom-call | tf_op jit(solution)/shard_map/pallas_call | solution.py:453
  60.7 1.4 %collective-permute-done.18.refs_1_ = f32[2,128,128]{2,1,0:T(8,128)S(1)} collective-permute-done((f32[2,128,128]{2,1,0:T(8,128)S(1)}, f32[2,128,128]{2,1,0:T(8,128)S(1)}, u32[]{:S(2)}, u32[]{:S(2)}) %collective-permute-start.18) | collective-permute-done | bytes 131104 | tf_op jit(solution)/shard_map/ppermute | solution.py:466
  62.1 0.7 %collective-permute-done.19.refs_2_ = f32[2,128,128]{2,1,0:T(8,128)S(1)} collective-permute-done((f32[2,128,128]{2,1,0:T(8,128)S(1)}, f32[2,128,128]{2,1,0:T(8,128)S(1)}, u32[]{:S(2)}, u32[]{:S(2)}) %collective-permute-start.19) | collective-permute-done | bytes 131104 | tf_op jit(solution)/shard_map/ppermute | solution.py:466
  62.8 0.7 %collective-permute-done.20.refs_3_ = f32[2,128,128]{2,1,0:T(8,128)S(1)} collective-permute-done((f32[2,128,128]{2,1,0:T(8,128)S(1)}, f32[2,128,128]{2,1,0:T(8,128)S(1)}, u32[]{:S(2)}, u32[]{:S(2)}) %collective-permute-start.20) | collective-permute-done | bytes 131104 | tf_op jit(solution)/shard_map/ppermute | solution.py:466
  63.5 0.8 %shard_map.65 = f32[16,128,128]{2,1,0:T(8,128)} custom-call(f32[2,128,128]{2,1,0:T(8,128)S(1)} %get-tuple-element.101.refs_0_, f32[2,128,128]{2,1,0:T(8,128)S(1)} %collective-permute-done.18.refs_1_, f32[2,128,128]{2,1,0:T(8,128)S(1)} %collective-permute-done.19.refs_2_, ...), custom_call_target="tpu_custom_call", output_to_operand_aliasing={{}: (4, {})} | custom-call | tf_op jit(solution)/shard_map/pallas_call | solution.py:453
  (24 shorter events, 0.5 us)
Async XLA Ops:
  0.6 1.0 %copy-start = (f32[16,32,128]{2,1,0:T(8,128)S(1)}, f32[16,32,128]{2,1,0:T(8,128)}, u32[]{:S(2)}) copy-start(f32[16,32,128]{2,1,0:T(8,128)} %param.2) | copy-start | bytes 786436
  1.6 3.2 %collective-permute-start = (f32[32,128]{1,0:T(8,128)S(1)}, f32[32,128]{1,0:T(8,128)S(1)}, u32[]{:S(2)}, u32[]{:S(2)}) collective-permute-start(f32[32,128]{1,0:T(8,128)S(1)} %get-tuple-element.54), channel_id=1, source_target_pairs={{0,1},{1,0},{2,3},{3,2},{4,5},{5,4},{6,7},{7,6},{8,9},{9,8},{10,11... | collective-permute-start | bytes 49160 | tf_op jit(solution)/shard_map/ppermute | solution.py:466
  2.2 4.0 %collective-permute-start.1 = (f32[32,128]{1,0:T(8,128)S(1)}, f32[32,128]{1,0:T(8,128)S(1)}, u32[]{:S(2)}, u32[]{:S(2)}) collective-permute-start(f32[32,128]{1,0:T(8,128)S(1)} %get-tuple-element.55), channel_id=1, source_target_pairs={{1,2},{3,0},{2,1},{0,3},{5,6},{7,4},{6,5},{4,7},{9,10},{11,8},{10,... | collective-permute-start | bytes 49160 | tf_op jit(solution)/shard_map/ppermute | solution.py:477
  6.2 3.9 %collective-permute-start.3 = (f32[80,128]{1,0:T(8,128)S(1)}, f32[80,128]{1,0:T(8,128)S(1)}, u32[]{:S(2)}, u32[]{:S(2)}) collective-permute-start(f32[80,128]{1,0:T(8,128)S(1)} %get-tuple-element.58), channel_id=1, source_target_pairs={{0,1},{1,0},{2,3},{3,2},{4,8},{5,9},{6,10},{7,11},{8,4},{9,5},{10,... | collective-permute-start | bytes 122888 | tf_op jit(solution)/shard_map/ppermute | solution.py:484
  6.4 3.1 %copy-start.1 = (s32[1,4,1]{1,2,0:T(1,128)S(1)}, s32[1,4,1]{1,2,0:T(1,128)}, u32[]{:S(2)}) copy-start(s32[1,4,1]{1,2,0:T(1,128)} %param.3) | copy-start | bytes 52
  6.4 5.1 %collective-permute-start.2 = (f32[80,128]{1,0:T(8,128)S(1)}, f32[80,128]{1,0:T(8,128)S(1)}, u32[]{:S(2)}, u32[]{:S(2)}) collective-permute-start(f32[80,128]{1,0:T(8,128)S(1)} %get-tuple-element.57.first), channel_id=1, source_target_pairs={{0,4},{4,0},{8,12},{12,8},{16,20},{20,16},{24,28},{28,24},{1,5},{5... | collective-permute-start | bytes 122888 | tf_op jit(solution)/shard_map/ppermute | solution.py:466
  12.1 4.9 %collective-permute-start.4 = (f32[176,128]{1,0:T(8,128)S(1)}, f32[176,128]{1,0:T(8,128)S(1)}, u32[]{:S(2)}, u32[]{:S(2)}) collective-permute-start(f32[176,128]{1,0:T(8,128)S(1)} %get-tuple-element.63), channel_id=1, source_target_pairs={{0,4},{4,0},{8,12},{12,8},{16,20},{20,16},{24,28},{28,24},{1,5},{5... | collective-permute-start | bytes 270344 | tf_op jit(solution)/shard_map/ppermute | solution.py:466
  14.7 1.7 %collective-permute-start.5 = (f32[7,24,128]{2,1,0:T(8,128)S(1)}, f32[7,24,128]{2,1,0:T(8,128)S(1)}, u32[]{:S(2)}, u32[]{:S(2)}) collective-permute-start(f32[7,24,128]{2,1,0:T(8,128)S(1)} %get-tuple-element.62.refs_2_.refs_0_.refs_6_), channel_id=1, source_target_pairs={{0,1},{1,0},{2,3},{3,2},{4,5},{5,4},{6,7},{7,6},{8,9},{9,8},{10,11... | collective-permute-start | bytes 258056 | tf_op jit(solution)/shard_map/ppermute | solution.py:466
  17.0 5.2 %collective-permute-start.6 = (f32[176,128]{1,0:T(8,128)S(1)}, f32[176,128]{1,0:T(8,128)S(1)}, u32[]{:S(2)}, u32[]{:S(2)}) collective-permute-start(f32[176,128]{1,0:T(8,128)S(1)} %get-tuple-element.66), channel_id=1, source_target_pairs={{0,8},{4,12},{8,0},{12,4},{16,24},{20,28},{24,16},{28,20},{1,9},{5... | collective-permute-start | bytes 270344 | tf_op jit(solution)/shard_map/ppermute | solution.py:466
  19.0 6.7 %collective-permute-start.7 = (f32[72,128]{1,0:T(8,128)S(1)}, f32[72,128]{1,0:T(8,128)S(1)}, u32[]{:S(2)}, u32[]{:S(2)}) collective-permute-start(f32[72,128]{1,0:T(8,128)S(1)} %get-tuple-element.71), channel_id=1, source_target_pairs={{0,2},{1,3},{2,0},{3,1},{4,6},{5,7},{6,4},{7,5},{8,10},{9,11},{10,... | collective-permute-start | bytes 110600 | tf_op jit(solution)/shard_map/ppermute | solution.py:466
  22.2 4.9 %collective-permute-start.8 = (f32[72,128]{1,0:T(8,128)S(1)}, f32[72,128]{1,0:T(8,128)S(1)}, u32[]{:S(2)}, u32[]{:S(2)}) collective-permute-start(f32[72,128]{1,0:T(8,128)S(1)} %get-tuple-element.77), channel_id=1, source_target_pairs={{0,16},{4,20},{8,24},{12,28},{16,0},{20,4},{24,8},{28,12},{1,17},{... | collective-permute-start | bytes 110600 | tf_op jit(solution)/shard_map/ppermute | solution.py:466
  27.7 4.9 %collective-permute-start.9 = (f32[7,32,128]{2,1,0:T(8,128)S(1)}, f32[7,32,128]{2,1,0:T(8,128)S(1)}, u32[]{:S(2)}, u32[]{:S(2)}) collective-permute-start(f32[7,32,128]{2,1,0:T(8,128)S(1)} %get-tuple-element.84.refs_2_.refs_0_.refs_5_), channel_id=1, source_target_pairs={{0,4},{4,0},{8,12},{12,8},{16,20},{20,16},{24,28},{28,24},{1,5},{5... | collective-permute-start | bytes 344072 | tf_op jit(solution)/shard_map/ppermute | solution.py:466
  29.7 1.5 %collective-permute-start.10 = (f32[7,16,128]{2,1,0:T(8,128)S(1)}, f32[7,16,128]{2,1,0:T(8,128)S(1)}, u32[]{:S(2)}, u32[]{:S(2)}) collective-permute-start(f32[7,16,128]{2,1,0:T(8,128)S(1)} %get-tuple-element.85.refs_2_.refs_0_.refs_5_), channel_id=1, source_target_pairs={{0,1},{1,0},{2,3},{3,2},{4,5},{5,4},{6,7},{7,6},{8,9},{9,8},{10,11... | collective-permute-start | bytes 172040 | tf_op jit(solution)/shard_map/ppermute | solution.py:466
  32.6 4.9 %collective-permute-start.12 = (f32[7,32,128]{2,1,0:T(8,128)S(1)}, f32[7,32,128]{2,1,0:T(8,128)S(1)}, u32[]{:S(2)}, u32[]{:S(2)}) collective-permute-start(f32[7,32,128]{2,1,0:T(8,128)S(1)} %shard_map.57.refs_2_.refs_0_.refs_7_), channel_id=1, source_target_pairs={{0,8},{4,12},{8,0},{12,4},{16,24},{20,28},{24,16},{28,20},{1,9},{5... | collective-permute-start | bytes 344072 | tf_op jit(solution)/shard_map/ppermute | solution.py:466
  37.5 6.9 %collective-permute-start.13 = (f32[96,128]{1,0:T(8,128)S(1)}, f32[96,128]{1,0:T(8,128)S(1)}, u32[]{:S(2)}, u32[]{:S(2)}) collective-permute-start(f32[96,128]{1,0:T(8,128)S(1)} %get-tuple-element.95), channel_id=1, source_target_pairs={{0,16},{4,20},{8,24},{12,28},{16,0},{20,4},{24,8},{28,12},{1,17},{... | collective-permute-start | bytes 147464 | tf_op jit(solution)/shard_map/ppermute | solution.py:466
  40.3 3.8 %collective-permute-start.11 = (f32[48,128]{1,0:T(8,128)S(1)}, f32[48,128]{1,0:T(8,128)S(1)}, u32[]{:S(2)}, u32[]{:S(2)}) collective-permute-start(f32[48,128]{1,0:T(8,128)S(1)} %get-tuple-element.90), channel_id=1, source_target_pairs={{0,2},{1,3},{2,0},{3,1},{4,6},{5,7},{6,4},{7,5},{8,10},{9,11},{10,... | collective-permute-start | bytes 73736 | tf_op jit(solution)/shard_map/ppermute | solution.py:466
  44.6 11.4 %collective-permute-start.17 = (f32[520,128]{1,0:T(8,128)S(1)}, f32[520,128]{1,0:T(8,128)S(1)}, u32[]{:S(2)}, u32[]{:S(2)}) collective-permute-start(f32[520,128]{1,0:T(8,128)S(1)} %shard_map.61.refs_0_.refs_4_), channel_id=1, source_target_pairs={{0,16},{4,20},{8,24},{12,28},{16,0},{20,4},{24,8},{28,12},{1,17},{... | collective-permute-start | bytes 798728 | tf_op jit(solution)/shard_map/ppermute | solution.py:466
  45.7 12.8 %collective-permute-start.14 = (f32[2,128,128]{2,1,0:T(8,128)S(1)}, f32[2,128,128]{2,1,0:T(8,128)S(1)}, u32[]{:S(2)}, u32[]{:S(2)}) collective-permute-start(f32[2,128,128]{2,1,0:T(8,128)S(1)} %get-tuple-element.97), channel_id=1, source_target_pairs={{0,12},{4,8},{8,4},{12,0},{16,28},{20,24},{24,20},{28,16},{1,13},{... | collective-permute-start | bytes 393224 | tf_op jit(solution)/shard_map/ppermute | solution.py:466
  47.5 12.3 %collective-permute-start.15 = (f32[2,128,128]{2,1,0:T(8,128)S(1)}, f32[2,128,128]{2,1,0:T(8,128)S(1)}, u32[]{:S(2)}, u32[]{:S(2)}) collective-permute-start(f32[2,128,128]{2,1,0:T(8,128)S(1)} %get-tuple-element.98), channel_id=1, source_target_pairs={{0,8},{4,12},{8,0},{12,4},{16,24},{20,28},{24,16},{28,20},{1,9},{5... | collective-permute-start | bytes 393224 | tf_op jit(solution)/shard_map/ppermute | solution.py:466
  51.3 8.5 %collective-permute-start.16 = (f32[2,128,128]{2,1,0:T(8,128)S(1)}, f32[2,128,128]{2,1,0:T(8,128)S(1)}, u32[]{:S(2)}, u32[]{:S(2)}) collective-permute-start(f32[2,128,128]{2,1,0:T(8,128)S(1)} %get-tuple-element.99), channel_id=1, source_target_pairs={{0,4},{4,0},{8,12},{12,8},{16,20},{20,16},{24,28},{28,24},{1,5},{5... | collective-permute-start | bytes 393224 | tf_op jit(solution)/shard_map/ppermute | solution.py:466
  56.2 5.9 %collective-permute-start.18 = (f32[2,128,128]{2,1,0:T(8,128)S(1)}, f32[2,128,128]{2,1,0:T(8,128)S(1)}, u32[]{:S(2)}, u32[]{:S(2)}) collective-permute-start(f32[2,128,128]{2,1,0:T(8,128)S(1)} %get-tuple-element.102), channel_id=1, source_target_pairs={{0,12},{4,8},{8,4},{12,0},{16,28},{20,24},{24,20},{28,16},{1,13},{... | collective-permute-start | bytes 393224 | tf_op jit(solution)/shard_map/ppermute | solution.py:466
  56.3 6.5 %collective-permute-start.19 = (f32[2,128,128]{2,1,0:T(8,128)S(1)}, f32[2,128,128]{2,1,0:T(8,128)S(1)}, u32[]{:S(2)}, u32[]{:S(2)}) collective-permute-start(f32[2,128,128]{2,1,0:T(8,128)S(1)} %get-tuple-element.103), channel_id=1, source_target_pairs={{0,8},{4,12},{8,0},{12,4},{16,24},{20,28},{24,16},{28,20},{1,9},{5... | collective-permute-start | bytes 393224 | tf_op jit(solution)/shard_map/ppermute | solution.py:466
  58.5 5.1 %collective-permute-start.20 = (f32[2,128,128]{2,1,0:T(8,128)S(1)}, f32[2,128,128]{2,1,0:T(8,128)S(1)}, u32[]{:S(2)}, u32[]{:S(2)}) collective-permute-start(f32[2,128,128]{2,1,0:T(8,128)S(1)} %get-tuple-element.104), channel_id=1, source_target_pairs={{0,4},{4,0},{8,12},{12,8},{16,20},{20,16},{24,28},{28,24},{1,5},{5... | collective-permute-start | bytes 393224 | tf_op jit(solution)/shard_map/ppermute | solution.py:466

commit v7 on v6

--- a/solution.py
+++ b/solution.py
@@ -541,12 +541,14 @@
         y_pairs += [y_element, swap(y_sent, "xy", 1 << level)]
         if level + 1 < y_rounds:
             y_element, y_sent = merge(*y_pairs[-2:], "xy", level)
-    cut, along_x = 8, []
+    cut, along_x = 8, {}
+    order = [0, 2, 1] if planes > 2 * cut else [0, 1]
 
     def x_part(after):
-        k = len(along_x)
+        turn = len(along_x)
+        k = order[turn]
         rows = min(cut, used - k * cut) * slab
-        along_x.extend(call(part(x_kernel, k * cut * slab, rows), [(cut * slab, width)], [g_field, field], after=after))
+        (along_x[k],) = call(part(x_kernel, k * cut * slab, rows), [(cut * slab, width)], [g_field, field], after=after)
 
     z_pairs = []
     for level in range(z_rounds):
@@ -554,14 +556,16 @@
         behind = []
         if level == 0:
             x_part([y_start])
-            behind = [along_x[0], y_element]
+            behind = [along_x[order[0]], y_element]
         if level == 1:
             x_part([z_element])
-            behind = [along_x[1]]
+            behind = [along_x[order[1]]]
         if level == 2:
-            while len(along_x) * cut < planes:
+            while len(along_x) < len(order):
                 x_part([z_element])
-            (total,) = call(part(sum_body, cut), [(planes * slab, width)], [*along_x, *y_pieces, *y_pairs])
+            (total,) = call(
+                part(sum_body, cut), [(planes * slab, width)], [*(along_x[k] for k in range(len(order))), *y_pieces, *y_pairs]
+            )
         if level + 1 < z_rounds:
             z_element, z_sent = merge(*z_pairs[-2:], "gz", level, behind)
     return total, z_pairs

time: 64.5 us -> 64.3 us (level)
  waiting for transfers between devices: 16.6 us -> 14.8 us
  starting transfers between devices: 33.4 us -> 35 us
    ppermute x19, waiting for transfers between devices: 15.2 us -> 13.4 us  [swap(): return lax.ppermute(values, axis, [(i, i ^ stride) for i in range(count)])]
    ppermute x19, starting transfers between devices: 30.6 us -> 32.2 us  [swap(): return lax.ppermute(values, axis, [(i, i ^ stride) for i in range(count)])]
  transfers between devices with their start and end apart: 21 -> 21, of which waited for: 11 -> 12; matrix products, arithmetic and copies ran while one was open for 0% -> 0% of each run, Pallas kernels for 16% -> 16%
where the time goes in v7:
time: 64.3 us; the launch traced here: 64.1 us
  starting transfers between devices  35 us (54%)
  waiting for transfers between devices  14.8 us (23%)
  Pallas kernels  12.5 us (19%)
  local copies, waits for them, and re-layouts  0.95 us (1%)
  between operations  0.88 us (1%)
    ppermute x19, starting transfers between devices, swap(): return lax.ppermute(values, axis, [(i, i ^ stride) for i in range(count)])  32.2 us
    ppermute x19, waiting for transfers between devices, swap(): return lax.ppermute(values, axis, [(i, i ^ stride) for i in range(count)])  13.4 us
    pallas_call x23, Pallas kernels, call(): pl.pallas_call(lambda *refs: body(*refs[:count], *refs[count + len(after)...  10.2 us
    ppermute x1, starting transfers between devices, far(): return lax.ppermute(second, axis, other + [(j, i) for i, j in other])  2.59 us
    pallas_call x2, Pallas kernels, place(): pl.pallas_call(functools.partial(place_kernel, plan, CHUNKS if kept else...  1.75 us
    ppermute x1, waiting for transfers between devices, far(): return lax.ppermute(second, axis, other + [(j, i) for i, j in other])  1.44 us
  transfers between devices with their start and end apart: 21, of which 12 were waited for; matrix products, arithmetic and copies ran while one was open for 0% of the time, Pallas kernels for 16%

profile of v7, /device:TPU:0, one launch (start us, length us, event | category | flops | bytes accessed | tf_op | source)
XLA Modules:
  0.0 64.1 jit_solution(6102319848241236748)
XLA Ops:
  0.6 0.9 %copy-done = f32[16,32,128]{2,1,0:T(8,128)S(1)} copy-done((f32[16,32,128]{2,1,0:T(8,128)S(1)}, f32[16,32,128]{2,1,0:T(8,128)}, u32[]{:S(2)}) %copy-start) | copy-done | bytes 262168
  1.6 0.6 collective-permute-start
  2.2 2.6 %collective-permute-start.1 = (f32[32,128]{1,0:T(8,128)S(1)}, f32[32,128]{1,0:T(8,128)S(1)}, u32[]{:S(2)}, u32[]{:S(2)}) collective-permute-start(f32[32,128]{1,0:T(8,128)S(1)} %get-tuple-element.55), channel_id=1, source_target_pairs={{1,2},{3,0},{2,1},{0,3},{5,6},{7,4},{6,5},{4,7},{9,10},{11,8},{10,... | collective-permute-start | bytes 49160 | tf_op jit(solution)/shard_map/ppermute | solution.py:477
  4.8 1.4 %collective-permute-done.1.refs_2_ = f32[32,128]{1,0:T(8,128)S(1)} collective-permute-done((f32[32,128]{1,0:T(8,128)S(1)}, f32[32,128]{1,0:T(8,128)S(1)}, u32[]{:S(2)}, u32[]{:S(2)}) %collective-permute-start.1) | collective-permute-done | bytes 16416 | tf_op jit(solution)/shard_map/ppermute | solution.py:477
  6.2 0.2 collective-permute-start.3
  6.4 3.1 %collective-permute-start.2 = (f32[80,128]{1,0:T(8,128)S(1)}, f32[80,128]{1,0:T(8,128)S(1)}, u32[]{:S(2)}, u32[]{:S(2)}) collective-permute-start(f32[80,128]{1,0:T(8,128)S(1)} %get-tuple-element.57.first), channel_id=1, source_target_pairs={{0,4},{4,0},{8,12},{12,8},{16,20},{20,16},{24,28},{28,24},{1,5},{5... | collective-permute-start | bytes 122888 | tf_op jit(solution)/shard_map/ppermute | solution.py:466
  9.5 0.6 slots.1.refs_3_.refs_4_.refs_1_
  10.1 1.4 %collective-permute-done.2.refs_1_ = f32[80,128]{1,0:T(8,128)S(1)} collective-permute-done((f32[80,128]{1,0:T(8,128)S(1)}, f32[80,128]{1,0:T(8,128)S(1)}, u32[]{:S(2)}, u32[]{:S(2)}) %collective-permute-start.2) | collective-permute-done | bytes 40992 | tf_op jit(solution)/shard_map/ppermute | solution.py:466
  11.5 0.5 shard_map.43
  12.1 2.2 %collective-permute-start.4 = (f32[176,128]{1,0:T(8,128)S(1)}, f32[176,128]{1,0:T(8,128)S(1)}, u32[]{:S(2)}, u32[]{:S(2)}) collective-permute-start(f32[176,128]{1,0:T(8,128)S(1)} %get-tuple-element.63), channel_id=1, source_target_pairs={{0,4},{4,0},{8,12},{12,8},{16,20},{20,16},{24,28},{28,24},{1,5},{5... | collective-permute-start | bytes 270344 | tf_op jit(solution)/shard_map/ppermute | solution.py:466
  14.3 0.4 shard_map.44
  14.8 1.7 %shard_map.45.refs_2_.refs_0_ = f32[320,128]{1,0:T(8,128)S(1)} custom-call(f32[960,128]{1,0:T(8,128)S(1)} %get-tuple-element.59.refs_0_, f32[960,128]{1,0:T(8,128)S(1)} %get-tuple-element.60.refs_1_, f32[7,24,128]{2,1,0:T(8,128)S(1)} %get-tuple-element.62.refs_2_.refs_0_.refs_6_), custom_call_target="tpu_custom_call" | custom-call | tf_op jit(solution)/shard_map/pallas_call | solution.py:27
  16.5 0.4 collective-permute-done.4.refs_1_.refs_7_
  17.0 2.0 %collective-permute-start.6 = (f32[176,128]{1,0:T(8,128)S(1)}, f32[176,128]{1,0:T(8,128)S(1)}, u32[]{:S(2)}, u32[]{:S(2)}) collective-permute-start(f32[176,128]{1,0:T(8,128)S(1)} %get-tuple-element.66), channel_id=1, source_target_pairs={{0,8},{4,12},{8,0},{12,4},{16,24},{20,28},{24,16},{28,20},{1,9},{5... | collective-permute-start | bytes 270344 | tf_op jit(solution)/shard_map/ppermute | solution.py:466
  19.0 1.5 %collective-permute-start.7 = (f32[72,128]{1,0:T(8,128)S(1)}, f32[72,128]{1,0:T(8,128)S(1)}, u32[]{:S(2)}, u32[]{:S(2)}) collective-permute-start(f32[72,128]{1,0:T(8,128)S(1)} %get-tuple-element.71), channel_id=1, source_target_pairs={{0,2},{1,3},{2,0},{3,1},{4,6},{5,7},{6,4},{7,5},{8,10},{9,11},{10,... | collective-permute-start | bytes 110600 | tf_op jit(solution)/shard_map/ppermute | solution.py:466
  20.5 0.9 %shard_map.48.refs_2_ = f32[320,128]{1,0:T(8,128)S(1)} custom-call(f32[960,128]{1,0:T(8,128)S(1)} %get-tuple-element.59.refs_0_, f32[960,128]{1,0:T(8,128)S(1)} %get-tuple-element.60.refs_1_, f32[5,40,128]{2,1,0:T(8,128)S(1)} %get-tuple-element.65.refs_2_.refs_0_.refs_8_), custom_call_target="tpu_custom_call" | custom-call | tf_op jit(solution)/shard_map/pallas_call | solution.py:27
  21.4 0.3 collective-permute-done.6.refs_1_.refs_9_
  21.7 3.0 %collective-permute-start.8 = (f32[72,128]{1,0:T(8,128)S(1)}, f32[72,128]{1,0:T(8,128)S(1)}, u32[]{:S(2)}, u32[]{:S(2)}) collective-permute-start(f32[72,128]{1,0:T(8,128)S(1)} %get-tuple-element.77), channel_id=1, source_target_pairs={{0,16},{4,20},{8,24},{12,28},{16,0},{20,4},{24,8},{28,12},{1,17},{... | collective-permute-start | bytes 110600 | tf_op jit(solution)/shard_map/ppermute | solution.py:466
  24.7 1.6 %shard_map.50.refs_1_ = f32[320,128]{1,0:T(8,128)S(1)} custom-call(f32[960,128]{1,0:T(8,128)S(1)} %get-tuple-element.59.refs_0_, f32[960,128]{1,0:T(8,128)S(1)} %get-tuple-element.60.refs_1_, f32[5,40,128]{2,1,0:T(8,128)S(1)} %get-tuple-element.67.refs_2_.refs_10_), custom_call_target="tpu_custom_call" | custom-call | tf_op jit(solution)/shard_map/pallas_call | solution.py:27
  26.3 0.2 shard_map.51.refs_0_
  26.6 0.1 shard_map.52
  26.8 0.4 shard_map.53
  27.2 1.9 %collective-permute-start.9 = (f32[7,32,128]{2,1,0:T(8,128)S(1)}, f32[7,32,128]{2,1,0:T(8,128)S(1)}, u32[]{:S(2)}, u32[]{:S(2)}) collective-permute-start(f32[7,32,128]{2,1,0:T(8,128)S(1)} %get-tuple-element.84.refs_2_.refs_0_.refs_5_), channel_id=1, source_target_pairs={{0,4},{4,0},{8,12},{12,8},{16,20},{20,16},{24,28},{28,24},{1,5},{5... | collective-permute-start | bytes 344072 | tf_op jit(solution)/shard_map/ppermute | solution.py:466
  29.1 0.4 shard_map.54
  29.6 1.4 %shard_map.55.refs_2_.refs_0_ = f32[256,128]{1,0:T(8,128)S(1)} custom-call(f32[512,128]{1,0:T(8,128)S(1)} %get-tuple-element.83.refs_0_, f32[512,128]{1,0:T(8,128)S(1)} %get-tuple-element.78.refs_0_.refs_1_, f32[7,16,128]{2,1,0:T(8,128)S(1)} %get-tuple-element.85.refs_2_.refs_0_.refs_5_), custom_call_target="tpu_custom_call" | custom-call | tf_op jit(solution)/shard_map/pallas_call | solution.py:27
  31.0 1.1 %collective-permute-done.9.refs_1_.refs_6_ = f32[7,32,128]{2,1,0:T(8,128)S(1)} collective-permute-done((f32[7,32,128]{2,1,0:T(8,128)S(1)}, f32[7,32,128]{2,1,0:T(8,128)S(1)}, u32[]{:S(2)}, u32[]{:S(2)}) %collective-permute-start.9) | collective-permute-done | bytes 114720 | tf_op jit(solution)/shard_map/ppermute | solution.py:466
  32.1 1.9 %collective-permute-start.12 = (f32[7,32,128]{2,1,0:T(8,128)S(1)}, f32[7,32,128]{2,1,0:T(8,128)S(1)}, u32[]{:S(2)}, u32[]{:S(2)}) collective-permute-start(f32[7,32,128]{2,1,0:T(8,128)S(1)} %shard_map.57.refs_2_.refs_0_.refs_7_), channel_id=1, source_target_pairs={{0,8},{4,12},{8,0},{12,4},{16,24},{20,28},{24,16},{28,20},{1,9},{5... | collective-permute-start | bytes 344072 | tf_op jit(solution)/shard_map/ppermute | solution.py:466
  34.0 1.4 %shard_map.58.refs_1_.refs_2_ = f32[256,128]{1,0:T(8,128)S(1)} custom-call(f32[512,128]{1,0:T(8,128)S(1)} %get-tuple-element.83.refs_0_, f32[512,128]{1,0:T(8,128)S(1)} %get-tuple-element.78.refs_0_.refs_1_, f32[7,32,128]{2,1,0:T(8,128)S(1)} %shard_map.57.refs_2_.refs_0_.refs_7_), custom_call_target="tpu_custom_call" | custom-call | tf_op jit(solution)/shard_map/pallas_call | solution.py:27
  35.4 1.5 %collective-permute-done.12.refs_1_.refs_8_ = f32[7,32,128]{2,1,0:T(8,128)S(1)} collective-permute-done((f32[7,32,128]{2,1,0:T(8,128)S(1)}, f32[7,32,128]{2,1,0:T(8,128)S(1)}, u32[]{:S(2)}, u32[]{:S(2)}) %collective-permute-start.12) | collective-permute-done | bytes 114720 | tf_op jit(solution)/shard_map/ppermute | solution.py:466
  37.0 3.0 %collective-permute-start.13 = (f32[96,128]{1,0:T(8,128)S(1)}, f32[96,128]{1,0:T(8,128)S(1)}, u32[]{:S(2)}, u32[]{:S(2)}) collective-permute-start(f32[96,128]{1,0:T(8,128)S(1)} %get-tuple-element.95), channel_id=1, source_target_pairs={{0,16},{4,20},{8,24},{12,28},{16,0},{20,4},{24,8},{28,12},{1,17},{... | collective-permute-start | bytes 147464 | tf_op jit(solution)/shard_map/ppermute | solution.py:466
  40.0 1.5 %collective-permute-start.11 = (f32[48,128]{1,0:T(8,128)S(1)}, f32[48,128]{1,0:T(8,128)S(1)}, u32[]{:S(2)}, u32[]{:S(2)}) collective-permute-start(f32[48,128]{1,0:T(8,128)S(1)} %get-tuple-element.90), channel_id=1, source_target_pairs={{0,2},{1,3},{2,0},{3,1},{4,6},{5,7},{6,4},{7,5},{8,10},{9,11},{10,... | collective-permute-start | bytes 73736 | tf_op jit(solution)/shard_map/ppermute | solution.py:466
  41.5 2.3 %collective-permute-done.11.refs_8_ = f32[48,128]{1,0:T(8,128)S(1)} collective-permute-done((f32[48,128]{1,0:T(8,128)S(1)}, f32[48,128]{1,0:T(8,128)S(1)}, u32[]{:S(2)}, u32[]{:S(2)}) %collective-permute-start.11) | collective-permute-done | bytes 24608 | tf_op jit(solution)/shard_map/ppermute | solution.py:466
  43.8 0.4 shard_map.59.refs_0_
  44.2 0.1 shard_map.61.refs_0_.refs_4_
  44.3 0.9 %collective-permute-start.17 = (f32[520,128]{1,0:T(8,128)S(1)}, f32[520,128]{1,0:T(8,128)S(1)}, u32[]{:S(2)}, u32[]{:S(2)}) collective-permute-start(f32[520,128]{1,0:T(8,128)S(1)} %shard_map.61.refs_0_.refs_4_), channel_id=1, source_target_pairs={{0,16},{4,20},{8,24},{12,28},{16,0},{20,4},{24,8},{28,12},{1,17},{... | collective-permute-start | bytes 798728 | tf_op jit(solution)/shard_map/ppermute | solution.py:466
  45.2 0.2 shard_map.62
  45.4 2.1 %collective-permute-start.14 = (f32[2,128,128]{2,1,0:T(8,128)S(1)}, f32[2,128,128]{2,1,0:T(8,128)S(1)}, u32[]{:S(2)}, u32[]{:S(2)}) collective-permute-start(f32[2,128,128]{2,1,0:T(8,128)S(1)} %get-tuple-element.97), channel_id=1, source_target_pairs={{0,12},{4,8},{8,4},{12,0},{16,28},{20,24},{24,20},{28,16},{1,13},{... | collective-permute-start | bytes 393224 | tf_op jit(solution)/shard_map/ppermute | solution.py:466
  47.5 3.5 %collective-permute-start.15 = (f32[2,128,128]{2,1,0:T(8,128)S(1)}, f32[2,128,128]{2,1,0:T(8,128)S(1)}, u32[]{:S(2)}, u32[]{:S(2)}) collective-permute-start(f32[2,128,128]{2,1,0:T(8,128)S(1)} %get-tuple-element.98), channel_id=1, source_target_pairs={{0,8},{4,12},{8,0},{12,4},{16,24},{20,28},{24,16},{28,20},{1,9},{5... | collective-permute-start | bytes 393224 | tf_op jit(solution)/shard_map/ppermute | solution.py:466
  51.0 1.4 %collective-permute-start.16 = (f32[2,128,128]{2,1,0:T(8,128)S(1)}, f32[2,128,128]{2,1,0:T(8,128)S(1)}, u32[]{:S(2)}, u32[]{:S(2)}) collective-permute-start(f32[2,128,128]{2,1,0:T(8,128)S(1)} %get-tuple-element.99), channel_id=1, source_target_pairs={{0,4},{4,0},{8,12},{12,8},{16,20},{20,16},{24,28},{28,24},{1,5},{5... | collective-permute-start | bytes 393224 | tf_op jit(solution)/shard_map/ppermute | solution.py:466
  52.4 3.4 %collective-permute-done.17.refs_0_ = f32[520,128]{1,0:T(8,128)S(1)} collective-permute-done((f32[520,128]{1,0:T(8,128)S(1)}, f32[520,128]{1,0:T(8,128)S(1)}, u32[]{:S(2)}, u32[]{:S(2)}) %collective-permute-start.17) | collective-permute-done | bytes 266272 | tf_op jit(solution)/shard_map/ppermute | solution.py:466
  55.8 0.2 shard_map.64
  56.1 2.2 %collective-permute-start.19 = (f32[2,128,128]{2,1,0:T(8,128)S(1)}, f32[2,128,128]{2,1,0:T(8,128)S(1)}, u32[]{:S(2)}, u32[]{:S(2)}) collective-permute-start(f32[2,128,128]{2,1,0:T(8,128)S(1)} %get-tuple-element.103), channel_id=1, source_target_pairs={{0,8},{4,12},{8,0},{12,4},{16,24},{20,28},{24,16},{28,20},{1,9},{5... | collective-permute-start | bytes 393224 | tf_op jit(solution)/shard_map/ppermute | solution.py:466
  58.3 1.3 %collective-permute-start.20 = (f32[2,128,128]{2,1,0:T(8,128)S(1)}, f32[2,128,128]{2,1,0:T(8,128)S(1)}, u32[]{:S(2)}, u32[]{:S(2)}) collective-permute-start(f32[2,128,128]{2,1,0:T(8,128)S(1)} %get-tuple-element.104), channel_id=1, source_target_pairs={{0,4},{4,0},{8,12},{12,8},{16,20},{20,16},{24,28},{28,24},{1,5},{5... | collective-permute-start | bytes 393224 | tf_op jit(solution)/shard_map/ppermute | solution.py:466
  59.5 0.9 %shard_map.63 = (f32[16,128,128]{2,1,0:T(8,128)}, f32[4,128,128]{2,1,0:T(8,128)}) custom-call(f32[2,128,128]{2,1,0:T(8,128)S(1)} %get-tuple-element.96.refs_0_, f32[2,128,128]{2,1,0:T(8,128)S(1)} %collective-permute-done.14.refs_1_, f32[2,128,128]{2,1,0:T(8,128)S(1)} %collective-permute-done.15.refs_2_, f32[2,128,128]{2,1,0:T(8,128)S(1)} %collective-permute-done.16.refs_3_, ...), custom_call_target="tpu_custom_call" | custom-call | tf_op jit(solution)/shard_map/pallas_call | solution.py:453
  60.5 1.4 %collective-permute-done.18.refs_1_ = f32[2,128,128]{2,1,0:T(8,128)S(1)} collective-permute-done((f32[2,128,128]{2,1,0:T(8,128)S(1)}, f32[2,128,128]{2,1,0:T(8,128)S(1)}, u32[]{:S(2)}, u32[]{:S(2)}) %collective-permute-start.18) | collective-permute-done | bytes 131104 | tf_op jit(solution)/shard_map/ppermute | solution.py:466
  61.9 0.7 %collective-permute-done.19.refs_2_ = f32[2,128,128]{2,1,0:T(8,128)S(1)} collective-permute-done((f32[2,128,128]{2,1,0:T(8,128)S(1)}, f32[2,128,128]{2,1,0:T(8,128)S(1)}, u32[]{:S(2)}, u32[]{:S(2)}) %collective-permute-start.19) | collective-permute-done | bytes 131104 | tf_op jit(solution)/shard_map/ppermute | solution.py:466
  62.6 0.7 %collective-permute-done.20.refs_3_ = f32[2,128,128]{2,1,0:T(8,128)S(1)} collective-permute-done((f32[2,128,128]{2,1,0:T(8,128)S(1)}, f32[2,128,128]{2,1,0:T(8,128)S(1)}, u32[]{:S(2)}, u32[]{:S(2)}) %collective-permute-start.20) | collective-permute-done | bytes 131104 | tf_op jit(solution)/shard_map/ppermute | solution.py:466
  63.3 0.8 %shard_map.65 = f32[16,128,128]{2,1,0:T(8,128)} custom-call(f32[2,128,128]{2,1,0:T(8,128)S(1)} %get-tuple-element.101.refs_0_, f32[2,128,128]{2,1,0:T(8,128)S(1)} %collective-permute-done.18.refs_1_, f32[2,128,128]{2,1,0:T(8,128)S(1)} %collective-permute-done.19.refs_2_, ...), custom_call_target="tpu_custom_call", output_to_operand_aliasing={{}: (4, {})} | custom-call | tf_op jit(solution)/shard_map/pallas_call | solution.py:453
  (24 shorter events, 0.6 us)
Async XLA Ops:
  0.6 1.0 %copy-start = (f32[16,32,128]{2,1,0:T(8,128)S(1)}, f32[16,32,128]{2,1,0:T(8,128)}, u32[]{:S(2)}) copy-start(f32[16,32,128]{2,1,0:T(8,128)} %param.2) | copy-start | bytes 786436
  1.6 3.2 %collective-permute-start = (f32[32,128]{1,0:T(8,128)S(1)}, f32[32,128]{1,0:T(8,128)S(1)}, u32[]{:S(2)}, u32[]{:S(2)}) collective-permute-start(f32[32,128]{1,0:T(8,128)S(1)} %get-tuple-element.54), channel_id=1, source_target_pairs={{0,1},{1,0},{2,3},{3,2},{4,5},{5,4},{6,7},{7,6},{8,9},{9,8},{10,11... | collective-permute-start | bytes 49160 | tf_op jit(solution)/shard_map/ppermute | solution.py:466
  2.2 4.0 %collective-permute-start.1 = (f32[32,128]{1,0:T(8,128)S(1)}, f32[32,128]{1,0:T(8,128)S(1)}, u32[]{:S(2)}, u32[]{:S(2)}) collective-permute-start(f32[32,128]{1,0:T(8,128)S(1)} %get-tuple-element.55), channel_id=1, source_target_pairs={{1,2},{3,0},{2,1},{0,3},{5,6},{7,4},{6,5},{4,7},{9,10},{11,8},{10,... | collective-permute-start | bytes 49160 | tf_op jit(solution)/shard_map/ppermute | solution.py:477
  6.2 3.9 %collective-permute-start.3 = (f32[80,128]{1,0:T(8,128)S(1)}, f32[80,128]{1,0:T(8,128)S(1)}, u32[]{:S(2)}, u32[]{:S(2)}) collective-permute-start(f32[80,128]{1,0:T(8,128)S(1)} %get-tuple-element.58), channel_id=1, source_target_pairs={{0,1},{1,0},{2,3},{3,2},{4,8},{5,9},{6,10},{7,11},{8,4},{9,5},{10,... | collective-permute-start | bytes 122888 | tf_op jit(solution)/shard_map/ppermute | solution.py:484
  6.4 3.1 %copy-start.1 = (s32[1,4,1]{1,2,0:T(1,128)S(1)}, s32[1,4,1]{1,2,0:T(1,128)}, u32[]{:S(2)}) copy-start(s32[1,4,1]{1,2,0:T(1,128)} %param.3) | copy-start | bytes 52
  6.4 5.1 %collective-permute-start.2 = (f32[80,128]{1,0:T(8,128)S(1)}, f32[80,128]{1,0:T(8,128)S(1)}, u32[]{:S(2)}, u32[]{:S(2)}) collective-permute-start(f32[80,128]{1,0:T(8,128)S(1)} %get-tuple-element.57.first), channel_id=1, source_target_pairs={{0,4},{4,0},{8,12},{12,8},{16,20},{20,16},{24,28},{28,24},{1,5},{5... | collective-permute-start | bytes 122888 | tf_op jit(solution)/shard_map/ppermute | solution.py:466
  12.1 4.9 %collective-permute-start.4 = (f32[176,128]{1,0:T(8,128)S(1)}, f32[176,128]{1,0:T(8,128)S(1)}, u32[]{:S(2)}, u32[]{:S(2)}) collective-permute-start(f32[176,128]{1,0:T(8,128)S(1)} %get-tuple-element.63), channel_id=1, source_target_pairs={{0,4},{4,0},{8,12},{12,8},{16,20},{20,16},{24,28},{28,24},{1,5},{5... | collective-permute-start | bytes 270344 | tf_op jit(solution)/shard_map/ppermute | solution.py:466
  14.7 1.7 %collective-permute-start.5 = (f32[7,24,128]{2,1,0:T(8,128)S(1)}, f32[7,24,128]{2,1,0:T(8,128)S(1)}, u32[]{:S(2)}, u32[]{:S(2)}) collective-permute-start(f32[7,24,128]{2,1,0:T(8,128)S(1)} %get-tuple-element.62.refs_2_.refs_0_.refs_6_), channel_id=1, source_target_pairs={{0,1},{1,0},{2,3},{3,2},{4,5},{5,4},{6,7},{7,6},{8,9},{9,8},{10,11... | collective-permute-start | bytes 258056 | tf_op jit(solution)/shard_map/ppermute | solution.py:466
  17.0 4.7 %collective-permute-start.6 = (f32[176,128]{1,0:T(8,128)S(1)}, f32[176,128]{1,0:T(8,128)S(1)}, u32[]{:S(2)}, u32[]{:S(2)}) collective-permute-start(f32[176,128]{1,0:T(8,128)S(1)} %get-tuple-element.66), channel_id=1, source_target_pairs={{0,8},{4,12},{8,0},{12,4},{16,24},{20,28},{24,16},{28,20},{1,9},{5... | collective-permute-start | bytes 270344 | tf_op jit(solution)/shard_map/ppermute | solution.py:466
  19.0 7.3 %collective-permute-start.7 = (f32[72,128]{1,0:T(8,128)S(1)}, f32[72,128]{1,0:T(8,128)S(1)}, u32[]{:S(2)}, u32[]{:S(2)}) collective-permute-start(f32[72,128]{1,0:T(8,128)S(1)} %get-tuple-element.71), channel_id=1, source_target_pairs={{0,2},{1,3},{2,0},{3,1},{4,6},{5,7},{6,4},{7,5},{8,10},{9,11},{10,... | collective-permute-start | bytes 110600 | tf_op jit(solution)/shard_map/ppermute | solution.py:466
  21.7 4.9 %collective-permute-start.8 = (f32[72,128]{1,0:T(8,128)S(1)}, f32[72,128]{1,0:T(8,128)S(1)}, u32[]{:S(2)}, u32[]{:S(2)}) collective-permute-start(f32[72,128]{1,0:T(8,128)S(1)} %get-tuple-element.77), channel_id=1, source_target_pairs={{0,16},{4,20},{8,24},{12,28},{16,0},{20,4},{24,8},{28,12},{1,17},{... | collective-permute-start | bytes 110600 | tf_op jit(solution)/shard_map/ppermute | solution.py:466
  27.2 4.9 %collective-permute-start.9 = (f32[7,32,128]{2,1,0:T(8,128)S(1)}, f32[7,32,128]{2,1,0:T(8,128)S(1)}, u32[]{:S(2)}, u32[]{:S(2)}) collective-permute-start(f32[7,32,128]{2,1,0:T(8,128)S(1)} %get-tuple-element.84.refs_2_.refs_0_.refs_5_), channel_id=1, source_target_pairs={{0,4},{4,0},{8,12},{12,8},{16,20},{20,16},{24,28},{28,24},{1,5},{5... | collective-permute-start | bytes 344072 | tf_op jit(solution)/shard_map/ppermute | solution.py:466
  29.5 1.5 %collective-permute-start.10 = (f32[7,16,128]{2,1,0:T(8,128)S(1)}, f32[7,16,128]{2,1,0:T(8,128)S(1)}, u32[]{:S(2)}, u32[]{:S(2)}) collective-permute-start(f32[7,16,128]{2,1,0:T(8,128)S(1)} %get-tuple-element.85.refs_2_.refs_0_.refs_5_), channel_id=1, source_target_pairs={{0,1},{1,0},{2,3},{3,2},{4,5},{5,4},{6,7},{7,6},{8,9},{9,8},{10,11... | collective-permute-start | bytes 172040 | tf_op jit(solution)/shard_map/ppermute | solution.py:466
  32.1 4.9 %collective-permute-start.12 = (f32[7,32,128]{2,1,0:T(8,128)S(1)}, f32[7,32,128]{2,1,0:T(8,128)S(1)}, u32[]{:S(2)}, u32[]{:S(2)}) collective-permute-start(f32[7,32,128]{2,1,0:T(8,128)S(1)} %shard_map.57.refs_2_.refs_0_.refs_7_), channel_id=1, source_target_pairs={{0,8},{4,12},{8,0},{12,4},{16,24},{20,28},{24,16},{28,20},{1,9},{5... | collective-permute-start | bytes 344072 | tf_op jit(solution)/shard_map/ppermute | solution.py:466
  37.0 7.2 %collective-permute-start.13 = (f32[96,128]{1,0:T(8,128)S(1)}, f32[96,128]{1,0:T(8,128)S(1)}, u32[]{:S(2)}, u32[]{:S(2)}) collective-permute-start(f32[96,128]{1,0:T(8,128)S(1)} %get-tuple-element.95), channel_id=1, source_target_pairs={{0,16},{4,20},{8,24},{12,28},{16,0},{20,4},{24,8},{28,12},{1,17},{... | collective-permute-start | bytes 147464 | tf_op jit(solution)/shard_map/ppermute | solution.py:466
  40.0 3.8 %collective-permute-start.11 = (f32[48,128]{1,0:T(8,128)S(1)}, f32[48,128]{1,0:T(8,128)S(1)}, u32[]{:S(2)}, u32[]{:S(2)}) collective-permute-start(f32[48,128]{1,0:T(8,128)S(1)} %get-tuple-element.90), channel_id=1, source_target_pairs={{0,2},{1,3},{2,0},{3,1},{4,6},{5,7},{6,4},{7,5},{8,10},{9,11},{10,... | collective-permute-start | bytes 73736 | tf_op jit(solution)/shard_map/ppermute | solution.py:466
  44.3 11.5 %collective-permute-start.17 = (f32[520,128]{1,0:T(8,128)S(1)}, f32[520,128]{1,0:T(8,128)S(1)}, u32[]{:S(2)}, u32[]{:S(2)}) collective-permute-start(f32[520,128]{1,0:T(8,128)S(1)} %shard_map.61.refs_0_.refs_4_), channel_id=1, source_target_pairs={{0,16},{4,20},{8,24},{12,28},{16,0},{20,4},{24,8},{28,12},{1,17},{... | collective-permute-start | bytes 798728 | tf_op jit(solution)/shard_map/ppermute | solution.py:466
  45.4 12.9 %collective-permute-start.14 = (f32[2,128,128]{2,1,0:T(8,128)S(1)}, f32[2,128,128]{2,1,0:T(8,128)S(1)}, u32[]{:S(2)}, u32[]{:S(2)}) collective-permute-start(f32[2,128,128]{2,1,0:T(8,128)S(1)} %get-tuple-element.97), channel_id=1, source_target_pairs={{0,12},{4,8},{8,4},{12,0},{16,28},{20,24},{24,20},{28,16},{1,13},{... | collective-permute-start | bytes 393224 | tf_op jit(solution)/shard_map/ppermute | solution.py:466
  47.5 12.1 %collective-permute-start.15 = (f32[2,128,128]{2,1,0:T(8,128)S(1)}, f32[2,128,128]{2,1,0:T(8,128)S(1)}, u32[]{:S(2)}, u32[]{:S(2)}) collective-permute-start(f32[2,128,128]{2,1,0:T(8,128)S(1)} %get-tuple-element.98), channel_id=1, source_target_pairs={{0,8},{4,12},{8,0},{12,4},{16,24},{20,28},{24,16},{28,20},{1,9},{5... | collective-permute-start | bytes 393224 | tf_op jit(solution)/shard_map/ppermute | solution.py:466
  51.0 8.6 %collective-permute-start.16 = (f32[2,128,128]{2,1,0:T(8,128)S(1)}, f32[2,128,128]{2,1,0:T(8,128)S(1)}, u32[]{:S(2)}, u32[]{:S(2)}) collective-permute-start(f32[2,128,128]{2,1,0:T(8,128)S(1)} %get-tuple-element.99), channel_id=1, source_target_pairs={{0,4},{4,0},{8,12},{12,8},{16,20},{20,16},{24,28},{28,24},{1,5},{5... | collective-permute-start | bytes 393224 | tf_op jit(solution)/shard_map/ppermute | solution.py:466
  56.0 5.9 %collective-permute-start.18 = (f32[2,128,128]{2,1,0:T(8,128)S(1)}, f32[2,128,128]{2,1,0:T(8,128)S(1)}, u32[]{:S(2)}, u32[]{:S(2)}) collective-permute-start(f32[2,128,128]{2,1,0:T(8,128)S(1)} %get-tuple-element.102), channel_id=1, source_target_pairs={{0,12},{4,8},{8,4},{12,0},{16,28},{20,24},{24,20},{28,16},{1,13},{... | collective-permute-start | bytes 393224 | tf_op jit(solution)/shard_map/ppermute | solution.py:466
  56.1 6.5 %collective-permute-start.19 = (f32[2,128,128]{2,1,0:T(8,128)S(1)}, f32[2,128,128]{2,1,0:T(8,128)S(1)}, u32[]{:S(2)}, u32[]{:S(2)}) collective-permute-start(f32[2,128,128]{2,1,0:T(8,128)S(1)} %get-tuple-element.103), channel_id=1, source_target_pairs={{0,8},{4,12},{8,0},{12,4},{16,24},{20,28},{24,16},{28,20},{1,9},{5... | collective-permute-start | bytes 393224 | tf_op jit(solution)/shard_map/ppermute | solution.py:466
  58.3 5.1 %collective-permute-start.20 = (f32[2,128,128]{2,1,0:T(8,128)S(1)}, f32[2,128,128]{2,1,0:T(8,128)S(1)}, u32[]{:S(2)}, u32[]{:S(2)}) collective-permute-start(f32[2,128,128]{2,1,0:T(8,128)S(1)} %get-tuple-element.104), channel_id=1, source_target_pairs={{0,4},{4,0},{8,12},{12,8},{16,20},{20,16},{24,28},{28,24},{1,5},{5... | collective-permute-start | bytes 393224 | tf_op jit(solution)/shard_map/ppermute | solution.py:466

commit v8 on v7

--- a/solution.py
+++ b/solution.py
@@ -525,7 +525,7 @@
     return field, incoming
 
 
-def lines(field, g_field, z_element, z_sent, planes, height, slab, used, sum_body):
+def lines(step, owners, field, g_field, z_element, z_sent, planes, height, slab, used, sum_body):
     width = field.shape[1]
     part = functools.partial
     z_rounds, y_rounds = (lax.axis_size(axis).bit_length() - 1 for axis in ("gz", "xy"))
@@ -550,7 +550,7 @@
         rows = min(cut, used - k * cut) * slab
         (along_x[k],) = call(part(x_kernel, k * cut * slab, rows), [(cut * slab, width)], [g_field, field], after=after)
 
-    z_pairs = []
+    z_pairs, slots = [], None
     for level in range(z_rounds):
         z_pairs += [z_element, swap(z_sent, "gz", 1 << level)]
         behind = []
@@ -560,6 +560,9 @@
         if level == 1:
             x_part([z_element])
             behind = [along_x[order[1]]]
+            if step == 0:
+                slots = slots_of(owners, width, z_element)
+                behind.append(slots)
         if level == 2:
             while len(along_x) < len(order):
                 x_part([z_element])
@@ -568,7 +571,7 @@
             )
         if level + 1 < z_rounds:
             z_element, z_sent = merge(*z_pairs[-2:], "gz", level, behind)
-    return total, z_pairs
+    return total, z_pairs, slots
 
 
 def on_device(volume, owners):
@@ -586,15 +589,13 @@
         part(slab_kernel, depth, height), [(depth * slab, width)] + [(2 * slab, width)] * 2, [field, *y_sides]
     )
     z_sides = neighbours(*edges, "gz")
-    slots = slots_of(owners, width, edges[0])
     field, g_field, *z_pieces, z_element, w_low, w_high, z_sent = call(
         part(wide_kernel, depth, height),
         [(planes * slab, width)] * 2 + [(depth, slab, width)] * 3 + [(5, slab, width)] + [(slab, width)] * 2 + [(packed(5, slab, True), width)],
         [slabs, *z_sides],
-        after=[slots],
-    )
-    total, z_pairs = lines(
-        field, g_field, z_element, z_sent, planes, height, slab, depth + 2, lambda cut, *refs: wide_sum_kernel(cut, height, slab, *refs)
+    )
+    total, z_pairs, slots = lines(
+        0, owners, field, g_field, z_element, z_sent, planes, height, slab, depth + 2, lambda cut, *refs: wide_sum_kernel(cut, height, slab, *refs)
     )
     field, *around = call(
         part(step_kernel, depth, height), [flat, side, side, plane, plane], [total, *z_pieces, w_low, w_high, *z_pairs]
@@ -602,8 +603,8 @@
     g_field, *z_pieces, z_element = call(
         part(z_kernel, depth, height), [flat] + [(depth, height, width)] * 3 + [(7, height, width)], [field, *around]
     )
-    total, z_pairs = lines(
-        field, g_field, z_element, z_element, depth, height, height, depth, lambda cut, *refs: sum_kernel(cut, height, *refs)
+    total, z_pairs, _ = lines(
+        1, None, field, g_field, z_element, z_element, depth, height, height, depth, lambda cut, *refs: sum_kernel(cut, height, *refs)
     )
     rows = slots.shape[0]
     chunks = call(

time: 64.3 us -> 65.7 us (1.022)
  waiting for transfers between devices: 14.8 us -> 19.3 us
  starting transfers between devices: 35 us -> 31.2 us
    ppermute x19, waiting for transfers between devices: 13.4 us -> 17.9 us  [swap(): return lax.ppermute(values, axis, [(i, i ^ stride) for i in range(count)])]
    ppermute x19, starting transfers between devices: 32.2 us -> 28.5 us  [swap(): return lax.ppermute(values, axis, [(i, i ^ stride) for i in range(count)])]
  transfers between devices with their start and end apart: 21 -> 21, of which waited for: 12 -> 11; matrix products, arithmetic and copies ran while one was open for 0% -> 0% of each run, Pallas kernels for 16% -> 16%
where the time goes in v8:
time: 65.7 us; the launch traced here: 65.6 us
  starting transfers between devices  31.2 us (47%)
  waiting for transfers between devices  19.3 us (29%)
  Pallas kernels  12.5 us (19%)
  local copies, waits for them, and re-layouts  1.59 us (2%)
  between operations  0.9 us (1%)
    ppermute x19, starting transfers between devices, swap(): return lax.ppermute(values, axis, [(i, i ^ stride) for i in range(count)])  28.5 us
    ppermute x19, waiting for transfers between devices, swap(): return lax.ppermute(values, axis, [(i, i ^ stride) for i in range(count)])  17.9 us
    pallas_call x23, Pallas kernels, call(): pl.pallas_call(lambda *refs: body(*refs[:count], *refs[count + len(after)...  10.2 us
    ppermute x1, starting transfers between devices, far(): return lax.ppermute(second, axis, other + [(j, i) for i, j in other])  2.59 us
    pallas_call x2, Pallas kernels, place(): pl.pallas_call(functools.partial(place_kernel, plan, CHUNKS if kept else...  1.75 us
    unnamed x4, local copies, waits for them, and re-layouts  1.59 us
    ppermute x1, waiting for transfers between devices, far(): return lax.ppermute(second, axis, other + [(j, i) for i, j in other])  1.44 us
  transfers between devices with their start and end apart: 21, of which 11 were waited for; matrix products, arithmetic and copies ran while one was open for 0% of the time, Pallas kernels for 16%

profile of v8, /device:TPU:0, one launch (start us, length us, event | category | flops | bytes accessed | tf_op | source)
XLA Modules:
  0.0 65.6 jit_solution(5640612157067815180)
XLA Ops:
  0.6 0.9 %copy-done = f32[16,32,128]{2,1,0:T(8,128)S(1)} copy-done((f32[16,32,128]{2,1,0:T(8,128)S(1)}, f32[16,32,128]{2,1,0:T(8,128)}, u32[]{:S(2)}) %copy-start) | copy-done | bytes 262168
  1.6 0.6 collective-permute-start
  2.2 2.6 %collective-permute-start.1 = (f32[32,128]{1,0:T(8,128)S(1)}, f32[32,128]{1,0:T(8,128)S(1)}, u32[]{:S(2)}, u32[]{:S(2)}) collective-permute-start(f32[32,128]{1,0:T(8,128)S(1)} %get-tuple-element.55), channel_id=1, source_target_pairs={{1,2},{3,0},{2,1},{0,3},{5,6},{7,4},{6,5},{4,7},{9,10},{11,8},{10,... | collective-permute-start | bytes 49160 | tf_op jit(solution)/shard_map/ppermute | solution.py:477
  4.8 1.4 %collective-permute-done.1.refs_2_ = f32[32,128]{1,0:T(8,128)S(1)} collective-permute-done((f32[32,128]{1,0:T(8,128)S(1)}, f32[32,128]{1,0:T(8,128)S(1)}, u32[]{:S(2)}, u32[]{:S(2)}) %collective-permute-start.1) | collective-permute-done | bytes 16416 | tf_op jit(solution)/shard_map/ppermute | solution.py:477
  6.2 1.8 %collective-permute-start.2 = (f32[80,128]{1,0:T(8,128)S(1)}, f32[80,128]{1,0:T(8,128)S(1)}, u32[]{:S(2)}, u32[]{:S(2)}) collective-permute-start(f32[80,128]{1,0:T(8,128)S(1)} %get-tuple-element.57), channel_id=1, source_target_pairs={{0,4},{4,0},{8,12},{12,8},{16,20},{20,16},{24,28},{28,24},{1,5},{5... | collective-permute-start | bytes 122888 | tf_op jit(solution)/shard_map/ppermute | solution.py:466
  8.0 0.2 collective-permute-start.3
  8.2 2.1 %collective-permute-done.2.refs_1_ = f32[80,128]{1,0:T(8,128)S(1)} collective-permute-done((f32[80,128]{1,0:T(8,128)S(1)}, f32[80,128]{1,0:T(8,128)S(1)}, u32[]{:S(2)}, u32[]{:S(2)}) %collective-permute-start.2) | collective-permute-done | bytes 40992 | tf_op jit(solution)/shard_map/ppermute | solution.py:466
  10.3 0.5 shard_map.43
  10.9 3.0 %collective-permute-start.4 = (f32[176,128]{1,0:T(8,128)S(1)}, f32[176,128]{1,0:T(8,128)S(1)}, u32[]{:S(2)}, u32[]{:S(2)}) collective-permute-start(f32[176,128]{1,0:T(8,128)S(1)} %get-tuple-element.63), channel_id=1, source_target_pairs={{0,4},{4,0},{8,12},{12,8},{16,20},{20,16},{24,28},{28,24},{1,5},{5... | collective-permute-start | bytes 270344 | tf_op jit(solution)/shard_map/ppermute | solution.py:466
  13.8 0.4 shard_map.44
  14.3 0.1 collective-permute-start.5
  14.3 1.7 %shard_map.45.refs_2_.refs_0_ = f32[320,128]{1,0:T(8,128)S(1)} custom-call(f32[960,128]{1,0:T(8,128)S(1)} %get-tuple-element.59.refs_0_, f32[960,128]{1,0:T(8,128)S(1)} %get-tuple-element.60.refs_1_, f32[7,24,128]{2,1,0:T(8,128)S(1)} %get-tuple-element.62.refs_2_.refs_0_.refs_6_), custom_call_target="tpu_custom_call" | custom-call | tf_op jit(solution)/shard_map/pallas_call | solution.py:27
  16.0 0.3 collective-permute-done.4.refs_1_.refs_7_
  16.4 3.3 %collective-permute-start.6 = (f32[176,128]{1,0:T(8,128)S(1)}, f32[176,128]{1,0:T(8,128)S(1)}, u32[]{:S(2)}, u32[]{:S(2)}) collective-permute-start(f32[176,128]{1,0:T(8,128)S(1)} %get-tuple-element.66), channel_id=1, source_target_pairs={{0,8},{4,12},{8,0},{12,4},{16,24},{20,28},{24,16},{28,20},{1,9},{5... | collective-permute-start | bytes 270344 | tf_op jit(solution)/shard_map/ppermute | solution.py:466
  19.7 1.5 %collective-permute-start.7 = (f32[72,128]{1,0:T(8,128)S(1)}, f32[72,128]{1,0:T(8,128)S(1)}, u32[]{:S(2)}, u32[]{:S(2)}) collective-permute-start(f32[72,128]{1,0:T(8,128)S(1)} %get-tuple-element.71), channel_id=1, source_target_pairs={{0,2},{1,3},{2,0},{3,1},{4,6},{5,7},{6,4},{7,5},{8,10},{9,11},{10,... | collective-permute-start | bytes 110600 | tf_op jit(solution)/shard_map/ppermute | solution.py:466
  21.2 0.9 %shard_map.48.refs_2_ = f32[320,128]{1,0:T(8,128)S(1)} custom-call(f32[960,128]{1,0:T(8,128)S(1)} %get-tuple-element.59.refs_0_, f32[960,128]{1,0:T(8,128)S(1)} %get-tuple-element.60.refs_1_, f32[5,40,128]{2,1,0:T(8,128)S(1)} %get-tuple-element.65.refs_2_.first.refs_0_.refs_8_), custom_call_target="tpu_custom_call" | custom-call | tf_op jit(solution)/shard_map/pallas_call | solution.py:27
  22.1 0.6 copy-done.1
  22.8 0.6 slots.1.refs_3_.refs_4_.refs_1_
  23.4 2.7 %collective-permute-start.8 = (f32[72,128]{1,0:T(8,128)S(1)}, f32[72,128]{1,0:T(8,128)S(1)}, u32[]{:S(2)}, u32[]{:S(2)}) collective-permute-start(f32[72,128]{1,0:T(8,128)S(1)} %get-tuple-element.77), channel_id=1, source_target_pairs={{0,16},{4,20},{8,24},{12,28},{16,0},{20,4},{24,8},{28,12},{1,17},{... | collective-permute-start | bytes 110600 | tf_op jit(solution)/shard_map/ppermute | solution.py:466
  26.0 1.7 %shard_map.50.refs_1_ = f32[320,128]{1,0:T(8,128)S(1)} custom-call(f32[960,128]{1,0:T(8,128)S(1)} %get-tuple-element.59.refs_0_, f32[960,128]{1,0:T(8,128)S(1)} %get-tuple-element.60.refs_1_, f32[5,40,128]{2,1,0:T(8,128)S(1)} %get-tuple-element.67.refs_2_.refs_10_), custom_call_target="tpu_custom_call" | custom-call | tf_op jit(solution)/shard_map/pallas_call | solution.py:27
  27.7 0.2 shard_map.51.refs_0_
  27.9 0.4 collective-permute-done.8.refs_11_
  28.3 0.1 shard_map.52
  28.5 0.4 shard_map.53
  28.9 0.6 collective-permute-start.9
  29.5 0.4 shard_map.54
  29.9 1.4 %shard_map.55.refs_2_.refs_0_ = f32[256,128]{1,0:T(8,128)S(1)} custom-call(f32[512,128]{1,0:T(8,128)S(1)} %get-tuple-element.83.refs_0_, f32[512,128]{1,0:T(8,128)S(1)} %get-tuple-element.78.refs_0_.refs_1_, f32[7,16,128]{2,1,0:T(8,128)S(1)} %get-tuple-element.85.refs_2_.refs_0_.refs_5_), custom_call_target="tpu_custom_call" | custom-call | tf_op jit(solution)/shard_map/pallas_call | solution.py:27
  31.4 2.4 %collective-permute-done.9.refs_1_.refs_6_ = f32[7,32,128]{2,1,0:T(8,128)S(1)} collective-permute-done((f32[7,32,128]{2,1,0:T(8,128)S(1)}, f32[7,32,128]{2,1,0:T(8,128)S(1)}, u32[]{:S(2)}, u32[]{:S(2)}) %collective-permute-start.9) | collective-permute-done | bytes 114720 | tf_op jit(solution)/shard_map/ppermute | solution.py:466
  33.8 1.0 %collective-permute-start.12 = (f32[7,32,128]{2,1,0:T(8,128)S(1)}, f32[7,32,128]{2,1,0:T(8,128)S(1)}, u32[]{:S(2)}, u32[]{:S(2)}) collective-permute-start(f32[7,32,128]{2,1,0:T(8,128)S(1)} %shard_map.57.refs_2_.refs_0_.refs_7_), channel_id=1, source_target_pairs={{0,8},{4,12},{8,0},{12,4},{16,24},{20,28},{24,16},{28,20},{1,9},{5... | collective-permute-start | bytes 344072 | tf_op jit(solution)/shard_map/ppermute | solution.py:466
  34.8 1.4 %shard_map.58.refs_1_.refs_2_ = f32[256,128]{1,0:T(8,128)S(1)} custom-call(f32[512,128]{1,0:T(8,128)S(1)} %get-tuple-element.83.refs_0_, f32[512,128]{1,0:T(8,128)S(1)} %get-tuple-element.78.refs_0_.refs_1_, f32[7,32,128]{2,1,0:T(8,128)S(1)} %shard_map.57.refs_2_.refs_0_.refs_7_), custom_call_target="tpu_custom_call" | custom-call | tf_op jit(solution)/shard_map/pallas_call | solution.py:27
  36.2 2.5 %collective-permute-done.12.refs_1_.refs_8_ = f32[7,32,128]{2,1,0:T(8,128)S(1)} collective-permute-done((f32[7,32,128]{2,1,0:T(8,128)S(1)}, f32[7,32,128]{2,1,0:T(8,128)S(1)}, u32[]{:S(2)}, u32[]{:S(2)}) %collective-permute-start.12) | collective-permute-done | bytes 114720 | tf_op jit(solution)/shard_map/ppermute | solution.py:466
  38.7 3.2 %collective-permute-start.13 = (f32[96,128]{1,0:T(8,128)S(1)}, f32[96,128]{1,0:T(8,128)S(1)}, u32[]{:S(2)}, u32[]{:S(2)}) collective-permute-start(f32[96,128]{1,0:T(8,128)S(1)} %get-tuple-element.95), channel_id=1, source_target_pairs={{0,16},{4,20},{8,24},{12,28},{16,0},{20,4},{24,8},{28,12},{1,17},{... | collective-permute-start | bytes 147464 | tf_op jit(solution)/shard_map/ppermute | solution.py:466
  41.9 0.7 %collective-permute-start.11 = (f32[48,128]{1,0:T(8,128)S(1)}, f32[48,128]{1,0:T(8,128)S(1)}, u32[]{:S(2)}, u32[]{:S(2)}) collective-permute-start(f32[48,128]{1,0:T(8,128)S(1)} %get-tuple-element.90), channel_id=1, source_target_pairs={{0,2},{1,3},{2,0},{3,1},{4,6},{5,7},{6,4},{7,5},{8,10},{9,11},{10,... | collective-permute-start | bytes 73736 | tf_op jit(solution)/shard_map/ppermute | solution.py:466
  42.6 3.1 %collective-permute-done.11.refs_8_ = f32[48,128]{1,0:T(8,128)S(1)} collective-permute-done((f32[48,128]{1,0:T(8,128)S(1)}, f32[48,128]{1,0:T(8,128)S(1)}, u32[]{:S(2)}, u32[]{:S(2)}) %collective-permute-start.11) | collective-permute-done | bytes 24608 | tf_op jit(solution)/shard_map/ppermute | solution.py:466
  45.7 0.4 shard_map.59.refs_0_
  46.0 0.1 shard_map.61.refs_0_.refs_4_
  46.2 1.5 %collective-permute-start.17 = (f32[520,128]{1,0:T(8,128)S(1)}, f32[520,128]{1,0:T(8,128)S(1)}, u32[]{:S(2)}, u32[]{:S(2)}) collective-permute-start(f32[520,128]{1,0:T(8,128)S(1)} %shard_map.61.refs_0_.refs_4_), channel_id=1, source_target_pairs={{0,16},{4,20},{8,24},{12,28},{16,0},{20,4},{24,8},{28,12},{1,17},{... | collective-permute-start | bytes 798728 | tf_op jit(solution)/shard_map/ppermute | solution.py:466
  47.7 0.2 shard_map.62
  48.0 3.6 %collective-permute-start.15 = (f32[2,128,128]{2,1,0:T(8,128)S(1)}, f32[2,128,128]{2,1,0:T(8,128)S(1)}, u32[]{:S(2)}, u32[]{:S(2)}) collective-permute-start(f32[2,128,128]{2,1,0:T(8,128)S(1)} %get-tuple-element.98), channel_id=1, source_target_pairs={{0,8},{4,12},{8,0},{12,4},{16,24},{20,28},{24,16},{28,20},{1,9},{5... | collective-permute-start | bytes 393224 | tf_op jit(solution)/shard_map/ppermute | solution.py:466
  51.5 1.4 %collective-permute-start.16 = (f32[2,128,128]{2,1,0:T(8,128)S(1)}, f32[2,128,128]{2,1,0:T(8,128)S(1)}, u32[]{:S(2)}, u32[]{:S(2)}) collective-permute-start(f32[2,128,128]{2,1,0:T(8,128)S(1)} %get-tuple-element.99), channel_id=1, source_target_pairs={{0,4},{4,0},{8,12},{12,8},{16,20},{20,16},{24,28},{28,24},{1,5},{5... | collective-permute-start | bytes 393224 | tf_op jit(solution)/shard_map/ppermute | solution.py:466
  52.9 3.6 %collective-permute-done.17.refs_0_ = f32[520,128]{1,0:T(8,128)S(1)} collective-permute-done((f32[520,128]{1,0:T(8,128)S(1)}, f32[520,128]{1,0:T(8,128)S(1)}, u32[]{:S(2)}, u32[]{:S(2)}) %collective-permute-start.17) | collective-permute-done | bytes 266272 | tf_op jit(solution)/shard_map/ppermute | solution.py:466
  56.5 0.2 shard_map.64
  56.8 2.7 %collective-permute-start.19 = (f32[2,128,128]{2,1,0:T(8,128)S(1)}, f32[2,128,128]{2,1,0:T(8,128)S(1)}, u32[]{:S(2)}, u32[]{:S(2)}) collective-permute-start(f32[2,128,128]{2,1,0:T(8,128)S(1)} %get-tuple-element.103), channel_id=1, source_target_pairs={{0,8},{4,12},{8,0},{12,4},{16,24},{20,28},{24,16},{28,20},{1,9},{5... | collective-permute-start | bytes 393224 | tf_op jit(solution)/shard_map/ppermute | solution.py:466
  59.6 0.7 %collective-permute-start.20 = (f32[2,128,128]{2,1,0:T(8,128)S(1)}, f32[2,128,128]{2,1,0:T(8,128)S(1)}, u32[]{:S(2)}, u32[]{:S(2)}) collective-permute-start(f32[2,128,128]{2,1,0:T(8,128)S(1)} %get-tuple-element.104), channel_id=1, source_target_pairs={{0,4},{4,0},{8,12},{12,8},{16,20},{20,16},{24,28},{28,24},{1,5},{5... | collective-permute-start | bytes 393224 | tf_op jit(solution)/shard_map/ppermute | solution.py:466
  60.3 0.9 %shard_map.63 = (f32[16,128,128]{2,1,0:T(8,128)}, f32[4,128,128]{2,1,0:T(8,128)}) custom-call(f32[2,128,128]{2,1,0:T(8,128)S(1)} %get-tuple-element.96.refs_0_, f32[2,128,128]{2,1,0:T(8,128)S(1)} %collective-permute-done.14.refs_1_, f32[2,128,128]{2,1,0:T(8,128)S(1)} %collective-permute-done.15.refs_2_, f32[2,128,128]{2,1,0:T(8,128)S(1)} %collective-permute-done.16.refs_3_, ...), custom_call_target="tpu_custom_call" | custom-call | tf_op jit(solution)/shard_map/pallas_call | solution.py:453
  61.3 1.6 %collective-permute-done.18.refs_1_ = f32[2,128,128]{2,1,0:T(8,128)S(1)} collective-permute-done((f32[2,128,128]{2,1,0:T(8,128)S(1)}, f32[2,128,128]{2,1,0:T(8,128)S(1)}, u32[]{:S(2)}, u32[]{:S(2)}) %collective-permute-start.18) | collective-permute-done | bytes 131104 | tf_op jit(solution)/shard_map/ppermute | solution.py:466
  62.9 1.8 %collective-permute-done.19.refs_2_ = f32[2,128,128]{2,1,0:T(8,128)S(1)} collective-permute-done((f32[2,128,128]{2,1,0:T(8,128)S(1)}, f32[2,128,128]{2,1,0:T(8,128)S(1)}, u32[]{:S(2)}, u32[]{:S(2)}) %collective-permute-start.19) | collective-permute-done | bytes 131104 | tf_op jit(solution)/shard_map/ppermute | solution.py:466
  64.7 0.8 %shard_map.65 = f32[16,128,128]{2,1,0:T(8,128)} custom-call(f32[2,128,128]{2,1,0:T(8,128)S(1)} %get-tuple-element.101.refs_0_, f32[2,128,128]{2,1,0:T(8,128)S(1)} %collective-permute-done.18.refs_1_, f32[2,128,128]{2,1,0:T(8,128)S(1)} %collective-permute-done.19.refs_2_, ...), custom_call_target="tpu_custom_call", output_to_operand_aliasing={{}: (4, {})} | custom-call | tf_op jit(solution)/shard_map/pallas_call | solution.py:453
  (24 shorter events, 0.6 us)
Async XLA Ops:
  0.6 1.0 %copy-start = (f32[16,32,128]{2,1,0:T(8,128)S(1)}, f32[16,32,128]{2,1,0:T(8,128)}, u32[]{:S(2)}) copy-start(f32[16,32,128]{2,1,0:T(8,128)} %param.2) | copy-start | bytes 786436
  1.6 3.2 %collective-permute-start = (f32[32,128]{1,0:T(8,128)S(1)}, f32[32,128]{1,0:T(8,128)S(1)}, u32[]{:S(2)}, u32[]{:S(2)}) collective-permute-start(f32[32,128]{1,0:T(8,128)S(1)} %get-tuple-element.54), channel_id=1, source_target_pairs={{0,1},{1,0},{2,3},{3,2},{4,5},{5,4},{6,7},{7,6},{8,9},{9,8},{10,11... | collective-permute-start | bytes 49160 | tf_op jit(solution)/shard_map/ppermute | solution.py:466
  2.2 4.0 %collective-permute-start.1 = (f32[32,128]{1,0:T(8,128)S(1)}, f32[32,128]{1,0:T(8,128)S(1)}, u32[]{:S(2)}, u32[]{:S(2)}) collective-permute-start(f32[32,128]{1,0:T(8,128)S(1)} %get-tuple-element.55), channel_id=1, source_target_pairs={{1,2},{3,0},{2,1},{0,3},{5,6},{7,4},{6,5},{4,7},{9,10},{11,8},{10,... | collective-permute-start | bytes 49160 | tf_op jit(solution)/shard_map/ppermute | solution.py:477
  6.2 4.1 %collective-permute-start.2 = (f32[80,128]{1,0:T(8,128)S(1)}, f32[80,128]{1,0:T(8,128)S(1)}, u32[]{:S(2)}, u32[]{:S(2)}) collective-permute-start(f32[80,128]{1,0:T(8,128)S(1)} %get-tuple-element.57), channel_id=1, source_target_pairs={{0,4},{4,0},{8,12},{12,8},{16,20},{20,16},{24,28},{28,24},{1,5},{5... | collective-permute-start | bytes 122888 | tf_op jit(solution)/shard_map/ppermute | solution.py:466
  8.0 2.3 %collective-permute-start.3 = (f32[80,128]{1,0:T(8,128)S(1)}, f32[80,128]{1,0:T(8,128)S(1)}, u32[]{:S(2)}, u32[]{:S(2)}) collective-permute-start(f32[80,128]{1,0:T(8,128)S(1)} %get-tuple-element.58), channel_id=1, source_target_pairs={{0,1},{1,0},{2,3},{3,2},{4,8},{5,9},{6,10},{7,11},{8,4},{9,5},{10,... | collective-permute-start | bytes 122888 | tf_op jit(solution)/shard_map/ppermute | solution.py:484
  10.9 5.5 %collective-permute-start.4 = (f32[176,128]{1,0:T(8,128)S(1)}, f32[176,128]{1,0:T(8,128)S(1)}, u32[]{:S(2)}, u32[]{:S(2)}) collective-permute-start(f32[176,128]{1,0:T(8,128)S(1)} %get-tuple-element.63), channel_id=1, source_target_pairs={{0,4},{4,0},{8,12},{12,8},{16,20},{20,16},{24,28},{28,24},{1,5},{5... | collective-permute-start | bytes 270344 | tf_op jit(solution)/shard_map/ppermute | solution.py:466
  14.3 1.7 %collective-permute-start.5 = (f32[7,24,128]{2,1,0:T(8,128)S(1)}, f32[7,24,128]{2,1,0:T(8,128)S(1)}, u32[]{:S(2)}, u32[]{:S(2)}) collective-permute-start(f32[7,24,128]{2,1,0:T(8,128)S(1)} %get-tuple-element.62.refs_2_.refs_0_.refs_6_), channel_id=1, source_target_pairs={{0,1},{1,0},{2,3},{3,2},{4,5},{5,4},{6,7},{7,6},{8,9},{9,8},{10,11... | collective-permute-start | bytes 258056 | tf_op jit(solution)/shard_map/ppermute | solution.py:466
  16.4 6.9 %collective-permute-start.6 = (f32[176,128]{1,0:T(8,128)S(1)}, f32[176,128]{1,0:T(8,128)S(1)}, u32[]{:S(2)}, u32[]{:S(2)}) collective-permute-start(f32[176,128]{1,0:T(8,128)S(1)} %get-tuple-element.66), channel_id=1, source_target_pairs={{0,8},{4,12},{8,0},{12,4},{16,24},{20,28},{24,16},{28,20},{1,9},{5... | collective-permute-start | bytes 270344 | tf_op jit(solution)/shard_map/ppermute | solution.py:466
  19.7 8.0 %collective-permute-start.7 = (f32[72,128]{1,0:T(8,128)S(1)}, f32[72,128]{1,0:T(8,128)S(1)}, u32[]{:S(2)}, u32[]{:S(2)}) collective-permute-start(f32[72,128]{1,0:T(8,128)S(1)} %get-tuple-element.71), channel_id=1, source_target_pairs={{0,2},{1,3},{2,0},{3,1},{4,6},{5,7},{6,4},{7,5},{8,10},{9,11},{10,... | collective-permute-start | bytes 110600 | tf_op jit(solution)/shard_map/ppermute | solution.py:466
  22.1 0.7 %copy-start.1 = (s32[1,4,1]{1,2,0:T(1,128)S(1)}, s32[1,4,1]{1,2,0:T(1,128)}, u32[]{:S(2)}) copy-start(s32[1,4,1]{1,2,0:T(1,128)} %param.3) | copy-start | bytes 52
  23.4 4.9 %collective-permute-start.8 = (f32[72,128]{1,0:T(8,128)S(1)}, f32[72,128]{1,0:T(8,128)S(1)}, u32[]{:S(2)}, u32[]{:S(2)}) collective-permute-start(f32[72,128]{1,0:T(8,128)S(1)} %get-tuple-element.77), channel_id=1, source_target_pairs={{0,16},{4,20},{8,24},{12,28},{16,0},{20,4},{24,8},{28,12},{1,17},{... | collective-permute-start | bytes 110600 | tf_op jit(solution)/shard_map/ppermute | solution.py:466
  28.9 4.9 %collective-permute-start.9 = (f32[7,32,128]{2,1,0:T(8,128)S(1)}, f32[7,32,128]{2,1,0:T(8,128)S(1)}, u32[]{:S(2)}, u32[]{:S(2)}) collective-permute-start(f32[7,32,128]{2,1,0:T(8,128)S(1)} %get-tuple-element.84.refs_2_.refs_0_.refs_5_), channel_id=1, source_target_pairs={{0,4},{4,0},{8,12},{12,8},{16,20},{20,16},{24,28},{28,24},{1,5},{5... | collective-permute-start | bytes 344072 | tf_op jit(solution)/shard_map/ppermute | solution.py:466
  29.9 1.5 %collective-permute-start.10 = (f32[7,16,128]{2,1,0:T(8,128)S(1)}, f32[7,16,128]{2,1,0:T(8,128)S(1)}, u32[]{:S(2)}, u32[]{:S(2)}) collective-permute-start(f32[7,16,128]{2,1,0:T(8,128)S(1)} %get-tuple-element.85.refs_2_.refs_0_.refs_5_), channel_id=1, source_target_pairs={{0,1},{1,0},{2,3},{3,2},{4,5},{5,4},{6,7},{7,6},{8,9},{9,8},{10,11... | collective-permute-start | bytes 172040 | tf_op jit(solution)/shard_map/ppermute | solution.py:466
  33.8 4.9 %collective-permute-start.12 = (f32[7,32,128]{2,1,0:T(8,128)S(1)}, f32[7,32,128]{2,1,0:T(8,128)S(1)}, u32[]{:S(2)}, u32[]{:S(2)}) collective-permute-start(f32[7,32,128]{2,1,0:T(8,128)S(1)} %shard_map.57.refs_2_.refs_0_.refs_7_), channel_id=1, source_target_pairs={{0,8},{4,12},{8,0},{12,4},{16,24},{20,28},{24,16},{28,20},{1,9},{5... | collective-permute-start | bytes 344072 | tf_op jit(solution)/shard_map/ppermute | solution.py:466
  38.7 7.4 %collective-permute-start.13 = (f32[96,128]{1,0:T(8,128)S(1)}, f32[96,128]{1,0:T(8,128)S(1)}, u32[]{:S(2)}, u32[]{:S(2)}) collective-permute-start(f32[96,128]{1,0:T(8,128)S(1)} %get-tuple-element.95), channel_id=1, source_target_pairs={{0,16},{4,20},{8,24},{12,28},{16,0},{20,4},{24,8},{28,12},{1,17},{... | collective-permute-start | bytes 147464 | tf_op jit(solution)/shard_map/ppermute | solution.py:466
  41.9 3.8 %collective-permute-start.11 = (f32[48,128]{1,0:T(8,128)S(1)}, f32[48,128]{1,0:T(8,128)S(1)}, u32[]{:S(2)}, u32[]{:S(2)}) collective-permute-start(f32[48,128]{1,0:T(8,128)S(1)} %get-tuple-element.90), channel_id=1, source_target_pairs={{0,2},{1,3},{2,0},{3,1},{4,6},{5,7},{6,4},{7,5},{8,10},{9,11},{10,... | collective-permute-start | bytes 73736 | tf_op jit(solution)/shard_map/ppermute | solution.py:466
  46.2 10.3 %collective-permute-start.17 = (f32[520,128]{1,0:T(8,128)S(1)}, f32[520,128]{1,0:T(8,128)S(1)}, u32[]{:S(2)}, u32[]{:S(2)}) collective-permute-start(f32[520,128]{1,0:T(8,128)S(1)} %shard_map.61.refs_0_.refs_4_), channel_id=1, source_target_pairs={{0,16},{4,20},{8,24},{12,28},{16,0},{20,4},{24,8},{28,12},{1,17},{... | collective-permute-start | bytes 798728 | tf_op jit(solution)/shard_map/ppermute | solution.py:466
  47.9 11.7 %collective-permute-start.14 = (f32[2,128,128]{2,1,0:T(8,128)S(1)}, f32[2,128,128]{2,1,0:T(8,128)S(1)}, u32[]{:S(2)}, u32[]{:S(2)}) collective-permute-start(f32[2,128,128]{2,1,0:T(8,128)S(1)} %get-tuple-element.97), channel_id=1, source_target_pairs={{0,12},{4,8},{8,4},{12,0},{16,28},{20,24},{24,20},{28,16},{1,13},{... | collective-permute-start | bytes 393224 | tf_op jit(solution)/shard_map/ppermute | solution.py:466
  48.0 12.3 %collective-permute-start.15 = (f32[2,128,128]{2,1,0:T(8,128)S(1)}, f32[2,128,128]{2,1,0:T(8,128)S(1)}, u32[]{:S(2)}, u32[]{:S(2)}) collective-permute-start(f32[2,128,128]{2,1,0:T(8,128)S(1)} %get-tuple-element.98), channel_id=1, source_target_pairs={{0,8},{4,12},{8,0},{12,4},{16,24},{20,28},{24,16},{28,20},{1,9},{5... | collective-permute-start | bytes 393224 | tf_op jit(solution)/shard_map/ppermute | solution.py:466
  51.5 8.8 %collective-permute-start.16 = (f32[2,128,128]{2,1,0:T(8,128)S(1)}, f32[2,128,128]{2,1,0:T(8,128)S(1)}, u32[]{:S(2)}, u32[]{:S(2)}) collective-permute-start(f32[2,128,128]{2,1,0:T(8,128)S(1)} %get-tuple-element.99), channel_id=1, source_target_pairs={{0,4},{4,0},{8,12},{12,8},{16,20},{20,16},{24,28},{28,24},{1,5},{5... | collective-permute-start | bytes 393224 | tf_op jit(solution)/shard_map/ppermute | solution.py:466
  56.7 6.1 %collective-permute-start.18 = (f32[2,128,128]{2,1,0:T(8,128)S(1)}, f32[2,128,128]{2,1,0:T(8,128)S(1)}, u32[]{:S(2)}, u32[]{:S(2)}) collective-permute-start(f32[2,128,128]{2,1,0:T(8,128)S(1)} %get-tuple-element.102), channel_id=1, source_target_pairs={{0,12},{4,8},{8,4},{12,0},{16,28},{20,24},{24,20},{28,16},{1,13},{... | collective-permute-start | bytes 393224 | tf_op jit(solution)/shard_map/ppermute | solution.py:466
  56.8 7.8 %collective-permute-start.19 = (f32[2,128,128]{2,1,0:T(8,128)S(1)}, f32[2,128,128]{2,1,0:T(8,128)S(1)}, u32[]{:S(2)}, u32[]{:S(2)}) collective-permute-start(f32[2,128,128]{2,1,0:T(8,128)S(1)} %get-tuple-element.103), channel_id=1, source_target_pairs={{0,8},{4,12},{8,0},{12,4},{16,24},{20,28},{24,16},{28,20},{1,9},{5... | collective-permute-start | bytes 393224 | tf_op jit(solution)/shard_map/ppermute | solution.py:466
  59.6 5.2 %collective-permute-start.20 = (f32[2,128,128]{2,1,0:T(8,128)S(1)}, f32[2,128,128]{2,1,0:T(8,128)S(1)}, u32[]{:S(2)}, u32[]{:S(2)}) collective-permute-start(f32[2,128,128]{2,1,0:T(8,128)S(1)} %get-tuple-element.104), channel_id=1, source_target_pairs={{0,4},{4,0},{8,12},{12,8},{16,20},{20,16},{24,28},{28,24},{1,5},{5... | collective-permute-start | bytes 393224 | tf_op jit(solution)/shard_map/ppermute | solution.py:466
